TPU v7x, 32 devices: a whole 2x2x4 slice. The times are simulated.
32 devices in a mesh: groups: 2 (over x), ctx: 16 (over z, y, core).
Axes of the slice: x: 2, y: 2, z: 4, core: 2. Of those that a mesh axis runs over, the one named last changes fastest.
Arguments:
- queries: bfloat16 [8192, 1024], P(('groups', 'ctx')), parts along dimension 0, may hold values from -5 to 5
- keys: bfloat16 [8192, 1024], P(('groups', 'ctx')), parts along dimension 0, may hold values from -5 to 5
- values: bfloat16 [8192, 1024], P(('groups', 'ctx')), parts along dimension 0, may hold values from -5 to 5
- grad_self: bfloat16 [8192, 1024], P(('groups', 'ctx')), parts along dimension 0, may hold values from -5 to 5
- doc_ids: int32 [8192], P('groups'), parts along dimension 0, may hold values from 0 to 31, never falling along the last dimension, each value on 1 to 512 neighbouring positions
- cross_queries: bfloat16 [8192, 1024], P(('groups', 'ctx')), parts along dimension 0, may hold values from -5 to 5
- grad_cross: bfloat16 [8192, 1024], P(('groups', 'ctx')), parts along dimension 0, may hold values from -5 to 5
- pool_kv: bfloat16 [2, 64, 128, 1024], P(None, ('groups', 'ctx')), parts along dimension 1, may hold values from -5 to 5
- neighbour_ids: int32 [128, 2], P(('groups', 'ctx')), parts along dimension 0, may hold values from 0 to 31, as said below
Outputs:
- grad_queries: bfloat16 [8192, 1024], P(('groups', 'ctx')), parts along dimension 0
- grad_keys: bfloat16 [8192, 1024], P(('groups', 'ctx')), parts along dimension 0
- grad_values: bfloat16 [8192, 1024], P(('groups', 'ctx')), parts along dimension 0
- grad_cross_queries: bfloat16 [8192, 1024], P(('groups', 'ctx')), parts along dimension 0
- grad_pool: bfloat16 [2, 64, 128, 1024], P(None, ('groups', 'ctx')), parts along dimension 1
There are 2 independent parts, one for each index of `groups`. A program takes and returns all parts, laid end to end along the dimension named above; each array names one. Nothing has to cross between parts.
Inputs may be any that keep to these rules, and one draw needn't show every extreme that they name: `doc_ids`: document numbers never fall along the tokens; a document spans 1 to 512 tokens. `neighbour_ids`: encoding e is owned by device e // 2 of the loop; the encodings of stretch c are owned by the device holding stretch c (c // 4) or by one of the two devices beside it on the loop, which wraps around.
All inputs are finite; a program needn't handle non-finite values.
Results may differ from a plain program's by a relative error of at most 0.0086.
Values may be sent and summed in bfloat16 or wider, within the bound.
No kernel may reach another device: no remote copies, remote signals or barrier semaphores. Data moves between devices by JAX's collectives and lax.ppermute only.
A program may use at most 128 MiB of HBM per device.

v0:
```python
import functools
import math

import jax
import jax.numpy as jnp
from jax import lax
from jax.experimental import pallas as pl
from jax.experimental.pallas import tpu as pltpu
from jax.sharding import PartitionSpec as P

HEADS = 8
HEAD_DIM = 128
STRETCH = 64
NBRS = 2
NBR_TOK = 128
REACH = 2
FACTOR = HEAD_DIM ** (-0.5)
MASKED = -1e30


def pairs_to(axis, steps, wrap=False, parity=None):
    count = lax.axis_size(axis)
    pairs = []
    for source in range(count):
        target = source + steps
        if parity is not None and source % 2 != parity:
            continue
        if wrap:
            pairs.append((source, target % count))
        elif 0 <= target < count:
            pairs.append((source, target))
    return pairs


def send(value, steps, wrap=False, parity=None):
    return lax.ppermute(value, "ctx", pairs_to("ctx", steps, wrap, parity))


def attend(bias, q, g, k, v):
    f32 = jnp.float32
    last = (((1,), (1,)), ((), ()))
    s = lax.dot_general(k, q, last, preferred_element_type=f32) * FACTOR + bias
    peak = jnp.max(s, axis=0, keepdims=True)
    e = jnp.exp(s - peak)
    p = e * (1.0 / jnp.sum(e, axis=0, keepdims=True))
    pb = p.astype(jnp.bfloat16)
    dp = lax.dot_general(v, g, last, preferred_element_type=f32)
    delta = jnp.sum(pb.astype(f32) * dp, axis=0, keepdims=True)
    ds = (p * (dp - delta)).astype(jnp.bfloat16)
    dv = jnp.dot(pb, g, preferred_element_type=f32)
    dk = jnp.dot(ds, q, preferred_element_type=f32) * FACTOR
    first = (((0,), (0,)), ((), ()))
    dq = lax.dot_general(ds, k, first, preferred_element_type=f32) * FACTOR
    return dq, dk, dv


def store(refs, dk, dv):
    rows = dk.shape[0] // len(refs)
    for index, ref in enumerate(refs):
        ref[0] = dk[index * rows : (index + 1) * rows].astype(jnp.bfloat16)
        ref[1] = dv[index * rows : (index + 1) * rows].astype(jnp.bfloat16)


def self_kernel(
    bias, q, g, k2a, k2b, k1, k0, v2a, v2b, v1, v0, dq_ref, kv2, kv1, kv0
):
    k = jnp.concatenate([k2a[...] + k2b[...], k1[...], k0[...]], axis=0)
    v = jnp.concatenate([v2a[...] + v2b[...], v1[...], v0[...]], axis=0)
    dq, dk, dv = attend(bias[...], q[...], g[...], k, v)
    dq_ref[...] = dq.astype(jnp.bfloat16)
    store((kv2, kv1, kv0), dk, dv)


def cross_kernel(bias, q, g, low, own, high, dq_ref, kv_low, kv_own, kv_high):
    k = jnp.concatenate([low[0], own[0], high[0]], axis=0)
    v = jnp.concatenate([low[1], own[1], high[1]], axis=0)
    dq, dk, dv = attend(bias[...], q[...], g[...], k, v)
    dq_ref[...] = dq.astype(jnp.bfloat16)
    store((kv_low, kv_own, kv_high), dk, dv)


def attention_call(kernel, name, bias, rows_in, pairs_in):
    rows, width = rows_in[0].shape
    keys = bias.shape[0]
    part = keys // 3
    row_spec = lambda r: pl.BlockSpec((r, HEAD_DIM), lambda h: (0, h))
    pair_spec = lambda r: pl.BlockSpec((2, r, HEAD_DIM), lambda h: (0, 0, h))
    bf16 = jnp.bfloat16
    return pl.pallas_call(
        kernel,
        name=name,
        grid=(width // HEAD_DIM,),
        in_specs=[pl.BlockSpec(bias.shape, lambda h: (0, 0))]
        + [row_spec(x.shape[0]) for x in rows_in]
        + [pair_spec(x.shape[1]) for x in pairs_in],
        out_specs=[row_spec(rows)] + [pair_spec(part)] * 3,
        out_shape=[jax.ShapeDtypeStruct((rows, width), bf16)]
        + [jax.ShapeDtypeStruct((2, part, width), bf16)] * 3,
        compiler_params=pltpu.CompilerParams(vmem_limit_bytes=40 << 20),
        cost_estimate=pl.CostEstimate(
            flops=10 * rows * keys * width,
            transcendentals=rows * keys * (width // HEAD_DIM),
            bytes_accessed=2 * width * (4 * rows + 8 * keys),
        ),
    )(bias, *rows_in, *pairs_in)


def body(
    queries, keys, values, grad_self, doc_ids, cross_queries, grad_cross, pool_kv, neighbour_ids
):
    f32 = jnp.float32
    tok_rows, width = queries.shape
    loop_size = lax.axis_size("ctx")
    my_index = lax.axis_index("ctx")
    enc_dev = pool_kv.shape[1]
    pool = pool_kv.reshape(2, enc_dev * NBR_TOK, width)

    low = send(pool, 1, wrap=True)
    high = send(pool, -1, wrap=True)
    k1, v1 = send((keys, values), 1)
    k2a, v2a = send((keys, values), 2, parity=0)
    k2b, v2b = send((k1, v1), 1, parity=0)

    window = (REACH + 1) * tok_rows
    padded_ids = jnp.pad(doc_ids, (REACH * tok_rows, 0), constant_values=-1)
    first_row = my_index * tok_rows
    query_ids = lax.dynamic_slice_in_dim(doc_ids, first_row, tok_rows, 0)
    key_ids = lax.dynamic_slice_in_dim(padded_ids, first_row, window, 0)
    row_pos = jnp.arange(tok_rows, dtype=jnp.int32)[None, :]
    col_pos = jnp.arange(window, dtype=jnp.int32)[:, None] - REACH * tok_rows
    allowed = (col_pos <= row_pos) & (key_ids[:, None] == query_ids[None, :])
    self_bias = jnp.where(allowed, 0.0, MASKED).astype(f32)

    relative = (neighbour_ids // enc_dev - my_index + 1) % loop_size
    local_ids = relative * enc_dev + neighbour_ids % enc_dev
    slots = jnp.arange(3 * enc_dev, dtype=jnp.int32)
    times = jnp.sum((local_ids[None] == slots[:, None, None]).astype(jnp.int32), axis=2)
    small = jnp.where(times == 0, MASKED, jnp.where(times == 1, 0.0, math.log(2.0))).astype(f32)
    cross_bias = jnp.repeat(jnp.repeat(small, NBR_TOK, axis=0), STRETCH, axis=1)

    grad_cq, pool_low, pool_own, pool_high = attention_call(
        cross_kernel, "cross_attention", cross_bias, (cross_queries, grad_cross), (low, pool, high)
    )
    back_low = send(pool_low, -1, wrap=True)
    back_high = send(pool_high, 1, wrap=True)

    grad_q, part2, part1, part0 = attention_call(
        self_kernel,
        "self_attention",
        self_bias,
        (queries, grad_self, k2a, k2b, k1, keys, v2a, v2b, v1, values),
        (),
    )
    from2 = send(part2, -2, parity=0)
    odd2 = send(part2, -1, parity=1)
    part1 = (part1.astype(f32) + odd2.astype(f32)).astype(jnp.bfloat16)
    from1 = send(part1, -1)

    grad_pool = (pool_own.astype(f32) + back_low.astype(f32) + back_high.astype(f32)).astype(
        jnp.bfloat16
    )
    total = part0.astype(f32) + from1.astype(f32) + from2.astype(f32)
    return (
        grad_q,
        total[0].astype(jnp.bfloat16),
        total[1].astype(jnp.bfloat16),
        grad_cq,
        grad_pool.reshape(pool_kv.shape),
    )


def solution(mesh):
    rows = P(("groups", "ctx"), None)
    pool = P(None, ("groups", "ctx"), None, None)
    return jax.shard_map(
        body,
        mesh=mesh,
        in_specs=(rows, rows, rows, rows, P("groups"), rows, rows, pool, rows),
        out_specs=(rows, rows, rows, rows, pool),
        check_vma=False,
    )
```

profile of v0, /device:TPU:1, one launch (start us, length us, event | category | flops | bytes accessed | tf_op | source)
XLA Modules:
  0.0 132.8 jit_solution(11476330874356638592)
XLA Ops:
  0.6 4.5 %collective-permute-start.1 = (bf16[256,1024]{1,0:T(8,128)(2,1)}, bf16[256,1024]{1,0:T(8,128)(2,1)S(1)}, u32[]{:S(2)}, u32[]{:S(2)}) collective-permute-start(bf16[256,1024]{1,0:T(8,128)(2,1)} %k0.1), channel_id=1, source_target_pairs={{0,1},{1,2},{2,3},{3,4},{4,5},{5,6},{6,7},{7,8},{8,9},{9,10},{10,1... | collective-permute-start | bytes 1572872 | tf_op jit(solution)/shard_map/ppermute | solution.py:36
  5.2 1.9 %collective-permute-start.4 = (bf16[256,1024]{1,0:T(8,128)(2,1)}, bf16[256,1024]{1,0:T(8,128)(2,1)S(1)}, u32[]{:S(2)}, u32[]{:S(2)}) collective-permute-start(bf16[256,1024]{1,0:T(8,128)(2,1)} %v0.1), channel_id=1, source_target_pairs={{0,1},{1,2},{2,3},{3,4},{4,5},{5,6},{6,7},{7,8},{8,9},{9,10},{10,1... | collective-permute-start | bytes 1572872 | tf_op jit(solution)/shard_map/ppermute | solution.py:36
  8.5 3.1 %collective-permute-done.1.k1 = bf16[256,1024]{1,0:T(8,128)(2,1)S(1)} collective-permute-done((bf16[256,1024]{1,0:T(8,128)(2,1)}, bf16[256,1024]{1,0:T(8,128)(2,1)S(1)}, u32[]{:S(2)}, u32[]{:S(2)}) %collective-permute-start.1) | collective-permute-done | bytes 524320 | tf_op jit(solution)/shard_map/ppermute | solution.py:36
  11.6 1.3 collective-permute-start.2
  12.9 9.4 %collective-permute-done.4.v1 = bf16[256,1024]{1,0:T(8,128)(2,1)S(1)} collective-permute-done((bf16[256,1024]{1,0:T(8,128)(2,1)}, bf16[256,1024]{1,0:T(8,128)(2,1)S(1)}, u32[]{:S(2)}, u32[]{:S(2)}) %collective-permute-start.4) | collective-permute-done | bytes 524320 | tf_op jit(solution)/shard_map/ppermute | solution.py:36
  22.3 1.3 collective-permute-start.5
  23.6 1.2 collective-permute-start.10
  26.4 1.3 collective-permute-start.9
  30.3 1.0 copy-done.1
  31.4 1.0 copy-done.2
  33.5 1.0 copy-done.4
  34.5 1.0 copy-done.8
  35.5 1.0 copy-done.10
  38.7 11.6 %self_attention.1 = (bf16[256,1024]{1,0:T(8,128)(2,1)}, bf16[2,256,1024]{2,1,0:T(8,128)(2,1)}, bf16[2,256,1024]{2,1,0:T(8,128)(2,1)S(1)}, bf16[2,256,1024]{2,1,0:T(8,128)(2,1)S(1)}) custom-call(f32[768,256]{1,0:T(8,128)S(1)} %fusion.1.bias, bf16[256,1024]{1,0:T(8,128)(2,1)S(1)} %copy-done.1, bf16[256,1024]{1,0:T(8,128)(2,1)S(1)} %copy-done.2, ...), custom_call_target="tpu_custom_call" | custom-call | flops 2013265920 | bytes 14680064 | tf_op jit(solution)/shard_map/self_attention/pallas_call | solution.py:89
  50.2 15.4 %collective-permute-start.6 = (bf16[2,256,1024]{2,1,0:T(8,128)(2,1)}, bf16[2,256,1024]{2,1,0:T(8,128)(2,1)}, u32[]{:S(2)}, u32[]{:S(2)}) collective-permute-start(bf16[2,256,1024]{2,1,0:T(8,128)(2,1)} %get-tuple-element.16), channel_id=1, source_target_pairs={{1,0},{3,2},{5,4},{7,6},{9,8},{11,10},{13,12},{15,14},{17,16},{19,... | collective-permute-start | bytes 3145736 | tf_op jit(solution)/shard_map/ppermute | solution.py:36
  66.8 1.4 %copy.19.bias = f32[768,256]{1,0:T(8,128)S(1)} copy(f32[768,256]{0,1:T(8,128)} %bitcast.17) | data formatting | bytes 1572864 | tf_op jit(solution)/shard_map/reshape | solution.py:139
  68.2 1.2 copy-done
  70.5 11.8 %cross_attention.1 = (bf16[256,1024]{1,0:T(8,128)(2,1)}, bf16[2,256,1024]{2,1,0:T(8,128)(2,1)S(1)}, bf16[2,256,1024]{2,1,0:T(8,128)(2,1)S(1)}, bf16[2,256,1024]{2,1,0:T(8,128)(2,1)S(1)}) custom-call(f32[768,256]{1,0:T(8,128)S(1)} %copy.19.bias, bf16[256,1024]{1,0:T(8,128)(2,1)S(1)} %copy-done.5, bf16[256,1024]{1,0:T(8,128)(2,1)S(1)} %copy-done.6, ...), custom_call_target="tpu_custom_call" | custom-call | flops 2013265920 | bytes 14680064 | tf_op jit(solution)/shard_map/cross_attention/pallas_call | solution.py:89
  82.3 1.7 %collective-permute-start.12 = (bf16[2,256,1024]{2,1,0:T(8,128)(2,1)S(1)}, bf16[2,256,1024]{2,1,0:T(8,128)(2,1)S(1)}, u32[]{:S(2)}, u32[]{:S(2)}) collective-permute-start(bf16[2,256,1024]{2,1,0:T(8,128)(2,1)S(1)} %get-tuple-element.20), channel_id=1, source_target_pairs={{0,1},{1,2},{2,3},{3,4},{4,5},{5,6},{6,7},{7,8},{8,9},{9,10},{10,1... | collective-permute-start | bytes 3145736 | tf_op jit(solution)/shard_map/ppermute | solution.py:36
  84.8 1.6 %add_convert_fusion.2 = bf16[2,256,1024]{2,1,0:T(8,128)(2,1)S(1)} fusion(bf16[2,256,1024]{2,1,0:T(8,128)(2,1)} %collective-permute-done.6, bf16[2,256,1024]{2,1,0:T(8,128)(2,1)S(1)} %get-tuple-element.15), kind=kLoop, calls=%fused_computation.2 | loop fusion | flops 2097152 | bytes 3145728 | tf_op jit(solution)/shard_map/convert_element_type | solution.py:156
  86.4 8.6 %collective-permute-start.7 = (bf16[2,256,1024]{2,1,0:T(8,128)(2,1)S(1)}, bf16[2,256,1024]{2,1,0:T(8,128)(2,1)S(1)}, u32[]{:S(2)}, u32[]{:S(2)}) collective-permute-start(bf16[2,256,1024]{2,1,0:T(8,128)(2,1)S(1)} %add_convert_fusion.2), channel_id=1, source_target_pairs={{1,0},{2,1},{3,2},{4,3},{5,4},{6,5},{7,6},{8,7},{9,8},{10,9},{11,1... | collective-permute-start | bytes 3145736 | tf_op jit(solution)/shard_map/ppermute | solution.py:36
  95.1 12.7 %collective-permute-done.11 = bf16[2,256,1024]{2,1,0:T(8,128)(2,1)S(1)} collective-permute-done((bf16[2,256,1024]{2,1,0:T(8,128)(2,1)S(1)}, bf16[2,256,1024]{2,1,0:T(8,128)(2,1)S(1)}, u32[]{:S(2)}, u32[]{:S(2)}) %collective-permute-start.11) | collective-permute-done | bytes 1048608 | tf_op jit(solution)/shard_map/ppermute | solution.py:36
  107.8 21.7 %collective-permute-done.12 = bf16[2,256,1024]{2,1,0:T(8,128)(2,1)S(1)} collective-permute-done((bf16[2,256,1024]{2,1,0:T(8,128)(2,1)S(1)}, bf16[2,256,1024]{2,1,0:T(8,128)(2,1)S(1)}, u32[]{:S(2)}, u32[]{:S(2)}) %collective-permute-start.12) | collective-permute-done | bytes 1048608 | tf_op jit(solution)/shard_map/ppermute | solution.py:36
  129.5 1.6 %add_convert_fusion = bf16[2,256,1024]{2,1,0:T(8,128)(2,1)} fusion(bf16[2,256,1024]{2,1,0:T(8,128)(2,1)S(1)} %collective-permute-done.12, bf16[2,256,1024]{2,1,0:T(8,128)(2,1)S(1)} %collective-permute-done.11, bf16[2,256,1024]{2,1,0:T(8,128)(2,1)S(1)} %get-tuple-element.18), kind=kLoop, calls=%fused_computation | loop fusion | flops 3145728 | bytes 4194304 | tf_op jit(solution)/shard_map/convert_element_type | solution.py:159
  (50 shorter events, 13.3 us)
Async XLA Ops:
  0.6 11.0 %collective-permute-start.1 = (bf16[256,1024]{1,0:T(8,128)(2,1)}, bf16[256,1024]{1,0:T(8,128)(2,1)S(1)}, u32[]{:S(2)}, u32[]{:S(2)}) collective-permute-start(bf16[256,1024]{1,0:T(8,128)(2,1)} %k0.1), channel_id=1, source_target_pairs={{0,1},{1,2},{2,3},{3,4},{4,5},{5,6},{6,7},{7,8},{8,9},{9,10},{10,1... | collective-permute-start | bytes 1572872 | tf_op jit(solution)/shard_map/ppermute | solution.py:36
  5.2 17.2 %collective-permute-start.4 = (bf16[256,1024]{1,0:T(8,128)(2,1)}, bf16[256,1024]{1,0:T(8,128)(2,1)S(1)}, u32[]{:S(2)}, u32[]{:S(2)}) collective-permute-start(bf16[256,1024]{1,0:T(8,128)(2,1)} %v0.1), channel_id=1, source_target_pairs={{0,1},{1,2},{2,3},{3,4},{4,5},{5,6},{6,7},{7,8},{8,9},{9,10},{10,1... | collective-permute-start | bytes 1572872 | tf_op jit(solution)/shard_map/ppermute | solution.py:36
  7.1 19.3 %collective-permute-start = (bf16[256,1024]{1,0:T(8,128)(2,1)}, bf16[256,1024]{1,0:T(8,128)(2,1)S(1)}, u32[]{:S(2)}, u32[]{:S(2)}) collective-permute-start(bf16[256,1024]{1,0:T(8,128)(2,1)} %k0.1), channel_id=1, source_target_pairs={{0,2},{2,4},{4,6},{6,8},{8,10},{10,12},{12,14},{16,18},{18,20},{20... | collective-permute-start | bytes 1572872 | tf_op jit(solution)/shard_map/ppermute | solution.py:36
  7.8 20.1 %collective-permute-start.3 = (bf16[256,1024]{1,0:T(8,128)(2,1)}, bf16[256,1024]{1,0:T(8,128)(2,1)S(1)}, u32[]{:S(2)}, u32[]{:S(2)}) collective-permute-start(bf16[256,1024]{1,0:T(8,128)(2,1)} %v0.1), channel_id=1, source_target_pairs={{0,2},{2,4},{4,6},{6,8},{8,10},{10,12},{12,14},{16,18},{18,20},{20... | collective-permute-start | bytes 1572872 | tf_op jit(solution)/shard_map/ppermute | solution.py:36
  11.6 17.1 %collective-permute-start.2 = (bf16[256,1024]{1,0:T(8,128)(2,1)S(1)}, bf16[256,1024]{1,0:T(8,128)(2,1)S(1)}, u32[]{:S(2)}, u32[]{:S(2)}) collective-permute-start(bf16[256,1024]{1,0:T(8,128)(2,1)S(1)} %collective-permute-done.1.k1), channel_id=1, source_target_pairs={{0,1},{2,3},{4,5},{6,7},{8,9},{10,11},{12,13},{14,15},{16,17},{18,... | collective-permute-start | bytes 1572872 | tf_op jit(solution)/shard_map/ppermute | solution.py:36
  22.3 7.2 %collective-permute-start.5 = (bf16[256,1024]{1,0:T(8,128)(2,1)S(1)}, bf16[256,1024]{1,0:T(8,128)(2,1)S(1)}, u32[]{:S(2)}, u32[]{:S(2)}) collective-permute-start(bf16[256,1024]{1,0:T(8,128)(2,1)S(1)} %collective-permute-done.4.v1), channel_id=1, source_target_pairs={{0,1},{2,3},{4,5},{6,7},{8,9},{10,11},{12,13},{14,15},{16,17},{18,... | collective-permute-start | bytes 1572872 | tf_op jit(solution)/shard_map/ppermute | solution.py:36
  23.6 44.6 %collective-permute-start.10 = (bf16[2,256,1024]{2,1,0:T(8,128)(2,1)}, bf16[2,256,1024]{2,1,0:T(8,128)(2,1)}, u32[]{:S(2)}, u32[]{:S(2)}) collective-permute-start(bf16[2,256,1024]{2,1,0:T(8,128)(2,1)} %bitcast.14), channel_id=1, source_target_pairs={{0,15},{1,0},{2,1},{3,2},{4,3},{5,4},{6,5},{7,6},{8,7},{9,8},{10,9... | collective-permute-start | bytes 3145736 | tf_op jit(solution)/shard_map/ppermute | solution.py:36
  26.4 2.4 %copy-start.7 = (bf16[256,1024]{1,0:T(8,128)(2,1)}, bf16[256,1024]{1,0:T(8,128)(2,1)S(1)}, u32[]{:S(2)}) copy-start(bf16[256,1024]{1,0:T(8,128)(2,1)S(1)} %collective-permute-done.k2a) | copy-start | bytes 1572868
  26.4 41.8 %collective-permute-start.9 = (bf16[2,256,1024]{2,1,0:T(8,128)(2,1)}, bf16[2,256,1024]{2,1,0:T(8,128)(2,1)}, u32[]{:S(2)}, u32[]{:S(2)}) collective-permute-start(bf16[2,256,1024]{2,1,0:T(8,128)(2,1)} %bitcast.15), channel_id=1, source_target_pairs={{0,1},{1,2},{2,3},{3,4},{4,5},{5,6},{6,7},{7,8},{8,9},{9,10},{10,1... | collective-permute-start | bytes 3145736 | tf_op jit(solution)/shard_map/ppermute | solution.py:36
  27.7 38.0 %copy-start.15 = (s32[4,2]{0,1:T(2,128)S(1)}, s32[4,2]{0,1:T(2,128)}, u32[]{:S(2)}) copy-start(s32[4,2]{0,1:T(2,128)} %param.17) | copy-start | bytes 100
  30.3 1.0 copy-start.1
  31.4 1.0 copy-start.2
  32.4 1.0 copy-start.3
  33.5 1.0 copy-start.4
  34.5 1.0 copy-start.8
  35.5 1.0 copy-start.10
  36.6 1.0 copy-start.12
  50.2 34.5 %collective-permute-start.6 = (bf16[2,256,1024]{2,1,0:T(8,128)(2,1)}, bf16[2,256,1024]{2,1,0:T(8,128)(2,1)}, u32[]{:S(2)}, u32[]{:S(2)}) collective-permute-start(bf16[2,256,1024]{2,1,0:T(8,128)(2,1)} %get-tuple-element.16), channel_id=1, source_target_pairs={{1,0},{3,2},{5,4},{7,6},{9,8},{11,10},{13,12},{15,14},{17,16},{19,... | collective-permute-start | bytes 3145736 | tf_op jit(solution)/shard_map/ppermute | solution.py:36
  65.8 2.4 %copy-start.5 = (bf16[256,1024]{1,0:T(8,128)(2,1)S(1)}, bf16[256,1024]{1,0:T(8,128)(2,1)}, u32[]{:S(2)}) copy-start(bf16[256,1024]{1,0:T(8,128)(2,1)} %q.3) | copy-start | bytes 1572868
  68.2 1.2 copy-start
  82.3 25.5 %collective-permute-start.11 = (bf16[2,256,1024]{2,1,0:T(8,128)(2,1)S(1)}, bf16[2,256,1024]{2,1,0:T(8,128)(2,1)S(1)}, u32[]{:S(2)}, u32[]{:S(2)}) collective-permute-start(bf16[2,256,1024]{2,1,0:T(8,128)(2,1)S(1)} %get-tuple-element.19), channel_id=1, source_target_pairs={{0,15},{1,0},{2,1},{3,2},{4,3},{5,4},{6,5},{7,6},{8,7},{9,8},{10,9... | collective-permute-start | bytes 3145736 | tf_op jit(solution)/shard_map/ppermute | solution.py:36
  82.3 47.2 %collective-permute-start.12 = (bf16[2,256,1024]{2,1,0:T(8,128)(2,1)S(1)}, bf16[2,256,1024]{2,1,0:T(8,128)(2,1)S(1)}, u32[]{:S(2)}, u32[]{:S(2)}) collective-permute-start(bf16[2,256,1024]{2,1,0:T(8,128)(2,1)S(1)} %get-tuple-element.20), channel_id=1, source_target_pairs={{0,1},{1,2},{2,3},{3,4},{4,5},{5,6},{6,7},{7,8},{8,9},{9,10},{10,1... | collective-permute-start | bytes 3145736 | tf_op jit(solution)/shard_map/ppermute | solution.py:36
  84.1 47.1 %collective-permute-start.8 = (bf16[2,256,1024]{2,1,0:T(8,128)(2,1)}, bf16[2,256,1024]{2,1,0:T(8,128)(2,1)S(1)}, u32[]{:S(2)}, u32[]{:S(2)}) collective-permute-start(bf16[2,256,1024]{2,1,0:T(8,128)(2,1)} %get-tuple-element.16), channel_id=1, source_target_pairs={{2,0},{4,2},{6,4},{8,6},{10,8},{12,10},{14,12},{18,16},{20,18},{22... | collective-permute-start | bytes 3145736 | tf_op jit(solution)/shard_map/ppermute | solution.py:36
  86.4 44.7 %collective-permute-start.7 = (bf16[2,256,1024]{2,1,0:T(8,128)(2,1)S(1)}, bf16[2,256,1024]{2,1,0:T(8,128)(2,1)S(1)}, u32[]{:S(2)}, u32[]{:S(2)}) collective-permute-start(bf16[2,256,1024]{2,1,0:T(8,128)(2,1)S(1)} %add_convert_fusion.2), channel_id=1, source_target_pairs={{1,0},{2,1},{3,2},{4,3},{5,4},{6,5},{7,6},{8,7},{9,8},{10,9},{11,1... | collective-permute-start | bytes 3145736 | tf_op jit(solution)/shard_map/ppermute | solution.py:36
  (5 other events, 4.5 us)
where the time goes:
time: 134 us; the launch traced here: 133 us
  waiting for transfers between devices  47 us (35%)
  starting transfers between devices  39.4 us (29%)
  Pallas kernels  23.4 us (17%)
  local copies, waits for them, and re-layouts  17.2 us (13%)
  other arithmetic  5 us (4%)
    ppermute x13, waiting for transfers between devices, send(): return lax.ppermute(value, 'ctx', pairs_to('ctx', steps, wrap, parity))  47 us
    ppermute x13, starting transfers between devices, send(): return lax.ppermute(value, 'ctx', pairs_to('ctx', steps, wrap, parity))  39.4 us
    pallas_call x2, Pallas kernels, attention_call(): pl.pallas_call(kernel, name=name, grid=(width // HEAD_DIM,), in_specs=[pl...  23.4 us
    unnamed x34, local copies, waits for them, and re-layouts  13.1 us
  transfers between devices with their start and end apart: 13, of which 4 were waited for; matrix products, arithmetic and copies ran while one was open for 6% of the time, Pallas kernels for 18%

commit v1 on v0

--- a/solution.py
+++ b/solution.py
@@ -61,11 +61,9 @@
         ref[1] = dv[index * rows : (index + 1) * rows].astype(jnp.bfloat16)
 
 
-def self_kernel(
-    bias, q, g, k2a, k2b, k1, k0, v2a, v2b, v1, v0, dq_ref, kv2, kv1, kv0
-):
-    k = jnp.concatenate([k2a[...] + k2b[...], k1[...], k0[...]], axis=0)
-    v = jnp.concatenate([v2a[...] + v2b[...], v1[...], v0[...]], axis=0)
+def self_kernel(bias, q, g, k0, v0, two_a, two_b, one, dq_ref, kv2, kv1, kv0):
+    k = jnp.concatenate([two_a[0] + two_b[0], one[0], k0[...]], axis=0)
+    v = jnp.concatenate([two_a[1] + two_b[1], one[1], v0[...]], axis=0)
     dq, dk, dv = attend(bias[...], q[...], g[...], k, v)
     dq_ref[...] = dq.astype(jnp.bfloat16)
     store((kv2, kv1, kv0), dk, dv)
@@ -96,9 +94,9 @@
         out_specs=[row_spec(rows)] + [pair_spec(part)] * 3,
         out_shape=[jax.ShapeDtypeStruct((rows, width), bf16)]
         + [jax.ShapeDtypeStruct((2, part, width), bf16)] * 3,
-        compiler_params=pltpu.CompilerParams(vmem_limit_bytes=40 << 20),
+        compiler_params=pltpu.CompilerParams(vmem_limit_bytes=60 << 20),
         cost_estimate=pl.CostEstimate(
-            flops=10 * rows * keys * width,
+            flops=60 * rows * keys * width,
             transcendentals=rows * keys * (width // HEAD_DIM),
             bytes_accessed=2 * width * (4 * rows + 8 * keys),
         ),
@@ -117,9 +115,6 @@
 
     low = send(pool, 1, wrap=True)
     high = send(pool, -1, wrap=True)
-    k1, v1 = send((keys, values), 1)
-    k2a, v2a = send((keys, values), 2, parity=0)
-    k2b, v2b = send((k1, v1), 1, parity=0)
 
     window = (REACH + 1) * tok_rows
     padded_ids = jnp.pad(doc_ids, (REACH * tok_rows, 0), constant_values=-1)
@@ -131,6 +126,7 @@
     allowed = (col_pos <= row_pos) & (key_ids[:, None] == query_ids[None, :])
     self_bias = jnp.where(allowed, 0.0, MASKED).astype(f32)
 
+    neighbour_ids, low, high = lax.optimization_barrier((neighbour_ids, low, high))
     relative = (neighbour_ids // enc_dev - my_index + 1) % loop_size
     local_ids = relative * enc_dev + neighbour_ids % enc_dev
     slots = jnp.arange(3 * enc_dev, dtype=jnp.int32)
@@ -138,27 +134,33 @@
     small = jnp.where(times == 0, MASKED, jnp.where(times == 1, 0.0, math.log(2.0))).astype(f32)
     cross_bias = jnp.repeat(jnp.repeat(small, NBR_TOK, axis=0), STRETCH, axis=1)
 
+    own_kv = jnp.stack([keys, values])
+    one = send(own_kv, 1)
+    two_a = send(own_kv, 2, parity=0)
+    two_b = send(one, 1, parity=0)
+
     grad_cq, pool_low, pool_own, pool_high = attention_call(
         cross_kernel, "cross_attention", cross_bias, (cross_queries, grad_cross), (low, pool, high)
     )
     back_low = send(pool_low, -1, wrap=True)
     back_high = send(pool_high, 1, wrap=True)
 
+    self_bias, pool_own = lax.optimization_barrier((self_bias, pool_own))
     grad_q, part2, part1, part0 = attention_call(
         self_kernel,
         "self_attention",
         self_bias,
-        (queries, grad_self, k2a, k2b, k1, keys, v2a, v2b, v1, values),
-        (),
+        (queries, grad_self, keys, values),
+        (two_a, two_b, one),
     )
     from2 = send(part2, -2, parity=0)
     odd2 = send(part2, -1, parity=1)
     part1 = (part1.astype(f32) + odd2.astype(f32)).astype(jnp.bfloat16)
-    from1 = send(part1, -1)
-
     grad_pool = (pool_own.astype(f32) + back_low.astype(f32) + back_high.astype(f32)).astype(
         jnp.bfloat16
     )
+    part1, grad_pool = lax.optimization_barrier((part1, grad_pool))
+    from1 = send(part1, -1)
     total = part0.astype(f32) + from1.astype(f32) + from2.astype(f32)
     return (
         grad_q,

time: 134 us -> 134 us (level)
  waiting for transfers between devices: 47 us -> 83.3 us
  starting transfers between devices: 39.4 us -> 17.1 us
  local copies, waits for them, and re-layouts: 17.2 us -> 2.43 us
  other arithmetic: 5 us -> 6.55 us
    ppermute x13 -> x10, waiting for transfers between devices: 47 us -> 83.3 us  [send(): return lax.ppermute(value, 'ctx', pairs_to('ctx', steps, wrap, parity))]
    ppermute x13 -> x10, starting transfers between devices: 39.4 us -> 17.1 us  [send(): return lax.ppermute(value, 'ctx', pairs_to('ctx', steps, wrap, parity))]
    unnamed x34 -> x14, local copies, waits for them, and re-layouts: 13.1 us -> 0.1 us
    another operation x1 -> x2, other arithmetic: 0.62 us -> 1.96 us  [the longest x1 1.32 us: body(): own_kv = jnp.stack([keys, values])]
  transfers between devices with their start and end apart: 13 -> 10, of which waited for: 4 -> 5; matrix products, arithmetic and copies ran while one was open for 6% -> 5% of each run, Pallas kernels for 18% -> 17%
where the time goes in v1:
time: 134 us; the launch traced here: 133 us
  waiting for transfers between devices  83.3 us (62%)
  Pallas kernels  22.7 us (17%)
  starting transfers between devices  17.1 us (13%)
  other arithmetic  6.55 us (5%)
  local copies, waits for them, and re-layouts  2.43 us (2%)
    ppermute x10, waiting for transfers between devices, send(): return lax.ppermute(value, 'ctx', pairs_to('ctx', steps, wrap, parity))  83.3 us
    pallas_call x2, Pallas kernels, attention_call(): pl.pallas_call(kernel, name=name, grid=(width // HEAD_DIM,), in_specs=[pl...  22.7 us
    ppermute x10, starting transfers between devices, send(): return lax.ppermute(value, 'ctx', pairs_to('ctx', steps, wrap, parity))  17.1 us
    convert_element_type x1, other arithmetic, body(): (pool_own.astype(f32) + back_low.astype(f32) + back_high.astype(f32)).ast...  2.83 us
  transfers between devices with their start and end apart: 10, of which 5 were waited for; matrix products, arithmetic and copies ran while one was open for 5% of the time, Pallas kernels for 17%

profile of v1, /device:TPU:1, one launch (start us, length us, event | category | flops | bytes accessed | tf_op | source)
XLA Modules:
  0.0 132.7 jit_solution(11608928781417295587)
XLA Ops:
  0.6 2.7 %collective-permute-start = (bf16[2,256,1024]{2,1,0:T(8,128)(2,1)}, bf16[2,256,1024]{2,1,0:T(8,128)(2,1)S(1)}, u32[]{:S(2)}, u32[]{:S(2)}) collective-permute-start(bf16[2,256,1024]{2,1,0:T(8,128)(2,1)} %bitcast.21), channel_id=1, source_target_pairs={{0,1},{1,2},{2,3},{3,4},{4,5},{5,6},{6,7},{7,8},{8,9},{9,10},{10,1... | collective-permute-start | bytes 3145736 | tf_op jit(solution)/shard_map/ppermute | solution.py:36
  3.3 1.3 pad_maximum_fusion
  4.6 3.7 %collective-permute-start.3 = (bf16[2,256,1024]{2,1,0:T(8,128)(2,1)S(1)}, bf16[2,256,1024]{2,1,0:T(8,128)(2,1)}, u32[]{:S(2)}, u32[]{:S(2)}) collective-permute-start(bf16[2,256,1024]{2,1,0:T(8,128)(2,1)S(1)} %pad_maximum_fusion), channel_id=1, source_target_pairs={{0,1},{1,2},{2,3},{3,4},{4,5},{5,6},{6,7},{7,8},{8,9},{9,10},{10,1... | collective-permute-start | bytes 3145736 | tf_op jit(solution)/shard_map/ppermute | solution.py:36
  8.3 1.7 %collective-permute-start.2 = (bf16[2,256,1024]{2,1,0:T(8,128)(2,1)S(1)}, bf16[2,256,1024]{2,1,0:T(8,128)(2,1)}, u32[]{:S(2)}, u32[]{:S(2)}) collective-permute-start(bf16[2,256,1024]{2,1,0:T(8,128)(2,1)S(1)} %pad_maximum_fusion), channel_id=1, source_target_pairs={{0,2},{2,4},{4,6},{6,8},{8,10},{10,12},{12,14},{16,18},{18,20},{20... | collective-permute-start | bytes 3145736 | tf_op jit(solution)/shard_map/ppermute | solution.py:36
  10.1 1.2 fusion.1.bias
  11.3 23.7 %collective-permute-done.low = bf16[2,256,1024]{2,1,0:T(8,128)(2,1)S(1)} collective-permute-done((bf16[2,256,1024]{2,1,0:T(8,128)(2,1)}, bf16[2,256,1024]{2,1,0:T(8,128)(2,1)S(1)}, u32[]{:S(2)}, u32[]{:S(2)}) %collective-permute-start) | collective-permute-done | bytes 1048608 | tf_op jit(solution)/shard_map/ppermute | solution.py:36
  35.0 0.1 convert_reduce_fusion
  35.2 1.2 copy.19.bias
  36.4 12.6 %collective-permute-done.3.one = bf16[2,256,1024]{2,1,0:T(8,128)(2,1)} collective-permute-done((bf16[2,256,1024]{2,1,0:T(8,128)(2,1)S(1)}, bf16[2,256,1024]{2,1,0:T(8,128)(2,1)}, u32[]{:S(2)}, u32[]{:S(2)}) %collective-permute-start.3) | collective-permute-done | bytes 1048608 | tf_op jit(solution)/shard_map/ppermute | solution.py:36
  49.0 1.3 collective-permute-start.4
  50.3 11.2 %cross_attention.1 = (bf16[256,1024]{1,0:T(8,128)(2,1)}, bf16[2,256,1024]{2,1,0:T(8,128)(2,1)}, bf16[2,256,1024]{2,1,0:T(8,128)(2,1)}, bf16[2,256,1024]{2,1,0:T(8,128)(2,1)}) custom-call(f32[768,256]{1,0:T(8,128)} %copy.19.bias, bf16[256,1024]{1,0:T(8,128)(2,1)} %q.2, bf16[256,1024]{1,0:T(8,128)(2,1)} %g.2, bf16[2,256,1024]{2,1,0:T(8,128)(2,1)} %copy-done.5, ...), custom_call_target="tpu_custom_call" | custom-call | flops 12079595520 | bytes 14680064 | tf_op jit(solution)/shard_map/cross_attention/pallas_call | solution.py:87
  61.5 2.1 %collective-permute-start.6 = (bf16[2,256,1024]{2,1,0:T(8,128)(2,1)}, bf16[2,256,1024]{2,1,0:T(8,128)(2,1)S(1)}, u32[]{:S(2)}, u32[]{:S(2)}) collective-permute-start(bf16[2,256,1024]{2,1,0:T(8,128)(2,1)} %get-tuple-element.30), channel_id=1, source_target_pairs={{0,15},{1,0},{2,1},{3,2},{4,3},{5,4},{6,5},{7,6},{8,7},{9,8},{10,9... | collective-permute-start | bytes 3145736 | tf_op jit(solution)/shard_map/ppermute | solution.py:36
  63.6 1.5 %collective-permute-start.7 = (bf16[2,256,1024]{2,1,0:T(8,128)(2,1)}, bf16[2,256,1024]{2,1,0:T(8,128)(2,1)}, u32[]{:S(2)}, u32[]{:S(2)}) collective-permute-start(bf16[2,256,1024]{2,1,0:T(8,128)(2,1)} %get-tuple-element.31), channel_id=1, source_target_pairs={{0,1},{1,2},{2,3},{3,4},{4,5},{5,6},{6,7},{7,8},{8,9},{9,10},{10,1... | collective-permute-start | bytes 3145736 | tf_op jit(solution)/shard_map/ppermute | solution.py:36
  65.1 11.4 %self_attention.1 = (bf16[256,1024]{1,0:T(8,128)(2,1)}, bf16[2,256,1024]{2,1,0:T(8,128)(2,1)}, bf16[2,256,1024]{2,1,0:T(8,128)(2,1)}, bf16[2,256,1024]{2,1,0:T(8,128)(2,1)}) custom-call(f32[768,256]{1,0:T(8,128)} %fusion.1.bias, bf16[256,1024]{1,0:T(8,128)(2,1)} %q.3, bf16[256,1024]{1,0:T(8,128)(2,1)} %g.3, bf16[256,1024]{1,0:T(8,128)(2,1)} %k0.1, ...), custom_call_target="tpu_custom_call" | custom-call | flops 12079595520 | bytes 14680064 | tf_op jit(solution)/shard_map/self_attention/pallas_call | solution.py:87
  76.6 1.5 %collective-permute-start.5 = (bf16[2,256,1024]{2,1,0:T(8,128)(2,1)}, bf16[2,256,1024]{2,1,0:T(8,128)(2,1)S(1)}, u32[]{:S(2)}, u32[]{:S(2)}) collective-permute-start(bf16[2,256,1024]{2,1,0:T(8,128)(2,1)} %get-tuple-element.28), channel_id=1, source_target_pairs={{1,0},{3,2},{5,4},{7,6},{9,8},{11,10},{13,12},{15,14},{17,16},{19,... | collective-permute-start | bytes 3145736 | tf_op jit(solution)/shard_map/ppermute | solution.py:36
  78.1 0.7 collective-permute-start.9
  78.8 10.2 %collective-permute-done.6 = bf16[2,256,1024]{2,1,0:T(8,128)(2,1)S(1)} collective-permute-done((bf16[2,256,1024]{2,1,0:T(8,128)(2,1)}, bf16[2,256,1024]{2,1,0:T(8,128)(2,1)S(1)}, u32[]{:S(2)}, u32[]{:S(2)}) %collective-permute-start.6) | collective-permute-done | bytes 1048608 | tf_op jit(solution)/shard_map/ppermute | solution.py:36
  89.0 21.9 %collective-permute-done.7 = bf16[2,256,1024]{2,1,0:T(8,128)(2,1)} collective-permute-done((bf16[2,256,1024]{2,1,0:T(8,128)(2,1)}, bf16[2,256,1024]{2,1,0:T(8,128)(2,1)}, u32[]{:S(2)}, u32[]{:S(2)}) %collective-permute-start.7) | collective-permute-done | bytes 1048608 | tf_op jit(solution)/shard_map/ppermute | solution.py:36
  110.9 2.8 %add_convert_fusion.1 = bf16[2,256,1024]{2,1,0:T(8,128)(2,1)} fusion(bf16[2,256,1024]{2,1,0:T(8,128)(2,1)} %collective-permute-done.7, bf16[2,256,1024]{2,1,0:T(8,128)(2,1)S(1)} %collective-permute-done.6, bf16[2,256,1024]{2,1,0:T(8,128)(2,1)S(1)} %copy-done.1), kind=kLoop, calls=%fused_computation.1 | loop fusion | flops 3145728 | bytes 4194304 | tf_op jit(solution)/shard_map/convert_element_type | solution.py:159
  113.7 0.4 add_convert_fusion.2
  114.2 1.9 %collective-permute-start.8 = (bf16[2,256,1024]{2,1,0:T(8,128)(2,1)S(1)}, bf16[2,256,1024]{2,1,0:T(8,128)(2,1)S(1)}, u32[]{:S(2)}, u32[]{:S(2)}) collective-permute-start(bf16[2,256,1024]{2,1,0:T(8,128)(2,1)S(1)} %add_convert_fusion.2), channel_id=1, source_target_pairs={{1,0},{2,1},{3,2},{4,3},{5,4},{6,5},{7,6},{8,7},{9,8},{10,9},{11,1... | collective-permute-start | bytes 3145736 | tf_op jit(solution)/shard_map/ppermute | solution.py:36
  116.1 14.9 %collective-permute-done.8 = bf16[2,256,1024]{2,1,0:T(8,128)(2,1)S(1)} collective-permute-done((bf16[2,256,1024]{2,1,0:T(8,128)(2,1)S(1)}, bf16[2,256,1024]{2,1,0:T(8,128)(2,1)S(1)}, u32[]{:S(2)}, u32[]{:S(2)}) %collective-permute-start.8) | collective-permute-done | bytes 1048608 | tf_op jit(solution)/shard_map/ppermute | solution.py:36
  131.0 0.6 add_convert_fusion
  131.7 1.0 slice_bitcast_fusion
  (25 shorter events, 0.4 us)
Async XLA Ops:
  0.6 34.3 %collective-permute-start = (bf16[2,256,1024]{2,1,0:T(8,128)(2,1)}, bf16[2,256,1024]{2,1,0:T(8,128)(2,1)S(1)}, u32[]{:S(2)}, u32[]{:S(2)}) collective-permute-start(bf16[2,256,1024]{2,1,0:T(8,128)(2,1)} %bitcast.21), channel_id=1, source_target_pairs={{0,1},{1,2},{2,3},{3,4},{4,5},{5,6},{6,7},{7,8},{8,9},{9,10},{10,1... | collective-permute-start | bytes 3145736 | tf_op jit(solution)/shard_map/ppermute | solution.py:36
  3.3 31.7 %collective-permute-start.1 = (bf16[2,256,1024]{2,1,0:T(8,128)(2,1)}, bf16[2,256,1024]{2,1,0:T(8,128)(2,1)}, u32[]{:S(2)}, u32[]{:S(2)}) collective-permute-start(bf16[2,256,1024]{2,1,0:T(8,128)(2,1)} %bitcast.22), channel_id=1, source_target_pairs={{0,15},{1,0},{2,1},{3,2},{4,3},{5,4},{6,5},{7,6},{8,7},{9,8},{10,9... | collective-permute-start | bytes 3145736 | tf_op jit(solution)/shard_map/ppermute | solution.py:36
  3.3 6.6 %copy-start.3 = (s32[4096]{0:T(1024)S(1)}, s32[4096]{0:T(1024)}, u32[]{:S(2)}) copy-start(s32[4096]{0:T(1024)} %param.13) | copy-start | bytes 49156
  3.3 31.7 %copy-start.4 = (s32[4,2]{0,1:T(2,128)S(1)}, s32[4,2]{0,1:T(2,128)}, u32[]{:S(2)}) copy-start(s32[4,2]{0,1:T(2,128)} %param.17) | copy-start | bytes 100
  4.6 44.3 %collective-permute-start.3 = (bf16[2,256,1024]{2,1,0:T(8,128)(2,1)S(1)}, bf16[2,256,1024]{2,1,0:T(8,128)(2,1)}, u32[]{:S(2)}, u32[]{:S(2)}) collective-permute-start(bf16[2,256,1024]{2,1,0:T(8,128)(2,1)S(1)} %pad_maximum_fusion), channel_id=1, source_target_pairs={{0,1},{1,2},{2,3},{3,4},{4,5},{5,6},{6,7},{7,8},{8,9},{9,10},{10,1... | collective-permute-start | bytes 3145736 | tf_op jit(solution)/shard_map/ppermute | solution.py:36
  8.3 56.8 %collective-permute-start.2 = (bf16[2,256,1024]{2,1,0:T(8,128)(2,1)S(1)}, bf16[2,256,1024]{2,1,0:T(8,128)(2,1)}, u32[]{:S(2)}, u32[]{:S(2)}) collective-permute-start(bf16[2,256,1024]{2,1,0:T(8,128)(2,1)S(1)} %pad_maximum_fusion), channel_id=1, source_target_pairs={{0,2},{2,4},{4,6},{6,8},{8,10},{10,12},{12,14},{16,18},{18,20},{20... | collective-permute-start | bytes 3145736 | tf_op jit(solution)/shard_map/ppermute | solution.py:36
  35.0 1.4 %copy-start.5 = (bf16[2,256,1024]{2,1,0:T(8,128)(2,1)}, bf16[2,256,1024]{2,1,0:T(8,128)(2,1)S(1)}, u32[]{:S(2)}) copy-start(bf16[2,256,1024]{2,1,0:T(8,128)(2,1)S(1)} %collective-permute-done.low) | copy-start | bytes 3145732
  49.0 16.2 %collective-permute-start.4 = (bf16[2,256,1024]{2,1,0:T(8,128)(2,1)}, bf16[2,256,1024]{2,1,0:T(8,128)(2,1)}, u32[]{:S(2)}, u32[]{:S(2)}) collective-permute-start(bf16[2,256,1024]{2,1,0:T(8,128)(2,1)} %collective-permute-done.3.one), channel_id=1, source_target_pairs={{0,1},{2,3},{4,5},{6,7},{8,9},{10,11},{12,13},{14,15},{16,17},{18,... | collective-permute-start | bytes 3145736 | tf_op jit(solution)/shard_map/ppermute | solution.py:36
  61.5 27.5 %collective-permute-start.6 = (bf16[2,256,1024]{2,1,0:T(8,128)(2,1)}, bf16[2,256,1024]{2,1,0:T(8,128)(2,1)S(1)}, u32[]{:S(2)}, u32[]{:S(2)}) collective-permute-start(bf16[2,256,1024]{2,1,0:T(8,128)(2,1)} %get-tuple-element.30), channel_id=1, source_target_pairs={{0,15},{1,0},{2,1},{3,2},{4,3},{5,4},{6,5},{7,6},{8,7},{9,8},{10,9... | collective-permute-start | bytes 3145736 | tf_op jit(solution)/shard_map/ppermute | solution.py:36
  63.6 47.3 %copy-start.1 = (bf16[2,256,1024]{2,1,0:T(8,128)(2,1)S(1)}, bf16[2,256,1024]{2,1,0:T(8,128)(2,1)}, u32[]{:S(2)}) copy-start(bf16[2,256,1024]{2,1,0:T(8,128)(2,1)} %get-tuple-element.29) | copy-start | bytes 3145732
  63.6 47.3 %collective-permute-start.7 = (bf16[2,256,1024]{2,1,0:T(8,128)(2,1)}, bf16[2,256,1024]{2,1,0:T(8,128)(2,1)}, u32[]{:S(2)}, u32[]{:S(2)}) collective-permute-start(bf16[2,256,1024]{2,1,0:T(8,128)(2,1)} %get-tuple-element.31), channel_id=1, source_target_pairs={{0,1},{1,2},{2,3},{3,4},{4,5},{5,6},{6,7},{7,8},{8,9},{9,10},{10,1... | collective-permute-start | bytes 3145736 | tf_op jit(solution)/shard_map/ppermute | solution.py:36
  76.6 37.1 %copy-start = (bf16[2,256,1024]{2,1,0:T(8,128)(2,1)S(1)}, bf16[2,256,1024]{2,1,0:T(8,128)(2,1)}, u32[]{:S(2)}) copy-start(bf16[2,256,1024]{2,1,0:T(8,128)(2,1)} %get-tuple-element.27) | copy-start | bytes 3145732
  76.6 37.1 %collective-permute-start.5 = (bf16[2,256,1024]{2,1,0:T(8,128)(2,1)}, bf16[2,256,1024]{2,1,0:T(8,128)(2,1)S(1)}, u32[]{:S(2)}, u32[]{:S(2)}) collective-permute-start(bf16[2,256,1024]{2,1,0:T(8,128)(2,1)} %get-tuple-element.28), channel_id=1, source_target_pairs={{1,0},{3,2},{5,4},{7,6},{9,8},{11,10},{13,12},{15,14},{17,16},{19,... | collective-permute-start | bytes 3145736 | tf_op jit(solution)/shard_map/ppermute | solution.py:36
  78.1 38.0 %collective-permute-start.9 = (bf16[2,256,1024]{2,1,0:T(8,128)(2,1)}, bf16[2,256,1024]{2,1,0:T(8,128)(2,1)S(1)}, u32[]{:S(2)}, u32[]{:S(2)}) collective-permute-start(bf16[2,256,1024]{2,1,0:T(8,128)(2,1)} %get-tuple-element.28), channel_id=1, source_target_pairs={{2,0},{4,2},{6,4},{8,6},{10,8},{12,10},{14,12},{18,16},{20,18},{22... | collective-permute-start | bytes 3145736 | tf_op jit(solution)/shard_map/ppermute | solution.py:36
  113.7 17.3 %copy-start.2 = (bf16[2,256,1024]{2,1,0:T(8,128)(2,1)S(1)}, bf16[2,256,1024]{2,1,0:T(8,128)(2,1)}, u32[]{:S(2)}) copy-start(bf16[2,256,1024]{2,1,0:T(8,128)(2,1)} %get-tuple-element.26) | copy-start | bytes 3145732
  114.2 16.9 %collective-permute-start.8 = (bf16[2,256,1024]{2,1,0:T(8,128)(2,1)S(1)}, bf16[2,256,1024]{2,1,0:T(8,128)(2,1)S(1)}, u32[]{:S(2)}, u32[]{:S(2)}) collective-permute-start(bf16[2,256,1024]{2,1,0:T(8,128)(2,1)S(1)} %add_convert_fusion.2), channel_id=1, source_target_pairs={{1,0},{2,1},{3,2},{4,3},{5,4},{6,5},{7,6},{8,7},{9,8},{10,9},{11,1... | collective-permute-start | bytes 3145736 | tf_op jit(solution)/shard_map/ppermute | solution.py:36

commit v2 on v0

v2 whole, which is shorter than its diff:
```python
import functools
import math

import jax
import jax.numpy as jnp
from jax import lax
from jax.experimental import pallas as pl
from jax.experimental.pallas import tpu as pltpu
from jax.sharding import PartitionSpec as P

HEADS = 8
HEAD_DIM = 128
HALF = HEADS // 2
WIDE = HALF * HEAD_DIM
STRETCH = 64
NBR_TOK = 128
ROWS = 256
EXTRA = 16
FACTOR = HEAD_DIM ** (-0.5)
MASKED = -1e30
BF16 = jnp.bfloat16
F32 = jnp.float32


def send(value, target_of, wrap):
    count = lax.axis_size("ctx")
    pairs = []
    for source in range(count):
        target = target_of(source)
        if wrap:
            pairs.append((source, target % count))
        elif 0 <= target < count:
            pairs.append((source, target))
    return lax.ppermute(value, "ctx", pairs)


def swap(d):
    return d ^ 1


def outward(d):
    return d - 2 if d % 2 == 0 else d + 2


def inward(d):
    return d + 2 if d % 2 == 0 else d - 2


def across(d):
    return d - 1 if d % 2 == 0 else d + 1


def spec(rows, row_block=0, cols=HEAD_DIM):
    return pl.BlockSpec((rows, cols), lambda h, info: (row_block, h))


def own_spec(lead=()):
    zeros = (0,) * len(lead)
    return pl.BlockSpec(
        lead + (ROWS, HEAD_DIM), lambda h, info: zeros + (0, info[0] % 2 * HALF + h)
    )


def other_spec(lead=()):
    zeros = (0,) * len(lead)
    return pl.BlockSpec(
        lead + (ROWS, HEAD_DIM), lambda h, info: zeros + (0, (1 - info[0] % 2) * HALF + h)
    )


def whole_spec(shape, index=None):
    index = (0,) * len(shape) if index is None else index
    return pl.BlockSpec(shape, lambda h, *info: index)


def stat_spec(rows):
    return pl.BlockSpec((1, 8, rows), lambda h, info: (h, 0, 0))


def call(kernel, name, info, in_specs, inputs, out_specs, outs, steps=HALF, flops=0, prefetch=None):
    prefetch = (info,) if prefetch is None else prefetch
    return pl.pallas_call(
        kernel,
        name=name,
        grid_spec=pltpu.PrefetchScalarGridSpec(
            num_scalar_prefetch=len(prefetch),
            grid=(steps,),
            in_specs=in_specs,
            out_specs=out_specs,
        ),
        out_shape=[jax.ShapeDtypeStruct(shape, dtype) for shape, dtype in outs],
        compiler_params=pltpu.CompilerParams(vmem_limit_bytes=60 << 20),
        cost_estimate=pl.CostEstimate(flops=flops, transcendentals=0, bytes_accessed=4 << 20),
    )(*prefetch, *inputs)


def dot_last(a, b):
    return lax.dot_general(a, b, (((1,), (1,)), ((), ())), preferred_element_type=F32)


def dot_first(a, b):
    return lax.dot_general(a, b, (((0,), (0,)), ((), ())), preferred_element_type=F32)


def dot(a, b):
    return jnp.dot(a, b, preferred_element_type=F32)


def both(a, b):
    return jnp.concatenate([a, b], axis=0)


def weight_rows(times):
    log_two = jnp.where(times > 1.5, math.log(2.0), 0.0)
    return jnp.where(times < 0.5, MASKED, log_two)


def slot_pair(ref, first, core, second=None):
    times = ref[...].astype(F32)[:, :ROWS]
    low = times[first : first + 2]
    if second is None:
        return weight_rows(low)
    return weight_rows(jnp.where(core == 0, low, times[second : second + 2]))


def add_rows(s, rows):
    parts = [
        s[e * NBR_TOK : (e + 1) * NBR_TOK] + rows[e : e + 1] for e in range(s.shape[0] // NBR_TOK)
    ]
    return jnp.concatenate(parts, axis=0)


def partial_stats(s, dp):
    peak = jnp.max(s, axis=0, keepdims=True)
    e = jnp.exp(s - peak)
    return e, peak, jnp.sum(e, axis=0, keepdims=True), jnp.sum(e * dp, axis=0, keepdims=True)


def stat_rows(a, b, c):
    return jnp.concatenate([a, b, c, jnp.zeros((5, a.shape[1]), F32)], axis=0)[None]


def merge(stats, mine):
    t_peak, t_total, t_moment = stats[0, 0:1], stats[0, 1:2], stats[0, 2:3]
    peak, total, moment = mine
    top = jnp.maximum(t_peak, peak)
    t_scale = jnp.exp(t_peak - top)
    scale = jnp.exp(peak - top)
    full = t_total * t_scale + total * scale
    inverse = jnp.where(full > 0, 1.0 / full, 0.0)
    delta = (t_moment * t_scale + moment * scale) * inverse
    return top, inverse, delta, scale * inverse


def gradients(p, dp, delta, q, g, k):
    pb = p.astype(BF16)
    ds = (p * (dp - delta)).astype(BF16)
    return dot_first(ds, k) * FACTOR, dot(ds, q) * FACTOR, dot(pb, g)


def pack_kernel(enc_dev, loop, info, ids, *refs):
    qm, gm, xqm, xgm, q, g, k, v, xq, xg, pool, swap_ref, xm, xo, sm, so = refs
    me = info[0]
    shape = (EXTRA, HEAD_DIM)
    row = lax.broadcasted_iota(jnp.int32, shape, 0)
    lane = lax.broadcasted_iota(jnp.int32, shape, 1) + pl.program_id(0) * HEAD_DIM
    times = jnp.zeros(shape, F32)
    for s in range(ids.shape[0]):
        for n in range(ids.shape[1]):
            relative = lax.rem(ids[s, n] // enc_dev - me + 1 + loop, loop)
            local = relative * enc_dev + lax.rem(ids[s, n], enc_dev)
            hit = (row == local) & (lane >= s * STRETCH) & (lane < (s + 1) * STRETCH)
            times = times + jnp.where(hit, 1.0, 0.0)
    times = times.astype(BF16)
    for index, ref in enumerate((q, g, k, v, xq, xg)):
        swap_ref[index * ROWS : (index + 1) * ROWS] = ref[...]
    swap_ref[6 * ROWS : 7 * ROWS] = pool[0]
    swap_ref[7 * ROWS : 8 * ROWS] = pool[1]
    swap_ref[8 * ROWS :] = times
    for out, first, second in ((xm, xqm, xgm), (xo, xq, xg), (sm, qm, gm), (so, q, g)):
        out[0:ROWS] = first[...]
        out[ROWS : 2 * ROWS] = second[...]
    xm[2 * ROWS :] = times
    xo[2 * ROWS :] = times


def local_self(bias, q, g, k, v, pq, pg, pk, pv):
    qs, gs = both(q[...], pq[...]), both(g[...], pg[...])
    ks, vs = both(k[...], pk[...]), both(v[...], pv[...])
    return dot_last(ks, qs) * FACTOR + bias[...], dot_last(vs, gs), qs, gs, ks


def local_cross(core, w, pw, q, g, pool, pq, pg, pk, pv):
    qs, gs = both(q[...], pq[...]), both(g[...], pg[...])
    ks, vs = both(pool[0], pk[...]), both(pool[1], pv[...])
    own = both(slot_pair(w, 2, core), slot_pair(w, 4, core, 0))
    partner = both(slot_pair(pw, 0, core, 4), slot_pair(pw, 2, core))
    s = add_rows(dot_last(ks, qs) * FACTOR, jnp.concatenate([own, partner], axis=1))
    return s, dot_last(vs, gs), qs, gs, ks


def self_stats_kernel(info, *refs):
    s, dp, _, _, _ = local_self(*refs[:-1])
    refs[-1][...] = stat_rows(*partial_stats(s, dp)[1:])


def cross_stats_kernel(info, *refs):
    s, dp, _, _, _ = local_cross(info[0] % 2, *refs[:-2])
    stats = stat_rows(*partial_stats(s, dp)[1:])
    refs[-2][...] = stats[:, :, :ROWS]
    refs[-1][...] = stats[:, :, ROWS:]


def self_remote_kernel(
    info, bias, sq, sg, cq, cg, k, v, pk, pv, stats, dq_same, dq_cross, kv_ref, out_stats
):
    qs, gs = both(sq[...], cq[...]), both(sg[...], cg[...])
    ks, vs = both(k[...], pk[...]), both(v[...], pv[...])
    s, dp = dot_last(ks, qs) * FACTOR + bias[...], dot_last(vs, gs)
    e, *mine = partial_stats(s, dp)
    top, inverse, delta, scale = merge(stats[...], mine)
    dq, dk, dv = gradients(e * scale, dp, delta, qs, gs, ks)
    dq_same[...] = dq[:ROWS].astype(BF16)
    dq_cross[...] = dq[ROWS:].astype(BF16)
    kv_ref[: 2 * ROWS] = dk.astype(BF16)
    kv_ref[2 * ROWS :] = dv.astype(BF16)
    out_stats[...] = stat_rows(top, inverse, delta)


def cross_remote_kernel(
    info, sw, cw, sq, sg, cq, cg, pool, pk, pv, s_stats, c_stats, *outs
):
    dq_same, dq_cross, kv_ref, out_same, out_cross = outs
    core = info[0] % 2
    jobs = (
        (cq, cg, pool[0], pool[1], slot_pair(cw, 4, core, 0), c_stats, dq_cross, out_cross, 0),
        (sq, sg, pk[...], pv[...], slot_pair(sw, 0, core, 4), s_stats, dq_same, out_same, 1),
    )
    for q, g, k, v, rows, stats, dq_ref, out_stats, place in jobs:
        s, dp = add_rows(dot_last(k, q[...]) * FACTOR, rows), dot_last(v, g[...])
        e, *mine = partial_stats(s, dp)
        top, inverse, delta, scale = merge(stats[...], mine)
        dq, dk, dv = gradients(e * scale, dp, delta, q[...], g[...], k)
        dq_ref[...] = dq.astype(BF16)
        kv_ref[place * ROWS : (place + 1) * ROWS] = dk.astype(BF16)
        kv_ref[(2 + place) * ROWS : (3 + place) * ROWS] = dv.astype(BF16)
        out_stats[...] = stat_rows(top, inverse, delta)


def finish_local(parts, top, inverse, delta, kv_ref, mine, theirs):
    s, dp, qs, gs, ks = parts
    dq, dk, dv = gradients(jnp.exp(s - top) * inverse, dp, delta, qs, gs, ks)
    dk = dk + kv_ref[: 2 * ROWS].astype(F32)
    dv = dv + kv_ref[2 * ROWS :].astype(F32)
    for index, grad in enumerate((dq, dk, dv)):
        mine[index * ROWS : (index + 1) * ROWS] = grad[:ROWS].astype(BF16)
        theirs[index * ROWS : (index + 1) * ROWS] = grad[ROWS:].astype(BF16)


def self_local_kernel(info, *refs):
    stats_ref, own_ref, kv_ref, mine, theirs = refs[-5:]
    stats, local = stats_ref[0], own_ref[0]
    first = info[0] < 2
    inverse = 1.0 / local[1:2]
    top = jnp.where(first, local[0:1], stats[0:1])
    delta = jnp.where(first, local[2:3] * inverse, stats[2:3])
    inverse = jnp.where(first, inverse, stats[1:2])
    finish_local(local_self(*refs[:-5]), top, inverse, delta, kv_ref, mine, theirs)


def cross_local_kernel(info, *refs):
    own_ref, partner_ref, kv_ref, mine, theirs = refs[-5:]
    stats = jnp.concatenate([own_ref[0], partner_ref[0]], axis=1)
    parts = local_cross(info[0] % 2, *refs[:-5])
    finish_local(parts, stats[0:1], stats[1:2], stats[2:3], kv_ref, mine, theirs)


def final_kernel(info, mine, theirs, dq_mine, dq_theirs, *outs):
    def write(source, extra):
        dq = source[:ROWS].astype(F32) + extra[...].astype(F32)
        outs[0][...] = dq.astype(BF16)
        if len(outs) == 3:
            outs[1][...] = source[ROWS : 2 * ROWS]
            outs[2][...] = source[2 * ROWS :]
        else:
            outs[1][0] = source[ROWS : 2 * ROWS]
            outs[1][1] = source[2 * ROWS :]

    @pl.when(pl.program_id(0) == 0)
    def _():
        write(mine, dq_mine)

    @pl.when(pl.program_id(0) == 1)
    def _():
        write(theirs, dq_theirs)


def assemble(name, info, mine, theirs, dq_mine, dq_theirs, pooled):
    half = lambda h, info: (info[0] + h) % 2
    rows_out = pl.BlockSpec((ROWS, WIDE), lambda h, info: (0, half(h, info)))
    pool_out = pl.BlockSpec((2, ROWS, WIDE), lambda h, info: (0, 0, half(h, info)))
    full = ((ROWS, 2 * WIDE), BF16)
    if pooled:
        out_specs, outs = [rows_out, pool_out], [full, ((2, ROWS, 2 * WIDE), BF16)]
    else:
        out_specs, outs = [rows_out] * 3, [full] * 3
    return call(
        final_kernel,
        name,
        info,
        [whole_spec((3 * ROWS, WIDE))] * 2 + [whole_spec((ROWS, WIDE))] * 2,
        (mine, theirs, dq_mine, dq_theirs),
        out_specs,
        outs,
        steps=2,
    )


def body(
    queries, keys, values, grad_self, doc_ids, cross_queries, grad_cross, pool_kv, neighbour_ids
):
    loop = lax.axis_size("ctx")
    me = lax.axis_index("ctx").astype(jnp.int32)
    info = jnp.full((1,), me, jnp.int32)
    enc_dev = pool_kv.shape[1]
    width = queries.shape[1]
    pool = pool_kv.reshape(2, ROWS, width)
    hd = HEAD_DIM
    gig = 10**9

    two = lambda: pl.BlockSpec((2 * ROWS + EXTRA, hd), lambda h, *info: (0, h))
    pair = lambda: pl.BlockSpec((2 * ROWS, hd), lambda h, *info: (0, h))
    mine_spec = pl.BlockSpec((ROWS, hd), lambda h, info, ids: (0, info[0] % 2 * HALF + h))
    their_spec = pl.BlockSpec((ROWS, hd), lambda h, info, ids: (0, (1 - info[0] % 2) * HALF + h))
    their_pool = pl.BlockSpec(
        (2, ROWS, hd), lambda h, info, ids: (0, 0, (1 - info[0] % 2) * HALF + h)
    )
    swap_rows = 8 * ROWS + EXTRA
    packed, x_mine, x_other, s_mine, s_other = call(
        functools.partial(pack_kernel, enc_dev, loop),
        "pack",
        info,
        [mine_spec] * 4 + [their_spec] * 6 + [their_pool],
        (queries, grad_self, cross_queries, grad_cross)
        + (queries, grad_self, keys, values, cross_queries, grad_cross, pool),
        [pl.BlockSpec((swap_rows, hd), lambda h, *info: (0, h)), two(), two(), pair(), pair()],
        [((swap_rows, WIDE), BF16)]
        + [((2 * ROWS + EXTRA, WIDE), BF16)] * 2
        + [((2 * ROWS, WIDE), BF16)] * 2,
        prefetch=(info, neighbour_ids),
    )
    partner = send(packed, swap, False)
    x_same = send(x_mine, outward, True)
    x_cross = send(x_other, across, True)

    ids_of = lambda d: lax.dynamic_slice_in_dim(doc_ids, d * ROWS, ROWS, 0)
    span = jnp.arange(ROWS, dtype=jnp.int32)
    beside = me + 1 - 2 * (me % 2)
    key_ids = jnp.concatenate([ids_of(me), ids_of(beside)])
    key_pos = jnp.concatenate([span + me * ROWS, span + beside * ROWS])
    far_ids = jnp.concatenate([ids_of(me + 2), ids_of(beside + 2)])
    same_doc = key_ids[:, None] == key_ids[None, :]
    local_ok = same_doc & (key_pos[:, None] <= key_pos[None, :])
    far_ok = (key_ids[:, None] == far_ids[None, :]) & (me + 2 < loop)
    local_bias = jnp.where(local_ok, 0.0, MASKED).astype(F32)
    far_bias = jnp.where(far_ok, 0.0, MASKED).astype(F32)

    bias_spec = whole_spec((2 * ROWS, 2 * ROWS))
    self_specs = [bias_spec] + [own_spec()] * 4 + [spec(ROWS, j) for j in range(4)]
    self_args = (local_bias, queries, grad_self, keys, values) + (partner,) * 4
    mine_w = whole_spec((EXTRA, WIDE), (2 * ROWS // EXTRA, 0))
    partner_w = whole_spec((EXTRA, WIDE), (8 * ROWS // EXTRA, 0))
    cross_specs = (
        [mine_w, partner_w, own_spec(), own_spec(), own_spec((2,))]
        + [spec(ROWS, j) for j in range(4, 8)]
    )
    cross_args = (x_mine, partner, cross_queries, grad_cross, pool) + (partner,) * 4
    stat = lambda rows: ((HALF, 8, rows), F32)

    x_own, x_partner = call(
        cross_stats_kernel, "cross_stats", info, cross_specs, cross_args,
        [stat_spec(ROWS)] * 2, [stat(ROWS)] * 2, flops=4 * gig,
    )
    t_same = send(x_own, outward, True)
    t_cross = send(x_partner, inward, True)
    s_mine, s_other, x_own = lax.optimization_barrier((s_mine, s_other, x_own))
    s_same = send(s_mine, lambda d: d - 2, False)
    s_cross = send(s_other, lambda d: (d - 2) ^ 1, False)

    (s_own,) = call(
        self_stats_kernel, "self_stats", info, self_specs, self_args,
        [stat_spec(2 * ROWS)], [stat(2 * ROWS)], flops=4 * gig,
    )
    t_self = send(s_own, lambda d: d - 2, False)

    kv_out = spec(4 * ROWS)
    kv_shape = ((4 * ROWS, WIDE), BF16)
    q_shape = ((ROWS, WIDE), BF16)
    xd_same, xd_cross, x_kv, x_fin_same, x_fin_cross = call(
        cross_remote_kernel, "cross_remote", info,
        [mine_w, mine_w, spec(ROWS, 0), spec(ROWS, 1), spec(ROWS, 0), spec(ROWS, 1)]
        + [own_spec((2,)), spec(ROWS, 6), spec(ROWS, 7), stat_spec(ROWS), stat_spec(ROWS)],
        (x_same, x_cross, x_same, x_same, x_cross, x_cross, pool, partner, partner, t_same, t_cross),
        [spec(ROWS), spec(ROWS), kv_out, stat_spec(ROWS), stat_spec(ROWS)],
        [q_shape, q_shape, kv_shape, stat(ROWS), stat(ROWS)], flops=6 * gig,
    )
    f_own = send(x_fin_same, inward, True)
    f_partner = send(x_fin_cross, outward, True)
    xr_same = send(xd_same, inward, True)
    xr_cross = send(xd_cross, across, True)

    sd_same, sd_cross, s_kv, s_fin = call(
        self_remote_kernel, "self_remote", info,
        [bias_spec, spec(ROWS, 0), spec(ROWS, 1), spec(ROWS, 0), spec(ROWS, 1)]
        + [own_spec(), own_spec(), spec(ROWS, 2), spec(ROWS, 3), stat_spec(2 * ROWS)],
        (far_bias, s_same, s_same, s_cross, s_cross, keys, values, partner, partner, t_self),
        [spec(ROWS), spec(ROWS), kv_out, stat_spec(2 * ROWS)],
        [q_shape, q_shape, kv_shape, stat(2 * ROWS)], flops=8 * gig,
    )
    f_self = send(s_fin, lambda d: d + 2, False)
    sr_same = send(sd_same, lambda d: d + 2, False)
    sr_cross = send(sd_cross, lambda d: (d + 2) ^ 1, False)

    half_out = spec(3 * ROWS)
    half_shape = ((3 * ROWS, WIDE), BF16)
    x_keep, x_give = call(
        cross_local_kernel, "cross_local", info,
        cross_specs + [stat_spec(ROWS), stat_spec(ROWS), spec(4 * ROWS)],
        cross_args + (f_own, f_partner, x_kv),
        [half_out] * 2, [half_shape] * 2, flops=8 * gig,
    )
    x_take = send(x_give, swap, False)
    s_keep, s_give = call(
        self_local_kernel, "self_local", info,
        self_specs + [stat_spec(2 * ROWS), stat_spec(2 * ROWS), spec(4 * ROWS)],
        self_args + (f_self, s_own, s_kv),
        [half_out] * 2, [half_shape] * 2, flops=8 * gig,
    )
    s_take = send(s_give, swap, False)
    grad_cq, grad_pool = assemble("cross_final", info, x_keep, x_take, xr_same, xr_cross, True)
    grad_q, grad_k, grad_v = assemble("self_final", info, s_keep, s_take, sr_same, sr_cross, False)
    return grad_q, grad_k, grad_v, grad_cq, grad_pool.reshape(pool_kv.shape)


def solution(mesh):
    rows = P(("groups", "ctx"), None)
    pool = P(None, ("groups", "ctx"), None, None)
    return jax.shard_map(
        body,
        mesh=mesh,
        in_specs=(rows, rows, rows, rows, P("groups"), rows, rows, pool, rows),
        out_specs=(rows, rows, rows, rows, pool),
        check_vma=False,
    )
```

time: 134 us -> 134 us (level)
  the two profiles are of different devices: /device:TPU:1 before, /device:TPU:15 now
where the time goes in v2:
time: 134 us; the launch traced here: 133 us
  Pallas kernels  49.9 us (37%)
  waiting for transfers between devices  45.4 us (34%)
  starting transfers between devices  26.5 us (20%)
  local copies, waits for them, and re-layouts  8.89 us (7%)
  other arithmetic  1.68 us (1%)
    pallas_call x9, Pallas kernels, call(): pl.pallas_call(kernel, name=name, grid_spec=pltpu.PrefetchScalarGridSpec(...  49.9 us
    ppermute x17, waiting for transfers between devices, send(): return lax.ppermute(value, 'ctx', pairs)  45.4 us
    ppermute x17, starting transfers between devices, send(): return lax.ppermute(value, 'ctx', pairs)  26.5 us
    unnamed x45, local copies, waits for them, and re-layouts  8.04 us
  transfers between devices with their start and end apart: 17, of which 4 were waited for; matrix products, arithmetic and copies ran while one was open for 2% of the time, Pallas kernels for 31%

profile of v2, /device:TPU:15, one launch (start us, length us, event | category | flops | bytes accessed | tf_op | source)
XLA Modules:
  0.0 133.2 jit_solution(8508524651320503721)
XLA Ops:
  2.0 5.5 %pack.1 = (bf16[2064,512]{1,0:T(8,128)(2,1)}, bf16[528,512]{1,0:T(8,128)(2,1)}, bf16[528,512]{1,0:T(8,128)(2,1)}, bf16[512,512]{1,0:T(8,128)(2,1)}, bf16[512,512]{1,0:T(8,128)(2,1)}) custom-call(s32[1]{0:T(128)} %bitcast.info, s32[4,2]{1,0:T(4,128)} %copy.14.ids, bf16[256,1024]{1,0:T(8,128)(2,1)} %refs_1_.5, bf16[256,1024]{1,0:T(8,128)(2,1)} %refs_2_.8, ...), custom_call_target="tpu_custom_call" | custom-call | bytes 4194304 | tf_op jit(solution)/shard_map/pack/pallas_call | solution.py:82
  9.5 1.4 %collective-permute-start.9 = (bf16[528,512]{1,0:T(8,128)(2,1)}, bf16[528,512]{1,0:T(8,128)(2,1)S(1)}, u32[]{:S(2)}, u32[]{:S(2)}) collective-permute-start(bf16[528,512]{1,0:T(8,128)(2,1)} %get-tuple-element.48), channel_id=1, source_target_pairs={{0,15},{1,2},{2,1},{3,4},{4,3},{5,6},{6,5},{7,8},{8,7},{9,10},{10,... | collective-permute-start | bytes 1622024 | tf_op jit(solution)/shard_map/ppermute | solution.py:34
  11.7 1.7 %and_select_fusion = (f32[512,512]{1,0:T(8,128)}, f32[512,512]{1,0:T(8,128)}) fusion(s32[512]{0:T(512)S(1)} %get-tuple-element.66, s32[512]{0:T(512)S(1)} %get-tuple-element.65, pred[]{:T(512)S(6)} %lt.26, s32[512]{0:T(512)S(1)} %pad_add_fusion.1), kind=kLoop, calls=%fused_computation | loop fusion | flops 1835008 | bytes 2103297 | tf_op jit(solution)/shard_map/jit(_where)/select_n | solution.py:366
  13.4 1.3 %copy-done.6 = bf16[2064,512]{1,0:T(8,128)(2,1)} copy-done((bf16[2064,512]{1,0:T(8,128)(2,1)}, bf16[2064,512]{1,0:T(8,128)(2,1)S(1)}, u32[]{:S(2)}) %copy-start.6) | copy-done | bytes 2113560
  14.7 4.6 %cross_stats.1 = (f32[4,8,256]{2,1,0:T(8,128)}, f32[4,8,256]{2,1,0:T(8,128)}) custom-call(s32[1]{0:T(128)} %bitcast.info, bf16[528,512]{1,0:T(8,128)(2,1)} %get-tuple-element.35.refs_0_, bf16[2064,512]{1,0:T(8,128)(2,1)} %copy-done.6, bf16[256,1024]{1,0:T(8,128)(2,1)} %refs_2_.9, bf16[256,1024]{1,0:T(8,128)(2,1)} %refs_3_.9, bf16[2,256,1024]{2,1,0:T(8,128)(2,1)} %bitcast.4, ...), custom_call_target="tpu_custom_call" | custom-call | flops 4000000000 | bytes 4194304 | tf_op jit(solution)/shard_map/cross_stats/pallas_call | solution.py:82
  19.8 3.0 %collective-permute-start.1 = (bf16[512,512]{1,0:T(8,128)(2,1)}, bf16[512,512]{1,0:T(8,128)(2,1)S(1)}, u32[]{:S(2)}, u32[]{:S(2)}) collective-permute-start(bf16[512,512]{1,0:T(8,128)(2,1)} %get-tuple-element.37), channel_id=1, source_target_pairs={{2,0},{3,1},{4,2},{5,3},{6,4},{7,5},{8,6},{9,7},{10,8},{11,9},{12,... | collective-permute-start | bytes 1572872 | tf_op jit(solution)/shard_map/ppermute | solution.py:34
  23.1 5.2 %self_stats.1.refs_10_ = f32[4,8,512]{2,1,0:T(8,128)} custom-call(s32[1]{0:T(128)} %bitcast.info, f32[512,512]{1,0:T(8,128)} %get-tuple-element.64.refs_0_, bf16[256,1024]{1,0:T(8,128)(2,1)} %refs_1_.5, bf16[256,1024]{1,0:T(8,128)(2,1)} %refs_2_.8, bf16[256,1024]{1,0:T(8,128)(2,1)} %refs_3_.8, bf16[256,1024]{1,0:T(8,128)(2,1)} %refs_4_.5, ...), custom_call_target="tpu_custom_call" | custom-call | flops 4000000000 | bytes 4194304 | tf_op jit(solution)/shard_map/self_stats/pallas_call | solution.py:82
  28.3 12.2 %collective-permute-done.8.sw.sq.sg = bf16[528,512]{1,0:T(8,128)(2,1)S(1)} collective-permute-done((bf16[528,512]{1,0:T(8,128)(2,1)}, bf16[528,512]{1,0:T(8,128)(2,1)S(1)}, u32[]{:S(2)}, u32[]{:S(2)}) %collective-permute-start.8) | collective-permute-done | bytes 540704 | tf_op jit(solution)/shard_map/ppermute | solution.py:34
  40.6 1.9 %collective-permute-start.2 = (bf16[512,512]{1,0:T(8,128)(2,1)S(1)}, bf16[512,512]{1,0:T(8,128)(2,1)S(1)}, u32[]{:S(2)}, u32[]{:S(2)}) collective-permute-start(bf16[512,512]{1,0:T(8,128)(2,1)S(1)} %copy-done.9), channel_id=1, source_target_pairs={{2,1},{3,0},{4,3},{5,2},{6,5},{7,4},{8,7},{9,6},{10,9},{11,8},{12,... | collective-permute-start | bytes 1572872 | tf_op jit(solution)/shard_map/ppermute | solution.py:34
  42.5 5.4 %collective-permute-start.3 = (f32[4,8,512]{2,1,0:T(8,128)}, f32[4,8,512]{2,1,0:T(8,128)S(1)}, u32[]{:S(2)}, u32[]{:S(2)}) collective-permute-start(f32[4,8,512]{2,1,0:T(8,128)} %self_stats.1.refs_10_), channel_id=1, source_target_pairs={{2,0},{3,1},{4,2},{5,3},{6,4},{7,5},{8,6},{9,7},{10,8},{11,9},{12,... | collective-permute-start | bytes 196616 | tf_op jit(solution)/shard_map/ppermute | solution.py:34
  47.9 11.4 %collective-permute-done.10.s_stats = f32[4,8,256]{2,1,0:T(8,128)S(1)} collective-permute-done((f32[4,8,256]{2,1,0:T(8,128)}, f32[4,8,256]{2,1,0:T(8,128)S(1)}, u32[]{:S(2)}, u32[]{:S(2)}) %collective-permute-start.10) | collective-permute-done | bytes 32800 | tf_op jit(solution)/shard_map/ppermute | solution.py:34
  60.6 6.4 %cross_remote.1 = (bf16[256,512]{1,0:T(8,128)(2,1)}, bf16[256,512]{1,0:T(8,128)(2,1)}, bf16[1024,512]{1,0:T(8,128)(2,1)}, f32[4,8,256]{2,1,0:T(8,128)}, f32[4,8,256]{2,1,0:T(8,128)}) custom-call(s32[1]{0:T(128)} %bitcast.info, bf16[528,512]{1,0:T(8,128)(2,1)} %copy-done.7, bf16[528,512]{1,0:T(8,128)(2,1)} %copy-done.8, bf16[528,512]{1,0:T(8,128)(2,1)} %copy-done.7, ...), custom_call_target="tpu_custom_call" | custom-call | flops 6000000000 | bytes 4194304 | tf_op jit(solution)/shard_map/cross_remote/pallas_call | solution.py:82
  67.0 2.4 %collective-permute-start.13 = (f32[4,8,256]{2,1,0:T(8,128)}, f32[4,8,256]{2,1,0:T(8,128)S(1)}, u32[]{:S(2)}, u32[]{:S(2)}) collective-permute-start(f32[4,8,256]{2,1,0:T(8,128)} %get-tuple-element.51), channel_id=1, source_target_pairs={{0,14},{1,3},{2,0},{3,5},{4,2},{5,7},{6,4},{7,9},{8,6},{9,11},{10,... | collective-permute-start | bytes 98312 | tf_op jit(solution)/shard_map/ppermute | solution.py:34
  70.4 8.4 %self_remote.1 = (bf16[256,512]{1,0:T(8,128)(2,1)}, bf16[256,512]{1,0:T(8,128)(2,1)}, bf16[1024,512]{1,0:T(8,128)(2,1)}, f32[4,8,512]{2,1,0:T(8,128)}) custom-call(s32[1]{0:T(128)} %bitcast.info, f32[512,512]{1,0:T(8,128)} %get-tuple-element.63.bias, bf16[512,512]{1,0:T(8,128)(2,1)} %copy-done.10, bf16[512,512]{1,0:T(8,128)(2,1)} %copy-done.10, ...), custom_call_target="tpu_custom_call" | custom-call | flops 8000000000 | bytes 4194304 | tf_op jit(solution)/shard_map/self_remote/pallas_call | solution.py:82
  78.8 2.3 %collective-permute-start.4 = (f32[4,8,512]{2,1,0:T(8,128)}, f32[4,8,512]{2,1,0:T(8,128)S(1)}, u32[]{:S(2)}, u32[]{:S(2)}) collective-permute-start(f32[4,8,512]{2,1,0:T(8,128)} %get-tuple-element.39), channel_id=1, source_target_pairs={{0,2},{1,3},{2,4},{3,5},{4,6},{5,7},{6,8},{7,9},{8,10},{9,11},{10,... | collective-permute-start | bytes 196616 | tf_op jit(solution)/shard_map/ppermute | solution.py:34
  81.7 6.8 %cross_local.1 = (bf16[768,512]{1,0:T(8,128)(2,1)}, bf16[768,512]{1,0:T(8,128)(2,1)}) custom-call(s32[1]{0:T(128)} %bitcast.info, bf16[528,512]{1,0:T(8,128)(2,1)} %get-tuple-element.35.refs_0_, bf16[2064,512]{1,0:T(8,128)(2,1)} %copy-done.6, bf16[256,1024]{1,0:T(8,128)(2,1)} %refs_2_.9, bf16[256,1024]{1,0:T(8,128)(2,1)} %refs_3_.9, ...), custom_call_target="tpu_custom_call" | custom-call | flops 8000000000 | bytes 4194304 | tf_op jit(solution)/shard_map/cross_local/pallas_call | solution.py:82
  90.0 7.4 %self_local.1 = (bf16[768,512]{1,0:T(8,128)(2,1)}, bf16[768,512]{1,0:T(8,128)(2,1)}) custom-call(s32[1]{0:T(128)} %bitcast.info, f32[512,512]{1,0:T(8,128)} %get-tuple-element.64.refs_0_, bf16[256,1024]{1,0:T(8,128)(2,1)} %refs_1_.5, bf16[256,1024]{1,0:T(8,128)(2,1)} %refs_2_.8, bf16[256,1024]{1,0:T(8,128)(2,1)} %refs_3_.8, bf16[256,1024]{1,0:T(8,128)(2,1)} %refs_4_.5, ...), custom_call_target="tpu_custom_call" | custom-call | flops 8000000000 | bytes 4194304 | tf_op jit(solution)/shard_map/self_local/pallas_call | solution.py:82
  97.6 2.6 %collective-permute-start.15 = (bf16[256,512]{1,0:T(8,128)(2,1)S(1)}, bf16[256,512]{1,0:T(8,128)(2,1)S(1)}, u32[]{:S(2)}, u32[]{:S(2)}) collective-permute-start(bf16[256,512]{1,0:T(8,128)(2,1)S(1)} %copy-done.13), channel_id=1, source_target_pairs={{0,2},{1,15},{2,4},{3,1},{4,6},{5,3},{6,8},{7,5},{8,10},{9,7},{10,... | collective-permute-start | bytes 786440 | tf_op jit(solution)/shard_map/ppermute | solution.py:34
  100.2 1.9 %collective-permute-start.6 = (bf16[256,512]{1,0:T(8,128)(2,1)S(1)}, bf16[256,512]{1,0:T(8,128)(2,1)S(1)}, u32[]{:S(2)}, u32[]{:S(2)}) collective-permute-start(bf16[256,512]{1,0:T(8,128)(2,1)S(1)} %copy-done.15), channel_id=1, source_target_pairs={{0,2},{1,3},{2,4},{3,5},{4,6},{5,7},{6,8},{7,9},{8,10},{9,11},{10,... | collective-permute-start | bytes 786440 | tf_op jit(solution)/shard_map/ppermute | solution.py:34
  102.1 16.6 %collective-permute-done.15.dq_mine = bf16[256,512]{1,0:T(8,128)(2,1)S(1)} collective-permute-done((bf16[256,512]{1,0:T(8,128)(2,1)S(1)}, bf16[256,512]{1,0:T(8,128)(2,1)S(1)}, u32[]{:S(2)}, u32[]{:S(2)}) %collective-permute-start.15) | collective-permute-done | bytes 262176 | tf_op jit(solution)/shard_map/ppermute | solution.py:34
  118.7 1.9 %collective-permute-start.7 = (bf16[256,512]{1,0:T(8,128)(2,1)S(1)}, bf16[256,512]{1,0:T(8,128)(2,1)S(1)}, u32[]{:S(2)}, u32[]{:S(2)}) collective-permute-start(bf16[256,512]{1,0:T(8,128)(2,1)S(1)} %copy-done.14), channel_id=1, source_target_pairs={{0,3},{1,2},{2,5},{3,4},{4,7},{5,6},{6,9},{7,8},{8,11},{9,10},{10,... | collective-permute-start | bytes 786440 | tf_op jit(solution)/shard_map/ppermute | solution.py:34
  121.7 2.8 %cross_final.1 = (bf16[256,1024]{1,0:T(8,128)(2,1)}, bf16[2,256,1024]{2,1,0:T(8,128)(2,1)}) custom-call(s32[1]{0:T(128)} %bitcast.info, bf16[768,512]{1,0:T(8,128)(2,1)} %get-tuple-element.53.mine, bf16[768,512]{1,0:T(8,128)(2,1)} %copy-done.1, bf16[256,512]{1,0:T(8,128)(2,1)} %copy-done.4, bf16[256,512]{1,0:T(8,128)(2,1)} %copy-done.5), custom_call_target="tpu_custom_call" | custom-call | bytes 4194304 | tf_op jit(solution)/shard_map/cross_final/pallas_call | solution.py:82
  124.4 5.1 %collective-permute-done.7.dq_theirs = bf16[256,512]{1,0:T(8,128)(2,1)S(1)} collective-permute-done((bf16[256,512]{1,0:T(8,128)(2,1)S(1)}, bf16[256,512]{1,0:T(8,128)(2,1)S(1)}, u32[]{:S(2)}, u32[]{:S(2)}) %collective-permute-start.7) | collective-permute-done | bytes 262176 | tf_op jit(solution)/shard_map/ppermute | solution.py:34
  130.5 2.8 %self_final.1 = (bf16[256,1024]{1,0:T(8,128)(2,1)}, bf16[256,1024]{1,0:T(8,128)(2,1)}, bf16[256,1024]{1,0:T(8,128)(2,1)}) custom-call(s32[1]{0:T(128)} %bitcast.info, bf16[768,512]{1,0:T(8,128)(2,1)} %get-tuple-element.41.mine, bf16[768,512]{1,0:T(8,128)(2,1)} %copy-done, bf16[256,512]{1,0:T(8,128)(2,1)} %copy-done.2, bf16[256,512]{1,0:T(8,128)(2,1)} %copy-done.3), custom_call_target="tpu_custom_call" | custom-call | bytes 4194304 | tf_op jit(solution)/shard_map/self_final/pallas_call | solution.py:82
  (70 shorter events, 11.4 us)
Async XLA Ops:
  7.5 5.9 %collective-permute-start = (bf16[2064,512]{1,0:T(8,128)(2,1)}, bf16[2064,512]{1,0:T(8,128)(2,1)S(1)}, u32[]{:S(2)}, u32[]{:S(2)}) collective-permute-start(bf16[2064,512]{1,0:T(8,128)(2,1)} %get-tuple-element.32), channel_id=1, source_target_pairs={{0,1},{1,0},{2,3},{3,2},{4,5},{5,4},{6,7},{7,6},{8,9},{9,8},{10,11... | collective-permute-start | bytes 6340616 | tf_op jit(solution)/shard_map/ppermute | solution.py:34
  8.3 32.3 %collective-permute-start.8 = (bf16[528,512]{1,0:T(8,128)(2,1)}, bf16[528,512]{1,0:T(8,128)(2,1)S(1)}, u32[]{:S(2)}, u32[]{:S(2)}) collective-permute-start(bf16[528,512]{1,0:T(8,128)(2,1)} %get-tuple-element.35.refs_0_), channel_id=1, source_target_pairs={{0,14},{1,3},{2,0},{3,5},{4,2},{5,7},{6,4},{7,9},{8,6},{9,11},{10,... | collective-permute-start | bytes 1622024 | tf_op jit(solution)/shard_map/ppermute | solution.py:34
  9.5 33.0 %collective-permute-start.9 = (bf16[528,512]{1,0:T(8,128)(2,1)}, bf16[528,512]{1,0:T(8,128)(2,1)S(1)}, u32[]{:S(2)}, u32[]{:S(2)}) collective-permute-start(bf16[528,512]{1,0:T(8,128)(2,1)} %get-tuple-element.48), channel_id=1, source_target_pairs={{0,15},{1,2},{2,1},{3,4},{4,3},{5,6},{6,5},{7,8},{8,7},{9,10},{10,... | collective-permute-start | bytes 1622024 | tf_op jit(solution)/shard_map/ppermute | solution.py:34
  19.4 40.0 %collective-permute-start.10 = (f32[4,8,256]{2,1,0:T(8,128)}, f32[4,8,256]{2,1,0:T(8,128)S(1)}, u32[]{:S(2)}, u32[]{:S(2)}) collective-permute-start(f32[4,8,256]{2,1,0:T(8,128)} %get-tuple-element.36), channel_id=1, source_target_pairs={{0,14},{1,3},{2,0},{3,5},{4,2},{5,7},{6,4},{7,9},{8,6},{9,11},{10,... | collective-permute-start | bytes 98312 | tf_op jit(solution)/shard_map/ppermute | solution.py:34
  19.8 49.6 %collective-permute-start.1 = (bf16[512,512]{1,0:T(8,128)(2,1)}, bf16[512,512]{1,0:T(8,128)(2,1)S(1)}, u32[]{:S(2)}, u32[]{:S(2)}) collective-permute-start(bf16[512,512]{1,0:T(8,128)(2,1)} %get-tuple-element.37), channel_id=1, source_target_pairs={{2,0},{3,1},{4,2},{5,3},{6,4},{7,5},{8,6},{9,7},{10,8},{11,9},{12,... | collective-permute-start | bytes 1572872 | tf_op jit(solution)/shard_map/ppermute | solution.py:34
  22.8 36.6 %collective-permute-start.11 = (f32[4,8,256]{2,1,0:T(8,128)}, f32[4,8,256]{2,1,0:T(8,128)S(1)}, u32[]{:S(2)}, u32[]{:S(2)}) collective-permute-start(f32[4,8,256]{2,1,0:T(8,128)} %get-tuple-element.49), channel_id=1, source_target_pairs={{0,2},{1,15},{2,4},{3,1},{4,6},{5,3},{6,8},{7,5},{8,10},{9,7},{10,... | collective-permute-start | bytes 98312 | tf_op jit(solution)/shard_map/ppermute | solution.py:34
  23.1 17.4 %copy-start.9 = (bf16[512,512]{1,0:T(8,128)(2,1)S(1)}, bf16[512,512]{1,0:T(8,128)(2,1)}, u32[]{:S(2)}) copy-start(bf16[512,512]{1,0:T(8,128)(2,1)} %get-tuple-element.38) | copy-start | bytes 1572868
  40.6 18.8 %copy-start.7 = (bf16[528,512]{1,0:T(8,128)(2,1)}, bf16[528,512]{1,0:T(8,128)(2,1)S(1)}, u32[]{:S(2)}) copy-start(bf16[528,512]{1,0:T(8,128)(2,1)S(1)} %collective-permute-done.8.sw.sq.sg) | copy-start | bytes 1622020
  40.6 28.8 %collective-permute-start.2 = (bf16[512,512]{1,0:T(8,128)(2,1)S(1)}, bf16[512,512]{1,0:T(8,128)(2,1)S(1)}, u32[]{:S(2)}, u32[]{:S(2)}) collective-permute-start(bf16[512,512]{1,0:T(8,128)(2,1)S(1)} %copy-done.9), channel_id=1, source_target_pairs={{2,1},{3,0},{4,3},{5,2},{6,5},{7,4},{8,7},{9,6},{10,9},{11,8},{12,... | collective-permute-start | bytes 1572872 | tf_op jit(solution)/shard_map/ppermute | solution.py:34
  42.5 16.9 %copy-start.8 = (bf16[528,512]{1,0:T(8,128)(2,1)}, bf16[528,512]{1,0:T(8,128)(2,1)S(1)}, u32[]{:S(2)}) copy-start(bf16[528,512]{1,0:T(8,128)(2,1)S(1)} %collective-permute-done.9.cw.cq.cg) | copy-start | bytes 1622020
  42.5 26.9 %collective-permute-start.3 = (f32[4,8,512]{2,1,0:T(8,128)}, f32[4,8,512]{2,1,0:T(8,128)S(1)}, u32[]{:S(2)}, u32[]{:S(2)}) collective-permute-start(f32[4,8,512]{2,1,0:T(8,128)} %self_stats.1.refs_10_), channel_id=1, source_target_pairs={{2,0},{3,1},{4,2},{5,3},{6,4},{7,5},{8,6},{9,7},{10,8},{11,9},{12,... | collective-permute-start | bytes 196616 | tf_op jit(solution)/shard_map/ppermute | solution.py:34
  66.9 14.1 %collective-permute-start.12 = (f32[4,8,256]{2,1,0:T(8,128)}, f32[4,8,256]{2,1,0:T(8,128)S(1)}, u32[]{:S(2)}, u32[]{:S(2)}) collective-permute-start(f32[4,8,256]{2,1,0:T(8,128)} %get-tuple-element.50), channel_id=1, source_target_pairs={{0,2},{1,15},{2,4},{3,1},{4,6},{5,3},{6,8},{7,5},{8,10},{9,7},{10,... | collective-permute-start | bytes 98312 | tf_op jit(solution)/shard_map/ppermute | solution.py:34
  67.0 14.1 %collective-permute-start.13 = (f32[4,8,256]{2,1,0:T(8,128)}, f32[4,8,256]{2,1,0:T(8,128)S(1)}, u32[]{:S(2)}, u32[]{:S(2)}) collective-permute-start(f32[4,8,256]{2,1,0:T(8,128)} %get-tuple-element.51), channel_id=1, source_target_pairs={{0,14},{1,3},{2,0},{3,5},{4,2},{5,7},{6,4},{7,9},{8,6},{9,11},{10,... | collective-permute-start | bytes 98312 | tf_op jit(solution)/shard_map/ppermute | solution.py:34
  78.8 10.6 %collective-permute-start.4 = (f32[4,8,512]{2,1,0:T(8,128)}, f32[4,8,512]{2,1,0:T(8,128)S(1)}, u32[]{:S(2)}, u32[]{:S(2)}) collective-permute-start(f32[4,8,512]{2,1,0:T(8,128)} %get-tuple-element.39), channel_id=1, source_target_pairs={{0,2},{1,3},{2,4},{3,5},{4,6},{5,7},{6,8},{7,9},{8,10},{9,11},{10,... | collective-permute-start | bytes 196616 | tf_op jit(solution)/shard_map/ppermute | solution.py:34
  88.5 32.2 %collective-permute-start.14 = (bf16[768,512]{1,0:T(8,128)(2,1)}, bf16[768,512]{1,0:T(8,128)(2,1)S(1)}, u32[]{:S(2)}, u32[]{:S(2)}) collective-permute-start(bf16[768,512]{1,0:T(8,128)(2,1)} %get-tuple-element.54), channel_id=1, source_target_pairs={{0,1},{1,0},{2,3},{3,2},{4,5},{5,4},{6,7},{7,6},{8,9},{9,8},{10,11... | collective-permute-start | bytes 2359304 | tf_op jit(solution)/shard_map/ppermute | solution.py:34
  90.0 7.5 %copy-start.13 = (bf16[256,512]{1,0:T(8,128)(2,1)S(1)}, bf16[256,512]{1,0:T(8,128)(2,1)}, u32[]{:S(2)}) copy-start(bf16[256,512]{1,0:T(8,128)(2,1)} %get-tuple-element.55) | copy-start | bytes 786436
  90.0 10.1 %copy-start.12 = (bf16[256,512]{1,0:T(8,128)(2,1)S(1)}, bf16[256,512]{1,0:T(8,128)(2,1)}, u32[]{:S(2)}) copy-start(bf16[256,512]{1,0:T(8,128)(2,1)} %get-tuple-element.56) | copy-start | bytes 786436
  90.0 10.1 %copy-start.15 = (bf16[256,512]{1,0:T(8,128)(2,1)S(1)}, bf16[256,512]{1,0:T(8,128)(2,1)}, u32[]{:S(2)}) copy-start(bf16[256,512]{1,0:T(8,128)(2,1)} %get-tuple-element.43) | copy-start | bytes 786436
  90.0 28.7 %copy-start.14 = (bf16[256,512]{1,0:T(8,128)(2,1)S(1)}, bf16[256,512]{1,0:T(8,128)(2,1)}, u32[]{:S(2)}) copy-start(bf16[256,512]{1,0:T(8,128)(2,1)} %get-tuple-element.44) | copy-start | bytes 786436
  97.5 32.1 %collective-permute-start.5 = (bf16[768,512]{1,0:T(8,128)(2,1)}, bf16[768,512]{1,0:T(8,128)(2,1)S(1)}, u32[]{:S(2)}, u32[]{:S(2)}) collective-permute-start(bf16[768,512]{1,0:T(8,128)(2,1)} %get-tuple-element.42), channel_id=1, source_target_pairs={{0,1},{1,0},{2,3},{3,2},{4,5},{5,4},{6,7},{7,6},{8,9},{9,8},{10,11... | collective-permute-start | bytes 2359304 | tf_op jit(solution)/shard_map/ppermute | solution.py:34
  97.6 21.2 %collective-permute-start.15 = (bf16[256,512]{1,0:T(8,128)(2,1)S(1)}, bf16[256,512]{1,0:T(8,128)(2,1)S(1)}, u32[]{:S(2)}, u32[]{:S(2)}) collective-permute-start(bf16[256,512]{1,0:T(8,128)(2,1)S(1)} %copy-done.13), channel_id=1, source_target_pairs={{0,2},{1,15},{2,4},{3,1},{4,6},{5,3},{6,8},{7,5},{8,10},{9,7},{10,... | collective-permute-start | bytes 786440 | tf_op jit(solution)/shard_map/ppermute | solution.py:34
  100.2 20.5 %collective-permute-start.16 = (bf16[256,512]{1,0:T(8,128)(2,1)S(1)}, bf16[256,512]{1,0:T(8,128)(2,1)S(1)}, u32[]{:S(2)}, u32[]{:S(2)}) collective-permute-start(bf16[256,512]{1,0:T(8,128)(2,1)S(1)} %copy-done.12), channel_id=1, source_target_pairs={{0,15},{1,2},{2,1},{3,4},{4,3},{5,6},{6,5},{7,8},{8,7},{9,10},{10,... | collective-permute-start | bytes 786440 | tf_op jit(solution)/shard_map/ppermute | solution.py:34
  100.2 24.2 %collective-permute-start.6 = (bf16[256,512]{1,0:T(8,128)(2,1)S(1)}, bf16[256,512]{1,0:T(8,128)(2,1)S(1)}, u32[]{:S(2)}, u32[]{:S(2)}) collective-permute-start(bf16[256,512]{1,0:T(8,128)(2,1)S(1)} %copy-done.15), channel_id=1, source_target_pairs={{0,2},{1,3},{2,4},{3,5},{4,6},{5,7},{6,8},{7,9},{8,10},{9,11},{10,... | collective-permute-start | bytes 786440 | tf_op jit(solution)/shard_map/ppermute | solution.py:34
  118.7 10.8 %collective-permute-start.7 = (bf16[256,512]{1,0:T(8,128)(2,1)S(1)}, bf16[256,512]{1,0:T(8,128)(2,1)S(1)}, u32[]{:S(2)}, u32[]{:S(2)}) collective-permute-start(bf16[256,512]{1,0:T(8,128)(2,1)S(1)} %copy-done.14), channel_id=1, source_target_pairs={{0,3},{1,2},{2,5},{3,4},{4,7},{5,6},{6,9},{7,8},{8,11},{9,10},{10,... | collective-permute-start | bytes 786440 | tf_op jit(solution)/shard_map/ppermute | solution.py:34
  (15 other events, 17.2 us)

commit v3 on v2

v3 whole, which is shorter than its diff:
```python
import functools
import math

import jax
import jax.numpy as jnp
from jax import lax
from jax.experimental import pallas as pl
from jax.experimental.pallas import tpu as pltpu
from jax.sharding import PartitionSpec as P

HEADS = 8
HEAD_DIM = 128
HALF = HEADS // 2
WIDE = HALF * HEAD_DIM
STRETCH = 64
NBR_TOK = 128
ROWS = 256
EXTRA = 16
STATS = 32
FACTOR = HEAD_DIM ** (-0.5)
MASKED = -1e30
BF16 = jnp.bfloat16
F32 = jnp.float32


def send(value, target_of, wrap):
    count = lax.axis_size("ctx")
    pairs = []
    for source in range(count):
        target = target_of(source)
        if wrap:
            pairs.append((source, target % count))
        elif 0 <= target < count:
            pairs.append((source, target))
    return lax.ppermute(value, "ctx", pairs)


def swap(d):
    return d ^ 1


def outward(d):
    return d - 2 if d % 2 == 0 else d + 2


def inward(d):
    return d + 2 if d % 2 == 0 else d - 2


def across(d):
    return d - 1 if d % 2 == 0 else d + 1


def spec(rows, row_block=0, cols=HEAD_DIM):
    return pl.BlockSpec((rows, cols), lambda h, info: (row_block, h))


def own_spec(lead=()):
    zeros = (0,) * len(lead)
    return pl.BlockSpec(
        lead + (ROWS, HEAD_DIM), lambda h, info: zeros + (0, info[0] % 2 * HALF + h)
    )


def other_spec(lead=()):
    zeros = (0,) * len(lead)
    return pl.BlockSpec(
        lead + (ROWS, HEAD_DIM), lambda h, info: zeros + (0, (1 - info[0] % 2) * HALF + h)
    )


def whole_spec(shape, index=None):
    index = (0,) * len(shape) if index is None else index
    return pl.BlockSpec(shape, lambda h, *info: index)


def stat_spec(rows):
    return pl.BlockSpec((1, 8, rows), lambda h, info: (h, 0, 0))


def call(kernel, name, info, in_specs, inputs, out_specs, outs, steps=HALF, flops=0, prefetch=None):
    prefetch = (info,) if prefetch is None else prefetch
    return pl.pallas_call(
        kernel,
        name=name,
        grid_spec=pltpu.PrefetchScalarGridSpec(
            num_scalar_prefetch=len(prefetch),
            grid=(steps,),
            in_specs=in_specs,
            out_specs=out_specs,
        ),
        out_shape=[jax.ShapeDtypeStruct(shape, dtype) for shape, dtype in outs],
        compiler_params=pltpu.CompilerParams(vmem_limit_bytes=63 << 20),
        cost_estimate=pl.CostEstimate(flops=flops, transcendentals=0, bytes_accessed=0),
    )(*prefetch, *inputs)


def dot_last(a, b):
    return lax.dot_general(a, b, (((1,), (1,)), ((), ())), preferred_element_type=F32)


def dot_first(a, b):
    return lax.dot_general(a, b, (((0,), (0,)), ((), ())), preferred_element_type=F32)


def dot(a, b):
    return jnp.dot(a, b, preferred_element_type=F32)


def both(a, b):
    return jnp.concatenate([a, b], axis=0)


def weight_rows(times):
    log_two = jnp.where(times > 1.5, math.log(2.0), 0.0)
    return jnp.where(times < 0.5, MASKED, log_two)


def slot_pair(ref, first, core, second=None):
    times = ref[...].astype(F32)[:, :ROWS]
    low = times[first : first + 2]
    if second is None:
        return weight_rows(low)
    return weight_rows(jnp.where(core == 0, low, times[second : second + 2]))


def add_rows(s, rows):
    parts = [
        s[e * NBR_TOK : (e + 1) * NBR_TOK] + rows[e : e + 1] for e in range(s.shape[0] // NBR_TOK)
    ]
    return jnp.concatenate(parts, axis=0)


def partial_stats(s, dp):
    peak = jnp.max(s, axis=0, keepdims=True)
    e = jnp.exp(s - peak)
    return e, peak, jnp.sum(e, axis=0, keepdims=True), jnp.sum(e * dp, axis=0, keepdims=True)


def stat_rows(a, b, c):
    return jnp.concatenate([a, b, c, jnp.zeros((5, a.shape[1]), F32)], axis=0)[None]


def merge(stats, mine):
    t_peak, t_total, t_moment = stats[0, 0:1], stats[0, 1:2], stats[0, 2:3]
    peak, total, moment = mine
    top = jnp.maximum(t_peak, peak)
    t_scale = jnp.exp(t_peak - top)
    scale = jnp.exp(peak - top)
    full = t_total * t_scale + total * scale
    inverse = jnp.where(full > 0, 1.0 / full, 0.0)
    delta = (t_moment * t_scale + moment * scale) * inverse
    return top, inverse, delta, scale * inverse


def gradients(p, dp, delta, q, g, k):
    pb = p.astype(BF16)
    ds = (p * (dp - delta)).astype(BF16)
    return dot_first(ds, k) * FACTOR, dot(ds, q) * FACTOR, dot(pb, g)


def pack_kernel(enc_dev, loop, info, ids_ref, *refs):
    qm, gm, xqm, xgm, q, g, k, v, xq, xg, pool, swap_ref, xm, xo, sm, so = refs
    shape = (EXTRA, xm.shape[1])
    row = lax.broadcasted_iota(jnp.int32, shape, 0)
    lane = lax.broadcasted_iota(jnp.int32, shape, 1) + pl.program_id(0) * shape[1]
    ids = ids_ref[...]
    owner = ids // enc_dev
    relative = owner - info[0] + 1
    relative = jnp.where(relative < 0, relative + loop, relative)
    relative = jnp.where(relative >= loop, relative - loop, relative)
    slots = relative * enc_dev + ids - owner * enc_dev
    times = jnp.zeros(shape, F32)
    for n in range(ids.shape[0]):
        for s in range(ids.shape[1]):
            hit = (row == slots[n : n + 1, s : s + 1]) & (lane // STRETCH == s)
            times = times + jnp.where(hit, 1.0, 0.0)
    times = times.astype(BF16)
    for index, ref in enumerate((q, g, k, v, xq, xg)):
        swap_ref[index * ROWS : (index + 1) * ROWS] = ref[...]
    swap_ref[6 * ROWS : 7 * ROWS] = pool[0]
    swap_ref[7 * ROWS : 8 * ROWS] = pool[1]
    swap_ref[8 * ROWS :] = times
    for out, first, second in ((xm, xqm, xgm), (xo, xq, xg), (sm, qm, gm), (so, q, g)):
        out[0:ROWS] = first[...]
        out[ROWS : 2 * ROWS] = second[...]
    xm[2 * ROWS :] = times
    xo[2 * ROWS :] = times


def ordered(core, a, b):
    return jnp.where(core == 0, a, b), jnp.where(core == 0, b, a)


def split3(x):
    high = x.astype(BF16)
    rest = x - high.astype(F32)
    middle = rest.astype(BF16)
    return [high, middle, (rest - middle.astype(F32)).astype(BF16)]


def put_stats(ref, stats):
    rows = []
    for low in range(0, stats[0].shape[1], HEAD_DIM):
        for x in stats:
            rows += split3(x[:, low : low + HEAD_DIM])
    rows.append(jnp.zeros((ref.shape[0] - ROWS - len(rows), HEAD_DIM), BF16))
    ref[ROWS:] = jnp.concatenate(rows, axis=0)


def take_stats(ref, lanes):
    x = ref[...].astype(F32)
    stats = []
    for index in range(3):
        parts = []
        for low in range(3 * index, 9 * (lanes // HEAD_DIM), 9):
            parts.append(x[low : low + 1] + x[low + 1 : low + 2] + x[low + 2 : low + 3])
        stats.append(jnp.concatenate(parts, axis=1))
    return stats


def wide_scores(keys_x, keys_y, values_x, values_y, qs, gs, bias):
    sx = dot_last(keys_x, qs) * FACTOR + bias[:ROWS]
    sy = dot_last(keys_y, qs[ROWS:]) * FACTOR + bias[ROWS:, ROWS:]
    return sx, sy, dot_last(values_x, gs), dot_last(values_y, gs[ROWS:])


def wide_stats(sx, sy, dpx, dpy):
    peak = jnp.max(sx, axis=0, keepdims=True)
    peak_y = jnp.maximum(peak[:, ROWS:], jnp.max(sy, axis=0, keepdims=True))
    peak = jnp.concatenate([peak[:, :ROWS], peak_y], axis=1)
    ex, ey = jnp.exp(sx - peak), jnp.exp(sy - peak_y)
    widen = lambda a, b: jnp.concatenate([a[:, :ROWS], a[:, ROWS:] + b], axis=1)
    add = lambda a: jnp.sum(a, axis=0, keepdims=True)
    return ex, ey, peak, widen(add(ex), add(ey)), widen(add(ex * dpx), add(ey * dpy))


def wide_gradients(px, py, dpx, dpy, delta, qs, gs, kx, ky):
    pbx, pby = px.astype(BF16), py.astype(BF16)
    dsx = (px * (dpx - delta)).astype(BF16)
    dsy = (py * (dpy - delta[:, ROWS:])).astype(BF16)
    dq_z = dot_first(dsx[:, :ROWS], kx) * FACTOR
    dq_y = dot_first(both(dsx[:, ROWS:], dsy), both(kx, ky)) * FACTOR
    dkx, dky = dot(dsx, qs) * FACTOR, dot(dsy, qs[ROWS:]) * FACTOR
    return dq_z, dq_y, dkx, dky, dot(pbx, gs), dot(pby, gs[ROWS:])


def local_self(core, bias, q, g, k, v, pq, pg, pk, pv):
    q0, q1 = ordered(core, q[...], pq[...])
    g0, g1 = ordered(core, g[...], pg[...])
    k0, k1 = ordered(core, k[...], pk[...])
    v0, v1 = ordered(core, v[...], pv[...])
    qs, gs = both(q0, q1), both(g0, g1)
    return wide_scores(k0, k1, v0, v1, qs, gs, bias[...]), qs, gs, k0, k1


def local_cross(core, w, pw, q, g, pool, pq, pg, pk, pv):
    qs, gs = both(q[...], pq[...]), both(g[...], pg[...])
    ks, vs = both(pool[0], pk[...]), both(pool[1], pv[...])
    own = both(slot_pair(w, 2, core), slot_pair(w, 4, core, 0))
    partner = both(slot_pair(pw, 0, core, 4), slot_pair(pw, 2, core))
    s = add_rows(dot_last(ks, qs) * FACTOR, jnp.concatenate([own, partner], axis=1))
    return s, dot_last(vs, gs), qs, gs, ks


def self_stats_kernel(info, *refs):
    scores = local_self(info[0] % 2, *refs[:-1])[0]
    refs[-1][...] = stat_rows(*wide_stats(*scores)[2:])


def cross_stats_kernel(info, *refs):
    s, dp, _, _, _ = local_cross(info[0] % 2, *refs[:-2])
    stats = stat_rows(*partial_stats(s, dp)[1:])
    refs[-2][...] = stats[:, :, :ROWS]
    refs[-1][...] = stats[:, :, ROWS:]


def self_remote_kernel(
    info, bias, sq, sg, cq, cg, k, v, pk, pv, stats, dq_same, dq_cross, kv_ref
):
    core = info[0] % 2
    q0, q1 = ordered(core, sq[...], cq[...])
    g0, g1 = ordered(core, sg[...], cg[...])
    k0, k1 = ordered(core, k[...], pk[...])
    v0, v1 = ordered(core, v[...], pv[...])
    qs, gs = both(q1, q0), both(g1, g0)
    sx, sy, dpx, dpy = wide_scores(k1, k0, v1, v0, qs, gs, bias[...])
    ex, ey, *mine = wide_stats(sx, sy, dpx, dpy)
    known = stats[...]
    known = jnp.concatenate([known[:, :, ROWS:], known[:, :, :ROWS]], axis=2)
    top, inverse, delta, scale = merge(known, mine)
    px, py = ex * scale, ey * scale[:, ROWS:]
    dq1, dq0, dk1, dk0, dv1, dv0 = wide_gradients(px, py, dpx, dpy, delta, qs, gs, k1, k0)
    same, cross = ordered(core, dq0, dq1)
    dq_same[:ROWS] = same.astype(BF16)
    put_stats(dq_same, (top, inverse, delta))
    dq_cross[...] = cross.astype(BF16)
    for index, grad in enumerate(ordered(core, dk0, dk1) + ordered(core, dv0, dv1)):
        kv_ref[index * ROWS : (index + 1) * ROWS] = grad.astype(BF16)


def cross_remote_kernel(
    info, sw, cw, sq, sg, cq, cg, pool, pk, pv, s_stats, c_stats, *outs
):
    dq_same, dq_cross, kv_ref = outs
    core = info[0] % 2
    jobs = (
        (cq, cg, pool[0], pool[1], slot_pair(cw, 4, core, 0), c_stats, dq_cross, 0),
        (sq, sg, pk[...], pv[...], slot_pair(sw, 0, core, 4), s_stats, dq_same, 1),
    )
    for q, g, k, v, rows, stats, dq_ref, place in jobs:
        s, dp = add_rows(dot_last(k, q[...]) * FACTOR, rows), dot_last(v, g[...])
        e, *mine = partial_stats(s, dp)
        top, inverse, delta, scale = merge(stats[...], mine)
        dq, dk, dv = gradients(e * scale, dp, delta, q[...], g[...], k)
        dq_ref[:ROWS] = dq.astype(BF16)
        put_stats(dq_ref, (top, inverse, delta))
        kv_ref[place * ROWS : (place + 1) * ROWS] = dk.astype(BF16)
        kv_ref[(2 + place) * ROWS : (3 + place) * ROWS] = dv.astype(BF16)


def self_local_kernel(info, *refs):
    stats_ref, dq_ref, own_ref, kv_ref, mine, theirs = refs[-6:]
    local = own_ref[0]
    core = info[0] % 2
    first = info[0] < 2
    stats = take_stats(stats_ref, 2 * ROWS)
    stats = [jnp.concatenate([x[:, ROWS:], x[:, :ROWS]], axis=1) for x in stats]
    inverse = 1.0 / local[1:2]
    top = jnp.where(first, local[0:1], stats[0])
    delta = jnp.where(first, local[2:3] * inverse, stats[2])
    inverse = jnp.where(first, inverse, stats[1])
    (sx, sy, dpx, dpy), qs, gs, k0, k1 = local_self(core, *refs[:-6])
    px = jnp.exp(sx - top) * inverse
    py = jnp.exp(sy - top[:, ROWS:]) * inverse[:, ROWS:]
    dq0, dq1, dk0, dk1, dv0, dv1 = wide_gradients(px, py, dpx, dpy, delta, qs, gs, k0, k1)
    grads = (ordered(core, dq0, dq1), ordered(core, dk0, dk1), ordered(core, dv0, dv1))
    for index, pair in enumerate(grads):
        for out, place, grad in ((mine, 0, pair[0]), (theirs, 1, pair[1])):
            if index == 0 and place == 0:
                grad = grad + dq_ref[...].astype(F32)
            if index > 0:
                low = (2 * index - 2 + place) * ROWS
                grad = grad + kv_ref[low : low + ROWS].astype(F32)
            out[index * ROWS : (index + 1) * ROWS] = grad.astype(BF16)


def cross_local_kernel(info, *refs):
    own_stats, partner_stats, own_dq, partner_dq, kv_ref, mine, theirs = refs[-7:]
    own, partner = take_stats(own_stats, ROWS), take_stats(partner_stats, ROWS)
    top, inverse, delta = [jnp.concatenate([own[i], partner[i]], axis=1) for i in range(3)]
    s, dp, qs, gs, ks = local_cross(info[0] % 2, *refs[:-7])
    dq, dk, dv = gradients(jnp.exp(s - top) * inverse, dp, delta, qs, gs, ks)
    dq = dq + both(own_dq[...], partner_dq[...]).astype(F32)
    dk = dk + kv_ref[: 2 * ROWS].astype(F32)
    dv = dv + kv_ref[2 * ROWS :].astype(F32)
    for index, grad in enumerate((dq, dk, dv)):
        mine[index * ROWS : (index + 1) * ROWS] = grad[:ROWS].astype(BF16)
        theirs[index * ROWS : (index + 1) * ROWS] = grad[ROWS:].astype(BF16)


def self_final_kernel(info, mine, theirs, dq_theirs, *outs):
    def write(source, dq):
        outs[0][...] = dq.astype(BF16)
        outs[1][...] = source[ROWS : 2 * ROWS]
        outs[2][...] = source[2 * ROWS :]

    @pl.when(pl.program_id(0) == 0)
    def _():
        write(mine, mine[:ROWS])

    @pl.when(pl.program_id(0) == 1)
    def _():
        write(theirs, theirs[:ROWS].astype(F32) + dq_theirs[...].astype(F32))


def cross_final_kernel(info, mine, theirs, dq_out, pool_out):
    def write(source):
        dq_out[...] = source[:ROWS]
        pool_out[0] = source[ROWS : 2 * ROWS]
        pool_out[1] = source[2 * ROWS :]

    pl.when(pl.program_id(0) == 0)(lambda: write(mine))
    pl.when(pl.program_id(0) == 1)(lambda: write(theirs))


def assemble(kernel, name, info, inputs, pooled):
    half = lambda h, info: (info[0] + h) % 2
    rows_out = pl.BlockSpec((ROWS, WIDE), lambda h, info: (0, half(h, info)))
    pool_out = pl.BlockSpec((2, ROWS, WIDE), lambda h, info: (0, 0, half(h, info)))
    full = ((ROWS, 2 * WIDE), BF16)
    if pooled:
        out_specs, outs = [rows_out, pool_out], [full, ((2, ROWS, 2 * WIDE), BF16)]
    else:
        out_specs, outs = [rows_out] * 3, [full] * 3
    in_specs = [whole_spec(x.shape) for x in inputs]
    return call(kernel, name, info, in_specs, inputs, out_specs, outs, steps=2)


def body(
    queries, keys, values, grad_self, doc_ids, cross_queries, grad_cross, pool_kv, neighbour_ids
):
    loop = lax.axis_size("ctx")
    me = lax.axis_index("ctx").astype(jnp.int32)
    info = jnp.full((1,), me, jnp.int32)
    enc_dev = pool_kv.shape[1]
    width = queries.shape[1]
    pool = pool_kv.reshape(2, ROWS, width)
    flops_l, flops_x, flops_s = 0, 0, 0

    cols = WIDE // 2
    block = lambda rows: pl.BlockSpec((rows, cols), lambda h, info: (0, h))
    mine_spec = pl.BlockSpec((ROWS, cols), lambda h, info: (0, info[0] % 2 * 2 + h))
    their_spec = pl.BlockSpec((ROWS, cols), lambda h, info: (0, (1 - info[0] % 2) * 2 + h))
    their_pool = pl.BlockSpec((2, ROWS, cols), lambda h, info: (0, 0, (1 - info[0] % 2) * 2 + h))
    sizes = (8 * ROWS + EXTRA, 2 * ROWS + EXTRA, 2 * ROWS + EXTRA, 2 * ROWS, 2 * ROWS)
    packed, x_mine, x_other, s_mine, s_other = call(
        functools.partial(pack_kernel, enc_dev, loop),
        "pack",
        info,
        [whole_spec(neighbour_ids.shape[::-1])] + [mine_spec] * 4 + [their_spec] * 6 + [their_pool],
        (neighbour_ids.T, queries, grad_self, cross_queries, grad_cross)
        + (queries, grad_self, keys, values, cross_queries, grad_cross, pool),
        [block(rows) for rows in sizes],
        [((rows, WIDE), BF16) for rows in sizes],
        steps=2,
    )
    partner = send(packed, swap, False)
    x_same = send(x_mine, outward, True)
    x_cross = send(x_other, across, True)

    ids_of = lambda d: lax.dynamic_slice_in_dim(doc_ids, d * ROWS, ROWS, 0)
    span = jnp.arange(ROWS, dtype=jnp.int32)
    base = me // 2 * 2
    places = jnp.concatenate([span + base * ROWS, span + (base + 1) * ROWS])
    near0, near1, far0, far1 = [ids_of(base + j) for j in range(4)]
    near = jnp.concatenate([near0, near1])
    near_flip = jnp.concatenate([near1, near0])
    far_flip = jnp.concatenate([far1, far0])
    local_ok = (near[:, None] == near[None, :]) & (places[:, None] <= places[None, :])
    far_ok = (near_flip[:, None] == far_flip[None, :]) & (base + 2 < loop)
    local_bias = jnp.where(local_ok, 0.0, MASKED).astype(F32)
    far_bias = jnp.where(far_ok, 0.0, MASKED).astype(F32)

    bias_spec = whole_spec((2 * ROWS, 2 * ROWS))
    self_specs = [bias_spec] + [own_spec()] * 4 + [spec(ROWS, j) for j in range(4)]
    self_args = (local_bias, queries, grad_self, keys, values) + (partner,) * 4
    mine_w = whole_spec((EXTRA, WIDE), (2 * ROWS // EXTRA, 0))
    partner_w = whole_spec((EXTRA, WIDE), (8 * ROWS // EXTRA, 0))
    cross_specs = (
        [mine_w, partner_w, own_spec(), own_spec(), own_spec((2,))]
        + [spec(ROWS, j) for j in range(4, 8)]
    )
    cross_args = (x_mine, partner, cross_queries, grad_cross, pool) + (partner,) * 4
    stat = lambda rows: ((HALF, 8, rows), F32)

    x_own, x_partner = call(
        cross_stats_kernel, "cross_stats", info, cross_specs, cross_args,
        [stat_spec(ROWS)] * 2, [stat(ROWS)] * 2, flops=flops_l,
    )
    t_same = send(x_own, outward, True)
    t_cross = send(x_partner, inward, True)
    s_mine, s_other, x_own = lax.optimization_barrier((s_mine, s_other, x_own))
    s_same = send(s_mine, lambda d: d - 2, False)
    s_cross = send(s_other, lambda d: (d - 2) ^ 1, False)

    (s_own,) = call(
        self_stats_kernel, "self_stats", info, self_specs, self_args,
        [stat_spec(2 * ROWS)], [stat(2 * ROWS)], flops=flops_l,
    )
    t_self = send(s_own, lambda d: d - 2, False)

    kv_out = spec(4 * ROWS)
    kv_shape = ((4 * ROWS, WIDE), BF16)
    q_shape = ((ROWS, WIDE), BF16)
    tagged = spec(ROWS + STATS)
    tagged_shape = ((ROWS + STATS, WIDE), BF16)
    xd_same, xd_cross, x_kv = call(
        cross_remote_kernel, "cross_remote", info,
        [mine_w, mine_w, spec(ROWS, 0), spec(ROWS, 1), spec(ROWS, 0), spec(ROWS, 1)]
        + [own_spec((2,)), spec(ROWS, 6), spec(ROWS, 7), stat_spec(ROWS), stat_spec(ROWS)],
        (x_same, x_cross, x_same, x_same, x_cross, x_cross, pool, partner, partner, t_same, t_cross),
        [tagged, tagged, kv_out],
        [tagged_shape, tagged_shape, kv_shape], flops=flops_x,
    )
    xr_same = send(xd_same, inward, True)
    xr_cross = send(xd_cross, outward, True)

    far_bias, x_kv = lax.optimization_barrier((far_bias, x_kv))
    sd_same, sd_cross, s_kv = call(
        self_remote_kernel, "self_remote", info,
        [bias_spec, spec(ROWS, 0), spec(ROWS, 1), spec(ROWS, 0), spec(ROWS, 1)]
        + [own_spec(), own_spec(), spec(ROWS, 2), spec(ROWS, 3), stat_spec(2 * ROWS)],
        (far_bias, s_same, s_same, s_cross, s_cross, keys, values, partner, partner, t_self),
        [spec(ROWS + 2 * STATS), spec(ROWS), kv_out],
        [((ROWS + 2 * STATS, WIDE), BF16), q_shape, kv_shape], flops=flops_s,
    )
    sr_same = send(sd_same, lambda d: d + 2, False)
    sr_cross = send(sd_cross, lambda d: (d + 2) ^ 1, False)

    half_out = spec(3 * ROWS)
    half_shape = ((3 * ROWS, WIDE), BF16)
    x_keep, x_give = call(
        cross_local_kernel, "cross_local", info,
        cross_specs
        + [spec(STATS, ROWS // STATS), spec(STATS, ROWS // STATS), spec(ROWS), spec(ROWS)]
        + [spec(4 * ROWS)],
        cross_args + (xr_same, xr_cross, xr_same, xr_cross, x_kv),
        [half_out] * 2, [half_shape] * 2, flops=0,
    )
    x_take = send(x_give, swap, False)
    s_keep, s_give = call(
        self_local_kernel, "self_local", info,
        self_specs
        + [spec(2 * STATS, ROWS // (2 * STATS)), spec(ROWS), stat_spec(2 * ROWS), spec(4 * ROWS)],
        self_args + (sr_same, sr_same, s_own, s_kv),
        [half_out] * 2, [half_shape] * 2, flops=flops_s,
    )
    s_take = send(s_give, swap, False)
    grad_cq, grad_pool = assemble(cross_final_kernel, "cross_final", info, (x_keep, x_take), True)
    grad_q, grad_k, grad_v = assemble(
        self_final_kernel, "self_final", info, (s_keep, s_take, sr_cross), False
    )
    return grad_q, grad_k, grad_v, grad_cq, grad_pool.reshape(pool_kv.shape)


def solution(mesh):
    rows = P(("groups", "ctx"), None)
    pool = P(None, ("groups", "ctx"), None, None)
    return jax.shard_map(
        body,
        mesh=mesh,
        in_specs=(rows, rows, rows, rows, P("groups"), rows, rows, pool, rows),
        out_specs=(rows, rows, rows, rows, pool),
        check_vma=False,
    )
```

time: 134 us -> 129 us (0.963)
  the two profiles are of different devices: /device:TPU:15 before, /device:TPU:17 now
where the time goes in v3:
time: 129 us; the launch traced here: 128 us
  waiting for transfers between devices  53.5 us (41%)
  Pallas kernels  45.4 us (35%)
  starting transfers between devices  21.2 us (16%)
  local copies, waits for them, and re-layouts  4.85 us (4%)
  other arithmetic  2.48 us (2%)
    ppermute x14, waiting for transfers between devices, send(): return lax.ppermute(value, 'ctx', pairs)  53.5 us
    pallas_call x9, Pallas kernels, call(): pl.pallas_call(kernel, name=name, grid_spec=pltpu.PrefetchScalarGridSpec(...  45.4 us
    ppermute x14, starting transfers between devices, send(): return lax.ppermute(value, 'ctx', pairs)  21.2 us
    unnamed x18, local copies, waits for them, and re-layouts  3.94 us
  transfers between devices with their start and end apart: 14, of which 5 were waited for; matrix products, arithmetic and copies ran while one was open for 3% of the time, Pallas kernels for 25%

profile of v3, /device:TPU:17, one launch (start us, length us, event | category | flops | bytes accessed | tf_op | source)
XLA Modules:
  0.0 128.2 jit_solution(4173906297933701192)
XLA Ops:
  0.6 3.7 %pack.1 = (bf16[2064,512]{1,0:T(8,128)(2,1)}, bf16[528,512]{1,0:T(8,128)(2,1)}, bf16[528,512]{1,0:T(8,128)(2,1)}, bf16[512,512]{1,0:T(8,128)(2,1)}, bf16[512,512]{1,0:T(8,128)(2,1)}) custom-call(s32[1]{0:T(128)} %bitcast.info, s32[2,4]{1,0:T(2,128)} %bitcast.8, bf16[256,1024]{1,0:T(8,128)(2,1)} %refs_1_.5, bf16[256,1024]{1,0:T(8,128)(2,1)} %refs_2_.8, ...), custom_call_target="tpu_custom_call" | custom-call | tf_op jit(solution)/shard_map/pack/pallas_call | solution.py:83
  5.0 1.2 collective-permute-start.1
  7.7 1.5 %collective-permute-done.refs_1_.refs_5_.refs_6_.refs_7_.refs_8_.pk.pv = bf16[2064,512]{1,0:T(8,128)(2,1)} collective-permute-done((bf16[2064,512]{1,0:T(8,128)(2,1)}, bf16[2064,512]{1,0:T(8,128)(2,1)}, u32[]{:S(2)}, u32[]{:S(2)}) %collective-permute-start) | collective-permute-done | bytes 2113568 | tf_op jit(solution)/shard_map/ppermute | solution.py:35
  9.2 4.6 %cross_stats.1 = (f32[4,8,256]{2,1,0:T(8,128)}, f32[4,8,256]{2,1,0:T(8,128)}) custom-call(s32[1]{0:T(128)} %bitcast.info, bf16[528,512]{1,0:T(8,128)(2,1)} %get-tuple-element.32.refs_0_, bf16[2064,512]{1,0:T(8,128)(2,1)} %collective-permute-done.refs_1_.refs_5_.refs_6_.refs_7_.refs_8_.pk.pv, bf16[256,1024]{1,0:T(8,128)(2,1)} %refs_2_.9, ...), custom_call_target="tpu_custom_call" | custom-call | tf_op jit(solution)/shard_map/cross_stats/pallas_call | solution.py:83
  13.8 3.0 %collective-permute-start.5 = (bf16[512,512]{1,0:T(8,128)(2,1)}, bf16[512,512]{1,0:T(8,128)(2,1)}, u32[]{:S(2)}, u32[]{:S(2)}) collective-permute-start(bf16[512,512]{1,0:T(8,128)(2,1)} %get-tuple-element.40), channel_id=1, source_target_pairs={{2,0},{3,1},{4,2},{5,3},{6,4},{7,5},{8,6},{9,7},{10,8},{11,9},{12,... | collective-permute-start | bytes 1572872 | tf_op jit(solution)/shard_map/ppermute | solution.py:35
  16.9 2.7 %collective-permute-start.6 = (bf16[512,512]{1,0:T(8,128)(2,1)}, bf16[512,512]{1,0:T(8,128)(2,1)}, u32[]{:S(2)}, u32[]{:S(2)}) collective-permute-start(bf16[512,512]{1,0:T(8,128)(2,1)} %get-tuple-element.41), channel_id=1, source_target_pairs={{2,1},{3,0},{4,3},{5,2},{6,5},{7,4},{8,7},{9,6},{10,9},{11,8},{12,... | collective-permute-start | bytes 1572872 | tf_op jit(solution)/shard_map/ppermute | solution.py:35
  19.6 1.2 and_select_fusion.1.refs_0_
  20.7 1.2 collective-permute-start.3
  22.0 4.8 %self_stats.1.refs_11_ = f32[4,8,512]{2,1,0:T(8,128)} custom-call(s32[1]{0:T(128)} %bitcast.info, f32[512,512]{1,0:T(8,128)} %and_select_fusion.1.refs_0_, bf16[256,1024]{1,0:T(8,128)(2,1)} %refs_1_.5, bf16[256,1024]{1,0:T(8,128)(2,1)} %refs_2_.8, bf16[256,1024]{1,0:T(8,128)(2,1)} %refs_3_.8, bf16[256,1024]{1,0:T(8,128)(2,1)} %refs_4_.5, ...), custom_call_target="tpu_custom_call" | custom-call | tf_op jit(solution)/shard_map/self_stats/pallas_call | solution.py:83
  26.8 20.9 %collective-permute-done.1.sw.sq.sg = bf16[528,512]{1,0:T(8,128)(2,1)S(1)} collective-permute-done((bf16[528,512]{1,0:T(8,128)(2,1)}, bf16[528,512]{1,0:T(8,128)(2,1)S(1)}, u32[]{:S(2)}, u32[]{:S(2)}) %collective-permute-start.1) | collective-permute-done | bytes 540704 | tf_op jit(solution)/shard_map/ppermute | solution.py:35
  47.7 1.7 %collective-permute-start.4 = (f32[4,8,256]{2,1,0:T(8,128)S(1)}, f32[4,8,256]{2,1,0:T(8,128)S(1)}, u32[]{:S(2)}, u32[]{:S(2)}) collective-permute-start(f32[4,8,256]{2,1,0:T(8,128)S(1)} %copy-done.8), channel_id=1, source_target_pairs={{0,2},{1,15},{2,4},{3,1},{4,6},{5,3},{6,8},{7,5},{8,10},{9,7},{10,... | collective-permute-start | bytes 98312 | tf_op jit(solution)/shard_map/ppermute | solution.py:35
  49.4 5.2 %collective-permute-done.2.cw.cq.cg = bf16[528,512]{1,0:T(8,128)(2,1)} collective-permute-done((bf16[528,512]{1,0:T(8,128)(2,1)}, bf16[528,512]{1,0:T(8,128)(2,1)}, u32[]{:S(2)}, u32[]{:S(2)}) %collective-permute-start.2) | collective-permute-done | bytes 540704 | tf_op jit(solution)/shard_map/ppermute | solution.py:35
  54.5 1.9 %collective-permute-start.7 = (f32[4,8,512]{2,1,0:T(8,128)}, f32[4,8,512]{2,1,0:T(8,128)S(1)}, u32[]{:S(2)}, u32[]{:S(2)}) collective-permute-start(f32[4,8,512]{2,1,0:T(8,128)} %self_stats.1.refs_11_), channel_id=1, source_target_pairs={{2,0},{3,1},{4,2},{5,3},{6,4},{7,5},{8,6},{9,7},{10,8},{11,9},{12,... | collective-permute-start | bytes 196616 | tf_op jit(solution)/shard_map/ppermute | solution.py:35
  56.5 1.3 and_select_fusion.bias
  59.0 6.4 %cross_remote.1 = (bf16[288,512]{1,0:T(8,128)(2,1)}, bf16[288,512]{1,0:T(8,128)(2,1)}, bf16[1024,512]{1,0:T(8,128)(2,1)}) custom-call(s32[1]{0:T(128)} %bitcast.info, bf16[528,512]{1,0:T(8,128)(2,1)} %copy-done, bf16[528,512]{1,0:T(8,128)(2,1)} %collective-permute-done.2.cw.cq.cg, bf16[528,512]{1,0:T(8,128)(2,1)} %copy-done, bf16[528,512]{1,0:T(8,128)(2,1)} %copy-done, ...), custom_call_target="tpu_custom_call" | custom-call | tf_op jit(solution)/shard_map/cross_remote/pallas_call | solution.py:83
  66.0 7.0 %self_remote.1 = (bf16[320,512]{1,0:T(8,128)(2,1)}, bf16[256,512]{1,0:T(8,128)(2,1)}, bf16[1024,512]{1,0:T(8,128)(2,1)}) custom-call(s32[1]{0:T(128)} %bitcast.info, f32[512,512]{1,0:T(8,128)} %and_select_fusion.bias, bf16[512,512]{1,0:T(8,128)(2,1)} %collective-permute-done.5.sq.sg, bf16[512,512]{1,0:T(8,128)(2,1)} %collective-permute-done.5.sq.sg, ...), custom_call_target="tpu_custom_call" | custom-call | tf_op jit(solution)/shard_map/self_remote/pallas_call | solution.py:83
  73.0 3.4 %collective-permute-start.8 = (bf16[320,512]{1,0:T(8,128)(2,1)}, bf16[320,512]{1,0:T(8,128)(2,1)S(1)}, u32[]{:S(2)}, u32[]{:S(2)}) collective-permute-start(bf16[320,512]{1,0:T(8,128)(2,1)} %get-tuple-element.42), channel_id=1, source_target_pairs={{0,2},{1,3},{2,4},{3,5},{4,6},{5,7},{6,8},{7,9},{8,10},{9,11},{10,... | collective-permute-start | bytes 983048 | tf_op jit(solution)/shard_map/ppermute | solution.py:35
  77.9 20.5 %collective-permute-done.11.refs_9_.refs_11_ = bf16[288,512]{1,0:T(8,128)(2,1)S(1)} collective-permute-done((bf16[288,512]{1,0:T(8,128)(2,1)}, bf16[288,512]{1,0:T(8,128)(2,1)S(1)}, u32[]{:S(2)}, u32[]{:S(2)}) %collective-permute-start.11) | collective-permute-done | bytes 294944 | tf_op jit(solution)/shard_map/ppermute | solution.py:35
  99.1 6.9 %cross_local.1 = (bf16[768,512]{1,0:T(8,128)(2,1)}, bf16[768,512]{1,0:T(8,128)(2,1)}) custom-call(s32[1]{0:T(128)} %bitcast.info, bf16[528,512]{1,0:T(8,128)(2,1)} %get-tuple-element.32.refs_0_, bf16[2064,512]{1,0:T(8,128)(2,1)} %collective-permute-done.refs_1_.refs_5_.refs_6_.refs_7_.refs_8_.pk.pv, bf16[256,1024]{1,0:T(8,128)(2,1)} %refs_2_.9, ...), custom_call_target="tpu_custom_call" | custom-call | tf_op jit(solution)/shard_map/cross_local/pallas_call | solution.py:83
  106.8 6.8 %self_local.1 = (bf16[768,512]{1,0:T(8,128)(2,1)}, bf16[768,512]{1,0:T(8,128)(2,1)}) custom-call(s32[1]{0:T(128)} %bitcast.info, f32[512,512]{1,0:T(8,128)} %and_select_fusion.1.refs_0_, bf16[256,1024]{1,0:T(8,128)(2,1)} %refs_1_.5, bf16[256,1024]{1,0:T(8,128)(2,1)} %refs_2_.8, bf16[256,1024]{1,0:T(8,128)(2,1)} %refs_3_.8, bf16[256,1024]{1,0:T(8,128)(2,1)} %refs_4_.5, ...), custom_call_target="tpu_custom_call" | custom-call | tf_op jit(solution)/shard_map/self_local/pallas_call | solution.py:83
  114.2 2.7 %collective-permute-start.10 = (bf16[256,512]{1,0:T(8,128)(2,1)S(1)}, bf16[256,512]{1,0:T(8,128)(2,1)S(1)}, u32[]{:S(2)}, u32[]{:S(2)}) collective-permute-start(bf16[256,512]{1,0:T(8,128)(2,1)S(1)} %copy-done.7), channel_id=1, source_target_pairs={{0,3},{1,2},{2,5},{3,4},{4,7},{5,6},{6,9},{7,8},{8,11},{9,10},{10,... | collective-permute-start | bytes 786440 | tf_op jit(solution)/shard_map/ppermute | solution.py:35
  116.9 2.6 %cross_final.1 = (bf16[256,1024]{1,0:T(8,128)(2,1)}, bf16[2,256,1024]{2,1,0:T(8,128)(2,1)}) custom-call(s32[1]{0:T(128)} %bitcast.info, bf16[768,512]{1,0:T(8,128)(2,1)} %get-tuple-element.53.mine, bf16[768,512]{1,0:T(8,128)(2,1)} %collective-permute-done.13.theirs), custom_call_target="tpu_custom_call" | custom-call | tf_op jit(solution)/shard_map/cross_final/pallas_call | solution.py:83
  119.5 5.4 %collective-permute-done.10.dq_theirs = bf16[256,512]{1,0:T(8,128)(2,1)S(1)} collective-permute-done((bf16[256,512]{1,0:T(8,128)(2,1)S(1)}, bf16[256,512]{1,0:T(8,128)(2,1)S(1)}, u32[]{:S(2)}, u32[]{:S(2)}) %collective-permute-start.10) | collective-permute-done | bytes 262176 | tf_op jit(solution)/shard_map/ppermute | solution.py:35
  125.6 2.6 %self_final.1 = (bf16[256,1024]{1,0:T(8,128)(2,1)}, bf16[256,1024]{1,0:T(8,128)(2,1)}, bf16[256,1024]{1,0:T(8,128)(2,1)}) custom-call(s32[1]{0:T(128)} %bitcast.info, bf16[768,512]{1,0:T(8,128)(2,1)} %get-tuple-element.44.mine, bf16[768,512]{1,0:T(8,128)(2,1)} %collective-permute-done.9.theirs, bf16[256,512]{1,0:T(8,128)(2,1)} %copy-done.3), custom_call_target="tpu_custom_call" | custom-call | tf_op jit(solution)/shard_map/self_final/pallas_call | solution.py:83
  (38 shorter events, 8.3 us)
Async XLA Ops:
  4.3 4.9 %collective-permute-start = (bf16[2064,512]{1,0:T(8,128)(2,1)}, bf16[2064,512]{1,0:T(8,128)(2,1)}, u32[]{:S(2)}, u32[]{:S(2)}) collective-permute-start(bf16[2064,512]{1,0:T(8,128)(2,1)} %get-tuple-element.31), channel_id=1, source_target_pairs={{0,1},{1,0},{2,3},{3,2},{4,5},{5,4},{6,7},{7,6},{8,9},{9,8},{10,11... | collective-permute-start | bytes 6340616 | tf_op jit(solution)/shard_map/ppermute | solution.py:35
  5.0 42.6 %collective-permute-start.1 = (bf16[528,512]{1,0:T(8,128)(2,1)}, bf16[528,512]{1,0:T(8,128)(2,1)S(1)}, u32[]{:S(2)}, u32[]{:S(2)}) collective-permute-start(bf16[528,512]{1,0:T(8,128)(2,1)} %get-tuple-element.32.refs_0_), channel_id=1, source_target_pairs={{0,14},{1,3},{2,0},{3,5},{4,2},{5,7},{6,4},{7,9},{8,6},{9,11},{10,... | collective-permute-start | bytes 1622024 | tf_op jit(solution)/shard_map/ppermute | solution.py:35
  6.3 48.3 %collective-permute-start.2 = (bf16[528,512]{1,0:T(8,128)(2,1)}, bf16[528,512]{1,0:T(8,128)(2,1)}, u32[]{:S(2)}, u32[]{:S(2)}) collective-permute-start(bf16[528,512]{1,0:T(8,128)(2,1)} %get-tuple-element.33), channel_id=1, source_target_pairs={{0,15},{1,2},{2,1},{3,4},{4,3},{5,6},{6,5},{7,8},{8,7},{9,10},{10,... | collective-permute-start | bytes 1622024 | tf_op jit(solution)/shard_map/ppermute | solution.py:35
  13.8 51.6 %collective-permute-start.5 = (bf16[512,512]{1,0:T(8,128)(2,1)}, bf16[512,512]{1,0:T(8,128)(2,1)}, u32[]{:S(2)}, u32[]{:S(2)}) collective-permute-start(bf16[512,512]{1,0:T(8,128)(2,1)} %get-tuple-element.40), channel_id=1, source_target_pairs={{2,0},{3,1},{4,2},{5,3},{6,4},{7,5},{8,6},{9,7},{10,8},{11,9},{12,... | collective-permute-start | bytes 1572872 | tf_op jit(solution)/shard_map/ppermute | solution.py:35
  16.9 48.5 %collective-permute-start.6 = (bf16[512,512]{1,0:T(8,128)(2,1)}, bf16[512,512]{1,0:T(8,128)(2,1)}, u32[]{:S(2)}, u32[]{:S(2)}) collective-permute-start(bf16[512,512]{1,0:T(8,128)(2,1)} %get-tuple-element.41), channel_id=1, source_target_pairs={{2,1},{3,0},{4,3},{5,2},{6,5},{7,4},{8,7},{9,6},{10,9},{11,8},{12,... | collective-permute-start | bytes 1572872 | tf_op jit(solution)/shard_map/ppermute | solution.py:35
  20.7 26.9 %copy-start.8 = (f32[4,8,256]{2,1,0:T(8,128)S(1)}, f32[4,8,256]{2,1,0:T(8,128)}, u32[]{:S(2)}) copy-start(f32[4,8,256]{2,1,0:T(8,128)} %get-tuple-element.35) | copy-start | bytes 98308
  20.7 37.0 %collective-permute-start.3 = (f32[4,8,256]{2,1,0:T(8,128)}, f32[4,8,256]{2,1,0:T(8,128)S(1)}, u32[]{:S(2)}, u32[]{:S(2)}) collective-permute-start(f32[4,8,256]{2,1,0:T(8,128)} %get-tuple-element.34), channel_id=1, source_target_pairs={{0,14},{1,3},{2,0},{3,5},{4,2},{5,7},{6,4},{7,9},{8,6},{9,11},{10,... | collective-permute-start | bytes 98312 | tf_op jit(solution)/shard_map/ppermute | solution.py:35
  47.7 10.1 %copy-start = (bf16[528,512]{1,0:T(8,128)(2,1)}, bf16[528,512]{1,0:T(8,128)(2,1)S(1)}, u32[]{:S(2)}) copy-start(bf16[528,512]{1,0:T(8,128)(2,1)S(1)} %collective-permute-done.1.sw.sq.sg) | copy-start | bytes 1622020
  47.7 10.1 %collective-permute-start.4 = (f32[4,8,256]{2,1,0:T(8,128)S(1)}, f32[4,8,256]{2,1,0:T(8,128)S(1)}, u32[]{:S(2)}, u32[]{:S(2)}) collective-permute-start(f32[4,8,256]{2,1,0:T(8,128)S(1)} %copy-done.8), channel_id=1, source_target_pairs={{0,2},{1,15},{2,4},{3,1},{4,6},{5,3},{6,8},{7,5},{8,10},{9,7},{10,... | collective-permute-start | bytes 98312 | tf_op jit(solution)/shard_map/ppermute | solution.py:35
  54.5 10.8 %collective-permute-start.7 = (f32[4,8,512]{2,1,0:T(8,128)}, f32[4,8,512]{2,1,0:T(8,128)S(1)}, u32[]{:S(2)}, u32[]{:S(2)}) collective-permute-start(f32[4,8,512]{2,1,0:T(8,128)} %self_stats.1.refs_11_), channel_id=1, source_target_pairs={{2,0},{3,1},{4,2},{5,3},{6,4},{7,5},{8,6},{9,7},{10,8},{11,9},{12,... | collective-permute-start | bytes 196616 | tf_op jit(solution)/shard_map/ppermute | solution.py:35
  57.7 0.6 copy-start.5
  58.3 0.6 copy-start.6
  65.4 0.6 copy-start.4
  73.0 33.1 %collective-permute-start.8 = (bf16[320,512]{1,0:T(8,128)(2,1)}, bf16[320,512]{1,0:T(8,128)(2,1)S(1)}, u32[]{:S(2)}, u32[]{:S(2)}) collective-permute-start(bf16[320,512]{1,0:T(8,128)(2,1)} %get-tuple-element.42), channel_id=1, source_target_pairs={{0,2},{1,3},{2,4},{3,5},{4,6},{5,7},{6,8},{7,9},{8,10},{9,11},{10,... | collective-permute-start | bytes 983048 | tf_op jit(solution)/shard_map/ppermute | solution.py:35
  76.3 22.0 %collective-permute-start.11 = (bf16[288,512]{1,0:T(8,128)(2,1)}, bf16[288,512]{1,0:T(8,128)(2,1)S(1)}, u32[]{:S(2)}, u32[]{:S(2)}) collective-permute-start(bf16[288,512]{1,0:T(8,128)(2,1)} %get-tuple-element.50), channel_id=1, source_target_pairs={{0,2},{1,15},{2,4},{3,1},{4,6},{5,3},{6,8},{7,5},{8,10},{9,7},{10,... | collective-permute-start | bytes 884744 | tf_op jit(solution)/shard_map/ppermute | solution.py:35
  77.3 21.1 %collective-permute-start.12 = (bf16[288,512]{1,0:T(8,128)(2,1)}, bf16[288,512]{1,0:T(8,128)(2,1)}, u32[]{:S(2)}, u32[]{:S(2)}) collective-permute-start(bf16[288,512]{1,0:T(8,128)(2,1)} %get-tuple-element.51), channel_id=1, source_target_pairs={{0,14},{1,3},{2,0},{3,5},{4,2},{5,7},{6,4},{7,9},{8,6},{9,11},{10,... | collective-permute-start | bytes 884744 | tf_op jit(solution)/shard_map/ppermute | solution.py:35
  98.3 0.7 copy-start.2
  106.0 10.9 %collective-permute-start.13 = (bf16[768,512]{1,0:T(8,128)(2,1)}, bf16[768,512]{1,0:T(8,128)(2,1)}, u32[]{:S(2)}, u32[]{:S(2)}) collective-permute-start(bf16[768,512]{1,0:T(8,128)(2,1)} %get-tuple-element.54), channel_id=1, source_target_pairs={{0,1},{1,0},{2,3},{3,2},{4,5},{5,4},{6,7},{7,6},{8,9},{9,8},{10,11... | collective-permute-start | bytes 2359304 | tf_op jit(solution)/shard_map/ppermute | solution.py:35
  106.1 0.7 copy-start.1
  106.8 7.4 %copy-start.7 = (bf16[256,512]{1,0:T(8,128)(2,1)S(1)}, bf16[256,512]{1,0:T(8,128)(2,1)}, u32[]{:S(2)}) copy-start(bf16[256,512]{1,0:T(8,128)(2,1)} %get-tuple-element.46) | copy-start | bytes 786436
  113.6 11.3 %collective-permute-start.9 = (bf16[768,512]{1,0:T(8,128)(2,1)}, bf16[768,512]{1,0:T(8,128)(2,1)}, u32[]{:S(2)}, u32[]{:S(2)}) collective-permute-start(bf16[768,512]{1,0:T(8,128)(2,1)} %get-tuple-element.45), channel_id=1, source_target_pairs={{0,1},{1,0},{2,3},{3,2},{4,5},{5,4},{6,7},{7,6},{8,9},{9,8},{10,11... | collective-permute-start | bytes 2359304 | tf_op jit(solution)/shard_map/ppermute | solution.py:35
  114.2 10.7 %collective-permute-start.10 = (bf16[256,512]{1,0:T(8,128)(2,1)S(1)}, bf16[256,512]{1,0:T(8,128)(2,1)S(1)}, u32[]{:S(2)}, u32[]{:S(2)}) collective-permute-start(bf16[256,512]{1,0:T(8,128)(2,1)S(1)} %copy-done.7), channel_id=1, source_target_pairs={{0,3},{1,2},{2,5},{3,4},{4,7},{5,6},{6,9},{7,8},{8,11},{9,10},{10,... | collective-permute-start | bytes 786440 | tf_op jit(solution)/shard_map/ppermute | solution.py:35
  124.9 0.7 copy-start.3

commit v4 on v3

--- a/solution.py
+++ b/solution.py
@@ -17,6 +17,7 @@
 ROWS = 256
 EXTRA = 16
 STATS = 32
+LONG = 12 * 10**9
 FACTOR = HEAD_DIM ** (-0.5)
 MASKED = -1e30
 BF16 = jnp.bfloat16
@@ -276,7 +277,7 @@
 
 
 def self_remote_kernel(
-    info, bias, sq, sg, cq, cg, k, v, pk, pv, stats, dq_same, dq_cross, kv_ref
+    info, bias, sq, sg, cq, cg, k, v, pk, pv, stats, dq_same, dq_cross, kv_ref, out_stats
 ):
     core = info[0] % 2
     q0, q1 = ordered(core, sq[...], cq[...])
@@ -292,11 +293,11 @@
     px, py = ex * scale, ey * scale[:, ROWS:]
     dq1, dq0, dk1, dk0, dv1, dv0 = wide_gradients(px, py, dpx, dpy, delta, qs, gs, k1, k0)
     same, cross = ordered(core, dq0, dq1)
-    dq_same[:ROWS] = same.astype(BF16)
-    put_stats(dq_same, (top, inverse, delta))
+    dq_same[...] = same.astype(BF16)
     dq_cross[...] = cross.astype(BF16)
     for index, grad in enumerate(ordered(core, dk0, dk1) + ordered(core, dv0, dv1)):
         kv_ref[index * ROWS : (index + 1) * ROWS] = grad.astype(BF16)
+    out_stats[...] = stat_rows(top, inverse, delta)
 
 
 def cross_remote_kernel(
@@ -320,25 +321,23 @@
 
 
 def self_local_kernel(info, *refs):
-    stats_ref, dq_ref, own_ref, kv_ref, mine, theirs = refs[-6:]
+    stats_ref, own_ref, kv_ref, mine, theirs = refs[-5:]
     local = own_ref[0]
     core = info[0] % 2
     first = info[0] < 2
-    stats = take_stats(stats_ref, 2 * ROWS)
-    stats = [jnp.concatenate([x[:, ROWS:], x[:, :ROWS]], axis=1) for x in stats]
+    stats = stats_ref[0]
+    stats = jnp.concatenate([stats[:, ROWS:], stats[:, :ROWS]], axis=1)
     inverse = 1.0 / local[1:2]
-    top = jnp.where(first, local[0:1], stats[0])
-    delta = jnp.where(first, local[2:3] * inverse, stats[2])
-    inverse = jnp.where(first, inverse, stats[1])
-    (sx, sy, dpx, dpy), qs, gs, k0, k1 = local_self(core, *refs[:-6])
+    top = jnp.where(first, local[0:1], stats[0:1])
+    delta = jnp.where(first, local[2:3] * inverse, stats[2:3])
+    inverse = jnp.where(first, inverse, stats[1:2])
+    (sx, sy, dpx, dpy), qs, gs, k0, k1 = local_self(core, *refs[:-5])
     px = jnp.exp(sx - top) * inverse
     py = jnp.exp(sy - top[:, ROWS:]) * inverse[:, ROWS:]
     dq0, dq1, dk0, dk1, dv0, dv1 = wide_gradients(px, py, dpx, dpy, delta, qs, gs, k0, k1)
     grads = (ordered(core, dq0, dq1), ordered(core, dk0, dk1), ordered(core, dv0, dv1))
     for index, pair in enumerate(grads):
         for out, place, grad in ((mine, 0, pair[0]), (theirs, 1, pair[1])):
-            if index == 0 and place == 0:
-                grad = grad + dq_ref[...].astype(F32)
             if index > 0:
                 low = (2 * index - 2 + place) * ROWS
                 grad = grad + kv_ref[low : low + ROWS].astype(F32)
@@ -359,19 +358,15 @@
         theirs[index * ROWS : (index + 1) * ROWS] = grad[ROWS:].astype(BF16)
 
 
-def self_final_kernel(info, mine, theirs, dq_theirs, *outs):
-    def write(source, dq):
+def self_final_kernel(info, mine, theirs, dq_mine, dq_theirs, *outs):
+    def write(source, extra):
+        dq = source[:ROWS].astype(F32) + extra[...].astype(F32)
         outs[0][...] = dq.astype(BF16)
         outs[1][...] = source[ROWS : 2 * ROWS]
         outs[2][...] = source[2 * ROWS :]
 
-    @pl.when(pl.program_id(0) == 0)
-    def _():
-        write(mine, mine[:ROWS])
-
-    @pl.when(pl.program_id(0) == 1)
-    def _():
-        write(theirs, theirs[:ROWS].astype(F32) + dq_theirs[...].astype(F32))
+    pl.when(pl.program_id(0) == 0)(lambda: write(mine, dq_mine))
+    pl.when(pl.program_id(0) == 1)(lambda: write(theirs, dq_theirs))
 
 
 def cross_final_kernel(info, mine, theirs, dq_out, pool_out):
@@ -406,7 +401,6 @@
     enc_dev = pool_kv.shape[1]
     width = queries.shape[1]
     pool = pool_kv.reshape(2, ROWS, width)
-    flops_l, flops_x, flops_s = 0, 0, 0
 
     cols = WIDE // 2
     block = lambda rows: pl.BlockSpec((rows, cols), lambda h, info: (0, h))
@@ -456,19 +450,23 @@
 
     x_own, x_partner = call(
         cross_stats_kernel, "cross_stats", info, cross_specs, cross_args,
-        [stat_spec(ROWS)] * 2, [stat(ROWS)] * 2, flops=flops_l,
+        [stat_spec(ROWS)] * 2, [stat(ROWS)] * 2, flops=0,
     )
     t_same = send(x_own, outward, True)
     t_cross = send(x_partner, inward, True)
-    s_mine, s_other, x_own = lax.optimization_barrier((s_mine, s_other, x_own))
+    local_bias, x_own = lax.optimization_barrier((local_bias, x_own))
+    self_args = (local_bias,) + self_args[1:]
+    (s_own,) = call(
+        self_stats_kernel, "self_stats", info, self_specs, self_args,
+        [stat_spec(2 * ROWS)], [stat(2 * ROWS)], flops=0,
+    )
+    t_self = send(s_own, lambda d: d - 2, False)
+    s_mine, s_other, x_same, x_cross, s_own = lax.optimization_barrier(
+        (s_mine, s_other, x_same, x_cross, s_own)
+    )
     s_same = send(s_mine, lambda d: d - 2, False)
     s_cross = send(s_other, lambda d: (d - 2) ^ 1, False)
 
-    (s_own,) = call(
-        self_stats_kernel, "self_stats", info, self_specs, self_args,
-        [stat_spec(2 * ROWS)], [stat(2 * ROWS)], flops=flops_l,
-    )
-    t_self = send(s_own, lambda d: d - 2, False)
 
     kv_out = spec(4 * ROWS)
     kv_shape = ((4 * ROWS, WIDE), BF16)
@@ -481,20 +479,21 @@
         + [own_spec((2,)), spec(ROWS, 6), spec(ROWS, 7), stat_spec(ROWS), stat_spec(ROWS)],
         (x_same, x_cross, x_same, x_same, x_cross, x_cross, pool, partner, partner, t_same, t_cross),
         [tagged, tagged, kv_out],
-        [tagged_shape, tagged_shape, kv_shape], flops=flops_x,
+        [tagged_shape, tagged_shape, kv_shape], flops=0,
     )
     xr_same = send(xd_same, inward, True)
     xr_cross = send(xd_cross, outward, True)
 
     far_bias, x_kv = lax.optimization_barrier((far_bias, x_kv))
-    sd_same, sd_cross, s_kv = call(
+    sd_same, sd_cross, s_kv, s_fin = call(
         self_remote_kernel, "self_remote", info,
         [bias_spec, spec(ROWS, 0), spec(ROWS, 1), spec(ROWS, 0), spec(ROWS, 1)]
         + [own_spec(), own_spec(), spec(ROWS, 2), spec(ROWS, 3), stat_spec(2 * ROWS)],
         (far_bias, s_same, s_same, s_cross, s_cross, keys, values, partner, partner, t_self),
-        [spec(ROWS + 2 * STATS), spec(ROWS), kv_out],
-        [((ROWS + 2 * STATS, WIDE), BF16), q_shape, kv_shape], flops=flops_s,
-    )
+        [spec(ROWS), spec(ROWS), kv_out, stat_spec(2 * ROWS)],
+        [q_shape, q_shape, kv_shape, stat(2 * ROWS)], flops=LONG,
+    )
+    f_self = send(s_fin, lambda d: d + 2, False)
     sr_same = send(sd_same, lambda d: d + 2, False)
     sr_cross = send(sd_cross, lambda d: (d + 2) ^ 1, False)
 
@@ -506,20 +505,22 @@
         + [spec(STATS, ROWS // STATS), spec(STATS, ROWS // STATS), spec(ROWS), spec(ROWS)]
         + [spec(4 * ROWS)],
         cross_args + (xr_same, xr_cross, xr_same, xr_cross, x_kv),
-        [half_out] * 2, [half_shape] * 2, flops=0,
+        [half_out] * 2, [half_shape] * 2, flops=LONG,
     )
     x_take = send(x_give, swap, False)
+    s_kv, x_keep = lax.optimization_barrier((s_kv, x_keep))
     s_keep, s_give = call(
         self_local_kernel, "self_local", info,
         self_specs
-        + [spec(2 * STATS, ROWS // (2 * STATS)), spec(ROWS), stat_spec(2 * ROWS), spec(4 * ROWS)],
-        self_args + (sr_same, sr_same, s_own, s_kv),
-        [half_out] * 2, [half_shape] * 2, flops=flops_s,
-    )
+        + [stat_spec(2 * ROWS), stat_spec(2 * ROWS), spec(4 * ROWS)],
+        self_args + (f_self, s_own, s_kv),
+        [half_out] * 2, [half_shape] * 2, flops=0,
+    )
+    s_give, sr_same, sr_cross = lax.optimization_barrier((s_give, sr_same, sr_cross))
     s_take = send(s_give, swap, False)
     grad_cq, grad_pool = assemble(cross_final_kernel, "cross_final", info, (x_keep, x_take), True)
     grad_q, grad_k, grad_v = assemble(
-        self_final_kernel, "self_final", info, (s_keep, s_take, sr_cross), False
+        self_final_kernel, "self_final", info, (s_keep, s_take, sr_same, sr_cross), False
     )
     return grad_q, grad_k, grad_v, grad_cq, grad_pool.reshape(pool_kv.shape)
 

time: 129 us -> 114 us (0.88)
  the two profiles are of different devices: /device:TPU:17 before, /device:TPU:1 now
where the time goes in v4:
time: 114 us; the launch traced here: 113 us
  Pallas kernels  45.6 us (40%)
  starting transfers between devices  32.6 us (29%)
  waiting for transfers between devices  26.7 us (23%)
  local copies, waits for them, and re-layouts  5.36 us (5%)
  other arithmetic  2.48 us (2%)
    pallas_call x9, Pallas kernels, call(): pl.pallas_call(kernel, name=name, grid_spec=pltpu.PrefetchScalarGridSpec(...  45.6 us
    ppermute x15, starting transfers between devices, send(): return lax.ppermute(value, 'ctx', pairs)  32.6 us
    ppermute x15, waiting for transfers between devices, send(): return lax.ppermute(value, 'ctx', pairs)  26.7 us
    unnamed x20, local copies, waits for them, and re-layouts  4.44 us
  transfers between devices with their start and end apart: 15, of which 4 were waited for; matrix products, arithmetic and copies ran while one was open for 3% of the time, Pallas kernels for 34%

profile of v4, /device:TPU:1, one launch (start us, length us, event | category | flops | bytes accessed | tf_op | source)
XLA Modules:
  0.0 113.5 jit_solution(5287688988649540722)
XLA Ops:
  0.6 3.7 %pack.1 = (bf16[2064,512]{1,0:T(8,128)(2,1)}, bf16[528,512]{1,0:T(8,128)(2,1)}, bf16[528,512]{1,0:T(8,128)(2,1)}, bf16[512,512]{1,0:T(8,128)(2,1)}, bf16[512,512]{1,0:T(8,128)(2,1)}) custom-call(s32[1]{0:T(128)} %bitcast.info, s32[2,4]{1,0:T(2,128)} %bitcast.8, bf16[256,1024]{1,0:T(8,128)(2,1)} %refs_1_.5, bf16[256,1024]{1,0:T(8,128)(2,1)} %refs_2_.9, ...), custom_call_target="tpu_custom_call" | custom-call | tf_op jit(solution)/shard_map/pack/pallas_call | solution.py:84
  4.4 2.7 %collective-permute-start.1 = (bf16[528,512]{1,0:T(8,128)(2,1)}, bf16[528,512]{1,0:T(8,128)(2,1)S(1)}, u32[]{:S(2)}, u32[]{:S(2)}) collective-permute-start(bf16[528,512]{1,0:T(8,128)(2,1)} %get-tuple-element.41.refs_0_), channel_id=1, source_target_pairs={{0,14},{1,3},{2,0},{3,5},{4,2},{5,7},{6,4},{7,9},{8,6},{9,11},{10,... | collective-permute-start | bytes 1622024 | tf_op jit(solution)/shard_map/ppermute | solution.py:36
  9.3 4.6 %cross_stats.1 = (f32[4,8,256]{2,1,0:T(8,128)}, f32[4,8,256]{2,1,0:T(8,128)}) custom-call(s32[1]{0:T(128)} %bitcast.info, bf16[528,512]{1,0:T(8,128)(2,1)} %get-tuple-element.41.refs_0_, bf16[2064,512]{1,0:T(8,128)(2,1)} %collective-permute-done.refs_1_.refs_5_.refs_6_.refs_7_.refs_8_.pk.pv, bf16[256,1024]{1,0:T(8,128)(2,1)} %refs_2_.8, ...), custom_call_target="tpu_custom_call" | custom-call | tf_op jit(solution)/shard_map/cross_stats/pallas_call | solution.py:84
  13.9 4.8 %self_stats.1.refs_10_ = f32[4,8,512]{2,1,0:T(8,128)} custom-call(s32[1]{0:T(128)} %bitcast.info, f32[512,512]{1,0:T(8,128)} %and_select_fusion.1.refs_0_, bf16[256,1024]{1,0:T(8,128)(2,1)} %refs_1_.5, bf16[256,1024]{1,0:T(8,128)(2,1)} %refs_2_.9, bf16[256,1024]{1,0:T(8,128)(2,1)} %refs_3_.9, bf16[256,1024]{1,0:T(8,128)(2,1)} %refs_4_.5, ...), custom_call_target="tpu_custom_call" | custom-call | tf_op jit(solution)/shard_map/self_stats/pallas_call | solution.py:84
  18.8 6.5 %collective-permute-done.1.sw.sq.sg = bf16[528,512]{1,0:T(8,128)(2,1)S(1)} collective-permute-done((bf16[528,512]{1,0:T(8,128)(2,1)}, bf16[528,512]{1,0:T(8,128)(2,1)S(1)}, u32[]{:S(2)}, u32[]{:S(2)}) %collective-permute-start.1) | collective-permute-done | bytes 540704 | tf_op jit(solution)/shard_map/ppermute | solution.py:36
  25.3 6.5 %collective-permute-done.2.cw.cq.cg = bf16[528,512]{1,0:T(8,128)(2,1)} collective-permute-done((bf16[528,512]{1,0:T(8,128)(2,1)}, bf16[528,512]{1,0:T(8,128)(2,1)}, u32[]{:S(2)}, u32[]{:S(2)}) %collective-permute-start.2) | collective-permute-done | bytes 540704 | tf_op jit(solution)/shard_map/ppermute | solution.py:36
  31.8 1.3 %collective-permute-start.5 = (bf16[512,512]{1,0:T(8,128)(2,1)}, bf16[512,512]{1,0:T(8,128)(2,1)}, u32[]{:S(2)}, u32[]{:S(2)}) collective-permute-start(bf16[512,512]{1,0:T(8,128)(2,1)} %get-tuple-element.53), channel_id=1, source_target_pairs={{2,0},{3,1},{4,2},{5,3},{6,4},{7,5},{8,6},{9,7},{10,8},{11,9},{12,... | collective-permute-start | bytes 1572872 | tf_op jit(solution)/shard_map/ppermute | solution.py:36
  33.1 1.3 %collective-permute-start.6 = (bf16[512,512]{1,0:T(8,128)(2,1)}, bf16[512,512]{1,0:T(8,128)(2,1)}, u32[]{:S(2)}, u32[]{:S(2)}) collective-permute-start(bf16[512,512]{1,0:T(8,128)(2,1)} %get-tuple-element.54), channel_id=1, source_target_pairs={{2,1},{3,0},{4,3},{5,2},{6,5},{7,4},{8,7},{9,6},{10,9},{11,8},{12,... | collective-permute-start | bytes 1572872 | tf_op jit(solution)/shard_map/ppermute | solution.py:36
  34.4 2.8 %collective-permute-start.3 = (f32[4,8,256]{2,1,0:T(8,128)S(1)}, f32[4,8,256]{2,1,0:T(8,128)S(1)}, u32[]{:S(2)}, u32[]{:S(2)}) collective-permute-start(f32[4,8,256]{2,1,0:T(8,128)S(1)} %copy-done.9), channel_id=1, source_target_pairs={{0,14},{1,3},{2,0},{3,5},{4,2},{5,7},{6,4},{7,9},{8,6},{9,11},{10,... | collective-permute-start | bytes 98312 | tf_op jit(solution)/shard_map/ppermute | solution.py:36
  37.2 1.3 %collective-permute-start.7 = (f32[4,8,512]{2,1,0:T(8,128)}, f32[4,8,512]{2,1,0:T(8,128)S(1)}, u32[]{:S(2)}, u32[]{:S(2)}) collective-permute-start(f32[4,8,512]{2,1,0:T(8,128)} %self_stats.1.refs_10_), channel_id=1, source_target_pairs={{2,0},{3,1},{4,2},{5,3},{6,4},{7,5},{8,6},{9,7},{10,8},{11,9},{12,... | collective-permute-start | bytes 196616 | tf_op jit(solution)/shard_map/ppermute | solution.py:36
  38.5 7.9 %collective-permute-start.4 = (f32[4,8,256]{2,1,0:T(8,128)S(1)}, f32[4,8,256]{2,1,0:T(8,128)S(1)}, u32[]{:S(2)}, u32[]{:S(2)}) collective-permute-start(f32[4,8,256]{2,1,0:T(8,128)S(1)} %copy-done.8), channel_id=1, source_target_pairs={{0,2},{1,15},{2,4},{3,1},{4,6},{5,3},{6,8},{7,5},{8,10},{9,7},{10,... | collective-permute-start | bytes 98312 | tf_op jit(solution)/shard_map/ppermute | solution.py:36
  46.4 1.3 %and_select_fusion.bias = f32[512,512]{1,0:T(8,128)} fusion(s32[512]{0:T(512)S(1)} %pad_add_fusion.3, s32[512]{0:T(512)S(1)} %get-tuple-element.81, pred[]{:T(512)S(6)} %lt.19), kind=kLoop, calls=%fused_computation | loop fusion | flops 786432 | bytes 1052673 | tf_op jit(solution)/shard_map/jit(_where)/select_n | solution.py:437
  47.6 13.3 %collective-permute-done.3.s_stats = f32[4,8,256]{2,1,0:T(8,128)S(1)} collective-permute-done((f32[4,8,256]{2,1,0:T(8,128)S(1)}, f32[4,8,256]{2,1,0:T(8,128)S(1)}, u32[]{:S(2)}, u32[]{:S(2)}) %collective-permute-start.3) | collective-permute-done | bytes 32800 | tf_op jit(solution)/shard_map/ppermute | solution.py:36
  62.2 6.4 %cross_remote.1 = (bf16[288,512]{1,0:T(8,128)(2,1)}, bf16[288,512]{1,0:T(8,128)(2,1)}, bf16[1024,512]{1,0:T(8,128)(2,1)}) custom-call(s32[1]{0:T(128)} %bitcast.info, bf16[528,512]{1,0:T(8,128)(2,1)} %copy-done, bf16[528,512]{1,0:T(8,128)(2,1)} %collective-permute-done.2.cw.cq.cg, bf16[528,512]{1,0:T(8,128)(2,1)} %copy-done, bf16[528,512]{1,0:T(8,128)(2,1)} %copy-done, ...), custom_call_target="tpu_custom_call" | custom-call | tf_op jit(solution)/shard_map/cross_remote/pallas_call | solution.py:84
  68.6 2.4 %collective-permute-start.10 = (bf16[288,512]{1,0:T(8,128)(2,1)}, bf16[288,512]{1,0:T(8,128)(2,1)S(1)}, u32[]{:S(2)}, u32[]{:S(2)}) collective-permute-start(bf16[288,512]{1,0:T(8,128)(2,1)} %get-tuple-element.59), channel_id=1, source_target_pairs={{0,14},{1,3},{2,0},{3,5},{4,2},{5,7},{6,4},{7,9},{8,6},{9,11},{10,... | collective-permute-start | bytes 884744 | tf_op jit(solution)/shard_map/ppermute | solution.py:36
  71.0 1.8 %collective-permute-start.9 = (bf16[288,512]{1,0:T(8,128)(2,1)}, bf16[288,512]{1,0:T(8,128)(2,1)S(1)}, u32[]{:S(2)}, u32[]{:S(2)}) collective-permute-start(bf16[288,512]{1,0:T(8,128)(2,1)} %get-tuple-element.58), channel_id=1, source_target_pairs={{0,2},{1,15},{2,4},{3,1},{4,6},{5,3},{6,8},{7,5},{8,10},{9,7},{10,... | collective-permute-start | bytes 884744 | tf_op jit(solution)/shard_map/ppermute | solution.py:36
  73.4 7.0 %self_remote.1 = (bf16[256,512]{1,0:T(8,128)(2,1)}, bf16[256,512]{1,0:T(8,128)(2,1)}, bf16[1024,512]{1,0:T(8,128)(2,1)}, f32[4,8,512]{2,1,0:T(8,128)}) custom-call(s32[1]{0:T(128)} %bitcast.info, f32[512,512]{1,0:T(8,128)} %and_select_fusion.bias, bf16[512,512]{1,0:T(8,128)(2,1)} %collective-permute-done.5.sq.sg, ...), custom_call_target="tpu_custom_call" | custom-call | flops 12000000000 | tf_op jit(solution)/shard_map/self_remote/pallas_call | solution.py:84
  80.4 1.6 %collective-permute-start.8 = (f32[4,8,512]{2,1,0:T(8,128)}, f32[4,8,512]{2,1,0:T(8,128)S(1)}, u32[]{:S(2)}, u32[]{:S(2)}) collective-permute-start(f32[4,8,512]{2,1,0:T(8,128)} %get-tuple-element.55), channel_id=1, source_target_pairs={{0,2},{1,3},{2,4},{3,5},{4,6},{5,7},{6,8},{7,9},{8,10},{9,11},{10,... | collective-permute-start | bytes 196616 | tf_op jit(solution)/shard_map/ppermute | solution.py:36
  82.0 4.4 %collective-permute-start.11 = (bf16[256,512]{1,0:T(8,128)(2,1)}, bf16[256,512]{1,0:T(8,128)(2,1)}, u32[]{:S(2)}, u32[]{:S(2)}) collective-permute-start(bf16[256,512]{1,0:T(8,128)(2,1)} %get-tuple-element.65), channel_id=1, source_target_pairs={{0,2},{1,3},{2,4},{3,5},{4,6},{5,7},{6,8},{7,9},{8,10},{9,11},{10,... | collective-permute-start | bytes 786440 | tf_op jit(solution)/shard_map/ppermute | solution.py:36
  86.3 4.5 %collective-permute-start.12 = (bf16[256,512]{1,0:T(8,128)(2,1)}, bf16[256,512]{1,0:T(8,128)(2,1)}, u32[]{:S(2)}, u32[]{:S(2)}) collective-permute-start(bf16[256,512]{1,0:T(8,128)(2,1)} %get-tuple-element.66), channel_id=1, source_target_pairs={{0,3},{1,2},{2,5},{3,4},{4,7},{5,6},{6,9},{7,8},{8,11},{9,10},{10,... | collective-permute-start | bytes 786440 | tf_op jit(solution)/shard_map/ppermute | solution.py:36
  92.2 6.9 %cross_local.1 = (bf16[768,512]{1,0:T(8,128)(2,1)}, bf16[768,512]{1,0:T(8,128)(2,1)}) custom-call(s32[1]{0:T(128)} %bitcast.info, bf16[528,512]{1,0:T(8,128)(2,1)} %get-tuple-element.41.refs_0_, bf16[2064,512]{1,0:T(8,128)(2,1)} %collective-permute-done.refs_1_.refs_5_.refs_6_.refs_7_.refs_8_.pk.pv, bf16[256,1024]{1,0:T(8,128)(2,1)} %refs_2_.8, ...), custom_call_target="tpu_custom_call" | custom-call | flops 12000000000 | tf_op jit(solution)/shard_map/cross_local/pallas_call | solution.py:84
  99.9 6.7 %self_local.1 = (bf16[768,512]{1,0:T(8,128)(2,1)}, bf16[768,512]{1,0:T(8,128)(2,1)}) custom-call(s32[1]{0:T(128)} %bitcast.info, f32[512,512]{1,0:T(8,128)} %and_select_fusion.1.refs_0_, bf16[256,1024]{1,0:T(8,128)(2,1)} %refs_1_.5, bf16[256,1024]{1,0:T(8,128)(2,1)} %refs_2_.9, bf16[256,1024]{1,0:T(8,128)(2,1)} %refs_3_.9, bf16[256,1024]{1,0:T(8,128)(2,1)} %refs_4_.5, ...), custom_call_target="tpu_custom_call" | custom-call | tf_op jit(solution)/shard_map/self_local/pallas_call | solution.py:84
  108.1 2.6 %cross_final.1 = (bf16[256,1024]{1,0:T(8,128)(2,1)}, bf16[2,256,1024]{2,1,0:T(8,128)(2,1)}) custom-call(s32[1]{0:T(128)} %bitcast.info, bf16[768,512]{1,0:T(8,128)(2,1)} %get-tuple-element.73.mine, bf16[768,512]{1,0:T(8,128)(2,1)} %copy-done.1), custom_call_target="tpu_custom_call" | custom-call | tf_op jit(solution)/shard_map/cross_final/pallas_call | solution.py:84
  110.7 2.8 %self_final.1 = (bf16[256,1024]{1,0:T(8,128)(2,1)}, bf16[256,1024]{1,0:T(8,128)(2,1)}, bf16[256,1024]{1,0:T(8,128)(2,1)}) custom-call(s32[1]{0:T(128)} %bitcast.info, bf16[768,512]{1,0:T(8,128)(2,1)} %get-tuple-element.63.mine, bf16[768,512]{1,0:T(8,128)(2,1)} %collective-permute-done.13.theirs, bf16[256,512]{1,0:T(8,128)(2,1)} %collective-permute-done.11.dq_mine, ...), custom_call_target="tpu_custom_call" | custom-call | tf_op jit(solution)/shard_map/self_final/pallas_call | solution.py:84
  (42 shorter events, 7.7 us)
Async XLA Ops:
  4.3 5.0 %collective-permute-start = (bf16[2064,512]{1,0:T(8,128)(2,1)}, bf16[2064,512]{1,0:T(8,128)(2,1)}, u32[]{:S(2)}, u32[]{:S(2)}) collective-permute-start(bf16[2064,512]{1,0:T(8,128)(2,1)} %get-tuple-element.42), channel_id=1, source_target_pairs={{0,1},{1,0},{2,3},{3,2},{4,5},{5,4},{6,7},{7,6},{8,9},{9,8},{10,11... | collective-permute-start | bytes 6340616 | tf_op jit(solution)/shard_map/ppermute | solution.py:36
  4.4 20.9 %collective-permute-start.1 = (bf16[528,512]{1,0:T(8,128)(2,1)}, bf16[528,512]{1,0:T(8,128)(2,1)S(1)}, u32[]{:S(2)}, u32[]{:S(2)}) collective-permute-start(bf16[528,512]{1,0:T(8,128)(2,1)} %get-tuple-element.41.refs_0_), channel_id=1, source_target_pairs={{0,14},{1,3},{2,0},{3,5},{4,2},{5,7},{6,4},{7,9},{8,6},{9,11},{10,... | collective-permute-start | bytes 1622024 | tf_op jit(solution)/shard_map/ppermute | solution.py:36
  7.1 24.7 %collective-permute-start.2 = (bf16[528,512]{1,0:T(8,128)(2,1)}, bf16[528,512]{1,0:T(8,128)(2,1)}, u32[]{:S(2)}, u32[]{:S(2)}) collective-permute-start(bf16[528,512]{1,0:T(8,128)(2,1)} %get-tuple-element.47), channel_id=1, source_target_pairs={{0,15},{1,2},{2,1},{3,4},{4,3},{5,6},{6,5},{7,8},{8,7},{9,10},{10,... | collective-permute-start | bytes 1622024 | tf_op jit(solution)/shard_map/ppermute | solution.py:36
  13.9 20.5 %copy-start.9 = (f32[4,8,256]{2,1,0:T(8,128)S(1)}, f32[4,8,256]{2,1,0:T(8,128)}, u32[]{:S(2)}) copy-start(f32[4,8,256]{2,1,0:T(8,128)} %get-tuple-element.43) | copy-start | bytes 98308
  13.9 24.6 %copy-start.8 = (f32[4,8,256]{2,1,0:T(8,128)S(1)}, f32[4,8,256]{2,1,0:T(8,128)}, u32[]{:S(2)}) copy-start(f32[4,8,256]{2,1,0:T(8,128)} %get-tuple-element.50) | copy-start | bytes 98308
  25.3 36.0 %copy-start = (bf16[528,512]{1,0:T(8,128)(2,1)}, bf16[528,512]{1,0:T(8,128)(2,1)S(1)}, u32[]{:S(2)}) copy-start(bf16[528,512]{1,0:T(8,128)(2,1)S(1)} %collective-permute-done.1.sw.sq.sg) | copy-start | bytes 1622020
  31.8 41.0 %collective-permute-start.5 = (bf16[512,512]{1,0:T(8,128)(2,1)}, bf16[512,512]{1,0:T(8,128)(2,1)}, u32[]{:S(2)}, u32[]{:S(2)}) collective-permute-start(bf16[512,512]{1,0:T(8,128)(2,1)} %get-tuple-element.53), channel_id=1, source_target_pairs={{2,0},{3,1},{4,2},{5,3},{6,4},{7,5},{8,6},{9,7},{10,8},{11,9},{12,... | collective-permute-start | bytes 1572872 | tf_op jit(solution)/shard_map/ppermute | solution.py:36
  33.1 39.7 %collective-permute-start.6 = (bf16[512,512]{1,0:T(8,128)(2,1)}, bf16[512,512]{1,0:T(8,128)(2,1)}, u32[]{:S(2)}, u32[]{:S(2)}) collective-permute-start(bf16[512,512]{1,0:T(8,128)(2,1)} %get-tuple-element.54), channel_id=1, source_target_pairs={{2,1},{3,0},{4,3},{5,2},{6,5},{7,4},{8,7},{9,6},{10,9},{11,8},{12,... | collective-permute-start | bytes 1572872 | tf_op jit(solution)/shard_map/ppermute | solution.py:36
  34.4 26.5 %collective-permute-start.3 = (f32[4,8,256]{2,1,0:T(8,128)S(1)}, f32[4,8,256]{2,1,0:T(8,128)S(1)}, u32[]{:S(2)}, u32[]{:S(2)}) collective-permute-start(f32[4,8,256]{2,1,0:T(8,128)S(1)} %copy-done.9), channel_id=1, source_target_pairs={{0,14},{1,3},{2,0},{3,5},{4,2},{5,7},{6,4},{7,9},{8,6},{9,11},{10,... | collective-permute-start | bytes 98312 | tf_op jit(solution)/shard_map/ppermute | solution.py:36
  37.2 35.6 %collective-permute-start.7 = (f32[4,8,512]{2,1,0:T(8,128)}, f32[4,8,512]{2,1,0:T(8,128)S(1)}, u32[]{:S(2)}, u32[]{:S(2)}) collective-permute-start(f32[4,8,512]{2,1,0:T(8,128)} %self_stats.1.refs_10_), channel_id=1, source_target_pairs={{2,0},{3,1},{4,2},{5,3},{6,4},{7,5},{8,6},{9,7},{10,8},{11,9},{12,... | collective-permute-start | bytes 196616 | tf_op jit(solution)/shard_map/ppermute | solution.py:36
  38.5 22.8 %collective-permute-start.4 = (f32[4,8,256]{2,1,0:T(8,128)S(1)}, f32[4,8,256]{2,1,0:T(8,128)S(1)}, u32[]{:S(2)}, u32[]{:S(2)}) collective-permute-start(f32[4,8,256]{2,1,0:T(8,128)S(1)} %copy-done.8), channel_id=1, source_target_pairs={{0,2},{1,15},{2,4},{3,1},{4,6},{5,3},{6,8},{7,5},{8,10},{9,7},{10,... | collective-permute-start | bytes 98312 | tf_op jit(solution)/shard_map/ppermute | solution.py:36
  61.6 0.6 copy-start.4
  68.6 22.2 %collective-permute-start.10 = (bf16[288,512]{1,0:T(8,128)(2,1)}, bf16[288,512]{1,0:T(8,128)(2,1)S(1)}, u32[]{:S(2)}, u32[]{:S(2)}) collective-permute-start(bf16[288,512]{1,0:T(8,128)(2,1)} %get-tuple-element.59), channel_id=1, source_target_pairs={{0,14},{1,3},{2,0},{3,5},{4,2},{5,7},{6,4},{7,9},{8,6},{9,11},{10,... | collective-permute-start | bytes 884744 | tf_op jit(solution)/shard_map/ppermute | solution.py:36
  71.0 19.8 %collective-permute-start.9 = (bf16[288,512]{1,0:T(8,128)(2,1)}, bf16[288,512]{1,0:T(8,128)(2,1)S(1)}, u32[]{:S(2)}, u32[]{:S(2)}) collective-permute-start(bf16[288,512]{1,0:T(8,128)(2,1)} %get-tuple-element.58), channel_id=1, source_target_pairs={{0,2},{1,15},{2,4},{3,1},{4,6},{5,3},{6,8},{7,5},{8,10},{9,7},{10,... | collective-permute-start | bytes 884744 | tf_op jit(solution)/shard_map/ppermute | solution.py:36
  72.8 0.6 copy-start.7
  80.4 18.8 %collective-permute-start.8 = (f32[4,8,512]{2,1,0:T(8,128)}, f32[4,8,512]{2,1,0:T(8,128)S(1)}, u32[]{:S(2)}, u32[]{:S(2)}) collective-permute-start(f32[4,8,512]{2,1,0:T(8,128)} %get-tuple-element.55), channel_id=1, source_target_pairs={{0,2},{1,3},{2,4},{3,5},{4,6},{5,7},{6,8},{7,9},{8,10},{9,11},{10,... | collective-permute-start | bytes 196616 | tf_op jit(solution)/shard_map/ppermute | solution.py:36
  82.0 24.6 %collective-permute-start.11 = (bf16[256,512]{1,0:T(8,128)(2,1)}, bf16[256,512]{1,0:T(8,128)(2,1)}, u32[]{:S(2)}, u32[]{:S(2)}) collective-permute-start(bf16[256,512]{1,0:T(8,128)(2,1)} %get-tuple-element.65), channel_id=1, source_target_pairs={{0,2},{1,3},{2,4},{3,5},{4,6},{5,7},{6,8},{7,9},{8,10},{9,11},{10,... | collective-permute-start | bytes 786440 | tf_op jit(solution)/shard_map/ppermute | solution.py:36
  86.3 20.3 %collective-permute-start.12 = (bf16[256,512]{1,0:T(8,128)(2,1)}, bf16[256,512]{1,0:T(8,128)(2,1)}, u32[]{:S(2)}, u32[]{:S(2)}) collective-permute-start(bf16[256,512]{1,0:T(8,128)(2,1)} %get-tuple-element.66), channel_id=1, source_target_pairs={{0,3},{1,2},{2,5},{3,4},{4,7},{5,6},{6,9},{7,8},{8,11},{9,10},{10,... | collective-permute-start | bytes 786440 | tf_op jit(solution)/shard_map/ppermute | solution.py:36
  90.8 0.7 copy-start.5
  91.5 0.7 copy-start.6
  99.1 8.0 %collective-permute-start.14 = (bf16[768,512]{1,0:T(8,128)(2,1)}, bf16[768,512]{1,0:T(8,128)(2,1)S(1)}, u32[]{:S(2)}, u32[]{:S(2)}) collective-permute-start(bf16[768,512]{1,0:T(8,128)(2,1)} %get-tuple-element.74), channel_id=1, source_target_pairs={{0,1},{1,0},{2,3},{3,2},{4,5},{5,4},{6,7},{7,6},{8,9},{9,8},{10,11... | collective-permute-start | bytes 2359304 | tf_op jit(solution)/shard_map/ppermute | solution.py:36
  99.2 0.6 copy-start.2
  106.6 4.0 %collective-permute-start.13 = (bf16[768,512]{1,0:T(8,128)(2,1)}, bf16[768,512]{1,0:T(8,128)(2,1)}, u32[]{:S(2)}, u32[]{:S(2)}) collective-permute-start(bf16[768,512]{1,0:T(8,128)(2,1)} %get-tuple-element.67), channel_id=1, source_target_pairs={{0,1},{1,0},{2,3},{3,2},{4,5},{5,4},{6,7},{7,6},{8,9},{9,8},{10,11... | collective-permute-start | bytes 2359304 | tf_op jit(solution)/shard_map/ppermute | solution.py:36
  107.2 0.9 copy-start.1
  (1 other events, 0.6 us)

commit v5 on v4

--- a/solution.py
+++ b/solution.py
@@ -461,8 +461,8 @@
         [stat_spec(2 * ROWS)], [stat(2 * ROWS)], flops=0,
     )
     t_self = send(s_own, lambda d: d - 2, False)
-    s_mine, s_other, x_same, x_cross, s_own = lax.optimization_barrier(
-        (s_mine, s_other, x_same, x_cross, s_own)
+    s_mine, s_other, x_same, x_cross, t_same, t_cross, s_own = lax.optimization_barrier(
+        (s_mine, s_other, x_same, x_cross, t_same, t_cross, s_own)
     )
     s_same = send(s_mine, lambda d: d - 2, False)
     s_cross = send(s_other, lambda d: (d - 2) ^ 1, False)

time: 114 us -> 111 us (0.974)
  waiting for transfers between devices: 26.7 us -> 21.2 us
  starting transfers between devices: 32.6 us -> 35.7 us
  local copies, waits for them, and re-layouts: 5.36 us -> 3.91 us
    ppermute x15, waiting for transfers between devices: 26.7 us -> 21.2 us  [send(): return lax.ppermute(value, 'ctx', pairs)]
    ppermute x15, starting transfers between devices: 32.6 us -> 35.7 us  [send(): return lax.ppermute(value, 'ctx', pairs)]
    unnamed x20 -> x16, local copies, waits for them, and re-layouts: 4.44 us -> 2.99 us
  transfers between devices with their start and end apart: 15 -> 15, of which waited for: 4 -> 5; matrix products, arithmetic and copies ran while one was open for 3% -> 3% of each run, Pallas kernels for 34% -> 36%
where the time goes in v5:
time: 111 us; the launch traced here: 110 us
  Pallas kernels  45.5 us (41%)
  starting transfers between devices  35.7 us (32%)
  waiting for transfers between devices  21.2 us (19%)
  local copies, waits for them, and re-layouts  3.91 us (4%)
  other arithmetic  2.48 us (2%)
    pallas_call x9, Pallas kernels, call(): pl.pallas_call(kernel, name=name, grid_spec=pltpu.PrefetchScalarGridSpec(...  45.5 us
    ppermute x15, starting transfers between devices, send(): return lax.ppermute(value, 'ctx', pairs)  35.7 us
    ppermute x15, waiting for transfers between devices, send(): return lax.ppermute(value, 'ctx', pairs)  21.2 us
    unnamed x16, local copies, waits for them, and re-layouts  2.99 us
  transfers between devices with their start and end apart: 15, of which 5 were waited for; matrix products, arithmetic and copies ran while one was open for 3% of the time, Pallas kernels for 36%

profile of v5, /device:TPU:1, one launch (start us, length us, event | category | flops | bytes accessed | tf_op | source)
XLA Modules:
  0.0 109.6 jit_solution(9366182018227460568)
XLA Ops:
  0.6 3.7 %pack.1 = (bf16[2064,512]{1,0:T(8,128)(2,1)}, bf16[528,512]{1,0:T(8,128)(2,1)}, bf16[528,512]{1,0:T(8,128)(2,1)}, bf16[512,512]{1,0:T(8,128)(2,1)}, bf16[512,512]{1,0:T(8,128)(2,1)}) custom-call(s32[1]{0:T(128)} %bitcast.info, s32[2,4]{1,0:T(2,128)} %bitcast.8, bf16[256,1024]{1,0:T(8,128)(2,1)} %refs_1_.5, bf16[256,1024]{1,0:T(8,128)(2,1)} %refs_2_.9, ...), custom_call_target="tpu_custom_call" | custom-call | tf_op jit(solution)/shard_map/pack/pallas_call | solution.py:84
  4.4 2.7 %collective-permute-start.1 = (bf16[528,512]{1,0:T(8,128)(2,1)}, bf16[528,512]{1,0:T(8,128)(2,1)S(1)}, u32[]{:S(2)}, u32[]{:S(2)}) collective-permute-start(bf16[528,512]{1,0:T(8,128)(2,1)} %get-tuple-element.43.refs_0_), channel_id=1, source_target_pairs={{0,14},{1,3},{2,0},{3,5},{4,2},{5,7},{6,4},{7,9},{8,6},{9,11},{10,... | collective-permute-start | bytes 1622024 | tf_op jit(solution)/shard_map/ppermute | solution.py:36
  8.9 4.6 %cross_stats.1 = (f32[4,8,256]{2,1,0:T(8,128)}, f32[4,8,256]{2,1,0:T(8,128)}) custom-call(s32[1]{0:T(128)} %bitcast.info, bf16[528,512]{1,0:T(8,128)(2,1)} %get-tuple-element.43.refs_0_, bf16[2064,512]{1,0:T(8,128)(2,1)} %collective-permute-done.refs_1_.refs_5_.refs_6_.refs_7_.refs_8_.pk.pv, bf16[256,1024]{1,0:T(8,128)(2,1)} %refs_2_.8, ...), custom_call_target="tpu_custom_call" | custom-call | tf_op jit(solution)/shard_map/cross_stats/pallas_call | solution.py:84
  13.5 2.4 %collective-permute-start.3 = (f32[4,8,256]{2,1,0:T(8,128)}, f32[4,8,256]{2,1,0:T(8,128)S(1)}, u32[]{:S(2)}, u32[]{:S(2)}) collective-permute-start(f32[4,8,256]{2,1,0:T(8,128)} %get-tuple-element.45), channel_id=1, source_target_pairs={{0,14},{1,3},{2,0},{3,5},{4,2},{5,7},{6,4},{7,9},{8,6},{9,11},{10,... | collective-permute-start | bytes 98312 | tf_op jit(solution)/shard_map/ppermute | solution.py:36
  15.9 4.3 %collective-permute-start.4 = (f32[4,8,256]{2,1,0:T(8,128)}, f32[4,8,256]{2,1,0:T(8,128)S(1)}, u32[]{:S(2)}, u32[]{:S(2)}) collective-permute-start(f32[4,8,256]{2,1,0:T(8,128)} %get-tuple-element.50), channel_id=1, source_target_pairs={{0,2},{1,15},{2,4},{3,1},{4,6},{5,3},{6,8},{7,5},{8,10},{9,7},{10,... | collective-permute-start | bytes 98312 | tf_op jit(solution)/shard_map/ppermute | solution.py:36
  21.4 4.8 %self_stats.1.refs_10_ = f32[4,8,512]{2,1,0:T(8,128)} custom-call(s32[1]{0:T(128)} %bitcast.info, f32[512,512]{1,0:T(8,128)} %and_select_fusion.1.refs_0_, bf16[256,1024]{1,0:T(8,128)(2,1)} %refs_1_.5, bf16[256,1024]{1,0:T(8,128)(2,1)} %refs_2_.9, bf16[256,1024]{1,0:T(8,128)(2,1)} %refs_3_.9, bf16[256,1024]{1,0:T(8,128)(2,1)} %refs_4_.5, ...), custom_call_target="tpu_custom_call" | custom-call | tf_op jit(solution)/shard_map/self_stats/pallas_call | solution.py:84
  26.4 6.5 %collective-permute-done.2.cw.cq.cg = bf16[528,512]{1,0:T(8,128)(2,1)} collective-permute-done((bf16[528,512]{1,0:T(8,128)(2,1)}, bf16[528,512]{1,0:T(8,128)(2,1)}, u32[]{:S(2)}, u32[]{:S(2)}) %collective-permute-start.2) | collective-permute-done | bytes 540704 | tf_op jit(solution)/shard_map/ppermute | solution.py:36
  32.9 1.3 %collective-permute-start.5 = (bf16[512,512]{1,0:T(8,128)(2,1)}, bf16[512,512]{1,0:T(8,128)(2,1)}, u32[]{:S(2)}, u32[]{:S(2)}) collective-permute-start(bf16[512,512]{1,0:T(8,128)(2,1)} %get-tuple-element.57), channel_id=1, source_target_pairs={{2,0},{3,1},{4,2},{5,3},{6,4},{7,5},{8,6},{9,7},{10,8},{11,9},{12,... | collective-permute-start | bytes 1572872 | tf_op jit(solution)/shard_map/ppermute | solution.py:36
  34.2 1.3 %collective-permute-start.6 = (bf16[512,512]{1,0:T(8,128)(2,1)}, bf16[512,512]{1,0:T(8,128)(2,1)}, u32[]{:S(2)}, u32[]{:S(2)}) collective-permute-start(bf16[512,512]{1,0:T(8,128)(2,1)} %get-tuple-element.58), channel_id=1, source_target_pairs={{2,1},{3,0},{4,3},{5,2},{6,5},{7,4},{8,7},{9,6},{10,9},{11,8},{12,... | collective-permute-start | bytes 1572872 | tf_op jit(solution)/shard_map/ppermute | solution.py:36
  35.5 1.3 %collective-permute-start.7 = (f32[4,8,512]{2,1,0:T(8,128)}, f32[4,8,512]{2,1,0:T(8,128)S(1)}, u32[]{:S(2)}, u32[]{:S(2)}) collective-permute-start(f32[4,8,512]{2,1,0:T(8,128)} %self_stats.1.refs_10_), channel_id=1, source_target_pairs={{2,0},{3,1},{4,2},{5,3},{6,4},{7,5},{8,6},{9,7},{10,8},{11,9},{12,... | collective-permute-start | bytes 196616 | tf_op jit(solution)/shard_map/ppermute | solution.py:36
  36.8 1.3 %and_select_fusion.bias = f32[512,512]{1,0:T(8,128)} fusion(s32[512]{0:T(512)S(1)} %pad_add_fusion.3, s32[512]{0:T(512)S(1)} %get-tuple-element.85, pred[]{:T(512)S(6)} %lt.19), kind=kLoop, calls=%fused_computation | loop fusion | flops 786432 | bytes 1052673 | tf_op jit(solution)/shard_map/jit(_where)/select_n | solution.py:437
  38.1 6.4 %cross_remote.1 = (bf16[288,512]{1,0:T(8,128)(2,1)}, bf16[288,512]{1,0:T(8,128)(2,1)}, bf16[1024,512]{1,0:T(8,128)(2,1)}) custom-call(s32[1]{0:T(128)} %bitcast.info, bf16[528,512]{1,0:T(8,128)(2,1)} %copy-done, bf16[528,512]{1,0:T(8,128)(2,1)} %collective-permute-done.2.cw.cq.cg, bf16[528,512]{1,0:T(8,128)(2,1)} %copy-done, bf16[528,512]{1,0:T(8,128)(2,1)} %copy-done, ...), custom_call_target="tpu_custom_call" | custom-call | tf_op jit(solution)/shard_map/cross_remote/pallas_call | solution.py:84
  44.5 3.6 %collective-permute-start.10 = (bf16[288,512]{1,0:T(8,128)(2,1)}, bf16[288,512]{1,0:T(8,128)(2,1)S(1)}, u32[]{:S(2)}, u32[]{:S(2)}) collective-permute-start(bf16[288,512]{1,0:T(8,128)(2,1)} %get-tuple-element.63), channel_id=1, source_target_pairs={{0,14},{1,3},{2,0},{3,5},{4,2},{5,7},{6,4},{7,9},{8,6},{9,11},{10,... | collective-permute-start | bytes 884744 | tf_op jit(solution)/shard_map/ppermute | solution.py:36
  48.1 5.8 %collective-permute-start.9 = (bf16[288,512]{1,0:T(8,128)(2,1)}, bf16[288,512]{1,0:T(8,128)(2,1)S(1)}, u32[]{:S(2)}, u32[]{:S(2)}) collective-permute-start(bf16[288,512]{1,0:T(8,128)(2,1)} %get-tuple-element.62), channel_id=1, source_target_pairs={{0,2},{1,15},{2,4},{3,1},{4,6},{5,3},{6,8},{7,5},{8,10},{9,7},{10,... | collective-permute-start | bytes 884744 | tf_op jit(solution)/shard_map/ppermute | solution.py:36
  53.9 12.3 %collective-permute-done.7.stats = f32[4,8,512]{2,1,0:T(8,128)S(1)} collective-permute-done((f32[4,8,512]{2,1,0:T(8,128)}, f32[4,8,512]{2,1,0:T(8,128)S(1)}, u32[]{:S(2)}, u32[]{:S(2)}) %collective-permute-start.7) | collective-permute-done | bytes 65568 | tf_op jit(solution)/shard_map/ppermute | solution.py:36
  66.2 1.5 %collective-permute-done.6.cq.cg = bf16[512,512]{1,0:T(8,128)(2,1)} collective-permute-done((bf16[512,512]{1,0:T(8,128)(2,1)}, bf16[512,512]{1,0:T(8,128)(2,1)}, u32[]{:S(2)}, u32[]{:S(2)}) %collective-permute-start.6) | collective-permute-done | bytes 524320 | tf_op jit(solution)/shard_map/ppermute | solution.py:36
  67.7 6.9 %self_remote.1 = (bf16[256,512]{1,0:T(8,128)(2,1)}, bf16[256,512]{1,0:T(8,128)(2,1)}, bf16[1024,512]{1,0:T(8,128)(2,1)}, f32[4,8,512]{2,1,0:T(8,128)}) custom-call(s32[1]{0:T(128)} %bitcast.info, f32[512,512]{1,0:T(8,128)} %and_select_fusion.bias, bf16[512,512]{1,0:T(8,128)(2,1)} %collective-permute-done.5.sq.sg, ...), custom_call_target="tpu_custom_call" | custom-call | flops 12000000000 | tf_op jit(solution)/shard_map/self_remote/pallas_call | solution.py:84
  74.7 1.3 %collective-permute-start.8 = (f32[4,8,512]{2,1,0:T(8,128)}, f32[4,8,512]{2,1,0:T(8,128)S(1)}, u32[]{:S(2)}, u32[]{:S(2)}) collective-permute-start(f32[4,8,512]{2,1,0:T(8,128)} %get-tuple-element.59), channel_id=1, source_target_pairs={{0,2},{1,3},{2,4},{3,5},{4,6},{5,7},{6,8},{7,9},{8,10},{9,11},{10,... | collective-permute-start | bytes 196616 | tf_op jit(solution)/shard_map/ppermute | solution.py:36
  76.0 6.2 %collective-permute-start.11 = (bf16[256,512]{1,0:T(8,128)(2,1)}, bf16[256,512]{1,0:T(8,128)(2,1)}, u32[]{:S(2)}, u32[]{:S(2)}) collective-permute-start(bf16[256,512]{1,0:T(8,128)(2,1)} %get-tuple-element.69), channel_id=1, source_target_pairs={{0,2},{1,3},{2,4},{3,5},{4,6},{5,7},{6,8},{7,9},{8,10},{9,11},{10,... | collective-permute-start | bytes 786440 | tf_op jit(solution)/shard_map/ppermute | solution.py:36
  82.2 4.7 %collective-permute-start.12 = (bf16[256,512]{1,0:T(8,128)(2,1)}, bf16[256,512]{1,0:T(8,128)(2,1)}, u32[]{:S(2)}, u32[]{:S(2)}) collective-permute-start(bf16[256,512]{1,0:T(8,128)(2,1)} %get-tuple-element.70), channel_id=1, source_target_pairs={{0,3},{1,2},{2,5},{3,4},{4,7},{5,6},{6,9},{7,8},{8,11},{9,10},{10,... | collective-permute-start | bytes 786440 | tf_op jit(solution)/shard_map/ppermute | solution.py:36
  88.3 6.9 %cross_local.1 = (bf16[768,512]{1,0:T(8,128)(2,1)}, bf16[768,512]{1,0:T(8,128)(2,1)}) custom-call(s32[1]{0:T(128)} %bitcast.info, bf16[528,512]{1,0:T(8,128)(2,1)} %get-tuple-element.43.refs_0_, bf16[2064,512]{1,0:T(8,128)(2,1)} %collective-permute-done.refs_1_.refs_5_.refs_6_.refs_7_.refs_8_.pk.pv, bf16[256,1024]{1,0:T(8,128)(2,1)} %refs_2_.8, ...), custom_call_target="tpu_custom_call" | custom-call | flops 12000000000 | tf_op jit(solution)/shard_map/cross_local/pallas_call | solution.py:84
  96.4 6.7 %self_local.1 = (bf16[768,512]{1,0:T(8,128)(2,1)}, bf16[768,512]{1,0:T(8,128)(2,1)}) custom-call(s32[1]{0:T(128)} %bitcast.info, f32[512,512]{1,0:T(8,128)} %and_select_fusion.1.refs_0_, bf16[256,1024]{1,0:T(8,128)(2,1)} %refs_1_.5, bf16[256,1024]{1,0:T(8,128)(2,1)} %refs_2_.9, bf16[256,1024]{1,0:T(8,128)(2,1)} %refs_3_.9, bf16[256,1024]{1,0:T(8,128)(2,1)} %refs_4_.5, ...), custom_call_target="tpu_custom_call" | custom-call | tf_op jit(solution)/shard_map/self_local/pallas_call | solution.py:84
  104.2 2.6 %cross_final.1 = (bf16[256,1024]{1,0:T(8,128)(2,1)}, bf16[2,256,1024]{2,1,0:T(8,128)(2,1)}) custom-call(s32[1]{0:T(128)} %bitcast.info, bf16[768,512]{1,0:T(8,128)(2,1)} %get-tuple-element.77.mine, bf16[768,512]{1,0:T(8,128)(2,1)} %copy-done.1), custom_call_target="tpu_custom_call" | custom-call | tf_op jit(solution)/shard_map/cross_final/pallas_call | solution.py:84
  106.8 2.8 %self_final.1 = (bf16[256,1024]{1,0:T(8,128)(2,1)}, bf16[256,1024]{1,0:T(8,128)(2,1)}, bf16[256,1024]{1,0:T(8,128)(2,1)}) custom-call(s32[1]{0:T(128)} %bitcast.info, bf16[768,512]{1,0:T(8,128)(2,1)} %get-tuple-element.67.mine, bf16[768,512]{1,0:T(8,128)(2,1)} %collective-permute-done.13.theirs, bf16[256,512]{1,0:T(8,128)(2,1)} %collective-permute-done.11.dq_mine, ...), custom_call_target="tpu_custom_call" | custom-call | tf_op jit(solution)/shard_map/self_final/pallas_call | solution.py:84
  (38 shorter events, 6.9 us)
Async XLA Ops:
  4.3 4.6 %collective-permute-start = (bf16[2064,512]{1,0:T(8,128)(2,1)}, bf16[2064,512]{1,0:T(8,128)(2,1)}, u32[]{:S(2)}, u32[]{:S(2)}) collective-permute-start(bf16[2064,512]{1,0:T(8,128)(2,1)} %get-tuple-element.44), channel_id=1, source_target_pairs={{0,1},{1,0},{2,3},{3,2},{4,5},{5,4},{6,7},{7,6},{8,9},{9,8},{10,11... | collective-permute-start | bytes 6340616 | tf_op jit(solution)/shard_map/ppermute | solution.py:36
  4.4 21.9 %collective-permute-start.1 = (bf16[528,512]{1,0:T(8,128)(2,1)}, bf16[528,512]{1,0:T(8,128)(2,1)S(1)}, u32[]{:S(2)}, u32[]{:S(2)}) collective-permute-start(bf16[528,512]{1,0:T(8,128)(2,1)} %get-tuple-element.43.refs_0_), channel_id=1, source_target_pairs={{0,14},{1,3},{2,0},{3,5},{4,2},{5,7},{6,4},{7,9},{8,6},{9,11},{10,... | collective-permute-start | bytes 1622024 | tf_op jit(solution)/shard_map/ppermute | solution.py:36
  7.1 25.7 %collective-permute-start.2 = (bf16[528,512]{1,0:T(8,128)(2,1)}, bf16[528,512]{1,0:T(8,128)(2,1)}, u32[]{:S(2)}, u32[]{:S(2)}) collective-permute-start(bf16[528,512]{1,0:T(8,128)(2,1)} %get-tuple-element.49), channel_id=1, source_target_pairs={{0,15},{1,2},{2,1},{3,4},{4,3},{5,6},{6,5},{7,8},{8,7},{9,10},{10,... | collective-permute-start | bytes 1622024 | tf_op jit(solution)/shard_map/ppermute | solution.py:36
  13.5 19.3 %collective-permute-start.3 = (f32[4,8,256]{2,1,0:T(8,128)}, f32[4,8,256]{2,1,0:T(8,128)S(1)}, u32[]{:S(2)}, u32[]{:S(2)}) collective-permute-start(f32[4,8,256]{2,1,0:T(8,128)} %get-tuple-element.45), channel_id=1, source_target_pairs={{0,14},{1,3},{2,0},{3,5},{4,2},{5,7},{6,4},{7,9},{8,6},{9,11},{10,... | collective-permute-start | bytes 98312 | tf_op jit(solution)/shard_map/ppermute | solution.py:36
  15.9 16.9 %collective-permute-start.4 = (f32[4,8,256]{2,1,0:T(8,128)}, f32[4,8,256]{2,1,0:T(8,128)S(1)}, u32[]{:S(2)}, u32[]{:S(2)}) collective-permute-start(f32[4,8,256]{2,1,0:T(8,128)} %get-tuple-element.50), channel_id=1, source_target_pairs={{0,2},{1,15},{2,4},{3,1},{4,6},{5,3},{6,8},{7,5},{8,10},{9,7},{10,... | collective-permute-start | bytes 98312 | tf_op jit(solution)/shard_map/ppermute | solution.py:36
  26.4 11.7 %copy-start = (bf16[528,512]{1,0:T(8,128)(2,1)}, bf16[528,512]{1,0:T(8,128)(2,1)S(1)}, u32[]{:S(2)}) copy-start(bf16[528,512]{1,0:T(8,128)(2,1)S(1)} %collective-permute-done.1.sw.sq.sg) | copy-start | bytes 1622020
  32.9 5.2 %copy-start.3 = (f32[4,8,256]{2,1,0:T(8,128)}, f32[4,8,256]{2,1,0:T(8,128)S(1)}, u32[]{:S(2)}) copy-start(f32[4,8,256]{2,1,0:T(8,128)S(1)} %collective-permute-done.3.s_stats) | copy-start | bytes 98308
  32.9 5.2 %copy-start.4 = (f32[4,8,256]{2,1,0:T(8,128)}, f32[4,8,256]{2,1,0:T(8,128)S(1)}, u32[]{:S(2)}) copy-start(f32[4,8,256]{2,1,0:T(8,128)S(1)} %collective-permute-done.4.c_stats) | copy-start | bytes 98308
  32.9 33.4 %collective-permute-start.5 = (bf16[512,512]{1,0:T(8,128)(2,1)}, bf16[512,512]{1,0:T(8,128)(2,1)}, u32[]{:S(2)}, u32[]{:S(2)}) collective-permute-start(bf16[512,512]{1,0:T(8,128)(2,1)} %get-tuple-element.57), channel_id=1, source_target_pairs={{2,0},{3,1},{4,2},{5,3},{6,4},{7,5},{8,6},{9,7},{10,8},{11,9},{12,... | collective-permute-start | bytes 1572872 | tf_op jit(solution)/shard_map/ppermute | solution.py:36
  34.2 33.5 %collective-permute-start.6 = (bf16[512,512]{1,0:T(8,128)(2,1)}, bf16[512,512]{1,0:T(8,128)(2,1)}, u32[]{:S(2)}, u32[]{:S(2)}) collective-permute-start(bf16[512,512]{1,0:T(8,128)(2,1)} %get-tuple-element.58), channel_id=1, source_target_pairs={{2,1},{3,0},{4,3},{5,2},{6,5},{7,4},{8,7},{9,6},{10,9},{11,8},{12,... | collective-permute-start | bytes 1572872 | tf_op jit(solution)/shard_map/ppermute | solution.py:36
  35.5 30.7 %collective-permute-start.7 = (f32[4,8,512]{2,1,0:T(8,128)}, f32[4,8,512]{2,1,0:T(8,128)S(1)}, u32[]{:S(2)}, u32[]{:S(2)}) collective-permute-start(f32[4,8,512]{2,1,0:T(8,128)} %self_stats.1.refs_10_), channel_id=1, source_target_pairs={{2,0},{3,1},{4,2},{5,3},{6,4},{7,5},{8,6},{9,7},{10,8},{11,9},{12,... | collective-permute-start | bytes 196616 | tf_op jit(solution)/shard_map/ppermute | solution.py:36
  44.5 42.4 %collective-permute-start.10 = (bf16[288,512]{1,0:T(8,128)(2,1)}, bf16[288,512]{1,0:T(8,128)(2,1)S(1)}, u32[]{:S(2)}, u32[]{:S(2)}) collective-permute-start(bf16[288,512]{1,0:T(8,128)(2,1)} %get-tuple-element.63), channel_id=1, source_target_pairs={{0,14},{1,3},{2,0},{3,5},{4,2},{5,7},{6,4},{7,9},{8,6},{9,11},{10,... | collective-permute-start | bytes 884744 | tf_op jit(solution)/shard_map/ppermute | solution.py:36
  48.1 38.8 %collective-permute-start.9 = (bf16[288,512]{1,0:T(8,128)(2,1)}, bf16[288,512]{1,0:T(8,128)(2,1)S(1)}, u32[]{:S(2)}, u32[]{:S(2)}) collective-permute-start(bf16[288,512]{1,0:T(8,128)(2,1)} %get-tuple-element.62), channel_id=1, source_target_pairs={{0,2},{1,15},{2,4},{3,1},{4,6},{5,3},{6,8},{7,5},{8,10},{9,7},{10,... | collective-permute-start | bytes 884744 | tf_op jit(solution)/shard_map/ppermute | solution.py:36
  66.2 1.5 %copy-start.7 = (f32[4,8,512]{2,1,0:T(8,128)}, f32[4,8,512]{2,1,0:T(8,128)S(1)}, u32[]{:S(2)}) copy-start(f32[4,8,512]{2,1,0:T(8,128)S(1)} %collective-permute-done.7.stats) | copy-start | bytes 196612
  74.7 21.1 %collective-permute-start.8 = (f32[4,8,512]{2,1,0:T(8,128)}, f32[4,8,512]{2,1,0:T(8,128)S(1)}, u32[]{:S(2)}, u32[]{:S(2)}) collective-permute-start(f32[4,8,512]{2,1,0:T(8,128)} %get-tuple-element.59), channel_id=1, source_target_pairs={{0,2},{1,3},{2,4},{3,5},{4,6},{5,7},{6,8},{7,9},{8,10},{9,11},{10,... | collective-permute-start | bytes 196616 | tf_op jit(solution)/shard_map/ppermute | solution.py:36
  76.0 27.2 %collective-permute-start.11 = (bf16[256,512]{1,0:T(8,128)(2,1)}, bf16[256,512]{1,0:T(8,128)(2,1)}, u32[]{:S(2)}, u32[]{:S(2)}) collective-permute-start(bf16[256,512]{1,0:T(8,128)(2,1)} %get-tuple-element.69), channel_id=1, source_target_pairs={{0,2},{1,3},{2,4},{3,5},{4,6},{5,7},{6,8},{7,9},{8,10},{9,11},{10,... | collective-permute-start | bytes 786440 | tf_op jit(solution)/shard_map/ppermute | solution.py:36
  82.2 21.0 %collective-permute-start.12 = (bf16[256,512]{1,0:T(8,128)(2,1)}, bf16[256,512]{1,0:T(8,128)(2,1)}, u32[]{:S(2)}, u32[]{:S(2)}) collective-permute-start(bf16[256,512]{1,0:T(8,128)(2,1)} %get-tuple-element.70), channel_id=1, source_target_pairs={{0,3},{1,2},{2,5},{3,4},{4,7},{5,6},{6,9},{7,8},{8,11},{9,10},{10,... | collective-permute-start | bytes 786440 | tf_op jit(solution)/shard_map/ppermute | solution.py:36
  86.9 0.7 copy-start.5
  87.6 0.7 copy-start.6
  95.2 8.0 %collective-permute-start.14 = (bf16[768,512]{1,0:T(8,128)(2,1)}, bf16[768,512]{1,0:T(8,128)(2,1)S(1)}, u32[]{:S(2)}, u32[]{:S(2)}) collective-permute-start(bf16[768,512]{1,0:T(8,128)(2,1)} %get-tuple-element.78), channel_id=1, source_target_pairs={{0,1},{1,0},{2,3},{3,2},{4,5},{5,4},{6,7},{7,6},{8,9},{9,8},{10,11... | collective-permute-start | bytes 2359304 | tf_op jit(solution)/shard_map/ppermute | solution.py:36
  95.8 0.6 copy-start.2
  103.2 3.6 %collective-permute-start.13 = (bf16[768,512]{1,0:T(8,128)(2,1)}, bf16[768,512]{1,0:T(8,128)(2,1)}, u32[]{:S(2)}, u32[]{:S(2)}) collective-permute-start(bf16[768,512]{1,0:T(8,128)(2,1)} %get-tuple-element.71), channel_id=1, source_target_pairs={{0,1},{1,0},{2,3},{3,2},{4,5},{5,4},{6,7},{7,6},{8,9},{9,8},{10,11... | collective-permute-start | bytes 2359304 | tf_op jit(solution)/shard_map/ppermute | solution.py:36
  103.3 0.9 copy-start.1

commit v6 on v5

--- a/solution.py
+++ b/solution.py
@@ -16,7 +16,6 @@
 NBR_TOK = 128
 ROWS = 256
 EXTRA = 16
-STATS = 32
 LONG = 12 * 10**9
 FACTOR = HEAD_DIM ** (-0.5)
 MASKED = -1e30
@@ -160,9 +159,8 @@
     return dot_first(ds, k) * FACTOR, dot(ds, q) * FACTOR, dot(pb, g)
 
 
-def pack_kernel(enc_dev, loop, info, ids_ref, *refs):
-    qm, gm, xqm, xgm, q, g, k, v, xq, xg, pool, swap_ref, xm, xo, sm, so = refs
-    shape = (EXTRA, xm.shape[1])
+def pack_cross_kernel(enc_dev, loop, info, ids_ref, qm, gm, q, g, pool, swap_ref, mine, other):
+    shape = (EXTRA, mine.shape[1])
     row = lax.broadcasted_iota(jnp.int32, shape, 0)
     lane = lax.broadcasted_iota(jnp.int32, shape, 1) + pl.program_id(0) * shape[1]
     ids = ids_ref[...]
@@ -177,47 +175,27 @@
             hit = (row == slots[n : n + 1, s : s + 1]) & (lane // STRETCH == s)
             times = times + jnp.where(hit, 1.0, 0.0)
     times = times.astype(BF16)
-    for index, ref in enumerate((q, g, k, v, xq, xg)):
-        swap_ref[index * ROWS : (index + 1) * ROWS] = ref[...]
-    swap_ref[6 * ROWS : 7 * ROWS] = pool[0]
-    swap_ref[7 * ROWS : 8 * ROWS] = pool[1]
-    swap_ref[8 * ROWS :] = times
-    for out, first, second in ((xm, xqm, xgm), (xo, xq, xg), (sm, qm, gm), (so, q, g)):
+    swap_ref[0:ROWS] = q[...]
+    swap_ref[ROWS : 2 * ROWS] = g[...]
+    swap_ref[2 * ROWS : 3 * ROWS] = pool[0]
+    swap_ref[3 * ROWS : 4 * ROWS] = pool[1]
+    swap_ref[4 * ROWS :] = times
+    for out, first, second in ((mine, qm, gm), (other, q, g)):
         out[0:ROWS] = first[...]
         out[ROWS : 2 * ROWS] = second[...]
-    xm[2 * ROWS :] = times
-    xo[2 * ROWS :] = times
+        out[2 * ROWS :] = times
+
+
+def pack_self_kernel(info, qm, gm, q, g, k, v, swap_ref, mine, other):
+    for index, ref in enumerate((q, g, k, v)):
+        swap_ref[index * ROWS : (index + 1) * ROWS] = ref[...]
+    for out, first, second in ((mine, qm, gm), (other, q, g)):
+        out[0:ROWS] = first[...]
+        out[ROWS : 2 * ROWS] = second[...]
 
 
 def ordered(core, a, b):
     return jnp.where(core == 0, a, b), jnp.where(core == 0, b, a)
-
-
-def split3(x):
-    high = x.astype(BF16)
-    rest = x - high.astype(F32)
-    middle = rest.astype(BF16)
-    return [high, middle, (rest - middle.astype(F32)).astype(BF16)]
-
-
-def put_stats(ref, stats):
-    rows = []
-    for low in range(0, stats[0].shape[1], HEAD_DIM):
-        for x in stats:
-            rows += split3(x[:, low : low + HEAD_DIM])
-    rows.append(jnp.zeros((ref.shape[0] - ROWS - len(rows), HEAD_DIM), BF16))
-    ref[ROWS:] = jnp.concatenate(rows, axis=0)
-
-
-def take_stats(ref, lanes):
-    x = ref[...].astype(F32)
-    stats = []
-    for index in range(3):
-        parts = []
-        for low in range(3 * index, 9 * (lanes // HEAD_DIM), 9):
-            parts.append(x[low : low + 1] + x[low + 1 : low + 2] + x[low + 2 : low + 3])
-        stats.append(jnp.concatenate(parts, axis=1))
-    return stats
 
 
 def wide_scores(keys_x, keys_y, values_x, values_y, qs, gs, bias):
@@ -303,19 +281,19 @@
 def cross_remote_kernel(
     info, sw, cw, sq, sg, cq, cg, pool, pk, pv, s_stats, c_stats, *outs
 ):
-    dq_same, dq_cross, kv_ref = outs
+    dq_same, dq_cross, kv_ref, out_same, out_cross = outs
     core = info[0] % 2
     jobs = (
-        (cq, cg, pool[0], pool[1], slot_pair(cw, 4, core, 0), c_stats, dq_cross, 0),
-        (sq, sg, pk[...], pv[...], slot_pair(sw, 0, core, 4), s_stats, dq_same, 1),
-    )
-    for q, g, k, v, rows, stats, dq_ref, place in jobs:
+        (cq, cg, pool[0], pool[1], slot_pair(cw, 4, core, 0), c_stats, dq_cross, out_cross, 0),
+        (sq, sg, pk[...], pv[...], slot_pair(sw, 0, core, 4), s_stats, dq_same, out_same, 1),
+    )
+    for q, g, k, v, rows, stats, dq_ref, out_stats, place in jobs:
         s, dp = add_rows(dot_last(k, q[...]) * FACTOR, rows), dot_last(v, g[...])
         e, *mine = partial_stats(s, dp)
         top, inverse, delta, scale = merge(stats[...], mine)
         dq, dk, dv = gradients(e * scale, dp, delta, q[...], g[...], k)
-        dq_ref[:ROWS] = dq.astype(BF16)
-        put_stats(dq_ref, (top, inverse, delta))
+        dq_ref[...] = dq.astype(BF16)
+        out_stats[...] = stat_rows(top, inverse, delta)
         kv_ref[place * ROWS : (place + 1) * ROWS] = dk.astype(BF16)
         kv_ref[(2 + place) * ROWS : (3 + place) * ROWS] = dv.astype(BF16)
 
@@ -345,12 +323,11 @@
 
 
 def cross_local_kernel(info, *refs):
-    own_stats, partner_stats, own_dq, partner_dq, kv_ref, mine, theirs = refs[-7:]
-    own, partner = take_stats(own_stats, ROWS), take_stats(partner_stats, ROWS)
-    top, inverse, delta = [jnp.concatenate([own[i], partner[i]], axis=1) for i in range(3)]
-    s, dp, qs, gs, ks = local_cross(info[0] % 2, *refs[:-7])
+    own_stats, partner_stats, kv_ref, mine, theirs = refs[-5:]
+    stats = jnp.concatenate([own_stats[0], partner_stats[0]], axis=1)
+    top, inverse, delta = stats[0:1], stats[1:2], stats[2:3]
+    s, dp, qs, gs, ks = local_cross(info[0] % 2, *refs[:-5])
     dq, dk, dv = gradients(jnp.exp(s - top) * inverse, dp, delta, qs, gs, ks)
-    dq = dq + both(own_dq[...], partner_dq[...]).astype(F32)
     dk = dk + kv_ref[: 2 * ROWS].astype(F32)
     dv = dv + kv_ref[2 * ROWS :].astype(F32)
     for index, grad in enumerate((dq, dk, dv)):
@@ -369,14 +346,15 @@
     pl.when(pl.program_id(0) == 1)(lambda: write(theirs, dq_theirs))
 
 
-def cross_final_kernel(info, mine, theirs, dq_out, pool_out):
-    def write(source):
-        dq_out[...] = source[:ROWS]
+def cross_final_kernel(info, mine, theirs, dq_mine, dq_theirs, dq_out, pool_out):
+    def write(source, extra):
+        dq = source[:ROWS].astype(F32) + extra[...].astype(F32)
+        dq_out[...] = dq.astype(BF16)
         pool_out[0] = source[ROWS : 2 * ROWS]
         pool_out[1] = source[2 * ROWS :]
 
-    pl.when(pl.program_id(0) == 0)(lambda: write(mine))
-    pl.when(pl.program_id(0) == 1)(lambda: write(theirs))
+    pl.when(pl.program_id(0) == 0)(lambda: write(mine, dq_mine))
+    pl.when(pl.program_id(0) == 1)(lambda: write(theirs, dq_theirs))
 
 
 def assemble(kernel, name, info, inputs, pooled):
@@ -407,21 +385,29 @@
     mine_spec = pl.BlockSpec((ROWS, cols), lambda h, info: (0, info[0] % 2 * 2 + h))
     their_spec = pl.BlockSpec((ROWS, cols), lambda h, info: (0, (1 - info[0] % 2) * 2 + h))
     their_pool = pl.BlockSpec((2, ROWS, cols), lambda h, info: (0, 0, (1 - info[0] % 2) * 2 + h))
-    sizes = (8 * ROWS + EXTRA, 2 * ROWS + EXTRA, 2 * ROWS + EXTRA, 2 * ROWS, 2 * ROWS)
-    packed, x_mine, x_other, s_mine, s_other = call(
-        functools.partial(pack_kernel, enc_dev, loop),
-        "pack",
-        info,
-        [whole_spec(neighbour_ids.shape[::-1])] + [mine_spec] * 4 + [their_spec] * 6 + [their_pool],
-        (neighbour_ids.T, queries, grad_self, cross_queries, grad_cross)
-        + (queries, grad_self, keys, values, cross_queries, grad_cross, pool),
+    sizes = (4 * ROWS + EXTRA, 2 * ROWS + EXTRA, 2 * ROWS + EXTRA)
+    packed, x_mine, x_other = call(
+        functools.partial(pack_cross_kernel, enc_dev, loop), "pack_cross", info,
+        [whole_spec(neighbour_ids.shape[::-1])] + [mine_spec] * 2 + [their_spec] * 2 + [their_pool],
+        (neighbour_ids.T, cross_queries, grad_cross, cross_queries, grad_cross, pool),
         [block(rows) for rows in sizes],
         [((rows, WIDE), BF16) for rows in sizes],
         steps=2,
     )
-    partner = send(packed, swap, False)
     x_same = send(x_mine, outward, True)
     x_cross = send(x_other, across, True)
+    x_pair = send(packed, swap, False)
+    queries_in, packed = lax.optimization_barrier((queries, packed))
+    sizes = (4 * ROWS, 2 * ROWS, 2 * ROWS)
+    packed, s_mine, s_other = call(
+        pack_self_kernel, "pack_self", info,
+        [mine_spec] * 2 + [their_spec] * 4,
+        (queries_in, grad_self, queries_in, grad_self, keys, values),
+        [block(rows) for rows in sizes],
+        [((rows, WIDE), BF16) for rows in sizes],
+        steps=2,
+    )
+    s_pair = send(packed, swap, False)
 
     ids_of = lambda d: lax.dynamic_slice_in_dim(doc_ids, d * ROWS, ROWS, 0)
     span = jnp.arange(ROWS, dtype=jnp.int32)
@@ -437,15 +423,16 @@
     far_bias = jnp.where(far_ok, 0.0, MASKED).astype(F32)
 
     bias_spec = whole_spec((2 * ROWS, 2 * ROWS))
+    local_bias, far_bias, x_pair = lax.optimization_barrier((local_bias, far_bias, x_pair))
     self_specs = [bias_spec] + [own_spec()] * 4 + [spec(ROWS, j) for j in range(4)]
-    self_args = (local_bias, queries, grad_self, keys, values) + (partner,) * 4
+    self_args = (local_bias, queries, grad_self, keys, values) + (s_pair,) * 4
     mine_w = whole_spec((EXTRA, WIDE), (2 * ROWS // EXTRA, 0))
-    partner_w = whole_spec((EXTRA, WIDE), (8 * ROWS // EXTRA, 0))
+    partner_w = whole_spec((EXTRA, WIDE), (4 * ROWS // EXTRA, 0))
     cross_specs = (
         [mine_w, partner_w, own_spec(), own_spec(), own_spec((2,))]
-        + [spec(ROWS, j) for j in range(4, 8)]
-    )
-    cross_args = (x_mine, partner, cross_queries, grad_cross, pool) + (partner,) * 4
+        + [spec(ROWS, j) for j in range(4)]
+    )
+    cross_args = (x_mine, x_pair, cross_queries, grad_cross, pool) + (x_pair,) * 4
     stat = lambda rows: ((HALF, 8, rows), F32)
 
     x_own, x_partner = call(
@@ -461,35 +448,48 @@
         [stat_spec(2 * ROWS)], [stat(2 * ROWS)], flops=0,
     )
     t_self = send(s_own, lambda d: d - 2, False)
-    s_mine, s_other, x_same, x_cross, t_same, t_cross, s_own = lax.optimization_barrier(
-        (s_mine, s_other, x_same, x_cross, t_same, t_cross, s_own)
+    s_mine, x_same, x_cross, t_same, t_cross, s_own = lax.optimization_barrier(
+        (s_mine, x_same, x_cross, t_same, t_cross, s_own)
     )
     s_same = send(s_mine, lambda d: d - 2, False)
-    s_cross = send(s_other, lambda d: (d - 2) ^ 1, False)
-
 
     kv_out = spec(4 * ROWS)
     kv_shape = ((4 * ROWS, WIDE), BF16)
     q_shape = ((ROWS, WIDE), BF16)
-    tagged = spec(ROWS + STATS)
-    tagged_shape = ((ROWS + STATS, WIDE), BF16)
-    xd_same, xd_cross, x_kv = call(
+    xd_same, xd_cross, x_kv, x_fin_same, x_fin_cross = call(
         cross_remote_kernel, "cross_remote", info,
         [mine_w, mine_w, spec(ROWS, 0), spec(ROWS, 1), spec(ROWS, 0), spec(ROWS, 1)]
-        + [own_spec((2,)), spec(ROWS, 6), spec(ROWS, 7), stat_spec(ROWS), stat_spec(ROWS)],
-        (x_same, x_cross, x_same, x_same, x_cross, x_cross, pool, partner, partner, t_same, t_cross),
-        [tagged, tagged, kv_out],
-        [tagged_shape, tagged_shape, kv_shape], flops=0,
+        + [own_spec((2,)), spec(ROWS, 2), spec(ROWS, 3), stat_spec(ROWS), stat_spec(ROWS)],
+        (x_same, x_cross, x_same, x_same, x_cross, x_cross, pool, x_pair, x_pair, t_same, t_cross),
+        [spec(ROWS), spec(ROWS), kv_out, stat_spec(ROWS), stat_spec(ROWS)],
+        [q_shape, q_shape, kv_shape, stat(ROWS), stat(ROWS)],
+    )
+    f_own = send(x_fin_same, inward, True)
+    f_partner = send(x_fin_cross, outward, True)
+    s_other, x_kv = lax.optimization_barrier((s_other, x_kv))
+    s_cross = send(s_other, lambda d: (d - 2) ^ 1, False)
+    xd_same, xd_cross, f_own, f_partner = lax.optimization_barrier(
+        (xd_same, xd_cross, f_own, f_partner)
     )
     xr_same = send(xd_same, inward, True)
-    xr_cross = send(xd_cross, outward, True)
-
-    far_bias, x_kv = lax.optimization_barrier((far_bias, x_kv))
+    xr_cross = send(xd_cross, across, True)
+
+    x_kv, s_same, t_self = lax.optimization_barrier((x_kv, s_same, t_self))
+    half_out = spec(3 * ROWS)
+    half_shape = ((3 * ROWS, WIDE), BF16)
+    x_keep, x_give = call(
+        cross_local_kernel, "cross_local", info,
+        cross_specs + [stat_spec(ROWS), stat_spec(ROWS), spec(4 * ROWS)],
+        cross_args + (f_own, f_partner, x_kv),
+        [half_out] * 2, [half_shape] * 2, flops=LONG,
+    )
+
+    far_bias, x_keep = lax.optimization_barrier((far_bias, x_keep))
     sd_same, sd_cross, s_kv, s_fin = call(
         self_remote_kernel, "self_remote", info,
         [bias_spec, spec(ROWS, 0), spec(ROWS, 1), spec(ROWS, 0), spec(ROWS, 1)]
         + [own_spec(), own_spec(), spec(ROWS, 2), spec(ROWS, 3), stat_spec(2 * ROWS)],
-        (far_bias, s_same, s_same, s_cross, s_cross, keys, values, partner, partner, t_self),
+        (far_bias, s_same, s_same, s_cross, s_cross, keys, values, s_pair, s_pair, t_self),
         [spec(ROWS), spec(ROWS), kv_out, stat_spec(2 * ROWS)],
         [q_shape, q_shape, kv_shape, stat(2 * ROWS)], flops=LONG,
     )
@@ -497,28 +497,23 @@
     sr_same = send(sd_same, lambda d: d + 2, False)
     sr_cross = send(sd_cross, lambda d: (d + 2) ^ 1, False)
 
-    half_out = spec(3 * ROWS)
-    half_shape = ((3 * ROWS, WIDE), BF16)
-    x_keep, x_give = call(
-        cross_local_kernel, "cross_local", info,
-        cross_specs
-        + [spec(STATS, ROWS // STATS), spec(STATS, ROWS // STATS), spec(ROWS), spec(ROWS)]
-        + [spec(4 * ROWS)],
-        cross_args + (xr_same, xr_cross, xr_same, xr_cross, x_kv),
-        [half_out] * 2, [half_shape] * 2, flops=LONG,
+    x_give, s_kv, xr_same, xr_cross, f_self = lax.optimization_barrier(
+        (x_give, s_kv, xr_same, xr_cross, f_self)
     )
     x_take = send(x_give, swap, False)
-    s_kv, x_keep = lax.optimization_barrier((s_kv, x_keep))
     s_keep, s_give = call(
         self_local_kernel, "self_local", info,
-        self_specs
-        + [stat_spec(2 * ROWS), stat_spec(2 * ROWS), spec(4 * ROWS)],
+        self_specs + [stat_spec(2 * ROWS), stat_spec(2 * ROWS), spec(4 * ROWS)],
         self_args + (f_self, s_own, s_kv),
-        [half_out] * 2, [half_shape] * 2, flops=0,
-    )
-    s_give, sr_same, sr_cross = lax.optimization_barrier((s_give, sr_same, sr_cross))
+        [half_out] * 2, [half_shape] * 2, flops=LONG,
+    )
+    grad_cq, grad_pool = assemble(
+        cross_final_kernel, "cross_final", info, (x_keep, x_take, xr_same, xr_cross), True
+    )
+    s_give, sr_same, sr_cross, grad_cq = lax.optimization_barrier(
+        (s_give, sr_same, sr_cross, grad_cq)
+    )
     s_take = send(s_give, swap, False)
-    grad_cq, grad_pool = assemble(cross_final_kernel, "cross_final", info, (x_keep, x_take), True)
     grad_q, grad_k, grad_v = assemble(
         self_final_kernel, "self_final", info, (s_keep, s_take, sr_same, sr_cross), False
     )

time: 111 us -> 105 us (0.946)
  starting transfers between devices: 35.7 us -> 29.7 us
  Pallas kernels: 45.5 us -> 47.3 us
    ppermute x15 -> x18, starting transfers between devices: 35.7 us -> 29.7 us  [send(): return lax.ppermute(value, 'ctx', pairs)]
    pallas_call x9 -> x10, Pallas kernels: 45.5 us -> 47.3 us  [call(): pl.pallas_call(kernel, name=name, grid_spec=pltpu.PrefetchScalarGridSpec(...]
    ppermute x15 -> x18, waiting for transfers between devices: 21.2 us -> 20.2 us  [send(): return lax.ppermute(value, 'ctx', pairs)]
    unnamed x16 -> x22, local copies, waits for them, and re-layouts: 2.99 us -> 2.55 us
  transfers between devices with their start and end apart: 15 -> 18, of which waited for: 5 -> 5; matrix products, arithmetic and copies ran while one was open for 3% -> 3% of each run, Pallas kernels for 36% -> 40%
where the time goes in v6:
time: 105 us; the launch traced here: 104 us
  Pallas kernels  47.3 us (45%)
  starting transfers between devices  29.7 us (28%)
  waiting for transfers between devices  20.2 us (19%)
  local copies, waits for them, and re-layouts  3.48 us (3%)
  other arithmetic  2.42 us (2%)
    pallas_call x10, Pallas kernels, call(): pl.pallas_call(kernel, name=name, grid_spec=pltpu.PrefetchScalarGridSpec(...  47.3 us
    ppermute x18, starting transfers between devices, send(): return lax.ppermute(value, 'ctx', pairs)  29.7 us
    ppermute x18, waiting for transfers between devices, send(): return lax.ppermute(value, 'ctx', pairs)  20.2 us
    unnamed x22, local copies, waits for them, and re-layouts  2.55 us
  transfers between devices with their start and end apart: 18, of which 5 were waited for; matrix products, arithmetic and copies ran while one was open for 3% of the time, Pallas kernels for 40%

profile of v6, /device:TPU:1, one launch (start us, length us, event | category | flops | bytes accessed | tf_op | source)
XLA Modules:
  0.0 104.0 jit_solution(3621092201549105044)
XLA Ops:
  0.6 2.8 %pack_cross.1 = (bf16[1040,512]{1,0:T(8,128)(2,1)}, bf16[528,512]{1,0:T(8,128)(2,1)}, bf16[528,512]{1,0:T(8,128)(2,1)}) custom-call(s32[1]{0:T(128)} %bitcast.info, s32[2,4]{1,0:T(2,128)} %bitcast.8, bf16[256,1024]{1,0:T(8,128)(2,1)} %refs_2_.6, bf16[256,1024]{1,0:T(8,128)(2,1)} %refs_3_.6, bf16[256,1024]{1,0:T(8,128)(2,1)} %refs_2_.6, ...), custom_call_target="tpu_custom_call" | custom-call | tf_op jit(solution)/shard_map/pack_cross/pallas_call | solution.py:83
  3.5 2.6 %collective-permute-start.3 = (bf16[528,512]{1,0:T(8,128)(2,1)}, bf16[528,512]{1,0:T(8,128)(2,1)S(1)}, u32[]{:S(2)}, u32[]{:S(2)}) collective-permute-start(bf16[528,512]{1,0:T(8,128)(2,1)} %get-tuple-element.71), channel_id=1, source_target_pairs={{0,15},{1,2},{2,1},{3,4},{4,3},{5,6},{6,5},{7,8},{8,7},{9,10},{10,... | collective-permute-start | bytes 1622024 | tf_op jit(solution)/shard_map/ppermute | solution.py:35
  7.3 2.3 %collective-permute-start = (bf16[1040,512]{1,0:T(8,128)(2,1)}, bf16[1040,512]{1,0:T(8,128)(2,1)}, u32[]{:S(2)}, u32[]{:S(2)}) collective-permute-start(bf16[1040,512]{1,0:T(8,128)(2,1)} %get-tuple-element.62), channel_id=1, source_target_pairs={{0,1},{1,0},{2,3},{3,2},{4,5},{5,4},{6,7},{7,6},{8,9},{9,8},{10,11... | collective-permute-start | bytes 3194888 | tf_op jit(solution)/shard_map/ppermute | solution.py:35
  9.6 2.6 %pack_self.1 = (bf16[1024,512]{1,0:T(8,128)(2,1)}, bf16[512,512]{1,0:T(8,128)(2,1)}, bf16[512,512]{1,0:T(8,128)(2,1)}) custom-call(s32[1]{0:T(128)} %bitcast.info, bf16[256,1024]{1,0:T(8,128)(2,1)} %refs_1_.3, bf16[256,1024]{1,0:T(8,128)(2,1)} %refs_2_.7, bf16[256,1024]{1,0:T(8,128)(2,1)} %refs_1_.3, bf16[256,1024]{1,0:T(8,128)(2,1)} %refs_2_.7, ...), custom_call_target="tpu_custom_call" | custom-call | tf_op jit(solution)/shard_map/pack_self/pallas_call | solution.py:83
  15.6 4.6 %cross_stats.1 = (f32[4,8,256]{2,1,0:T(8,128)}, f32[4,8,256]{2,1,0:T(8,128)}) custom-call(s32[1]{0:T(128)} %bitcast.info, bf16[528,512]{1,0:T(8,128)(2,1)} %get-tuple-element.64.refs_0_, bf16[1040,512]{1,0:T(8,128)(2,1)} %collective-permute-done.refs_1_.refs_5_.refs_6_.refs_7_.refs_8_.pk.pv, bf16[256,1024]{1,0:T(8,128)(2,1)} %refs_2_.6, ...), custom_call_target="tpu_custom_call" | custom-call | tf_op jit(solution)/shard_map/cross_stats/pallas_call | solution.py:83
  21.8 4.8 %self_stats.1.refs_10_ = f32[4,8,512]{2,1,0:T(8,128)} custom-call(s32[1]{0:T(128)} %bitcast.info, f32[512,512]{1,0:T(8,128)} %and_select_fusion.1.refs_0_, bf16[256,1024]{1,0:T(8,128)(2,1)} %refs_1_.3, bf16[256,1024]{1,0:T(8,128)(2,1)} %refs_2_.7, bf16[256,1024]{1,0:T(8,128)(2,1)} %refs_3_.7, bf16[256,1024]{1,0:T(8,128)(2,1)} %refs_4_.3, ...), custom_call_target="tpu_custom_call" | custom-call | tf_op jit(solution)/shard_map/self_stats/pallas_call | solution.py:83
  26.6 4.5 %collective-permute-done.2.sw.sq.sg = bf16[528,512]{1,0:T(8,128)(2,1)} collective-permute-done((bf16[528,512]{1,0:T(8,128)(2,1)}, bf16[528,512]{1,0:T(8,128)(2,1)}, u32[]{:S(2)}, u32[]{:S(2)}) %collective-permute-start.2) | collective-permute-done | bytes 540704 | tf_op jit(solution)/shard_map/ppermute | solution.py:35
  31.5 1.3 %collective-permute-start.8 = (bf16[512,512]{1,0:T(8,128)(2,1)}, bf16[512,512]{1,0:T(8,128)(2,1)}, u32[]{:S(2)}, u32[]{:S(2)}) collective-permute-start(bf16[512,512]{1,0:T(8,128)(2,1)} %get-tuple-element.86), channel_id=1, source_target_pairs={{2,0},{3,1},{4,2},{5,3},{6,4},{7,5},{8,6},{9,7},{10,8},{11,9},{12,... | collective-permute-start | bytes 1572872 | tf_op jit(solution)/shard_map/ppermute | solution.py:35
  32.8 1.3 %collective-permute-start.9 = (f32[4,8,512]{2,1,0:T(8,128)}, f32[4,8,512]{2,1,0:T(8,128)S(1)}, u32[]{:S(2)}, u32[]{:S(2)}) collective-permute-start(f32[4,8,512]{2,1,0:T(8,128)} %self_stats.1.refs_10_), channel_id=1, source_target_pairs={{2,0},{3,1},{4,2},{5,3},{6,4},{7,5},{8,6},{9,7},{10,8},{11,9},{12,... | collective-permute-start | bytes 196616 | tf_op jit(solution)/shard_map/ppermute | solution.py:35
  34.1 6.4 %cross_remote.1 = (bf16[256,512]{1,0:T(8,128)(2,1)}, bf16[256,512]{1,0:T(8,128)(2,1)}, bf16[1024,512]{1,0:T(8,128)(2,1)}, f32[4,8,256]{2,1,0:T(8,128)}, f32[4,8,256]{2,1,0:T(8,128)}) custom-call(s32[1]{0:T(128)} %bitcast.info, bf16[528,512]{1,0:T(8,128)(2,1)} %collective-permute-done.2.sw.sq.sg, bf16[528,512]{1,0:T(8,128)(2,1)} %copy-done, ...), custom_call_target="tpu_custom_call" | custom-call | tf_op jit(solution)/shard_map/cross_remote/pallas_call | solution.py:83
  40.5 7.5 %collective-permute-start.6 = (f32[4,8,256]{2,1,0:T(8,128)}, f32[4,8,256]{2,1,0:T(8,128)S(1)}, u32[]{:S(2)}, u32[]{:S(2)}) collective-permute-start(f32[4,8,256]{2,1,0:T(8,128)} %get-tuple-element.79), channel_id=1, source_target_pairs={{0,2},{1,15},{2,4},{3,1},{4,6},{5,3},{6,8},{7,5},{8,10},{9,7},{10,... | collective-permute-start | bytes 98312 | tf_op jit(solution)/shard_map/ppermute | solution.py:35
  48.0 1.3 %collective-permute-start.10 = (bf16[512,512]{1,0:T(8,128)(2,1)}, bf16[512,512]{1,0:T(8,128)(2,1)}, u32[]{:S(2)}, u32[]{:S(2)}) collective-permute-start(bf16[512,512]{1,0:T(8,128)(2,1)} %get-tuple-element.93), channel_id=1, source_target_pairs={{2,1},{3,0},{4,3},{5,2},{6,5},{7,4},{8,7},{9,6},{10,9},{11,8},{12,... | collective-permute-start | bytes 1572872 | tf_op jit(solution)/shard_map/ppermute | solution.py:35
  49.3 4.4 %collective-permute-done.7.refs_10_ = f32[4,8,256]{2,1,0:T(8,128)S(1)} collective-permute-done((f32[4,8,256]{2,1,0:T(8,128)}, f32[4,8,256]{2,1,0:T(8,128)S(1)}, u32[]{:S(2)}, u32[]{:S(2)}) %collective-permute-start.7) | collective-permute-done | bytes 32800 | tf_op jit(solution)/shard_map/ppermute | solution.py:35
  53.8 1.4 %collective-permute-start.11 = (bf16[256,512]{1,0:T(8,128)(2,1)}, bf16[256,512]{1,0:T(8,128)(2,1)S(1)}, u32[]{:S(2)}, u32[]{:S(2)}) collective-permute-start(bf16[256,512]{1,0:T(8,128)(2,1)} %get-tuple-element.96), channel_id=1, source_target_pairs={{0,2},{1,15},{2,4},{3,1},{4,6},{5,3},{6,8},{7,5},{8,10},{9,7},{10,... | collective-permute-start | bytes 786440 | tf_op jit(solution)/shard_map/ppermute | solution.py:35
  55.2 6.8 %cross_local.1 = (bf16[768,512]{1,0:T(8,128)(2,1)}, bf16[768,512]{1,0:T(8,128)(2,1)}) custom-call(s32[1]{0:T(128)} %bitcast.info, bf16[528,512]{1,0:T(8,128)(2,1)} %get-tuple-element.64.refs_0_, bf16[1040,512]{1,0:T(8,128)(2,1)} %collective-permute-done.refs_1_.refs_5_.refs_6_.refs_7_.refs_8_.pk.pv, bf16[256,1024]{1,0:T(8,128)(2,1)} %refs_2_.6, ...), custom_call_target="tpu_custom_call" | custom-call | flops 12000000000 | tf_op jit(solution)/shard_map/cross_local/pallas_call | solution.py:83
  62.0 8.4 %collective-permute-done.10.cq.cg = bf16[512,512]{1,0:T(8,128)(2,1)} collective-permute-done((bf16[512,512]{1,0:T(8,128)(2,1)}, bf16[512,512]{1,0:T(8,128)(2,1)}, u32[]{:S(2)}, u32[]{:S(2)}) %collective-permute-start.10) | collective-permute-done | bytes 524320 | tf_op jit(solution)/shard_map/ppermute | solution.py:35
  70.4 7.0 %self_remote.1 = (bf16[256,512]{1,0:T(8,128)(2,1)}, bf16[256,512]{1,0:T(8,128)(2,1)}, bf16[1024,512]{1,0:T(8,128)(2,1)}, f32[4,8,512]{2,1,0:T(8,128)}) custom-call(s32[1]{0:T(128)} %bitcast.info, f32[512,512]{1,0:T(8,128)} %and_select_fusion.bias, bf16[512,512]{1,0:T(8,128)(2,1)} %collective-permute-done.8.sq.sg, ...), custom_call_target="tpu_custom_call" | custom-call | flops 12000000000 | tf_op jit(solution)/shard_map/self_remote/pallas_call | solution.py:83
  77.4 1.3 %collective-permute-start.13 = (f32[4,8,512]{2,1,0:T(8,128)}, f32[4,8,512]{2,1,0:T(8,128)S(1)}, u32[]{:S(2)}, u32[]{:S(2)}) collective-permute-start(f32[4,8,512]{2,1,0:T(8,128)} %get-tuple-element.98), channel_id=1, source_target_pairs={{0,2},{1,3},{2,4},{3,5},{4,6},{5,7},{6,8},{7,9},{8,10},{9,11},{10,... | collective-permute-start | bytes 196616 | tf_op jit(solution)/shard_map/ppermute | solution.py:35
  78.7 2.4 %collective-permute-start.14 = (bf16[256,512]{1,0:T(8,128)(2,1)}, bf16[256,512]{1,0:T(8,128)(2,1)}, u32[]{:S(2)}, u32[]{:S(2)}) collective-permute-start(bf16[256,512]{1,0:T(8,128)(2,1)} %get-tuple-element.104), channel_id=1, source_target_pairs={{0,2},{1,3},{2,4},{3,5},{4,6},{5,7},{6,8},{7,9},{8,10},{9,11},{10,... | collective-permute-start | bytes 786440 | tf_op jit(solution)/shard_map/ppermute | solution.py:35
  81.0 5.1 %collective-permute-start.15 = (bf16[256,512]{1,0:T(8,128)(2,1)}, bf16[256,512]{1,0:T(8,128)(2,1)}, u32[]{:S(2)}, u32[]{:S(2)}) collective-permute-start(bf16[256,512]{1,0:T(8,128)(2,1)} %get-tuple-element.105), channel_id=1, source_target_pairs={{0,3},{1,2},{2,5},{3,4},{4,7},{5,6},{6,9},{7,8},{8,11},{9,10},{10,... | collective-permute-start | bytes 786440 | tf_op jit(solution)/shard_map/ppermute | solution.py:35
  87.4 6.7 %self_local.1 = (bf16[768,512]{1,0:T(8,128)(2,1)}, bf16[768,512]{1,0:T(8,128)(2,1)}) custom-call(s32[1]{0:T(128)} %bitcast.info, f32[512,512]{1,0:T(8,128)} %and_select_fusion.1.refs_0_, bf16[256,1024]{1,0:T(8,128)(2,1)} %refs_1_.3, bf16[256,1024]{1,0:T(8,128)(2,1)} %refs_2_.7, bf16[256,1024]{1,0:T(8,128)(2,1)} %refs_3_.7, bf16[256,1024]{1,0:T(8,128)(2,1)} %refs_4_.3, ...), custom_call_target="tpu_custom_call" | custom-call | flops 12000000000 | tf_op jit(solution)/shard_map/self_local/pallas_call | solution.py:83
  95.0 2.8 %cross_final.1 = (bf16[256,1024]{1,0:T(8,128)(2,1)}, bf16[2,256,1024]{2,1,0:T(8,128)(2,1)}) custom-call(s32[1]{0:T(128)} %bitcast.info, bf16[768,512]{1,0:T(8,128)(2,1)} %get-tuple-element.106.mine, bf16[768,512]{1,0:T(8,128)(2,1)} %copy-done.1, bf16[256,512]{1,0:T(8,128)(2,1)} %copy-done.3, bf16[256,512]{1,0:T(8,128)(2,1)} %copy-done.4), custom_call_target="tpu_custom_call" | custom-call | tf_op jit(solution)/shard_map/cross_final/pallas_call | solution.py:83
  97.9 2.5 %collective-permute-done.17.theirs = bf16[768,512]{1,0:T(8,128)(2,1)S(1)} collective-permute-done((bf16[768,512]{1,0:T(8,128)(2,1)}, bf16[768,512]{1,0:T(8,128)(2,1)S(1)}, u32[]{:S(2)}, u32[]{:S(2)}) %collective-permute-start.17) | collective-permute-done | bytes 786464 | tf_op jit(solution)/shard_map/ppermute | solution.py:35
  101.2 2.8 %self_final.1 = (bf16[256,1024]{1,0:T(8,128)(2,1)}, bf16[256,1024]{1,0:T(8,128)(2,1)}, bf16[256,1024]{1,0:T(8,128)(2,1)}) custom-call(s32[1]{0:T(128)} %bitcast.info, bf16[768,512]{1,0:T(8,128)(2,1)} %get-tuple-element.102.mine, bf16[768,512]{1,0:T(8,128)(2,1)} %copy-done.2, bf16[256,512]{1,0:T(8,128)(2,1)} %collective-permute-done.14.dq_mine, ...), custom_call_target="tpu_custom_call" | custom-call | tf_op jit(solution)/shard_map/self_final/pallas_call | solution.py:83
  (51 shorter events, 9.7 us)
Async XLA Ops:
  3.5 23.2 %collective-permute-start.3 = (bf16[528,512]{1,0:T(8,128)(2,1)}, bf16[528,512]{1,0:T(8,128)(2,1)S(1)}, u32[]{:S(2)}, u32[]{:S(2)}) collective-permute-start(bf16[528,512]{1,0:T(8,128)(2,1)} %get-tuple-element.71), channel_id=1, source_target_pairs={{0,15},{1,2},{2,1},{3,4},{4,3},{5,6},{6,5},{7,8},{8,7},{9,10},{10,... | collective-permute-start | bytes 1622024 | tf_op jit(solution)/shard_map/ppermute | solution.py:35
  6.1 25.1 %collective-permute-start.2 = (bf16[528,512]{1,0:T(8,128)(2,1)}, bf16[528,512]{1,0:T(8,128)(2,1)}, u32[]{:S(2)}, u32[]{:S(2)}) collective-permute-start(bf16[528,512]{1,0:T(8,128)(2,1)} %get-tuple-element.64.refs_0_), channel_id=1, source_target_pairs={{0,14},{1,3},{2,0},{3,5},{4,2},{5,7},{6,4},{7,9},{8,6},{9,11},{10,... | collective-permute-start | bytes 1622024 | tf_op jit(solution)/shard_map/ppermute | solution.py:35
  7.3 8.3 %collective-permute-start = (bf16[1040,512]{1,0:T(8,128)(2,1)}, bf16[1040,512]{1,0:T(8,128)(2,1)}, u32[]{:S(2)}, u32[]{:S(2)}) collective-permute-start(bf16[1040,512]{1,0:T(8,128)(2,1)} %get-tuple-element.62), channel_id=1, source_target_pairs={{0,1},{1,0},{2,3},{3,2},{4,5},{5,4},{6,7},{7,6},{8,9},{9,8},{10,11... | collective-permute-start | bytes 3194888 | tf_op jit(solution)/shard_map/ppermute | solution.py:35
  12.2 9.6 %collective-permute-start.1 = (bf16[1024,512]{1,0:T(8,128)(2,1)}, bf16[1024,512]{1,0:T(8,128)(2,1)}, u32[]{:S(2)}, u32[]{:S(2)}) collective-permute-start(bf16[1024,512]{1,0:T(8,128)(2,1)} %get-tuple-element.69), channel_id=1, source_target_pairs={{0,1},{1,0},{2,3},{3,2},{4,5},{5,4},{6,7},{7,6},{8,9},{9,8},{10,11... | collective-permute-start | bytes 3145736 | tf_op jit(solution)/shard_map/ppermute | solution.py:35
  20.3 10.9 %collective-permute-start.5 = (f32[4,8,256]{2,1,0:T(8,128)}, f32[4,8,256]{2,1,0:T(8,128)S(1)}, u32[]{:S(2)}, u32[]{:S(2)}) collective-permute-start(f32[4,8,256]{2,1,0:T(8,128)} %get-tuple-element.72), channel_id=1, source_target_pairs={{0,2},{1,15},{2,4},{3,1},{4,6},{5,3},{6,8},{7,5},{8,10},{9,7},{10,... | collective-permute-start | bytes 98312 | tf_op jit(solution)/shard_map/ppermute | solution.py:35
  21.4 10.1 %collective-permute-start.4 = (f32[4,8,256]{2,1,0:T(8,128)}, f32[4,8,256]{2,1,0:T(8,128)S(1)}, u32[]{:S(2)}, u32[]{:S(2)}) collective-permute-start(f32[4,8,256]{2,1,0:T(8,128)} %get-tuple-element.66), channel_id=1, source_target_pairs={{0,14},{1,3},{2,0},{3,5},{4,2},{5,7},{6,4},{7,9},{8,6},{9,11},{10,... | collective-permute-start | bytes 98312 | tf_op jit(solution)/shard_map/ppermute | solution.py:35
  26.6 7.5 %copy-start = (bf16[528,512]{1,0:T(8,128)(2,1)}, bf16[528,512]{1,0:T(8,128)(2,1)S(1)}, u32[]{:S(2)}) copy-start(bf16[528,512]{1,0:T(8,128)(2,1)S(1)} %collective-permute-done.3.cw.cq.cg) | copy-start | bytes 1622020
  31.1 3.0 %copy-start.5 = (f32[4,8,256]{2,1,0:T(8,128)}, f32[4,8,256]{2,1,0:T(8,128)S(1)}, u32[]{:S(2)}) copy-start(f32[4,8,256]{2,1,0:T(8,128)S(1)} %collective-permute-done.5.c_stats) | copy-start | bytes 98308
  31.5 2.6 %copy-start.6 = (f32[4,8,256]{2,1,0:T(8,128)}, f32[4,8,256]{2,1,0:T(8,128)S(1)}, u32[]{:S(2)}) copy-start(f32[4,8,256]{2,1,0:T(8,128)S(1)} %collective-permute-done.4.s_stats) | copy-start | bytes 98308
  31.5 23.7 %collective-permute-start.8 = (bf16[512,512]{1,0:T(8,128)(2,1)}, bf16[512,512]{1,0:T(8,128)(2,1)}, u32[]{:S(2)}, u32[]{:S(2)}) collective-permute-start(bf16[512,512]{1,0:T(8,128)(2,1)} %get-tuple-element.86), channel_id=1, source_target_pairs={{2,0},{3,1},{4,2},{5,3},{6,4},{7,5},{8,6},{9,7},{10,8},{11,9},{12,... | collective-permute-start | bytes 1572872 | tf_op jit(solution)/shard_map/ppermute | solution.py:35
  32.8 22.4 %collective-permute-start.9 = (f32[4,8,512]{2,1,0:T(8,128)}, f32[4,8,512]{2,1,0:T(8,128)S(1)}, u32[]{:S(2)}, u32[]{:S(2)}) collective-permute-start(f32[4,8,512]{2,1,0:T(8,128)} %self_stats.1.refs_10_), channel_id=1, source_target_pairs={{2,0},{3,1},{4,2},{5,3},{6,4},{7,5},{8,6},{9,7},{10,8},{11,9},{12,... | collective-permute-start | bytes 196616 | tf_op jit(solution)/shard_map/ppermute | solution.py:35
  40.5 8.8 %collective-permute-start.6 = (f32[4,8,256]{2,1,0:T(8,128)}, f32[4,8,256]{2,1,0:T(8,128)S(1)}, u32[]{:S(2)}, u32[]{:S(2)}) collective-permute-start(f32[4,8,256]{2,1,0:T(8,128)} %get-tuple-element.79), channel_id=1, source_target_pairs={{0,2},{1,15},{2,4},{3,1},{4,6},{5,3},{6,8},{7,5},{8,10},{9,7},{10,... | collective-permute-start | bytes 98312 | tf_op jit(solution)/shard_map/ppermute | solution.py:35
  48.0 5.8 %collective-permute-start.7 = (f32[4,8,256]{2,1,0:T(8,128)}, f32[4,8,256]{2,1,0:T(8,128)S(1)}, u32[]{:S(2)}, u32[]{:S(2)}) collective-permute-start(f32[4,8,256]{2,1,0:T(8,128)} %get-tuple-element.80), channel_id=1, source_target_pairs={{0,14},{1,3},{2,0},{3,5},{4,2},{5,7},{6,4},{7,9},{8,6},{9,11},{10,... | collective-permute-start | bytes 98312 | tf_op jit(solution)/shard_map/ppermute | solution.py:35
  48.0 22.4 %collective-permute-start.10 = (bf16[512,512]{1,0:T(8,128)(2,1)}, bf16[512,512]{1,0:T(8,128)(2,1)}, u32[]{:S(2)}, u32[]{:S(2)}) collective-permute-start(bf16[512,512]{1,0:T(8,128)(2,1)} %get-tuple-element.93), channel_id=1, source_target_pairs={{2,1},{3,0},{4,3},{5,2},{6,5},{7,4},{8,7},{9,6},{10,9},{11,8},{12,... | collective-permute-start | bytes 1572872 | tf_op jit(solution)/shard_map/ppermute | solution.py:35
  49.3 5.8 %copy-start.9 = (f32[4,8,256]{2,1,0:T(8,128)}, f32[4,8,256]{2,1,0:T(8,128)S(1)}, u32[]{:S(2)}) copy-start(f32[4,8,256]{2,1,0:T(8,128)S(1)} %collective-permute-done.6.refs_9_) | copy-start | bytes 98308
  53.8 1.4 %copy-start.10 = (f32[4,8,256]{2,1,0:T(8,128)}, f32[4,8,256]{2,1,0:T(8,128)S(1)}, u32[]{:S(2)}) copy-start(f32[4,8,256]{2,1,0:T(8,128)S(1)} %collective-permute-done.7.refs_10_) | copy-start | bytes 98308
  53.8 32.3 %collective-permute-start.11 = (bf16[256,512]{1,0:T(8,128)(2,1)}, bf16[256,512]{1,0:T(8,128)(2,1)S(1)}, u32[]{:S(2)}, u32[]{:S(2)}) collective-permute-start(bf16[256,512]{1,0:T(8,128)(2,1)} %get-tuple-element.96), channel_id=1, source_target_pairs={{0,2},{1,15},{2,4},{3,1},{4,6},{5,3},{6,8},{7,5},{8,10},{9,7},{10,... | collective-permute-start | bytes 786440 | tf_op jit(solution)/shard_map/ppermute | solution.py:35
  55.1 31.0 %collective-permute-start.12 = (bf16[256,512]{1,0:T(8,128)(2,1)}, bf16[256,512]{1,0:T(8,128)(2,1)S(1)}, u32[]{:S(2)}, u32[]{:S(2)}) collective-permute-start(bf16[256,512]{1,0:T(8,128)(2,1)} %get-tuple-element.97), channel_id=1, source_target_pairs={{0,15},{1,2},{2,1},{3,4},{4,3},{5,6},{6,5},{7,8},{8,7},{9,10},{10,... | collective-permute-start | bytes 786440 | tf_op jit(solution)/shard_map/ppermute | solution.py:35
  55.1 6.9 %copy-start.7 = (f32[4,8,512]{2,1,0:T(8,128)}, f32[4,8,512]{2,1,0:T(8,128)S(1)}, u32[]{:S(2)}) copy-start(f32[4,8,512]{2,1,0:T(8,128)S(1)} %collective-permute-done.9.stats) | copy-start | bytes 196612
  77.4 8.8 %collective-permute-start.13 = (f32[4,8,512]{2,1,0:T(8,128)}, f32[4,8,512]{2,1,0:T(8,128)S(1)}, u32[]{:S(2)}, u32[]{:S(2)}) collective-permute-start(f32[4,8,512]{2,1,0:T(8,128)} %get-tuple-element.98), channel_id=1, source_target_pairs={{0,2},{1,3},{2,4},{3,5},{4,6},{5,7},{6,8},{7,9},{8,10},{9,11},{10,... | collective-permute-start | bytes 196616 | tf_op jit(solution)/shard_map/ppermute | solution.py:35
  78.7 19.1 %collective-permute-start.14 = (bf16[256,512]{1,0:T(8,128)(2,1)}, bf16[256,512]{1,0:T(8,128)(2,1)}, u32[]{:S(2)}, u32[]{:S(2)}) collective-permute-start(bf16[256,512]{1,0:T(8,128)(2,1)} %get-tuple-element.104), channel_id=1, source_target_pairs={{0,2},{1,3},{2,4},{3,5},{4,6},{5,7},{6,8},{7,9},{8,10},{9,11},{10,... | collective-permute-start | bytes 786440 | tf_op jit(solution)/shard_map/ppermute | solution.py:35
  81.0 16.8 %collective-permute-start.15 = (bf16[256,512]{1,0:T(8,128)(2,1)}, bf16[256,512]{1,0:T(8,128)(2,1)}, u32[]{:S(2)}, u32[]{:S(2)}) collective-permute-start(bf16[256,512]{1,0:T(8,128)(2,1)} %get-tuple-element.105), channel_id=1, source_target_pairs={{0,3},{1,2},{2,5},{3,4},{4,7},{5,6},{6,9},{7,8},{8,11},{9,10},{10,... | collective-permute-start | bytes 786440 | tf_op jit(solution)/shard_map/ppermute | solution.py:35
  86.9 7.2 %collective-permute-start.16 = (bf16[768,512]{1,0:T(8,128)(2,1)}, bf16[768,512]{1,0:T(8,128)(2,1)S(1)}, u32[]{:S(2)}, u32[]{:S(2)}) collective-permute-start(bf16[768,512]{1,0:T(8,128)(2,1)} %get-tuple-element.107), channel_id=1, source_target_pairs={{0,1},{1,0},{2,3},{3,2},{4,5},{5,4},{6,7},{7,6},{8,9},{9,8},{10,11... | collective-permute-start | bytes 2359304 | tf_op jit(solution)/shard_map/ppermute | solution.py:35
  97.8 2.6 %collective-permute-start.17 = (bf16[768,512]{1,0:T(8,128)(2,1)}, bf16[768,512]{1,0:T(8,128)(2,1)S(1)}, u32[]{:S(2)}, u32[]{:S(2)}) collective-permute-start(bf16[768,512]{1,0:T(8,128)(2,1)} %get-tuple-element.111), channel_id=1, source_target_pairs={{0,1},{1,0},{2,3},{3,2},{4,5},{5,4},{6,7},{7,6},{8,9},{9,8},{10,11... | collective-permute-start | bytes 2359304 | tf_op jit(solution)/shard_map/ppermute | solution.py:35
  (5 other events, 4.5 us)

commit v7 on v6

--- a/solution.py
+++ b/solution.py
@@ -12,6 +12,9 @@
 HEAD_DIM = 128
 HALF = HEADS // 2
 WIDE = HALF * HEAD_DIM
+STEP = 2
+COLS = STEP * HEAD_DIM
+STEPS = HALF // STEP
 STRETCH = 64
 NBR_TOK = 128
 ROWS = 256
@@ -51,21 +54,19 @@
     return d - 1 if d % 2 == 0 else d + 1
 
 
-def spec(rows, row_block=0, cols=HEAD_DIM):
-    return pl.BlockSpec((rows, cols), lambda h, info: (row_block, h))
+def spec(rows, row_block=0):
+    return pl.BlockSpec((rows, COLS), lambda h, info: (row_block, h))
 
 
 def own_spec(lead=()):
     zeros = (0,) * len(lead)
-    return pl.BlockSpec(
-        lead + (ROWS, HEAD_DIM), lambda h, info: zeros + (0, info[0] % 2 * HALF + h)
-    )
+    return pl.BlockSpec(lead + (ROWS, COLS), lambda h, info: zeros + (0, info[0] % 2 * STEPS + h))
 
 
 def other_spec(lead=()):
     zeros = (0,) * len(lead)
     return pl.BlockSpec(
-        lead + (ROWS, HEAD_DIM), lambda h, info: zeros + (0, (1 - info[0] % 2) * HALF + h)
+        lead + (ROWS, COLS), lambda h, info: zeros + (0, (1 - info[0] % 2) * STEPS + h)
     )
 
 
@@ -75,16 +76,15 @@
 
 
 def stat_spec(rows):
-    return pl.BlockSpec((1, 8, rows), lambda h, info: (h, 0, 0))
-
-
-def call(kernel, name, info, in_specs, inputs, out_specs, outs, steps=HALF, flops=0, prefetch=None):
-    prefetch = (info,) if prefetch is None else prefetch
+    return pl.BlockSpec((STEP, 8, rows), lambda h, info: (h, 0, 0))
+
+
+def call(kernel, name, info, in_specs, inputs, out_specs, outs, steps=STEPS, flops=0):
     return pl.pallas_call(
         kernel,
         name=name,
         grid_spec=pltpu.PrefetchScalarGridSpec(
-            num_scalar_prefetch=len(prefetch),
+            num_scalar_prefetch=1,
             grid=(steps,),
             in_specs=in_specs,
             out_specs=out_specs,
@@ -92,7 +92,25 @@
         out_shape=[jax.ShapeDtypeStruct(shape, dtype) for shape, dtype in outs],
         compiler_params=pltpu.CompilerParams(vmem_limit_bytes=63 << 20),
         cost_estimate=pl.CostEstimate(flops=flops, transcendentals=0, bytes_accessed=0),
-    )(*prefetch, *inputs)
+    )(info, *inputs)
+
+
+def head_of(ref, j):
+    shape = ref.shape
+    if len(shape) == 3 and shape[1] == 8:
+        return ref.at[j : j + 1]
+    if shape[-1] != COLS:
+        return ref
+    place = pl.ds(j * HEAD_DIM, HEAD_DIM)
+    return ref.at[:, place] if len(shape) == 2 else ref.at[:, :, place]
+
+
+def per_head(kernel):
+    def run(info, *refs):
+        for j in range(STEP):
+            kernel(info, *[head_of(ref, j) for ref in refs])
+
+    return run
 
 
 def dot_last(a, b):
@@ -380,19 +398,14 @@
     width = queries.shape[1]
     pool = pool_kv.reshape(2, ROWS, width)
 
-    cols = WIDE // 2
-    block = lambda rows: pl.BlockSpec((rows, cols), lambda h, info: (0, h))
-    mine_spec = pl.BlockSpec((ROWS, cols), lambda h, info: (0, info[0] % 2 * 2 + h))
-    their_spec = pl.BlockSpec((ROWS, cols), lambda h, info: (0, (1 - info[0] % 2) * 2 + h))
-    their_pool = pl.BlockSpec((2, ROWS, cols), lambda h, info: (0, 0, (1 - info[0] % 2) * 2 + h))
+    mine_spec, their_spec, their_pool = own_spec(), other_spec(), other_spec((2,))
     sizes = (4 * ROWS + EXTRA, 2 * ROWS + EXTRA, 2 * ROWS + EXTRA)
     packed, x_mine, x_other = call(
         functools.partial(pack_cross_kernel, enc_dev, loop), "pack_cross", info,
         [whole_spec(neighbour_ids.shape[::-1])] + [mine_spec] * 2 + [their_spec] * 2 + [their_pool],
         (neighbour_ids.T, cross_queries, grad_cross, cross_queries, grad_cross, pool),
-        [block(rows) for rows in sizes],
+        [spec(rows) for rows in sizes],
         [((rows, WIDE), BF16) for rows in sizes],
-        steps=2,
     )
     x_same = send(x_mine, outward, True)
     x_cross = send(x_other, across, True)
@@ -403,9 +416,8 @@
         pack_self_kernel, "pack_self", info,
         [mine_spec] * 2 + [their_spec] * 4,
         (queries_in, grad_self, queries_in, grad_self, keys, values),
-        [block(rows) for rows in sizes],
+        [spec(rows) for rows in sizes],
         [((rows, WIDE), BF16) for rows in sizes],
-        steps=2,
     )
     s_pair = send(packed, swap, False)
 
@@ -436,7 +448,7 @@
     stat = lambda rows: ((HALF, 8, rows), F32)
 
     x_own, x_partner = call(
-        cross_stats_kernel, "cross_stats", info, cross_specs, cross_args,
+        per_head(cross_stats_kernel), "cross_stats", info, cross_specs, cross_args,
         [stat_spec(ROWS)] * 2, [stat(ROWS)] * 2, flops=0,
     )
     t_same = send(x_own, outward, True)
@@ -444,7 +456,7 @@
     local_bias, x_own = lax.optimization_barrier((local_bias, x_own))
     self_args = (local_bias,) + self_args[1:]
     (s_own,) = call(
-        self_stats_kernel, "self_stats", info, self_specs, self_args,
+        per_head(self_stats_kernel), "self_stats", info, self_specs, self_args,
         [stat_spec(2 * ROWS)], [stat(2 * ROWS)], flops=0,
     )
     t_self = send(s_own, lambda d: d - 2, False)
@@ -457,7 +469,7 @@
     kv_shape = ((4 * ROWS, WIDE), BF16)
     q_shape = ((ROWS, WIDE), BF16)
     xd_same, xd_cross, x_kv, x_fin_same, x_fin_cross = call(
-        cross_remote_kernel, "cross_remote", info,
+        per_head(cross_remote_kernel), "cross_remote", info,
         [mine_w, mine_w, spec(ROWS, 0), spec(ROWS, 1), spec(ROWS, 0), spec(ROWS, 1)]
         + [own_spec((2,)), spec(ROWS, 2), spec(ROWS, 3), stat_spec(ROWS), stat_spec(ROWS)],
         (x_same, x_cross, x_same, x_same, x_cross, x_cross, pool, x_pair, x_pair, t_same, t_cross),
@@ -478,7 +490,7 @@
     half_out = spec(3 * ROWS)
     half_shape = ((3 * ROWS, WIDE), BF16)
     x_keep, x_give = call(
-        cross_local_kernel, "cross_local", info,
+        per_head(cross_local_kernel), "cross_local", info,
         cross_specs + [stat_spec(ROWS), stat_spec(ROWS), spec(4 * ROWS)],
         cross_args + (f_own, f_partner, x_kv),
         [half_out] * 2, [half_shape] * 2, flops=LONG,
@@ -486,7 +498,7 @@
 
     far_bias, x_keep = lax.optimization_barrier((far_bias, x_keep))
     sd_same, sd_cross, s_kv, s_fin = call(
-        self_remote_kernel, "self_remote", info,
+        per_head(self_remote_kernel), "self_remote", info,
         [bias_spec, spec(ROWS, 0), spec(ROWS, 1), spec(ROWS, 0), spec(ROWS, 1)]
         + [own_spec(), own_spec(), spec(ROWS, 2), spec(ROWS, 3), stat_spec(2 * ROWS)],
         (far_bias, s_same, s_same, s_cross, s_cross, keys, values, s_pair, s_pair, t_self),
@@ -502,7 +514,7 @@
     )
     x_take = send(x_give, swap, False)
     s_keep, s_give = call(
-        self_local_kernel, "self_local", info,
+        per_head(self_local_kernel), "self_local", info,
         self_specs + [stat_spec(2 * ROWS), stat_spec(2 * ROWS), spec(4 * ROWS)],
         self_args + (f_self, s_own, s_kv),
         [half_out] * 2, [half_shape] * 2, flops=LONG,

time: 105 us -> 103 us (0.981)
  Pallas kernels: 47.3 us -> 44.2 us
  waiting for transfers between devices: 20.2 us -> 21.9 us
    pallas_call x10, Pallas kernels: 47.3 us -> 44.2 us  [call(): pl.pallas_call(kernel, name=name, grid_spec=pltpu.PrefetchScalarGridSpec(...]
    ppermute x18, waiting for transfers between devices: 20.2 us -> 21.9 us  [send(): return lax.ppermute(value, 'ctx', pairs)]
  transfers between devices with their start and end apart: 18 -> 18, of which waited for: 5 -> 6; matrix products, arithmetic and copies ran while one was open for 3% -> 3% of each run, Pallas kernels for 40% -> 38%
where the time goes in v7:
time: 103 us
  Pallas kernels  44.2 us (43%)
  starting transfers between devices  29.7 us (29%)
  waiting for transfers between devices  21.9 us (21%)
  local copies, waits for them, and re-layouts  3.48 us (3%)
  other arithmetic  2.42 us (2%)
    pallas_call x10, Pallas kernels, call(): pl.pallas_call(kernel, name=name, grid_spec=pltpu.PrefetchScalarGridSpec(...  44.2 us
    ppermute x18, starting transfers between devices, send(): return lax.ppermute(value, 'ctx', pairs)  29.7 us
    ppermute x18, waiting for transfers between devices, send(): return lax.ppermute(value, 'ctx', pairs)  21.9 us
    unnamed x22, local copies, waits for them, and re-layouts  2.55 us
  transfers between devices with their start and end apart: 18, of which 6 were waited for; matrix products, arithmetic and copies ran while one was open for 3% of the time, Pallas kernels for 38%

profile of v7, /device:TPU:1, one launch (start us, length us, event | category | flops | bytes accessed | tf_op | source)
XLA Modules:
  0.0 102.6 jit_solution(4530251644163256685)
XLA Ops:
  0.6 2.8 %pack_cross.1 = (bf16[1040,512]{1,0:T(8,128)(2,1)}, bf16[528,512]{1,0:T(8,128)(2,1)}, bf16[528,512]{1,0:T(8,128)(2,1)}) custom-call(s32[1]{0:T(128)} %bitcast.info, s32[2,4]{1,0:T(2,128)} %bitcast.8, bf16[256,1024]{1,0:T(8,128)(2,1)} %refs_2_.6, bf16[256,1024]{1,0:T(8,128)(2,1)} %refs_3_.6, bf16[256,1024]{1,0:T(8,128)(2,1)} %refs_2_.6, ...), custom_call_target="tpu_custom_call" | custom-call | tf_op jit(solution)/shard_map/pack_cross/pallas_call | solution.py:83
  3.5 2.6 %collective-permute-start.3 = (bf16[528,512]{1,0:T(8,128)(2,1)}, bf16[528,512]{1,0:T(8,128)(2,1)S(1)}, u32[]{:S(2)}, u32[]{:S(2)}) collective-permute-start(bf16[528,512]{1,0:T(8,128)(2,1)} %get-tuple-element.71), channel_id=1, source_target_pairs={{0,15},{1,2},{2,1},{3,4},{4,3},{5,6},{6,5},{7,8},{8,7},{9,10},{10,... | collective-permute-start | bytes 1622024 | tf_op jit(solution)/shard_map/ppermute | solution.py:38
  7.3 2.3 %collective-permute-start = (bf16[1040,512]{1,0:T(8,128)(2,1)}, bf16[1040,512]{1,0:T(8,128)(2,1)}, u32[]{:S(2)}, u32[]{:S(2)}) collective-permute-start(bf16[1040,512]{1,0:T(8,128)(2,1)} %get-tuple-element.62), channel_id=1, source_target_pairs={{0,1},{1,0},{2,3},{3,2},{4,5},{5,4},{6,7},{7,6},{8,9},{9,8},{10,11... | collective-permute-start | bytes 3194888 | tf_op jit(solution)/shard_map/ppermute | solution.py:38
  9.6 2.6 %pack_self.1 = (bf16[1024,512]{1,0:T(8,128)(2,1)}, bf16[512,512]{1,0:T(8,128)(2,1)}, bf16[512,512]{1,0:T(8,128)(2,1)}) custom-call(s32[1]{0:T(128)} %bitcast.info, bf16[256,1024]{1,0:T(8,128)(2,1)} %refs_1_.3, bf16[256,1024]{1,0:T(8,128)(2,1)} %refs_2_.7, bf16[256,1024]{1,0:T(8,128)(2,1)} %refs_1_.3, bf16[256,1024]{1,0:T(8,128)(2,1)} %refs_2_.7, ...), custom_call_target="tpu_custom_call" | custom-call | tf_op jit(solution)/shard_map/pack_self/pallas_call | solution.py:83
  15.6 4.0 %cross_stats.1 = (f32[4,8,256]{2,1,0:T(8,128)}, f32[4,8,256]{2,1,0:T(8,128)}) custom-call(s32[1]{0:T(128)} %bitcast.info, bf16[528,512]{1,0:T(8,128)(2,1)} %get-tuple-element.64.refs_0_, bf16[1040,512]{1,0:T(8,128)(2,1)} %collective-permute-done.refs_1_.refs_5_.refs_6_.refs_7_.refs_8_, bf16[256,1024]{1,0:T(8,128)(2,1)} %refs_2_.6, ...), custom_call_target="tpu_custom_call" | custom-call | tf_op jit(solution)/shard_map/cross_stats/pallas_call | solution.py:83
  21.2 4.2 %self_stats.1.refs_10_ = f32[4,8,512]{2,1,0:T(8,128)} custom-call(s32[1]{0:T(128)} %bitcast.info, f32[512,512]{1,0:T(8,128)} %and_select_fusion.1.refs_0_, bf16[256,1024]{1,0:T(8,128)(2,1)} %refs_1_.3, bf16[256,1024]{1,0:T(8,128)(2,1)} %refs_2_.7, bf16[256,1024]{1,0:T(8,128)(2,1)} %refs_3_.7, bf16[256,1024]{1,0:T(8,128)(2,1)} %refs_4_.3, ...), custom_call_target="tpu_custom_call" | custom-call | tf_op jit(solution)/shard_map/self_stats/pallas_call | solution.py:83
  25.6 5.6 %collective-permute-done.2.refs_0_.refs_2_.refs_3_ = bf16[528,512]{1,0:T(8,128)(2,1)} collective-permute-done((bf16[528,512]{1,0:T(8,128)(2,1)}, bf16[528,512]{1,0:T(8,128)(2,1)}, u32[]{:S(2)}, u32[]{:S(2)}) %collective-permute-start.2) | collective-permute-done | bytes 540704 | tf_op jit(solution)/shard_map/ppermute | solution.py:38
  31.5 1.3 %collective-permute-start.8 = (bf16[512,512]{1,0:T(8,128)(2,1)}, bf16[512,512]{1,0:T(8,128)(2,1)}, u32[]{:S(2)}, u32[]{:S(2)}) collective-permute-start(bf16[512,512]{1,0:T(8,128)(2,1)} %get-tuple-element.86), channel_id=1, source_target_pairs={{2,0},{3,1},{4,2},{5,3},{6,4},{7,5},{8,6},{9,7},{10,8},{11,9},{12,... | collective-permute-start | bytes 1572872 | tf_op jit(solution)/shard_map/ppermute | solution.py:38
  32.8 1.3 %collective-permute-start.9 = (f32[4,8,512]{2,1,0:T(8,128)}, f32[4,8,512]{2,1,0:T(8,128)S(1)}, u32[]{:S(2)}, u32[]{:S(2)}) collective-permute-start(f32[4,8,512]{2,1,0:T(8,128)} %self_stats.1.refs_10_), channel_id=1, source_target_pairs={{2,0},{3,1},{4,2},{5,3},{6,4},{7,5},{8,6},{9,7},{10,8},{11,9},{12,... | collective-permute-start | bytes 196616 | tf_op jit(solution)/shard_map/ppermute | solution.py:38
  34.1 5.9 %cross_remote.1 = (bf16[256,512]{1,0:T(8,128)(2,1)}, bf16[256,512]{1,0:T(8,128)(2,1)}, bf16[1024,512]{1,0:T(8,128)(2,1)}, f32[4,8,256]{2,1,0:T(8,128)}, f32[4,8,256]{2,1,0:T(8,128)}) custom-call(s32[1]{0:T(128)} %bitcast.info, bf16[528,512]{1,0:T(8,128)(2,1)} %collective-permute-done.2.refs_0_.refs_2_.refs_3_, bf16[528,512]{1,0:T(8,128)(2,1)} %copy-done, ...), custom_call_target="tpu_custom_call" | custom-call | tf_op jit(solution)/shard_map/cross_remote/pallas_call | solution.py:83
  40.0 7.5 %collective-permute-start.6 = (f32[4,8,256]{2,1,0:T(8,128)}, f32[4,8,256]{2,1,0:T(8,128)S(1)}, u32[]{:S(2)}, u32[]{:S(2)}) collective-permute-start(f32[4,8,256]{2,1,0:T(8,128)} %get-tuple-element.79), channel_id=1, source_target_pairs={{0,2},{1,15},{2,4},{3,1},{4,6},{5,3},{6,8},{7,5},{8,10},{9,7},{10,... | collective-permute-start | bytes 98312 | tf_op jit(solution)/shard_map/ppermute | solution.py:38
  47.5 1.3 %collective-permute-start.10 = (bf16[512,512]{1,0:T(8,128)(2,1)}, bf16[512,512]{1,0:T(8,128)(2,1)}, u32[]{:S(2)}, u32[]{:S(2)}) collective-permute-start(bf16[512,512]{1,0:T(8,128)(2,1)} %get-tuple-element.93), channel_id=1, source_target_pairs={{2,1},{3,0},{4,3},{5,2},{6,5},{7,4},{8,7},{9,6},{10,9},{11,8},{12,... | collective-permute-start | bytes 1572872 | tf_op jit(solution)/shard_map/ppermute | solution.py:38
  48.9 4.4 %collective-permute-done.7.refs_10_ = f32[4,8,256]{2,1,0:T(8,128)S(1)} collective-permute-done((f32[4,8,256]{2,1,0:T(8,128)}, f32[4,8,256]{2,1,0:T(8,128)S(1)}, u32[]{:S(2)}, u32[]{:S(2)}) %collective-permute-start.7) | collective-permute-done | bytes 32800 | tf_op jit(solution)/shard_map/ppermute | solution.py:38
  53.3 1.4 %collective-permute-start.11 = (bf16[256,512]{1,0:T(8,128)(2,1)}, bf16[256,512]{1,0:T(8,128)(2,1)S(1)}, u32[]{:S(2)}, u32[]{:S(2)}) collective-permute-start(bf16[256,512]{1,0:T(8,128)(2,1)} %get-tuple-element.96), channel_id=1, source_target_pairs={{0,2},{1,15},{2,4},{3,1},{4,6},{5,3},{6,8},{7,5},{8,10},{9,7},{10,... | collective-permute-start | bytes 786440 | tf_op jit(solution)/shard_map/ppermute | solution.py:38
  54.7 6.4 %cross_local.1 = (bf16[768,512]{1,0:T(8,128)(2,1)}, bf16[768,512]{1,0:T(8,128)(2,1)}) custom-call(s32[1]{0:T(128)} %bitcast.info, bf16[528,512]{1,0:T(8,128)(2,1)} %get-tuple-element.64.refs_0_, bf16[1040,512]{1,0:T(8,128)(2,1)} %collective-permute-done.refs_1_.refs_5_.refs_6_.refs_7_.refs_8_, bf16[256,1024]{1,0:T(8,128)(2,1)} %refs_2_.6, ...), custom_call_target="tpu_custom_call" | custom-call | flops 12000000000 | tf_op jit(solution)/shard_map/cross_local/pallas_call | solution.py:83
  61.1 8.8 %collective-permute-done.10.refs_3_.refs_4_ = bf16[512,512]{1,0:T(8,128)(2,1)} collective-permute-done((bf16[512,512]{1,0:T(8,128)(2,1)}, bf16[512,512]{1,0:T(8,128)(2,1)}, u32[]{:S(2)}, u32[]{:S(2)}) %collective-permute-start.10) | collective-permute-done | bytes 524320 | tf_op jit(solution)/shard_map/ppermute | solution.py:38
  69.9 6.7 %self_remote.1 = (bf16[256,512]{1,0:T(8,128)(2,1)}, bf16[256,512]{1,0:T(8,128)(2,1)}, bf16[1024,512]{1,0:T(8,128)(2,1)}, f32[4,8,512]{2,1,0:T(8,128)}) custom-call(s32[1]{0:T(128)} %bitcast.info, f32[512,512]{1,0:T(8,128)} %and_select_fusion.refs_0_, bf16[512,512]{1,0:T(8,128)(2,1)} %collective-permute-done.8.refs_1_.refs_2_, ...), custom_call_target="tpu_custom_call" | custom-call | flops 12000000000 | tf_op jit(solution)/shard_map/self_remote/pallas_call | solution.py:83
  76.6 1.3 %collective-permute-start.13 = (f32[4,8,512]{2,1,0:T(8,128)}, f32[4,8,512]{2,1,0:T(8,128)S(1)}, u32[]{:S(2)}, u32[]{:S(2)}) collective-permute-start(f32[4,8,512]{2,1,0:T(8,128)} %get-tuple-element.98), channel_id=1, source_target_pairs={{0,2},{1,3},{2,4},{3,5},{4,6},{5,7},{6,8},{7,9},{8,10},{9,11},{10,... | collective-permute-start | bytes 196616 | tf_op jit(solution)/shard_map/ppermute | solution.py:38
  77.9 2.4 %collective-permute-start.14 = (bf16[256,512]{1,0:T(8,128)(2,1)}, bf16[256,512]{1,0:T(8,128)(2,1)}, u32[]{:S(2)}, u32[]{:S(2)}) collective-permute-start(bf16[256,512]{1,0:T(8,128)(2,1)} %get-tuple-element.104), channel_id=1, source_target_pairs={{0,2},{1,3},{2,4},{3,5},{4,6},{5,7},{6,8},{7,9},{8,10},{9,11},{10,... | collective-permute-start | bytes 786440 | tf_op jit(solution)/shard_map/ppermute | solution.py:38
  80.3 5.1 %collective-permute-start.15 = (bf16[256,512]{1,0:T(8,128)(2,1)}, bf16[256,512]{1,0:T(8,128)(2,1)}, u32[]{:S(2)}, u32[]{:S(2)}) collective-permute-start(bf16[256,512]{1,0:T(8,128)(2,1)} %get-tuple-element.105), channel_id=1, source_target_pairs={{0,3},{1,2},{2,5},{3,4},{4,7},{5,6},{6,9},{7,8},{8,11},{9,10},{10,... | collective-permute-start | bytes 786440 | tf_op jit(solution)/shard_map/ppermute | solution.py:38
  86.6 6.1 %self_local.1 = (bf16[768,512]{1,0:T(8,128)(2,1)}, bf16[768,512]{1,0:T(8,128)(2,1)}) custom-call(s32[1]{0:T(128)} %bitcast.info, f32[512,512]{1,0:T(8,128)} %and_select_fusion.1.refs_0_, bf16[256,1024]{1,0:T(8,128)(2,1)} %refs_1_.3, bf16[256,1024]{1,0:T(8,128)(2,1)} %refs_2_.7, bf16[256,1024]{1,0:T(8,128)(2,1)} %refs_3_.7, bf16[256,1024]{1,0:T(8,128)(2,1)} %refs_4_.3, ...), custom_call_target="tpu_custom_call" | custom-call | flops 12000000000 | tf_op jit(solution)/shard_map/self_local/pallas_call | solution.py:83
  93.6 2.8 %cross_final.1 = (bf16[256,1024]{1,0:T(8,128)(2,1)}, bf16[2,256,1024]{2,1,0:T(8,128)(2,1)}) custom-call(s32[1]{0:T(128)} %bitcast.info, bf16[768,512]{1,0:T(8,128)(2,1)} %get-tuple-element.106.mine, bf16[768,512]{1,0:T(8,128)(2,1)} %copy-done.1, bf16[256,512]{1,0:T(8,128)(2,1)} %copy-done.3, bf16[256,512]{1,0:T(8,128)(2,1)} %copy-done.4), custom_call_target="tpu_custom_call" | custom-call | tf_op jit(solution)/shard_map/cross_final/pallas_call | solution.py:83
  96.5 2.4 %collective-permute-done.17.theirs = bf16[768,512]{1,0:T(8,128)(2,1)S(1)} collective-permute-done((bf16[768,512]{1,0:T(8,128)(2,1)}, bf16[768,512]{1,0:T(8,128)(2,1)S(1)}, u32[]{:S(2)}, u32[]{:S(2)}) %collective-permute-start.17) | collective-permute-done | bytes 786464 | tf_op jit(solution)/shard_map/ppermute | solution.py:38
  99.8 2.8 %self_final.1 = (bf16[256,1024]{1,0:T(8,128)(2,1)}, bf16[256,1024]{1,0:T(8,128)(2,1)}, bf16[256,1024]{1,0:T(8,128)(2,1)}) custom-call(s32[1]{0:T(128)} %bitcast.info, bf16[768,512]{1,0:T(8,128)(2,1)} %get-tuple-element.102.mine, bf16[768,512]{1,0:T(8,128)(2,1)} %copy-done.2, bf16[256,512]{1,0:T(8,128)(2,1)} %collective-permute-done.14.dq_mine, ...), custom_call_target="tpu_custom_call" | custom-call | tf_op jit(solution)/shard_map/self_final/pallas_call | solution.py:83
  (51 shorter events, 10.0 us)
Async XLA Ops:
  3.5 22.1 %collective-permute-start.3 = (bf16[528,512]{1,0:T(8,128)(2,1)}, bf16[528,512]{1,0:T(8,128)(2,1)S(1)}, u32[]{:S(2)}, u32[]{:S(2)}) collective-permute-start(bf16[528,512]{1,0:T(8,128)(2,1)} %get-tuple-element.71), channel_id=1, source_target_pairs={{0,15},{1,2},{2,1},{3,4},{4,3},{5,6},{6,5},{7,8},{8,7},{9,10},{10,... | collective-permute-start | bytes 1622024 | tf_op jit(solution)/shard_map/ppermute | solution.py:38
  6.1 25.1 %collective-permute-start.2 = (bf16[528,512]{1,0:T(8,128)(2,1)}, bf16[528,512]{1,0:T(8,128)(2,1)}, u32[]{:S(2)}, u32[]{:S(2)}) collective-permute-start(bf16[528,512]{1,0:T(8,128)(2,1)} %get-tuple-element.64.refs_0_), channel_id=1, source_target_pairs={{0,14},{1,3},{2,0},{3,5},{4,2},{5,7},{6,4},{7,9},{8,6},{9,11},{10,... | collective-permute-start | bytes 1622024 | tf_op jit(solution)/shard_map/ppermute | solution.py:38
  7.3 8.3 %collective-permute-start = (bf16[1040,512]{1,0:T(8,128)(2,1)}, bf16[1040,512]{1,0:T(8,128)(2,1)}, u32[]{:S(2)}, u32[]{:S(2)}) collective-permute-start(bf16[1040,512]{1,0:T(8,128)(2,1)} %get-tuple-element.62), channel_id=1, source_target_pairs={{0,1},{1,0},{2,3},{3,2},{4,5},{5,4},{6,7},{7,6},{8,9},{9,8},{10,11... | collective-permute-start | bytes 3194888 | tf_op jit(solution)/shard_map/ppermute | solution.py:38
  12.2 9.0 %collective-permute-start.1 = (bf16[1024,512]{1,0:T(8,128)(2,1)}, bf16[1024,512]{1,0:T(8,128)(2,1)}, u32[]{:S(2)}, u32[]{:S(2)}) collective-permute-start(bf16[1024,512]{1,0:T(8,128)(2,1)} %get-tuple-element.69), channel_id=1, source_target_pairs={{0,1},{1,0},{2,3},{3,2},{4,5},{5,4},{6,7},{7,6},{8,9},{9,8},{10,11... | collective-permute-start | bytes 3145736 | tf_op jit(solution)/shard_map/ppermute | solution.py:38
  19.6 11.5 %collective-permute-start.5 = (f32[4,8,256]{2,1,0:T(8,128)}, f32[4,8,256]{2,1,0:T(8,128)S(1)}, u32[]{:S(2)}, u32[]{:S(2)}) collective-permute-start(f32[4,8,256]{2,1,0:T(8,128)} %get-tuple-element.72), channel_id=1, source_target_pairs={{0,2},{1,15},{2,4},{3,1},{4,6},{5,3},{6,8},{7,5},{8,10},{9,7},{10,... | collective-permute-start | bytes 98312 | tf_op jit(solution)/shard_map/ppermute | solution.py:38
  20.8 10.7 %collective-permute-start.4 = (f32[4,8,256]{2,1,0:T(8,128)}, f32[4,8,256]{2,1,0:T(8,128)S(1)}, u32[]{:S(2)}, u32[]{:S(2)}) collective-permute-start(f32[4,8,256]{2,1,0:T(8,128)} %get-tuple-element.66), channel_id=1, source_target_pairs={{0,14},{1,3},{2,0},{3,5},{4,2},{5,7},{6,4},{7,9},{8,6},{9,11},{10,... | collective-permute-start | bytes 98312 | tf_op jit(solution)/shard_map/ppermute | solution.py:38
  25.6 8.5 %copy-start = (bf16[528,512]{1,0:T(8,128)(2,1)}, bf16[528,512]{1,0:T(8,128)(2,1)S(1)}, u32[]{:S(2)}) copy-start(bf16[528,512]{1,0:T(8,128)(2,1)S(1)} %collective-permute-done.3.refs_1_.refs_4_.refs_5_) | copy-start | bytes 1622020
  31.1 3.0 %copy-start.5 = (f32[4,8,256]{2,1,0:T(8,128)}, f32[4,8,256]{2,1,0:T(8,128)S(1)}, u32[]{:S(2)}) copy-start(f32[4,8,256]{2,1,0:T(8,128)S(1)} %collective-permute-done.5.refs_10_) | copy-start | bytes 98308
  31.5 2.6 %copy-start.6 = (f32[4,8,256]{2,1,0:T(8,128)}, f32[4,8,256]{2,1,0:T(8,128)S(1)}, u32[]{:S(2)}) copy-start(f32[4,8,256]{2,1,0:T(8,128)S(1)} %collective-permute-done.4.refs_9_) | copy-start | bytes 98308
  31.5 23.2 %collective-permute-start.8 = (bf16[512,512]{1,0:T(8,128)(2,1)}, bf16[512,512]{1,0:T(8,128)(2,1)}, u32[]{:S(2)}, u32[]{:S(2)}) collective-permute-start(bf16[512,512]{1,0:T(8,128)(2,1)} %get-tuple-element.86), channel_id=1, source_target_pairs={{2,0},{3,1},{4,2},{5,3},{6,4},{7,5},{8,6},{9,7},{10,8},{11,9},{12,... | collective-permute-start | bytes 1572872 | tf_op jit(solution)/shard_map/ppermute | solution.py:38
  32.8 21.9 %collective-permute-start.9 = (f32[4,8,512]{2,1,0:T(8,128)}, f32[4,8,512]{2,1,0:T(8,128)S(1)}, u32[]{:S(2)}, u32[]{:S(2)}) collective-permute-start(f32[4,8,512]{2,1,0:T(8,128)} %self_stats.1.refs_10_), channel_id=1, source_target_pairs={{2,0},{3,1},{4,2},{5,3},{6,4},{7,5},{8,6},{9,7},{10,8},{11,9},{12,... | collective-permute-start | bytes 196616 | tf_op jit(solution)/shard_map/ppermute | solution.py:38
  40.0 8.8 %collective-permute-start.6 = (f32[4,8,256]{2,1,0:T(8,128)}, f32[4,8,256]{2,1,0:T(8,128)S(1)}, u32[]{:S(2)}, u32[]{:S(2)}) collective-permute-start(f32[4,8,256]{2,1,0:T(8,128)} %get-tuple-element.79), channel_id=1, source_target_pairs={{0,2},{1,15},{2,4},{3,1},{4,6},{5,3},{6,8},{7,5},{8,10},{9,7},{10,... | collective-permute-start | bytes 98312 | tf_op jit(solution)/shard_map/ppermute | solution.py:38
  47.5 5.8 %collective-permute-start.7 = (f32[4,8,256]{2,1,0:T(8,128)}, f32[4,8,256]{2,1,0:T(8,128)S(1)}, u32[]{:S(2)}, u32[]{:S(2)}) collective-permute-start(f32[4,8,256]{2,1,0:T(8,128)} %get-tuple-element.80), channel_id=1, source_target_pairs={{0,14},{1,3},{2,0},{3,5},{4,2},{5,7},{6,4},{7,9},{8,6},{9,11},{10,... | collective-permute-start | bytes 98312 | tf_op jit(solution)/shard_map/ppermute | solution.py:38
  47.5 22.4 %collective-permute-start.10 = (bf16[512,512]{1,0:T(8,128)(2,1)}, bf16[512,512]{1,0:T(8,128)(2,1)}, u32[]{:S(2)}, u32[]{:S(2)}) collective-permute-start(bf16[512,512]{1,0:T(8,128)(2,1)} %get-tuple-element.93), channel_id=1, source_target_pairs={{2,1},{3,0},{4,3},{5,2},{6,5},{7,4},{8,7},{9,6},{10,9},{11,8},{12,... | collective-permute-start | bytes 1572872 | tf_op jit(solution)/shard_map/ppermute | solution.py:38
  48.9 5.8 %copy-start.9 = (f32[4,8,256]{2,1,0:T(8,128)}, f32[4,8,256]{2,1,0:T(8,128)S(1)}, u32[]{:S(2)}) copy-start(f32[4,8,256]{2,1,0:T(8,128)S(1)} %collective-permute-done.6.refs_9_) | copy-start | bytes 98308
  53.3 1.4 %copy-start.10 = (f32[4,8,256]{2,1,0:T(8,128)}, f32[4,8,256]{2,1,0:T(8,128)S(1)}, u32[]{:S(2)}) copy-start(f32[4,8,256]{2,1,0:T(8,128)S(1)} %collective-permute-done.7.refs_10_) | copy-start | bytes 98308
  53.3 32.1 %collective-permute-start.11 = (bf16[256,512]{1,0:T(8,128)(2,1)}, bf16[256,512]{1,0:T(8,128)(2,1)S(1)}, u32[]{:S(2)}, u32[]{:S(2)}) collective-permute-start(bf16[256,512]{1,0:T(8,128)(2,1)} %get-tuple-element.96), channel_id=1, source_target_pairs={{0,2},{1,15},{2,4},{3,1},{4,6},{5,3},{6,8},{7,5},{8,10},{9,7},{10,... | collective-permute-start | bytes 786440 | tf_op jit(solution)/shard_map/ppermute | solution.py:38
  54.7 30.7 %collective-permute-start.12 = (bf16[256,512]{1,0:T(8,128)(2,1)}, bf16[256,512]{1,0:T(8,128)(2,1)S(1)}, u32[]{:S(2)}, u32[]{:S(2)}) collective-permute-start(bf16[256,512]{1,0:T(8,128)(2,1)} %get-tuple-element.97), channel_id=1, source_target_pairs={{0,15},{1,2},{2,1},{3,4},{4,3},{5,6},{6,5},{7,8},{8,7},{9,10},{10,... | collective-permute-start | bytes 786440 | tf_op jit(solution)/shard_map/ppermute | solution.py:38
  54.7 6.4 %copy-start.7 = (f32[4,8,512]{2,1,0:T(8,128)}, f32[4,8,512]{2,1,0:T(8,128)S(1)}, u32[]{:S(2)}) copy-start(f32[4,8,512]{2,1,0:T(8,128)S(1)} %collective-permute-done.9.refs_9_) | copy-start | bytes 196612
  76.6 8.8 %collective-permute-start.13 = (f32[4,8,512]{2,1,0:T(8,128)}, f32[4,8,512]{2,1,0:T(8,128)S(1)}, u32[]{:S(2)}, u32[]{:S(2)}) collective-permute-start(f32[4,8,512]{2,1,0:T(8,128)} %get-tuple-element.98), channel_id=1, source_target_pairs={{0,2},{1,3},{2,4},{3,5},{4,6},{5,7},{6,8},{7,9},{8,10},{9,11},{10,... | collective-permute-start | bytes 196616 | tf_op jit(solution)/shard_map/ppermute | solution.py:38
  77.9 18.4 %collective-permute-start.14 = (bf16[256,512]{1,0:T(8,128)(2,1)}, bf16[256,512]{1,0:T(8,128)(2,1)}, u32[]{:S(2)}, u32[]{:S(2)}) collective-permute-start(bf16[256,512]{1,0:T(8,128)(2,1)} %get-tuple-element.104), channel_id=1, source_target_pairs={{0,2},{1,3},{2,4},{3,5},{4,6},{5,7},{6,8},{7,9},{8,10},{9,11},{10,... | collective-permute-start | bytes 786440 | tf_op jit(solution)/shard_map/ppermute | solution.py:38
  80.3 16.1 %collective-permute-start.15 = (bf16[256,512]{1,0:T(8,128)(2,1)}, bf16[256,512]{1,0:T(8,128)(2,1)}, u32[]{:S(2)}, u32[]{:S(2)}) collective-permute-start(bf16[256,512]{1,0:T(8,128)(2,1)} %get-tuple-element.105), channel_id=1, source_target_pairs={{0,3},{1,2},{2,5},{3,4},{4,7},{5,6},{6,9},{7,8},{8,11},{9,10},{10,... | collective-permute-start | bytes 786440 | tf_op jit(solution)/shard_map/ppermute | solution.py:38
  86.2 6.5 %collective-permute-start.16 = (bf16[768,512]{1,0:T(8,128)(2,1)}, bf16[768,512]{1,0:T(8,128)(2,1)S(1)}, u32[]{:S(2)}, u32[]{:S(2)}) collective-permute-start(bf16[768,512]{1,0:T(8,128)(2,1)} %get-tuple-element.107), channel_id=1, source_target_pairs={{0,1},{1,0},{2,3},{3,2},{4,5},{5,4},{6,7},{7,6},{8,9},{9,8},{10,11... | collective-permute-start | bytes 2359304 | tf_op jit(solution)/shard_map/ppermute | solution.py:38
  96.3 2.6 %collective-permute-start.17 = (bf16[768,512]{1,0:T(8,128)(2,1)}, bf16[768,512]{1,0:T(8,128)(2,1)S(1)}, u32[]{:S(2)}, u32[]{:S(2)}) collective-permute-start(bf16[768,512]{1,0:T(8,128)(2,1)} %get-tuple-element.111), channel_id=1, source_target_pairs={{0,1},{1,0},{2,3},{3,2},{4,5},{5,4},{6,7},{7,6},{8,9},{9,8},{10,11... | collective-permute-start | bytes 2359304 | tf_op jit(solution)/shard_map/ppermute | solution.py:38
  (5 other events, 4.5 us)

commit v8 on v7

--- a/solution.py
+++ b/solution.py
@@ -92,7 +92,7 @@
         out_shape=[jax.ShapeDtypeStruct(shape, dtype) for shape, dtype in outs],
         compiler_params=pltpu.CompilerParams(vmem_limit_bytes=63 << 20),
         cost_estimate=pl.CostEstimate(flops=flops, transcendentals=0, bytes_accessed=0),
-    )(info, *inputs)
+    )(info, *[pltpu.with_memory_space_constraint(x, pltpu.HBM) for x in inputs])
 
 
 def head_of(ref, j):
@@ -273,7 +273,7 @@
 
 
 def self_remote_kernel(
-    info, bias, sq, sg, cq, cg, k, v, pk, pv, stats, dq_same, dq_cross, kv_ref, out_stats
+    info, bias, sq, sg, cq, cg, k, v, pk, pv, stats, dq_ref, kv_ref, out_stats
 ):
     core = info[0] % 2
     q0, q1 = ordered(core, sq[...], cq[...])
@@ -289,8 +289,8 @@
     px, py = ex * scale, ey * scale[:, ROWS:]
     dq1, dq0, dk1, dk0, dv1, dv0 = wide_gradients(px, py, dpx, dpy, delta, qs, gs, k1, k0)
     same, cross = ordered(core, dq0, dq1)
-    dq_same[...] = same.astype(BF16)
-    dq_cross[...] = cross.astype(BF16)
+    dq_ref[:ROWS] = same.astype(BF16)
+    dq_ref[ROWS:] = cross.astype(BF16)
     for index, grad in enumerate(ordered(core, dk0, dk1) + ordered(core, dv0, dv1)):
         kv_ref[index * ROWS : (index + 1) * ROWS] = grad.astype(BF16)
     out_stats[...] = stat_rows(top, inverse, delta)
@@ -385,6 +385,8 @@
     else:
         out_specs, outs = [rows_out] * 3, [full] * 3
     in_specs = [whole_spec(x.shape) for x in inputs]
+    if not pooled:
+        in_specs[2:] = [whole_spec((ROWS, WIDE)), whole_spec((ROWS, WIDE), (1, 0))]
     return call(kernel, name, info, in_specs, inputs, out_specs, outs, steps=2)
 
 
@@ -480,12 +482,6 @@
     f_partner = send(x_fin_cross, outward, True)
     s_other, x_kv = lax.optimization_barrier((s_other, x_kv))
     s_cross = send(s_other, lambda d: (d - 2) ^ 1, False)
-    xd_same, xd_cross, f_own, f_partner = lax.optimization_barrier(
-        (xd_same, xd_cross, f_own, f_partner)
-    )
-    xr_same = send(xd_same, inward, True)
-    xr_cross = send(xd_cross, across, True)
-
     x_kv, s_same, t_self = lax.optimization_barrier((x_kv, s_same, t_self))
     half_out = spec(3 * ROWS)
     half_shape = ((3 * ROWS, WIDE), BF16)
@@ -496,18 +492,22 @@
         [half_out] * 2, [half_shape] * 2, flops=LONG,
     )
 
+    xd_same, xd_cross, s_cross, x_keep = lax.optimization_barrier(
+        (xd_same, xd_cross, s_cross, x_keep)
+    )
+    xr_same = send(xd_same, inward, True)
+    xr_cross = send(xd_cross, across, True)
     far_bias, x_keep = lax.optimization_barrier((far_bias, x_keep))
-    sd_same, sd_cross, s_kv, s_fin = call(
+    sd, s_kv, s_fin = call(
         per_head(self_remote_kernel), "self_remote", info,
         [bias_spec, spec(ROWS, 0), spec(ROWS, 1), spec(ROWS, 0), spec(ROWS, 1)]
         + [own_spec(), own_spec(), spec(ROWS, 2), spec(ROWS, 3), stat_spec(2 * ROWS)],
         (far_bias, s_same, s_same, s_cross, s_cross, keys, values, s_pair, s_pair, t_self),
-        [spec(ROWS), spec(ROWS), kv_out, stat_spec(2 * ROWS)],
-        [q_shape, q_shape, kv_shape, stat(2 * ROWS)], flops=LONG,
+        [spec(2 * ROWS), kv_out, stat_spec(2 * ROWS)],
+        [((2 * ROWS, WIDE), BF16), kv_shape, stat(2 * ROWS)], flops=LONG,
     )
     f_self = send(s_fin, lambda d: d + 2, False)
-    sr_same = send(sd_same, lambda d: d + 2, False)
-    sr_cross = send(sd_cross, lambda d: (d + 2) ^ 1, False)
+    sr = send(sd, lambda d: d + 2, False)
 
     x_give, s_kv, xr_same, xr_cross, f_self = lax.optimization_barrier(
         (x_give, s_kv, xr_same, xr_cross, f_self)
@@ -522,12 +522,11 @@
     grad_cq, grad_pool = assemble(
         cross_final_kernel, "cross_final", info, (x_keep, x_take, xr_same, xr_cross), True
     )
-    s_give, sr_same, sr_cross, grad_cq = lax.optimization_barrier(
-        (s_give, sr_same, sr_cross, grad_cq)
-    )
+    s_give, sr, grad_cq = lax.optimization_barrier((s_give, sr, grad_cq))
     s_take = send(s_give, swap, False)
+    sr_take = send(sr, swap, False)
     grad_q, grad_k, grad_v = assemble(
-        self_final_kernel, "self_final", info, (s_keep, s_take, sr_same, sr_cross), False
+        self_final_kernel, "self_final", info, (s_keep, s_take, sr, sr_take), False
     )
     return grad_q, grad_k, grad_v, grad_cq, grad_pool.reshape(pool_kv.shape)
 

time: 103 us -> 99.9 us (0.970)
  waiting for transfers between devices: 21.9 us -> 17.1 us
  local copies, waits for them, and re-layouts: 3.48 us -> 5.72 us
    ppermute x18, waiting for transfers between devices: 21.9 us -> 17.1 us  [send(): return lax.ppermute(value, 'ctx', pairs)]
    unnamed x22 -> x28, local copies, waits for them, and re-layouts: 2.55 us -> 4.8 us
  transfers between devices with their start and end apart: 18 -> 18, of which waited for: 6 -> 6; matrix products, arithmetic and copies ran while one was open for 3% -> 3% of each run, Pallas kernels for 38% -> 39%
where the time goes in v8:
time: 99.9 us; the launch traced here: 99.2 us
  Pallas kernels  44.1 us (44%)
  starting transfers between devices  29.1 us (29%)
  waiting for transfers between devices  17.1 us (17%)
  local copies, waits for them, and re-layouts  5.72 us (6%)
  other arithmetic  2.42 us (2%)
    pallas_call x10, Pallas kernels, call(): pl.pallas_call(kernel, name=name, grid_spec=pltpu.PrefetchScalarGridSpec(...  44.1 us
    ppermute x18, starting transfers between devices, send(): return lax.ppermute(value, 'ctx', pairs)  29.1 us
    ppermute x18, waiting for transfers between devices, send(): return lax.ppermute(value, 'ctx', pairs)  17.1 us
    unnamed x28, local copies, waits for them, and re-layouts  4.8 us
  transfers between devices with their start and end apart: 18, of which 6 were waited for; matrix products, arithmetic and copies ran while one was open for 3% of the time, Pallas kernels for 39%

profile of v8, /device:TPU:1, one launch (start us, length us, event | category | flops | bytes accessed | tf_op | source)
XLA Modules:
  0.0 99.2 jit_solution(7154731132108349853)
XLA Ops:
  0.6 2.8 %pack_cross.1 = (bf16[1040,512]{1,0:T(8,128)(2,1)}, bf16[528,512]{1,0:T(8,128)(2,1)}, bf16[528,512]{1,0:T(8,128)(2,1)}) custom-call(s32[1]{0:T(128)} %bitcast.info, s32[2,4]{1,0:T(2,128)} %bitcast.8, bf16[256,1024]{1,0:T(8,128)(2,1)} %refs_2_.6, bf16[256,1024]{1,0:T(8,128)(2,1)} %refs_3_.6, bf16[256,1024]{1,0:T(8,128)(2,1)} %refs_2_.6, ...), custom_call_target="tpu_custom_call" | custom-call | tf_op jit(solution)/shard_map/pack_cross/pallas_call | solution.py:83
  3.4 2.6 %collective-permute-start.3 = (bf16[528,512]{1,0:T(8,128)(2,1)}, bf16[528,512]{1,0:T(8,128)(2,1)S(1)}, u32[]{:S(2)}, u32[]{:S(2)}) collective-permute-start(bf16[528,512]{1,0:T(8,128)(2,1)} %get-tuple-element.69), channel_id=1, source_target_pairs={{0,15},{1,2},{2,1},{3,4},{4,3},{5,6},{6,5},{7,8},{8,7},{9,10},{10,... | collective-permute-start | bytes 1622024 | tf_op jit(solution)/shard_map/ppermute | solution.py:38
  6.1 1.2 %collective-permute-start.2 = (bf16[528,512]{1,0:T(8,128)(2,1)}, bf16[528,512]{1,0:T(8,128)(2,1)}, u32[]{:S(2)}, u32[]{:S(2)}) collective-permute-start(bf16[528,512]{1,0:T(8,128)(2,1)} %get-tuple-element.62.refs_0_), channel_id=1, source_target_pairs={{0,14},{1,3},{2,0},{3,5},{4,2},{5,7},{6,4},{7,9},{8,6},{9,11},{10,... | collective-permute-start | bytes 1622024 | tf_op jit(solution)/shard_map/ppermute | solution.py:38
  7.3 2.3 %collective-permute-start = (bf16[1040,512]{1,0:T(8,128)(2,1)}, bf16[1040,512]{1,0:T(8,128)(2,1)}, u32[]{:S(2)}, u32[]{:S(2)}) collective-permute-start(bf16[1040,512]{1,0:T(8,128)(2,1)} %get-tuple-element.60), channel_id=1, source_target_pairs={{0,1},{1,0},{2,3},{3,2},{4,5},{5,4},{6,7},{7,6},{8,9},{9,8},{10,11... | collective-permute-start | bytes 3194888 | tf_op jit(solution)/shard_map/ppermute | solution.py:38
  9.6 2.6 %pack_self.1 = (bf16[1024,512]{1,0:T(8,128)(2,1)}, bf16[512,512]{1,0:T(8,128)(2,1)}, bf16[512,512]{1,0:T(8,128)(2,1)}) custom-call(s32[1]{0:T(128)} %bitcast.info, bf16[256,1024]{1,0:T(8,128)(2,1)} %refs_1_.3, bf16[256,1024]{1,0:T(8,128)(2,1)} %refs_2_.7, bf16[256,1024]{1,0:T(8,128)(2,1)} %refs_1_.3, bf16[256,1024]{1,0:T(8,128)(2,1)} %refs_2_.7, ...), custom_call_target="tpu_custom_call" | custom-call | tf_op jit(solution)/shard_map/pack_self/pallas_call | solution.py:83
  13.2 1.2 %and_select_fusion.refs_0_ = f32[512,512]{1,0:T(8,128)} fusion(s32[512]{0:T(512)S(1)} %pad_add_fusion.3, s32[512]{0:T(512)S(1)} %get-tuple-element.119, pred[]{:T(512)S(6)} %lt.19), kind=kLoop, calls=%fused_computation | loop fusion | flops 786432 | bytes 1052673 | tf_op jit(solution)/shard_map/jit(_where)/select_n | solution.py:437
  15.6 4.0 %cross_stats.1 = (f32[4,8,256]{2,1,0:T(8,128)}, f32[4,8,256]{2,1,0:T(8,128)}) custom-call(s32[1]{0:T(128)} %bitcast.info, bf16[528,512]{1,0:T(8,128)(2,1)} %get-tuple-element.62.refs_0_, bf16[1040,512]{1,0:T(8,128)(2,1)} %collective-permute-done.refs_1_.refs_5_.refs_6_.refs_7_.refs_8_, bf16[256,1024]{1,0:T(8,128)(2,1)} %refs_2_.6, ...), custom_call_target="tpu_custom_call" | custom-call | tf_op jit(solution)/shard_map/cross_stats/pallas_call | solution.py:83
  21.1 4.2 %self_stats.1.refs_10_ = f32[4,8,512]{2,1,0:T(8,128)} custom-call(s32[1]{0:T(128)} %bitcast.info, f32[512,512]{1,0:T(8,128)} %and_select_fusion.1.refs_0_, bf16[256,1024]{1,0:T(8,128)(2,1)} %refs_1_.3, bf16[256,1024]{1,0:T(8,128)(2,1)} %refs_2_.7, bf16[256,1024]{1,0:T(8,128)(2,1)} %refs_3_.7, bf16[256,1024]{1,0:T(8,128)(2,1)} %refs_4_.3, ...), custom_call_target="tpu_custom_call" | custom-call | tf_op jit(solution)/shard_map/self_stats/pallas_call | solution.py:83
  25.6 5.6 %collective-permute-done.2.refs_0_.refs_2_.refs_3_ = bf16[528,512]{1,0:T(8,128)(2,1)} collective-permute-done((bf16[528,512]{1,0:T(8,128)(2,1)}, bf16[528,512]{1,0:T(8,128)(2,1)}, u32[]{:S(2)}, u32[]{:S(2)}) %collective-permute-start.2) | collective-permute-done | bytes 540704 | tf_op jit(solution)/shard_map/ppermute | solution.py:38
  31.5 1.3 %collective-permute-start.8 = (bf16[512,512]{1,0:T(8,128)(2,1)}, bf16[512,512]{1,0:T(8,128)(2,1)}, u32[]{:S(2)}, u32[]{:S(2)}) collective-permute-start(bf16[512,512]{1,0:T(8,128)(2,1)} %get-tuple-element.80), channel_id=1, source_target_pairs={{2,0},{3,1},{4,2},{5,3},{6,4},{7,5},{8,6},{9,7},{10,8},{11,9},{12,... | collective-permute-start | bytes 1572872 | tf_op jit(solution)/shard_map/ppermute | solution.py:38
  32.8 1.3 %collective-permute-start.9 = (f32[4,8,512]{2,1,0:T(8,128)}, f32[4,8,512]{2,1,0:T(8,128)S(1)}, u32[]{:S(2)}, u32[]{:S(2)}) collective-permute-start(f32[4,8,512]{2,1,0:T(8,128)} %self_stats.1.refs_10_), channel_id=1, source_target_pairs={{2,0},{3,1},{4,2},{5,3},{6,4},{7,5},{8,6},{9,7},{10,8},{11,9},{12,... | collective-permute-start | bytes 196616 | tf_op jit(solution)/shard_map/ppermute | solution.py:38
  34.1 5.9 %cross_remote.1 = (bf16[256,512]{1,0:T(8,128)(2,1)}, bf16[256,512]{1,0:T(8,128)(2,1)}, bf16[1024,512]{1,0:T(8,128)(2,1)}, f32[4,8,256]{2,1,0:T(8,128)}, f32[4,8,256]{2,1,0:T(8,128)}) custom-call(s32[1]{0:T(128)} %bitcast.info, bf16[528,512]{1,0:T(8,128)(2,1)} %collective-permute-done.2.refs_0_.refs_2_.refs_3_, bf16[528,512]{1,0:T(8,128)(2,1)} %copy-done, ...), custom_call_target="tpu_custom_call" | custom-call | tf_op jit(solution)/shard_map/cross_remote/pallas_call | solution.py:83
  40.0 7.5 %collective-permute-start.6 = (f32[4,8,256]{2,1,0:T(8,128)}, f32[4,8,256]{2,1,0:T(8,128)S(1)}, u32[]{:S(2)}, u32[]{:S(2)}) collective-permute-start(f32[4,8,256]{2,1,0:T(8,128)} %get-tuple-element.75), channel_id=1, source_target_pairs={{0,2},{1,15},{2,4},{3,1},{4,6},{5,3},{6,8},{7,5},{8,10},{9,7},{10,... | collective-permute-start | bytes 98312 | tf_op jit(solution)/shard_map/ppermute | solution.py:38
  47.5 1.4 %collective-permute-start.10 = (bf16[512,512]{1,0:T(8,128)(2,1)}, bf16[512,512]{1,0:T(8,128)(2,1)S(1)}, u32[]{:S(2)}, u32[]{:S(2)}) collective-permute-start(bf16[512,512]{1,0:T(8,128)(2,1)} %get-tuple-element.86), channel_id=1, source_target_pairs={{2,1},{3,0},{4,3},{5,2},{6,5},{7,4},{8,7},{9,6},{10,9},{11,8},{12,... | collective-permute-start | bytes 1572872 | tf_op jit(solution)/shard_map/ppermute | solution.py:38
  49.0 4.3 %collective-permute-done.7.refs_10_ = f32[4,8,256]{2,1,0:T(8,128)S(1)} collective-permute-done((f32[4,8,256]{2,1,0:T(8,128)}, f32[4,8,256]{2,1,0:T(8,128)S(1)}, u32[]{:S(2)}, u32[]{:S(2)}) %collective-permute-start.7) | collective-permute-done | bytes 32800 | tf_op jit(solution)/shard_map/ppermute | solution.py:38
  53.9 6.4 %cross_local.1 = (bf16[768,512]{1,0:T(8,128)(2,1)}, bf16[768,512]{1,0:T(8,128)(2,1)}) custom-call(s32[1]{0:T(128)} %bitcast.info, bf16[528,512]{1,0:T(8,128)(2,1)} %get-tuple-element.62.refs_0_, bf16[1040,512]{1,0:T(8,128)(2,1)} %collective-permute-done.refs_1_.refs_5_.refs_6_.refs_7_.refs_8_, bf16[256,1024]{1,0:T(8,128)(2,1)} %refs_2_.6, ...), custom_call_target="tpu_custom_call" | custom-call | flops 12000000000 | tf_op jit(solution)/shard_map/cross_local/pallas_call | solution.py:83
  60.3 3.8 %collective-permute-done.10.refs_3_.refs_4_ = bf16[512,512]{1,0:T(8,128)(2,1)S(1)} collective-permute-done((bf16[512,512]{1,0:T(8,128)(2,1)}, bf16[512,512]{1,0:T(8,128)(2,1)S(1)}, u32[]{:S(2)}, u32[]{:S(2)}) %collective-permute-start.10) | collective-permute-done | bytes 524320 | tf_op jit(solution)/shard_map/ppermute | solution.py:38
  66.0 6.6 %self_remote.1 = (bf16[512,512]{1,0:T(8,128)(2,1)}, bf16[1024,512]{1,0:T(8,128)(2,1)}, f32[4,8,512]{2,1,0:T(8,128)}) custom-call(s32[1]{0:T(128)} %bitcast.info, f32[512,512]{1,0:T(8,128)} %and_select_fusion.refs_0_, bf16[512,512]{1,0:T(8,128)(2,1)} %collective-permute-done.8.refs_1_.refs_2_, bf16[512,512]{1,0:T(8,128)(2,1)} %collective-permute-done.8.refs_1_.refs_2_, ...), custom_call_target="tpu_custom_call" | custom-call | flops 12000000000 | tf_op jit(solution)/shard_map/self_remote/pallas_call | solution.py:83
  72.7 3.4 %collective-permute-start.13 = (f32[4,8,512]{2,1,0:T(8,128)}, f32[4,8,512]{2,1,0:T(8,128)S(1)}, u32[]{:S(2)}, u32[]{:S(2)}) collective-permute-start(f32[4,8,512]{2,1,0:T(8,128)} %get-tuple-element.96), channel_id=1, source_target_pairs={{0,2},{1,3},{2,4},{3,5},{4,6},{5,7},{6,8},{7,9},{8,10},{9,11},{10,... | collective-permute-start | bytes 196616 | tf_op jit(solution)/shard_map/ppermute | solution.py:38
  76.2 3.7 %collective-permute-start.14 = (bf16[512,512]{1,0:T(8,128)(2,1)}, bf16[512,512]{1,0:T(8,128)(2,1)}, u32[]{:S(2)}, u32[]{:S(2)}) collective-permute-start(bf16[512,512]{1,0:T(8,128)(2,1)} %get-tuple-element.102), channel_id=1, source_target_pairs={{0,2},{1,3},{2,4},{3,5},{4,6},{5,7},{6,8},{7,9},{8,10},{9,11},{10,... | collective-permute-start | bytes 1572872 | tf_op jit(solution)/shard_map/ppermute | solution.py:38
  81.8 6.1 %self_local.1 = (bf16[768,512]{1,0:T(8,128)(2,1)}, bf16[768,512]{1,0:T(8,128)(2,1)}) custom-call(s32[1]{0:T(128)} %bitcast.info, f32[512,512]{1,0:T(8,128)} %and_select_fusion.1.refs_0_, bf16[256,1024]{1,0:T(8,128)(2,1)} %refs_1_.3, bf16[256,1024]{1,0:T(8,128)(2,1)} %refs_2_.7, bf16[256,1024]{1,0:T(8,128)(2,1)} %refs_3_.7, bf16[256,1024]{1,0:T(8,128)(2,1)} %refs_4_.3, ...), custom_call_target="tpu_custom_call" | custom-call | flops 12000000000 | tf_op jit(solution)/shard_map/self_local/pallas_call | solution.py:83
  88.8 2.8 %cross_final.1 = (bf16[256,1024]{1,0:T(8,128)(2,1)}, bf16[2,256,1024]{2,1,0:T(8,128)(2,1)}) custom-call(s32[1]{0:T(128)} %bitcast.info, bf16[768,512]{1,0:T(8,128)(2,1)} %get-tuple-element.103.mine, bf16[768,512]{1,0:T(8,128)(2,1)} %copy-done.1, bf16[256,512]{1,0:T(8,128)(2,1)} %copy-done.4, bf16[256,512]{1,0:T(8,128)(2,1)} %copy-done.5), custom_call_target="tpu_custom_call" | custom-call | tf_op jit(solution)/shard_map/cross_final/pallas_call | solution.py:83
  92.1 2.7 %collective-permute-done.17.dq_theirs = bf16[512,512]{1,0:T(8,128)(2,1)S(1)} collective-permute-done((bf16[512,512]{1,0:T(8,128)(2,1)}, bf16[512,512]{1,0:T(8,128)(2,1)S(1)}, u32[]{:S(2)}, u32[]{:S(2)}) %collective-permute-start.17) | collective-permute-done | bytes 524320 | tf_op jit(solution)/shard_map/ppermute | solution.py:38
  96.5 2.7 %self_final.1 = (bf16[256,1024]{1,0:T(8,128)(2,1)}, bf16[256,1024]{1,0:T(8,128)(2,1)}, bf16[256,1024]{1,0:T(8,128)(2,1)}) custom-call(s32[1]{0:T(128)} %bitcast.info, bf16[768,512]{1,0:T(8,128)(2,1)} %get-tuple-element.100.mine, bf16[768,512]{1,0:T(8,128)(2,1)} %copy-done.2, bf16[512,512]{1,0:T(8,128)(2,1)} %collective-permute-done.14.dq_mine, ...), custom_call_target="tpu_custom_call" | custom-call | tf_op jit(solution)/shard_map/self_final/pallas_call | solution.py:83
  (57 shorter events, 11.9 us)
Async XLA Ops:
  3.4 22.1 %collective-permute-start.3 = (bf16[528,512]{1,0:T(8,128)(2,1)}, bf16[528,512]{1,0:T(8,128)(2,1)S(1)}, u32[]{:S(2)}, u32[]{:S(2)}) collective-permute-start(bf16[528,512]{1,0:T(8,128)(2,1)} %get-tuple-element.69), channel_id=1, source_target_pairs={{0,15},{1,2},{2,1},{3,4},{4,3},{5,6},{6,5},{7,8},{8,7},{9,10},{10,... | collective-permute-start | bytes 1622024 | tf_op jit(solution)/shard_map/ppermute | solution.py:38
  6.1 25.1 %collective-permute-start.2 = (bf16[528,512]{1,0:T(8,128)(2,1)}, bf16[528,512]{1,0:T(8,128)(2,1)}, u32[]{:S(2)}, u32[]{:S(2)}) collective-permute-start(bf16[528,512]{1,0:T(8,128)(2,1)} %get-tuple-element.62.refs_0_), channel_id=1, source_target_pairs={{0,14},{1,3},{2,0},{3,5},{4,2},{5,7},{6,4},{7,9},{8,6},{9,11},{10,... | collective-permute-start | bytes 1622024 | tf_op jit(solution)/shard_map/ppermute | solution.py:38
  7.3 8.3 %collective-permute-start = (bf16[1040,512]{1,0:T(8,128)(2,1)}, bf16[1040,512]{1,0:T(8,128)(2,1)}, u32[]{:S(2)}, u32[]{:S(2)}) collective-permute-start(bf16[1040,512]{1,0:T(8,128)(2,1)} %get-tuple-element.60), channel_id=1, source_target_pairs={{0,1},{1,0},{2,3},{3,2},{4,5},{5,4},{6,7},{7,6},{8,9},{9,8},{10,11... | collective-permute-start | bytes 3194888 | tf_op jit(solution)/shard_map/ppermute | solution.py:38
  12.2 9.0 %collective-permute-start.1 = (bf16[1024,512]{1,0:T(8,128)(2,1)}, bf16[1024,512]{1,0:T(8,128)(2,1)}, u32[]{:S(2)}, u32[]{:S(2)}) collective-permute-start(bf16[1024,512]{1,0:T(8,128)(2,1)} %get-tuple-element.67), channel_id=1, source_target_pairs={{0,1},{1,0},{2,3},{3,2},{4,5},{5,4},{6,7},{7,6},{8,9},{9,8},{10,11... | collective-permute-start | bytes 3145736 | tf_op jit(solution)/shard_map/ppermute | solution.py:38
  19.6 11.5 %collective-permute-start.5 = (f32[4,8,256]{2,1,0:T(8,128)}, f32[4,8,256]{2,1,0:T(8,128)S(1)}, u32[]{:S(2)}, u32[]{:S(2)}) collective-permute-start(f32[4,8,256]{2,1,0:T(8,128)} %get-tuple-element.70), channel_id=1, source_target_pairs={{0,2},{1,15},{2,4},{3,1},{4,6},{5,3},{6,8},{7,5},{8,10},{9,7},{10,... | collective-permute-start | bytes 98312 | tf_op jit(solution)/shard_map/ppermute | solution.py:38
  20.8 10.7 %collective-permute-start.4 = (f32[4,8,256]{2,1,0:T(8,128)}, f32[4,8,256]{2,1,0:T(8,128)S(1)}, u32[]{:S(2)}, u32[]{:S(2)}) collective-permute-start(f32[4,8,256]{2,1,0:T(8,128)} %get-tuple-element.64), channel_id=1, source_target_pairs={{0,14},{1,3},{2,0},{3,5},{4,2},{5,7},{6,4},{7,9},{8,6},{9,11},{10,... | collective-permute-start | bytes 98312 | tf_op jit(solution)/shard_map/ppermute | solution.py:38
  25.5 8.5 %copy-start = (bf16[528,512]{1,0:T(8,128)(2,1)}, bf16[528,512]{1,0:T(8,128)(2,1)S(1)}, u32[]{:S(2)}) copy-start(bf16[528,512]{1,0:T(8,128)(2,1)S(1)} %collective-permute-done.3.refs_1_.refs_4_.refs_5_) | copy-start | bytes 1622020
  31.1 3.0 %copy-start.6 = (f32[4,8,256]{2,1,0:T(8,128)}, f32[4,8,256]{2,1,0:T(8,128)S(1)}, u32[]{:S(2)}) copy-start(f32[4,8,256]{2,1,0:T(8,128)S(1)} %collective-permute-done.5.refs_10_) | copy-start | bytes 98308
  31.5 2.6 %copy-start.7 = (f32[4,8,256]{2,1,0:T(8,128)}, f32[4,8,256]{2,1,0:T(8,128)S(1)}, u32[]{:S(2)}) copy-start(f32[4,8,256]{2,1,0:T(8,128)S(1)} %collective-permute-done.4.refs_9_) | copy-start | bytes 98308
  31.5 17.5 %collective-permute-start.8 = (bf16[512,512]{1,0:T(8,128)(2,1)}, bf16[512,512]{1,0:T(8,128)(2,1)}, u32[]{:S(2)}, u32[]{:S(2)}) collective-permute-start(bf16[512,512]{1,0:T(8,128)(2,1)} %get-tuple-element.80), channel_id=1, source_target_pairs={{2,0},{3,1},{4,2},{5,3},{6,4},{7,5},{8,6},{9,7},{10,8},{11,9},{12,... | collective-permute-start | bytes 1572872 | tf_op jit(solution)/shard_map/ppermute | solution.py:38
  32.8 16.2 %collective-permute-start.9 = (f32[4,8,512]{2,1,0:T(8,128)}, f32[4,8,512]{2,1,0:T(8,128)S(1)}, u32[]{:S(2)}, u32[]{:S(2)}) collective-permute-start(f32[4,8,512]{2,1,0:T(8,128)} %self_stats.1.refs_10_), channel_id=1, source_target_pairs={{2,0},{3,1},{4,2},{5,3},{6,4},{7,5},{8,6},{9,7},{10,8},{11,9},{12,... | collective-permute-start | bytes 196616 | tf_op jit(solution)/shard_map/ppermute | solution.py:38
  40.0 8.9 %collective-permute-start.6 = (f32[4,8,256]{2,1,0:T(8,128)}, f32[4,8,256]{2,1,0:T(8,128)S(1)}, u32[]{:S(2)}, u32[]{:S(2)}) collective-permute-start(f32[4,8,256]{2,1,0:T(8,128)} %get-tuple-element.75), channel_id=1, source_target_pairs={{0,2},{1,15},{2,4},{3,1},{4,6},{5,3},{6,8},{7,5},{8,10},{9,7},{10,... | collective-permute-start | bytes 98312 | tf_op jit(solution)/shard_map/ppermute | solution.py:38
  47.5 5.8 %collective-permute-start.7 = (f32[4,8,256]{2,1,0:T(8,128)}, f32[4,8,256]{2,1,0:T(8,128)S(1)}, u32[]{:S(2)}, u32[]{:S(2)}) collective-permute-start(f32[4,8,256]{2,1,0:T(8,128)} %get-tuple-element.76), channel_id=1, source_target_pairs={{0,14},{1,3},{2,0},{3,5},{4,2},{5,7},{6,4},{7,9},{8,6},{9,11},{10,... | collective-permute-start | bytes 98312 | tf_op jit(solution)/shard_map/ppermute | solution.py:38
  47.5 17.4 %copy-start.9 = (bf16[256,512]{1,0:T(8,128)(2,1)S(1)}, bf16[256,512]{1,0:T(8,128)(2,1)}, u32[]{:S(2)}) copy-start(bf16[256,512]{1,0:T(8,128)(2,1)} %get-tuple-element.95) | copy-start | bytes 786436
  47.5 16.6 %collective-permute-start.10 = (bf16[512,512]{1,0:T(8,128)(2,1)}, bf16[512,512]{1,0:T(8,128)(2,1)S(1)}, u32[]{:S(2)}, u32[]{:S(2)}) collective-permute-start(bf16[512,512]{1,0:T(8,128)(2,1)} %get-tuple-element.86), channel_id=1, source_target_pairs={{2,1},{3,0},{4,3},{5,2},{6,5},{7,4},{8,7},{9,6},{10,9},{11,8},{12,... | collective-permute-start | bytes 1572872 | tf_op jit(solution)/shard_map/ppermute | solution.py:38
  48.9 11.3 %copy-start.10 = (f32[4,8,512]{2,1,0:T(8,128)}, f32[4,8,512]{2,1,0:T(8,128)S(1)}, u32[]{:S(2)}) copy-start(f32[4,8,512]{2,1,0:T(8,128)S(1)} %collective-permute-done.9.refs_9_) | copy-start | bytes 196612
  49.0 4.3 %copy-start.12 = (f32[4,8,256]{2,1,0:T(8,128)}, f32[4,8,256]{2,1,0:T(8,128)S(1)}, u32[]{:S(2)}) copy-start(f32[4,8,256]{2,1,0:T(8,128)S(1)} %collective-permute-done.6.refs_9_) | copy-start | bytes 98308
  64.9 14.9 %collective-permute-start.11 = (bf16[256,512]{1,0:T(8,128)(2,1)}, bf16[256,512]{1,0:T(8,128)(2,1)S(1)}, u32[]{:S(2)}, u32[]{:S(2)}) collective-permute-start(bf16[256,512]{1,0:T(8,128)(2,1)} %get-tuple-element.94), channel_id=1, source_target_pairs={{0,2},{1,15},{2,4},{3,1},{4,6},{5,3},{6,8},{7,5},{8,10},{9,7},{10,... | collective-permute-start | bytes 786440 | tf_op jit(solution)/shard_map/ppermute | solution.py:38
  64.9 14.9 %collective-permute-start.12 = (bf16[256,512]{1,0:T(8,128)(2,1)S(1)}, bf16[256,512]{1,0:T(8,128)(2,1)S(1)}, u32[]{:S(2)}, u32[]{:S(2)}) collective-permute-start(bf16[256,512]{1,0:T(8,128)(2,1)S(1)} %copy-done.9), channel_id=1, source_target_pairs={{0,15},{1,2},{2,1},{3,4},{4,3},{5,6},{6,5},{7,8},{8,7},{9,10},{10,... | collective-permute-start | bytes 786440 | tf_op jit(solution)/shard_map/ppermute | solution.py:38
  72.7 7.1 %collective-permute-start.13 = (f32[4,8,512]{2,1,0:T(8,128)}, f32[4,8,512]{2,1,0:T(8,128)S(1)}, u32[]{:S(2)}, u32[]{:S(2)}) collective-permute-start(f32[4,8,512]{2,1,0:T(8,128)} %get-tuple-element.96), channel_id=1, source_target_pairs={{0,2},{1,3},{2,4},{3,5},{4,6},{5,7},{6,8},{7,9},{8,10},{9,11},{10,... | collective-permute-start | bytes 196616 | tf_op jit(solution)/shard_map/ppermute | solution.py:38
  76.2 15.4 %collective-permute-start.14 = (bf16[512,512]{1,0:T(8,128)(2,1)}, bf16[512,512]{1,0:T(8,128)(2,1)}, u32[]{:S(2)}, u32[]{:S(2)}) collective-permute-start(bf16[512,512]{1,0:T(8,128)(2,1)} %get-tuple-element.102), channel_id=1, source_target_pairs={{0,2},{1,3},{2,4},{3,5},{4,6},{5,7},{6,8},{7,9},{8,10},{9,11},{10,... | collective-permute-start | bytes 1572872 | tf_op jit(solution)/shard_map/ppermute | solution.py:38
  80.6 7.3 %collective-permute-start.15 = (bf16[768,512]{1,0:T(8,128)(2,1)}, bf16[768,512]{1,0:T(8,128)(2,1)S(1)}, u32[]{:S(2)}, u32[]{:S(2)}) collective-permute-start(bf16[768,512]{1,0:T(8,128)(2,1)} %get-tuple-element.104), channel_id=1, source_target_pairs={{0,1},{1,0},{2,3},{3,2},{4,5},{5,4},{6,7},{7,6},{8,9},{9,8},{10,11... | collective-permute-start | bytes 2359304 | tf_op jit(solution)/shard_map/ppermute | solution.py:38
  91.6 3.3 %collective-permute-start.16 = (bf16[768,512]{1,0:T(8,128)(2,1)}, bf16[768,512]{1,0:T(8,128)(2,1)S(1)}, u32[]{:S(2)}, u32[]{:S(2)}) collective-permute-start(bf16[768,512]{1,0:T(8,128)(2,1)} %get-tuple-element.108), channel_id=1, source_target_pairs={{0,1},{1,0},{2,3},{3,2},{4,5},{5,4},{6,7},{7,6},{8,9},{9,8},{10,11... | collective-permute-start | bytes 2359304 | tf_op jit(solution)/shard_map/ppermute | solution.py:38
  91.6 3.2 %collective-permute-start.17 = (bf16[512,512]{1,0:T(8,128)(2,1)}, bf16[512,512]{1,0:T(8,128)(2,1)S(1)}, u32[]{:S(2)}, u32[]{:S(2)}) collective-permute-start(bf16[512,512]{1,0:T(8,128)(2,1)} %collective-permute-done.14.dq_mine), channel_id=1, source_target_pairs={{0,1},{1,0},{2,3},{3,2},{4,5},{5,4},{6,7},{7,6},{8,9},{9,8},{10,11... | collective-permute-start | bytes 1572872 | tf_op jit(solution)/shard_map/ppermute | solution.py:38
  (8 other events, 7.5 us)

commit v9 on v8

--- a/solution.py
+++ b/solution.py
@@ -90,9 +90,9 @@
             out_specs=out_specs,
         ),
         out_shape=[jax.ShapeDtypeStruct(shape, dtype) for shape, dtype in outs],
-        compiler_params=pltpu.CompilerParams(vmem_limit_bytes=63 << 20),
+        compiler_params=pltpu.CompilerParams(vmem_limit_bytes=64 << 20),
         cost_estimate=pl.CostEstimate(flops=flops, transcendentals=0, bytes_accessed=0),
-    )(info, *[pltpu.with_memory_space_constraint(x, pltpu.HBM) for x in inputs])
+    )(info, *inputs)
 
 
 def head_of(ref, j):
@@ -462,10 +462,12 @@
         [stat_spec(2 * ROWS)], [stat(2 * ROWS)], flops=0,
     )
     t_self = send(s_own, lambda d: d - 2, False)
-    s_mine, x_same, x_cross, t_same, t_cross, s_own = lax.optimization_barrier(
-        (s_mine, x_same, x_cross, t_same, t_cross, s_own)
-    )
+    s_mine, s_own = lax.optimization_barrier((s_mine, s_own))
     s_same = send(s_mine, lambda d: d - 2, False)
+    s_other, x_same, x_cross, t_same, t_cross, s_own = lax.optimization_barrier(
+        (s_other, x_same, x_cross, t_same, t_cross, s_own)
+    )
+    s_cross = send(s_other, lambda d: (d - 2) ^ 1, False)
 
     kv_out = spec(4 * ROWS)
     kv_shape = ((4 * ROWS, WIDE), BF16)
@@ -480,16 +482,13 @@
     )
     f_own = send(x_fin_same, inward, True)
     f_partner = send(x_fin_cross, outward, True)
-    s_other, x_kv = lax.optimization_barrier((s_other, x_kv))
-    s_cross = send(s_other, lambda d: (d - 2) ^ 1, False)
-    x_kv, s_same, t_self = lax.optimization_barrier((x_kv, s_same, t_self))
     half_out = spec(3 * ROWS)
     half_shape = ((3 * ROWS, WIDE), BF16)
     x_keep, x_give = call(
         per_head(cross_local_kernel), "cross_local", info,
         cross_specs + [stat_spec(ROWS), stat_spec(ROWS), spec(4 * ROWS)],
         cross_args + (f_own, f_partner, x_kv),
-        [half_out] * 2, [half_shape] * 2, flops=LONG,
+        [half_out] * 2, [half_shape] * 2, flops=0,
     )
 
     xd_same, xd_cross, s_cross, x_keep = lax.optimization_barrier(

time: 99.9 us -> 107 us (1.071)
  starting transfers between devices: 29.1 us -> 35.7 us
  waiting for transfers between devices: 17.1 us -> 22.6 us
  local copies, waits for them, and re-layouts: 5.72 us -> 0.91 us
    ppermute x18, starting transfers between devices: 29.1 us -> 35.7 us  [send(): return lax.ppermute(value, 'ctx', pairs)]
    ppermute x18, waiting for transfers between devices: 17.1 us -> 22.6 us  [send(): return lax.ppermute(value, 'ctx', pairs)]
    unnamed x28 -> x0, local copies, waits for them, and re-layouts: 4.8 us -> none
  transfers between devices with their start and end apart: 18 -> 18, of which waited for: 6 -> 4; matrix products, arithmetic and copies ran while one was open for 3% -> 3% of each run, Pallas kernels for 39% -> 36%
where the time goes in v9:
time: 107 us
  Pallas kernels  44.1 us (41%)
  starting transfers between devices  35.7 us (33%)
  waiting for transfers between devices  22.6 us (21%)
  other arithmetic  2.41 us (2%)
    pallas_call x10, Pallas kernels, call(): pl.pallas_call(kernel, name=name, grid_spec=pltpu.PrefetchScalarGridSpec(...  44.1 us
    ppermute x18, starting transfers between devices, send(): return lax.ppermute(value, 'ctx', pairs)  35.7 us
    ppermute x18, waiting for transfers between devices, send(): return lax.ppermute(value, 'ctx', pairs)  22.6 us
  transfers between devices with their start and end apart: 18, of which 4 were waited for; matrix products, arithmetic and copies ran while one was open for 3% of the time, Pallas kernels for 36%

profile of v9, /device:TPU:1, one launch (start us, length us, event | category | flops | bytes accessed | tf_op | source)
XLA Modules:
  0.0 106.5 jit_solution(4113397312399404385)
XLA Ops:
  0.6 2.8 %pack_cross.1 = (bf16[1040,512]{1,0:T(8,128)(2,1)}, bf16[528,512]{1,0:T(8,128)(2,1)}, bf16[528,512]{1,0:T(8,128)(2,1)}) custom-call(s32[1]{0:T(128)} %bitcast.info, s32[2,4]{1,0:T(2,128)} %bitcast.8, bf16[256,1024]{1,0:T(8,128)(2,1)} %refs_2_.6, bf16[256,1024]{1,0:T(8,128)(2,1)} %refs_3_.6, bf16[256,1024]{1,0:T(8,128)(2,1)} %refs_2_.6, ...), custom_call_target="tpu_custom_call" | custom-call | tf_op jit(solution)/shard_map/pack_cross/pallas_call | solution.py:83
  3.5 2.6 %pack_self.1 = (bf16[1024,512]{1,0:T(8,128)(2,1)}, bf16[512,512]{1,0:T(8,128)(2,1)}, bf16[512,512]{1,0:T(8,128)(2,1)}) custom-call(s32[1]{0:T(128)} %bitcast.info, bf16[256,1024]{1,0:T(8,128)(2,1)} %refs_1_.3, bf16[256,1024]{1,0:T(8,128)(2,1)} %refs_2_.7, bf16[256,1024]{1,0:T(8,128)(2,1)} %refs_1_.3, bf16[256,1024]{1,0:T(8,128)(2,1)} %refs_2_.7, ...), custom_call_target="tpu_custom_call" | custom-call | tf_op jit(solution)/shard_map/pack_self/pallas_call | solution.py:83
  6.6 2.3 %collective-permute-start.2 = (bf16[528,512]{1,0:T(8,128)(2,1)}, bf16[528,512]{1,0:T(8,128)(2,1)}, u32[]{:S(2)}, u32[]{:S(2)}) collective-permute-start(bf16[528,512]{1,0:T(8,128)(2,1)} %get-tuple-element.59.refs_0_), channel_id=1, source_target_pairs={{0,14},{1,3},{2,0},{3,5},{4,2},{5,7},{6,4},{7,9},{8,6},{9,11},{10,... | collective-permute-start | bytes 1622024 | tf_op jit(solution)/shard_map/ppermute | solution.py:38
  12.5 4.0 %cross_stats.1 = (f32[4,8,256]{2,1,0:T(8,128)}, f32[4,8,256]{2,1,0:T(8,128)}) custom-call(s32[1]{0:T(128)} %bitcast.info, bf16[528,512]{1,0:T(8,128)(2,1)} %get-tuple-element.59.refs_0_, bf16[1040,512]{1,0:T(8,128)(2,1)} %collective-permute-done.refs_1_.refs_5_.refs_6_.refs_7_.refs_8_, bf16[256,1024]{1,0:T(8,128)(2,1)} %refs_2_.6, ...), custom_call_target="tpu_custom_call" | custom-call | tf_op jit(solution)/shard_map/cross_stats/pallas_call | solution.py:83
  16.5 2.6 %collective-permute-start.4 = (f32[4,8,256]{2,1,0:T(8,128)}, f32[4,8,256]{2,1,0:T(8,128)}, u32[]{:S(2)}, u32[]{:S(2)}) collective-permute-start(f32[4,8,256]{2,1,0:T(8,128)} %get-tuple-element.61), channel_id=1, source_target_pairs={{0,14},{1,3},{2,0},{3,5},{4,2},{5,7},{6,4},{7,9},{8,6},{9,11},{10,... | collective-permute-start | bytes 98312 | tf_op jit(solution)/shard_map/ppermute | solution.py:38
  19.2 5.0 %collective-permute-start.5 = (f32[4,8,256]{2,1,0:T(8,128)}, f32[4,8,256]{2,1,0:T(8,128)}, u32[]{:S(2)}, u32[]{:S(2)}) collective-permute-start(f32[4,8,256]{2,1,0:T(8,128)} %get-tuple-element.67), channel_id=1, source_target_pairs={{0,2},{1,15},{2,4},{3,1},{4,6},{5,3},{6,8},{7,5},{8,10},{9,7},{10,... | collective-permute-start | bytes 98312 | tf_op jit(solution)/shard_map/ppermute | solution.py:38
  24.1 4.1 %self_stats.1.refs_10_ = f32[4,8,512]{2,1,0:T(8,128)} custom-call(s32[1]{0:T(128)} %bitcast.info, f32[512,512]{1,0:T(8,128)} %and_select_fusion.1.refs_0_, bf16[256,1024]{1,0:T(8,128)(2,1)} %refs_1_.3, bf16[256,1024]{1,0:T(8,128)(2,1)} %refs_2_.7, bf16[256,1024]{1,0:T(8,128)(2,1)} %refs_3_.7, bf16[256,1024]{1,0:T(8,128)(2,1)} %refs_4_.3, ...), custom_call_target="tpu_custom_call" | custom-call | tf_op jit(solution)/shard_map/self_stats/pallas_call | solution.py:83
  28.3 6.7 %collective-permute-done.3.refs_1_.refs_4_.refs_5_ = bf16[528,512]{1,0:T(8,128)(2,1)} collective-permute-done((bf16[528,512]{1,0:T(8,128)(2,1)}, bf16[528,512]{1,0:T(8,128)(2,1)}, u32[]{:S(2)}, u32[]{:S(2)}) %collective-permute-start.3) | collective-permute-done | bytes 540704 | tf_op jit(solution)/shard_map/ppermute | solution.py:38
  35.0 1.3 %collective-permute-start.8 = (bf16[512,512]{1,0:T(8,128)(2,1)}, bf16[512,512]{1,0:T(8,128)(2,1)}, u32[]{:S(2)}, u32[]{:S(2)}) collective-permute-start(bf16[512,512]{1,0:T(8,128)(2,1)} %get-tuple-element.81), channel_id=1, source_target_pairs={{2,1},{3,0},{4,3},{5,2},{6,5},{7,4},{8,7},{9,6},{10,9},{11,8},{12,... | collective-permute-start | bytes 1572872 | tf_op jit(solution)/shard_map/ppermute | solution.py:38
  36.3 1.3 %collective-permute-start.9 = (bf16[512,512]{1,0:T(8,128)(2,1)}, bf16[512,512]{1,0:T(8,128)(2,1)}, u32[]{:S(2)}, u32[]{:S(2)}) collective-permute-start(bf16[512,512]{1,0:T(8,128)(2,1)} %get-tuple-element.85), channel_id=1, source_target_pairs={{2,0},{3,1},{4,2},{5,3},{6,4},{7,5},{8,6},{9,7},{10,8},{11,9},{12,... | collective-permute-start | bytes 1572872 | tf_op jit(solution)/shard_map/ppermute | solution.py:38
  37.6 1.3 %collective-permute-start.10 = (f32[4,8,512]{2,1,0:T(8,128)}, f32[4,8,512]{2,1,0:T(8,128)}, u32[]{:S(2)}, u32[]{:S(2)}) collective-permute-start(f32[4,8,512]{2,1,0:T(8,128)} %self_stats.1.refs_10_), channel_id=1, source_target_pairs={{2,0},{3,1},{4,2},{5,3},{6,4},{7,5},{8,6},{9,7},{10,8},{11,9},{12,... | collective-permute-start | bytes 196616 | tf_op jit(solution)/shard_map/ppermute | solution.py:38
  38.9 5.9 %cross_remote.1 = (bf16[256,512]{1,0:T(8,128)(2,1)}, bf16[256,512]{1,0:T(8,128)(2,1)}, bf16[1024,512]{1,0:T(8,128)(2,1)}, f32[4,8,256]{2,1,0:T(8,128)}, f32[4,8,256]{2,1,0:T(8,128)}) custom-call(s32[1]{0:T(128)} %bitcast.info, bf16[528,512]{1,0:T(8,128)(2,1)} %collective-permute-done.2.refs_0_.refs_2_.refs_3_, ...), custom_call_target="tpu_custom_call" | custom-call | tf_op jit(solution)/shard_map/cross_remote/pallas_call | solution.py:83
  44.8 9.8 %collective-permute-start.6 = (f32[4,8,256]{2,1,0:T(8,128)}, f32[4,8,256]{2,1,0:T(8,128)}, u32[]{:S(2)}, u32[]{:S(2)}) collective-permute-start(f32[4,8,256]{2,1,0:T(8,128)} %get-tuple-element.74), channel_id=1, source_target_pairs={{0,2},{1,15},{2,4},{3,1},{4,6},{5,3},{6,8},{7,5},{8,10},{9,7},{10,... | collective-permute-start | bytes 98312 | tf_op jit(solution)/shard_map/ppermute | solution.py:38
  54.6 10.9 %collective-permute-done.6.refs_9_ = f32[4,8,256]{2,1,0:T(8,128)} collective-permute-done((f32[4,8,256]{2,1,0:T(8,128)}, f32[4,8,256]{2,1,0:T(8,128)}, u32[]{:S(2)}, u32[]{:S(2)}) %collective-permute-start.6) | collective-permute-done | bytes 32800 | tf_op jit(solution)/shard_map/ppermute | solution.py:38
  65.5 6.4 %cross_local.1 = (bf16[768,512]{1,0:T(8,128)(2,1)}, bf16[768,512]{1,0:T(8,128)(2,1)}) custom-call(s32[1]{0:T(128)} %bitcast.info, bf16[528,512]{1,0:T(8,128)(2,1)} %get-tuple-element.59.refs_0_, bf16[1040,512]{1,0:T(8,128)(2,1)} %collective-permute-done.refs_1_.refs_5_.refs_6_.refs_7_.refs_8_, bf16[256,1024]{1,0:T(8,128)(2,1)} %refs_2_.6, ...), custom_call_target="tpu_custom_call" | custom-call | tf_op jit(solution)/shard_map/cross_local/pallas_call | solution.py:83
  71.9 3.1 %collective-permute-start.11 = (bf16[256,512]{1,0:T(8,128)(2,1)}, bf16[256,512]{1,0:T(8,128)(2,1)}, u32[]{:S(2)}, u32[]{:S(2)}) collective-permute-start(bf16[256,512]{1,0:T(8,128)(2,1)} %get-tuple-element.88), channel_id=1, source_target_pairs={{0,2},{1,15},{2,4},{3,1},{4,6},{5,3},{6,8},{7,5},{8,10},{9,7},{10,... | collective-permute-start | bytes 786440 | tf_op jit(solution)/shard_map/ppermute | solution.py:38
  75.5 6.7 %self_remote.1 = (bf16[512,512]{1,0:T(8,128)(2,1)}, bf16[1024,512]{1,0:T(8,128)(2,1)}, f32[4,8,512]{2,1,0:T(8,128)}) custom-call(s32[1]{0:T(128)} %bitcast.info, f32[512,512]{1,0:T(8,128)} %and_select_fusion.refs_0_, bf16[512,512]{1,0:T(8,128)(2,1)} %collective-permute-done.9.refs_1_.refs_2_, bf16[512,512]{1,0:T(8,128)(2,1)} %collective-permute-done.9.refs_1_.refs_2_, ...), custom_call_target="tpu_custom_call" | custom-call | flops 12000000000 | tf_op jit(solution)/shard_map/self_remote/pallas_call | solution.py:83
  82.2 4.0 %collective-permute-start.13 = (f32[4,8,512]{2,1,0:T(8,128)}, f32[4,8,512]{2,1,0:T(8,128)}, u32[]{:S(2)}, u32[]{:S(2)}) collective-permute-start(f32[4,8,512]{2,1,0:T(8,128)} %get-tuple-element.90), channel_id=1, source_target_pairs={{0,2},{1,3},{2,4},{3,5},{4,6},{5,7},{6,8},{7,9},{8,10},{9,11},{10,... | collective-permute-start | bytes 196616 | tf_op jit(solution)/shard_map/ppermute | solution.py:38
  86.2 3.1 %collective-permute-start.14 = (bf16[512,512]{1,0:T(8,128)(2,1)}, bf16[512,512]{1,0:T(8,128)(2,1)}, u32[]{:S(2)}, u32[]{:S(2)}) collective-permute-start(bf16[512,512]{1,0:T(8,128)(2,1)} %get-tuple-element.96), channel_id=1, source_target_pairs={{0,2},{1,3},{2,4},{3,5},{4,6},{5,7},{6,8},{7,9},{8,10},{9,11},{10,... | collective-permute-start | bytes 1572872 | tf_op jit(solution)/shard_map/ppermute | solution.py:38
  89.4 6.1 %self_local.1 = (bf16[768,512]{1,0:T(8,128)(2,1)}, bf16[768,512]{1,0:T(8,128)(2,1)}) custom-call(s32[1]{0:T(128)} %bitcast.info, f32[512,512]{1,0:T(8,128)} %and_select_fusion.1.refs_0_, bf16[256,1024]{1,0:T(8,128)(2,1)} %refs_1_.3, bf16[256,1024]{1,0:T(8,128)(2,1)} %refs_2_.7, bf16[256,1024]{1,0:T(8,128)(2,1)} %refs_3_.7, bf16[256,1024]{1,0:T(8,128)(2,1)} %refs_4_.3, ...), custom_call_target="tpu_custom_call" | custom-call | flops 12000000000 | tf_op jit(solution)/shard_map/self_local/pallas_call | solution.py:83
  95.5 2.8 %cross_final.1 = (bf16[256,1024]{1,0:T(8,128)(2,1)}, bf16[2,256,1024]{2,1,0:T(8,128)(2,1)}) custom-call(s32[1]{0:T(128)} %bitcast.info, bf16[768,512]{1,0:T(8,128)(2,1)} %get-tuple-element.97.mine, bf16[768,512]{1,0:T(8,128)(2,1)} %collective-permute-done.15.theirs, bf16[256,512]{1,0:T(8,128)(2,1)} %collective-permute-done.11.dq_mine, ...), custom_call_target="tpu_custom_call" | custom-call | tf_op jit(solution)/shard_map/cross_final/pallas_call | solution.py:83
  98.3 2.1 %collective-permute-done.14.dq_mine = bf16[512,512]{1,0:T(8,128)(2,1)} collective-permute-done((bf16[512,512]{1,0:T(8,128)(2,1)}, bf16[512,512]{1,0:T(8,128)(2,1)}, u32[]{:S(2)}, u32[]{:S(2)}) %collective-permute-start.14) | collective-permute-done | bytes 524320 | tf_op jit(solution)/shard_map/ppermute | solution.py:38
  100.9 2.9 %collective-permute-done.17.dq_theirs = bf16[512,512]{1,0:T(8,128)(2,1)} collective-permute-done((bf16[512,512]{1,0:T(8,128)(2,1)}, bf16[512,512]{1,0:T(8,128)(2,1)}, u32[]{:S(2)}, u32[]{:S(2)}) %collective-permute-start.17) | collective-permute-done | bytes 524320 | tf_op jit(solution)/shard_map/ppermute | solution.py:38
  103.8 2.7 %self_final.1 = (bf16[256,1024]{1,0:T(8,128)(2,1)}, bf16[256,1024]{1,0:T(8,128)(2,1)}, bf16[256,1024]{1,0:T(8,128)(2,1)}) custom-call(s32[1]{0:T(128)} %bitcast.info, bf16[768,512]{1,0:T(8,128)(2,1)} %get-tuple-element.94.mine, bf16[768,512]{1,0:T(8,128)(2,1)} %collective-permute-done.16.theirs, bf16[512,512]{1,0:T(8,128)(2,1)} %collective-permute-done.14.dq_mine, ...), custom_call_target="tpu_custom_call" | custom-call | tf_op jit(solution)/shard_map/self_final/pallas_call | solution.py:83
  (29 shorter events, 5.3 us)
Async XLA Ops:
  3.4 9.1 %collective-permute-start = (bf16[1040,512]{1,0:T(8,128)(2,1)}, bf16[1040,512]{1,0:T(8,128)(2,1)}, u32[]{:S(2)}, u32[]{:S(2)}) collective-permute-start(bf16[1040,512]{1,0:T(8,128)(2,1)} %get-tuple-element.57), channel_id=1, source_target_pairs={{0,1},{1,0},{2,3},{3,2},{4,5},{5,4},{6,7},{7,6},{8,9},{9,8},{10,11... | collective-permute-start | bytes 3194888 | tf_op jit(solution)/shard_map/ppermute | solution.py:38
  6.1 18.0 %collective-permute-start.1 = (bf16[1024,512]{1,0:T(8,128)(2,1)}, bf16[1024,512]{1,0:T(8,128)(2,1)}, u32[]{:S(2)}, u32[]{:S(2)}) collective-permute-start(bf16[1024,512]{1,0:T(8,128)(2,1)} %get-tuple-element.64), channel_id=1, source_target_pairs={{0,1},{1,0},{2,3},{3,2},{4,5},{5,4},{6,7},{7,6},{8,9},{9,8},{10,11... | collective-permute-start | bytes 3145736 | tf_op jit(solution)/shard_map/ppermute | solution.py:38
  6.6 21.7 %collective-permute-start.2 = (bf16[528,512]{1,0:T(8,128)(2,1)}, bf16[528,512]{1,0:T(8,128)(2,1)}, u32[]{:S(2)}, u32[]{:S(2)}) collective-permute-start(bf16[528,512]{1,0:T(8,128)(2,1)} %get-tuple-element.59.refs_0_), channel_id=1, source_target_pairs={{0,14},{1,3},{2,0},{3,5},{4,2},{5,7},{6,4},{7,9},{8,6},{9,11},{10,... | collective-permute-start | bytes 1622024 | tf_op jit(solution)/shard_map/ppermute | solution.py:38
  8.9 26.1 %collective-permute-start.3 = (bf16[528,512]{1,0:T(8,128)(2,1)}, bf16[528,512]{1,0:T(8,128)(2,1)}, u32[]{:S(2)}, u32[]{:S(2)}) collective-permute-start(bf16[528,512]{1,0:T(8,128)(2,1)} %get-tuple-element.66), channel_id=1, source_target_pairs={{0,15},{1,2},{2,1},{3,4},{4,3},{5,6},{6,5},{7,8},{8,7},{9,10},{10,... | collective-permute-start | bytes 1622024 | tf_op jit(solution)/shard_map/ppermute | solution.py:38
  16.5 18.4 %collective-permute-start.4 = (f32[4,8,256]{2,1,0:T(8,128)}, f32[4,8,256]{2,1,0:T(8,128)}, u32[]{:S(2)}, u32[]{:S(2)}) collective-permute-start(f32[4,8,256]{2,1,0:T(8,128)} %get-tuple-element.61), channel_id=1, source_target_pairs={{0,14},{1,3},{2,0},{3,5},{4,2},{5,7},{6,4},{7,9},{8,6},{9,11},{10,... | collective-permute-start | bytes 98312 | tf_op jit(solution)/shard_map/ppermute | solution.py:38
  19.2 15.8 %collective-permute-start.5 = (f32[4,8,256]{2,1,0:T(8,128)}, f32[4,8,256]{2,1,0:T(8,128)}, u32[]{:S(2)}, u32[]{:S(2)}) collective-permute-start(f32[4,8,256]{2,1,0:T(8,128)} %get-tuple-element.67), channel_id=1, source_target_pairs={{0,2},{1,15},{2,4},{3,1},{4,6},{5,3},{6,8},{7,5},{8,10},{9,7},{10,... | collective-permute-start | bytes 98312 | tf_op jit(solution)/shard_map/ppermute | solution.py:38
  35.0 36.9 %collective-permute-start.8 = (bf16[512,512]{1,0:T(8,128)(2,1)}, bf16[512,512]{1,0:T(8,128)(2,1)}, u32[]{:S(2)}, u32[]{:S(2)}) collective-permute-start(bf16[512,512]{1,0:T(8,128)(2,1)} %get-tuple-element.81), channel_id=1, source_target_pairs={{2,1},{3,0},{4,3},{5,2},{6,5},{7,4},{8,7},{9,6},{10,9},{11,8},{12,... | collective-permute-start | bytes 1572872 | tf_op jit(solution)/shard_map/ppermute | solution.py:38
  36.3 39.2 %collective-permute-start.9 = (bf16[512,512]{1,0:T(8,128)(2,1)}, bf16[512,512]{1,0:T(8,128)(2,1)}, u32[]{:S(2)}, u32[]{:S(2)}) collective-permute-start(bf16[512,512]{1,0:T(8,128)(2,1)} %get-tuple-element.85), channel_id=1, source_target_pairs={{2,0},{3,1},{4,2},{5,3},{6,4},{7,5},{8,6},{9,7},{10,8},{11,9},{12,... | collective-permute-start | bytes 1572872 | tf_op jit(solution)/shard_map/ppermute | solution.py:38
  37.6 37.9 %collective-permute-start.10 = (f32[4,8,512]{2,1,0:T(8,128)}, f32[4,8,512]{2,1,0:T(8,128)}, u32[]{:S(2)}, u32[]{:S(2)}) collective-permute-start(f32[4,8,512]{2,1,0:T(8,128)} %self_stats.1.refs_10_), channel_id=1, source_target_pairs={{2,0},{3,1},{4,2},{5,3},{6,4},{7,5},{8,6},{9,7},{10,8},{11,9},{12,... | collective-permute-start | bytes 196616 | tf_op jit(solution)/shard_map/ppermute | solution.py:38
  44.8 20.7 %collective-permute-start.6 = (f32[4,8,256]{2,1,0:T(8,128)}, f32[4,8,256]{2,1,0:T(8,128)}, u32[]{:S(2)}, u32[]{:S(2)}) collective-permute-start(f32[4,8,256]{2,1,0:T(8,128)} %get-tuple-element.74), channel_id=1, source_target_pairs={{0,2},{1,15},{2,4},{3,1},{4,6},{5,3},{6,8},{7,5},{8,10},{9,7},{10,... | collective-permute-start | bytes 98312 | tf_op jit(solution)/shard_map/ppermute | solution.py:38
  54.6 10.9 %collective-permute-start.7 = (f32[4,8,256]{2,1,0:T(8,128)}, f32[4,8,256]{2,1,0:T(8,128)}, u32[]{:S(2)}, u32[]{:S(2)}) collective-permute-start(f32[4,8,256]{2,1,0:T(8,128)} %get-tuple-element.75), channel_id=1, source_target_pairs={{0,14},{1,3},{2,0},{3,5},{4,2},{5,7},{6,4},{7,9},{8,6},{9,11},{10,... | collective-permute-start | bytes 98312 | tf_op jit(solution)/shard_map/ppermute | solution.py:38
  71.9 17.4 %collective-permute-start.11 = (bf16[256,512]{1,0:T(8,128)(2,1)}, bf16[256,512]{1,0:T(8,128)(2,1)}, u32[]{:S(2)}, u32[]{:S(2)}) collective-permute-start(bf16[256,512]{1,0:T(8,128)(2,1)} %get-tuple-element.88), channel_id=1, source_target_pairs={{0,2},{1,15},{2,4},{3,1},{4,6},{5,3},{6,8},{7,5},{8,10},{9,7},{10,... | collective-permute-start | bytes 786440 | tf_op jit(solution)/shard_map/ppermute | solution.py:38
  75.0 14.3 %collective-permute-start.12 = (bf16[256,512]{1,0:T(8,128)(2,1)}, bf16[256,512]{1,0:T(8,128)(2,1)}, u32[]{:S(2)}, u32[]{:S(2)}) collective-permute-start(bf16[256,512]{1,0:T(8,128)(2,1)} %get-tuple-element.89), channel_id=1, source_target_pairs={{0,15},{1,2},{2,1},{3,4},{4,3},{5,6},{6,5},{7,8},{8,7},{9,10},{10,... | collective-permute-start | bytes 786440 | tf_op jit(solution)/shard_map/ppermute | solution.py:38
  82.2 7.1 %collective-permute-start.13 = (f32[4,8,512]{2,1,0:T(8,128)}, f32[4,8,512]{2,1,0:T(8,128)}, u32[]{:S(2)}, u32[]{:S(2)}) collective-permute-start(f32[4,8,512]{2,1,0:T(8,128)} %get-tuple-element.90), channel_id=1, source_target_pairs={{0,2},{1,3},{2,4},{3,5},{4,6},{5,7},{6,8},{7,9},{8,10},{9,11},{10,... | collective-permute-start | bytes 196616 | tf_op jit(solution)/shard_map/ppermute | solution.py:38
  86.2 14.2 %collective-permute-start.14 = (bf16[512,512]{1,0:T(8,128)(2,1)}, bf16[512,512]{1,0:T(8,128)(2,1)}, u32[]{:S(2)}, u32[]{:S(2)}) collective-permute-start(bf16[512,512]{1,0:T(8,128)(2,1)} %get-tuple-element.96), channel_id=1, source_target_pairs={{0,2},{1,3},{2,4},{3,5},{4,6},{5,7},{6,8},{7,9},{8,10},{9,11},{10,... | collective-permute-start | bytes 1572872 | tf_op jit(solution)/shard_map/ppermute | solution.py:38
  89.3 6.2 %collective-permute-start.15 = (bf16[768,512]{1,0:T(8,128)(2,1)}, bf16[768,512]{1,0:T(8,128)(2,1)}, u32[]{:S(2)}, u32[]{:S(2)}) collective-permute-start(bf16[768,512]{1,0:T(8,128)(2,1)} %get-tuple-element.98), channel_id=1, source_target_pairs={{0,1},{1,0},{2,3},{3,2},{4,5},{5,4},{6,7},{7,6},{8,9},{9,8},{10,11... | collective-permute-start | bytes 2359304 | tf_op jit(solution)/shard_map/ppermute | solution.py:38
  100.4 3.4 %collective-permute-start.16 = (bf16[768,512]{1,0:T(8,128)(2,1)}, bf16[768,512]{1,0:T(8,128)(2,1)}, u32[]{:S(2)}, u32[]{:S(2)}) collective-permute-start(bf16[768,512]{1,0:T(8,128)(2,1)} %get-tuple-element.102), channel_id=1, source_target_pairs={{0,1},{1,0},{2,3},{3,2},{4,5},{5,4},{6,7},{7,6},{8,9},{9,8},{10,11... | collective-permute-start | bytes 2359304 | tf_op jit(solution)/shard_map/ppermute | solution.py:38
  100.7 3.1 %collective-permute-start.17 = (bf16[512,512]{1,0:T(8,128)(2,1)}, bf16[512,512]{1,0:T(8,128)(2,1)}, u32[]{:S(2)}, u32[]{:S(2)}) collective-permute-start(bf16[512,512]{1,0:T(8,128)(2,1)} %collective-permute-done.14.dq_mine), channel_id=1, source_target_pairs={{0,1},{1,0},{2,3},{3,2},{4,5},{5,4},{6,7},{7,6},{8,9},{9,8},{10,11... | collective-permute-start | bytes 1572872 | tf_op jit(solution)/shard_map/ppermute | solution.py:38

commit v10 on v8

--- a/solution.py
+++ b/solution.py
@@ -90,9 +90,9 @@
             out_specs=out_specs,
         ),
         out_shape=[jax.ShapeDtypeStruct(shape, dtype) for shape, dtype in outs],
-        compiler_params=pltpu.CompilerParams(vmem_limit_bytes=63 << 20),
+        compiler_params=pltpu.CompilerParams(vmem_limit_bytes=64 << 20),
         cost_estimate=pl.CostEstimate(flops=flops, transcendentals=0, bytes_accessed=0),
-    )(info, *[pltpu.with_memory_space_constraint(x, pltpu.HBM) for x in inputs])
+    )(info, *inputs)
 
 
 def head_of(ref, j):
@@ -461,7 +461,6 @@
         per_head(self_stats_kernel), "self_stats", info, self_specs, self_args,
         [stat_spec(2 * ROWS)], [stat(2 * ROWS)], flops=0,
     )
-    t_self = send(s_own, lambda d: d - 2, False)
     s_mine, x_same, x_cross, t_same, t_cross, s_own = lax.optimization_barrier(
         (s_mine, x_same, x_cross, t_same, t_cross, s_own)
     )
@@ -482,7 +481,9 @@
     f_partner = send(x_fin_cross, outward, True)
     s_other, x_kv = lax.optimization_barrier((s_other, x_kv))
     s_cross = send(s_other, lambda d: (d - 2) ^ 1, False)
-    x_kv, s_same, t_self = lax.optimization_barrier((x_kv, s_same, t_self))
+    s_own, f_own = lax.optimization_barrier((s_own, f_own))
+    t_self = send(s_own, lambda d: d - 2, False)
+    x_kv, s_same = lax.optimization_barrier((x_kv, s_same))
     half_out = spec(3 * ROWS)
     half_shape = ((3 * ROWS, WIDE), BF16)
     x_keep, x_give = call(

time: 99.9 us -> 107 us (1.071); the launches traced: 99.2 us -> 104 us
  waiting for transfers between devices: 17.1 us -> 23.7 us
  local copies, waits for them, and re-layouts: 5.72 us -> 0.92 us
  starting transfers between devices: 29.1 us -> 32.6 us
    ppermute x18, waiting for transfers between devices: 17.1 us -> 23.7 us  [send(): return lax.ppermute(value, 'ctx', pairs)]
    unnamed x28 -> x0, local copies, waits for them, and re-layouts: 4.8 us -> none
    ppermute x18, starting transfers between devices: 29.1 us -> 32.6 us  [send(): return lax.ppermute(value, 'ctx', pairs)]
  transfers between devices with their start and end apart: 18 -> 18, of which waited for: 6 -> 7; matrix products, arithmetic and copies ran while one was open for 3% -> 3% of each run, Pallas kernels for 39% -> 37%
where the time goes in v10:
time: 107 us; the launch traced here: 104 us
  Pallas kernels  44.1 us (41%)
  starting transfers between devices  32.6 us (30%)
  waiting for transfers between devices  23.7 us (22%)
  other arithmetic  2.4 us (2%)
    pallas_call x10, Pallas kernels, call(): pl.pallas_call(kernel, name=name, grid_spec=pltpu.PrefetchScalarGridSpec(...  44.1 us
    ppermute x18, starting transfers between devices, send(): return lax.ppermute(value, 'ctx', pairs)  32.6 us
    ppermute x18, waiting for transfers between devices, send(): return lax.ppermute(value, 'ctx', pairs)  23.7 us
  transfers between devices with their start and end apart: 18, of which 7 were waited for; matrix products, arithmetic and copies ran while one was open for 3% of the time, Pallas kernels for 37%

profile of v10, /device:TPU:1, one launch (start us, length us, event | category | flops | bytes accessed | tf_op | source)
XLA Modules:
  0.0 104.5 jit_solution(3509519431934271409)
XLA Ops:
  0.6 2.7 %pack_cross.1 = (bf16[1040,512]{1,0:T(8,128)(2,1)}, bf16[528,512]{1,0:T(8,128)(2,1)}, bf16[528,512]{1,0:T(8,128)(2,1)}) custom-call(s32[1]{0:T(128)} %bitcast.info, s32[2,4]{1,0:T(2,128)} %bitcast.8, bf16[256,1024]{1,0:T(8,128)(2,1)} %refs_2_.6, bf16[256,1024]{1,0:T(8,128)(2,1)} %refs_3_.6, bf16[256,1024]{1,0:T(8,128)(2,1)} %refs_2_.6, ...), custom_call_target="tpu_custom_call" | custom-call | tf_op jit(solution)/shard_map/pack_cross/pallas_call | solution.py:83
  3.4 2.6 %collective-permute-start.3 = (bf16[528,512]{1,0:T(8,128)(2,1)}, bf16[528,512]{1,0:T(8,128)(2,1)}, u32[]{:S(2)}, u32[]{:S(2)}) collective-permute-start(bf16[528,512]{1,0:T(8,128)(2,1)} %get-tuple-element.70), channel_id=1, source_target_pairs={{0,15},{1,2},{2,1},{3,4},{4,3},{5,6},{6,5},{7,8},{8,7},{9,10},{10,... | collective-permute-start | bytes 1622024 | tf_op jit(solution)/shard_map/ppermute | solution.py:38
  6.0 1.2 %collective-permute-start.2 = (bf16[528,512]{1,0:T(8,128)(2,1)}, bf16[528,512]{1,0:T(8,128)(2,1)}, u32[]{:S(2)}, u32[]{:S(2)}) collective-permute-start(bf16[528,512]{1,0:T(8,128)(2,1)} %get-tuple-element.63.refs_0_), channel_id=1, source_target_pairs={{0,14},{1,3},{2,0},{3,5},{4,2},{5,7},{6,4},{7,9},{8,6},{9,11},{10,... | collective-permute-start | bytes 1622024 | tf_op jit(solution)/shard_map/ppermute | solution.py:38
  7.2 2.3 %collective-permute-start = (bf16[1040,512]{1,0:T(8,128)(2,1)}, bf16[1040,512]{1,0:T(8,128)(2,1)}, u32[]{:S(2)}, u32[]{:S(2)}) collective-permute-start(bf16[1040,512]{1,0:T(8,128)(2,1)} %get-tuple-element.61), channel_id=1, source_target_pairs={{0,1},{1,0},{2,3},{3,2},{4,5},{5,4},{6,7},{7,6},{8,9},{9,8},{10,11... | collective-permute-start | bytes 3194888 | tf_op jit(solution)/shard_map/ppermute | solution.py:38
  9.5 2.6 %pack_self.1 = (bf16[1024,512]{1,0:T(8,128)(2,1)}, bf16[512,512]{1,0:T(8,128)(2,1)}, bf16[512,512]{1,0:T(8,128)(2,1)}) custom-call(s32[1]{0:T(128)} %bitcast.info, bf16[256,1024]{1,0:T(8,128)(2,1)} %refs_1_.3, bf16[256,1024]{1,0:T(8,128)(2,1)} %refs_2_.7, bf16[256,1024]{1,0:T(8,128)(2,1)} %refs_1_.3, bf16[256,1024]{1,0:T(8,128)(2,1)} %refs_2_.7, ...), custom_call_target="tpu_custom_call" | custom-call | tf_op jit(solution)/shard_map/pack_self/pallas_call | solution.py:83
  15.5 4.0 %cross_stats.1 = (f32[4,8,256]{2,1,0:T(8,128)}, f32[4,8,256]{2,1,0:T(8,128)}) custom-call(s32[1]{0:T(128)} %bitcast.info, bf16[528,512]{1,0:T(8,128)(2,1)} %get-tuple-element.63.refs_0_, bf16[1040,512]{1,0:T(8,128)(2,1)} %collective-permute-done.refs_1_.refs_5_.refs_6_.refs_7_.refs_8_, bf16[256,1024]{1,0:T(8,128)(2,1)} %refs_2_.6, ...), custom_call_target="tpu_custom_call" | custom-call | tf_op jit(solution)/shard_map/cross_stats/pallas_call | solution.py:83
  21.0 4.2 %self_stats.1.refs_10_ = f32[4,8,512]{2,1,0:T(8,128)} custom-call(s32[1]{0:T(128)} %bitcast.info, f32[512,512]{1,0:T(8,128)} %and_select_fusion.1.refs_0_, bf16[256,1024]{1,0:T(8,128)(2,1)} %refs_1_.3, bf16[256,1024]{1,0:T(8,128)(2,1)} %refs_2_.7, bf16[256,1024]{1,0:T(8,128)(2,1)} %refs_3_.7, bf16[256,1024]{1,0:T(8,128)(2,1)} %refs_4_.3, ...), custom_call_target="tpu_custom_call" | custom-call | tf_op jit(solution)/shard_map/self_stats/pallas_call | solution.py:83
  25.6 5.5 %collective-permute-done.2.refs_0_.refs_2_.refs_3_ = bf16[528,512]{1,0:T(8,128)(2,1)} collective-permute-done((bf16[528,512]{1,0:T(8,128)(2,1)}, bf16[528,512]{1,0:T(8,128)(2,1)}, u32[]{:S(2)}, u32[]{:S(2)}) %collective-permute-start.2) | collective-permute-done | bytes 540704 | tf_op jit(solution)/shard_map/ppermute | solution.py:38
  31.4 1.3 %collective-permute-start.8 = (bf16[512,512]{1,0:T(8,128)(2,1)}, bf16[512,512]{1,0:T(8,128)(2,1)}, u32[]{:S(2)}, u32[]{:S(2)}) collective-permute-start(bf16[512,512]{1,0:T(8,128)(2,1)} %get-tuple-element.83), channel_id=1, source_target_pairs={{2,0},{3,1},{4,2},{5,3},{6,4},{7,5},{8,6},{9,7},{10,8},{11,9},{12,... | collective-permute-start | bytes 1572872 | tf_op jit(solution)/shard_map/ppermute | solution.py:38
  32.7 5.9 %cross_remote.1 = (bf16[256,512]{1,0:T(8,128)(2,1)}, bf16[256,512]{1,0:T(8,128)(2,1)}, bf16[1024,512]{1,0:T(8,128)(2,1)}, f32[4,8,256]{2,1,0:T(8,128)}, f32[4,8,256]{2,1,0:T(8,128)}) custom-call(s32[1]{0:T(128)} %bitcast.info, bf16[528,512]{1,0:T(8,128)(2,1)} %collective-permute-done.2.refs_0_.refs_2_.refs_3_, ...), custom_call_target="tpu_custom_call" | custom-call | tf_op jit(solution)/shard_map/cross_remote/pallas_call | solution.py:83
  38.6 6.0 %collective-permute-start.6 = (f32[4,8,256]{2,1,0:T(8,128)}, f32[4,8,256]{2,1,0:T(8,128)}, u32[]{:S(2)}, u32[]{:S(2)}) collective-permute-start(f32[4,8,256]{2,1,0:T(8,128)} %get-tuple-element.77), channel_id=1, source_target_pairs={{0,2},{1,15},{2,4},{3,1},{4,6},{5,3},{6,8},{7,5},{8,10},{9,7},{10,... | collective-permute-start | bytes 98312 | tf_op jit(solution)/shard_map/ppermute | solution.py:38
  44.6 1.3 %collective-permute-start.9 = (bf16[512,512]{1,0:T(8,128)(2,1)}, bf16[512,512]{1,0:T(8,128)(2,1)}, u32[]{:S(2)}, u32[]{:S(2)}) collective-permute-start(bf16[512,512]{1,0:T(8,128)(2,1)} %get-tuple-element.89), channel_id=1, source_target_pairs={{2,1},{3,0},{4,3},{5,2},{6,5},{7,4},{8,7},{9,6},{10,9},{11,8},{12,... | collective-permute-start | bytes 1572872 | tf_op jit(solution)/shard_map/ppermute | solution.py:38
  45.9 1.3 %collective-permute-done.6.refs_9_ = f32[4,8,256]{2,1,0:T(8,128)} collective-permute-done((f32[4,8,256]{2,1,0:T(8,128)}, f32[4,8,256]{2,1,0:T(8,128)}, u32[]{:S(2)}, u32[]{:S(2)}) %collective-permute-start.6) | collective-permute-done | bytes 32800 | tf_op jit(solution)/shard_map/ppermute | solution.py:38
  47.2 1.3 %collective-permute-start.10 = (f32[4,8,512]{2,1,0:T(8,128)}, f32[4,8,512]{2,1,0:T(8,128)}, u32[]{:S(2)}, u32[]{:S(2)}) collective-permute-start(f32[4,8,512]{2,1,0:T(8,128)} %self_stats.1.refs_10_), channel_id=1, source_target_pairs={{2,0},{3,1},{4,2},{5,3},{6,4},{7,5},{8,6},{9,7},{10,8},{11,9},{12,... | collective-permute-start | bytes 196616 | tf_op jit(solution)/shard_map/ppermute | solution.py:38
  48.5 12.9 %collective-permute-done.7.refs_10_ = f32[4,8,256]{2,1,0:T(8,128)} collective-permute-done((f32[4,8,256]{2,1,0:T(8,128)}, f32[4,8,256]{2,1,0:T(8,128)}, u32[]{:S(2)}, u32[]{:S(2)}) %collective-permute-start.7) | collective-permute-done | bytes 32800 | tf_op jit(solution)/shard_map/ppermute | solution.py:38
  61.4 6.4 %cross_local.1 = (bf16[768,512]{1,0:T(8,128)(2,1)}, bf16[768,512]{1,0:T(8,128)(2,1)}) custom-call(s32[1]{0:T(128)} %bitcast.info, bf16[528,512]{1,0:T(8,128)(2,1)} %get-tuple-element.63.refs_0_, bf16[1040,512]{1,0:T(8,128)(2,1)} %collective-permute-done.refs_1_.refs_5_.refs_6_.refs_7_.refs_8_, bf16[256,1024]{1,0:T(8,128)(2,1)} %refs_2_.6, ...), custom_call_target="tpu_custom_call" | custom-call | flops 12000000000 | tf_op jit(solution)/shard_map/cross_local/pallas_call | solution.py:83
  67.8 7.2 %collective-permute-start.12 = (bf16[256,512]{1,0:T(8,128)(2,1)}, bf16[256,512]{1,0:T(8,128)(2,1)}, u32[]{:S(2)}, u32[]{:S(2)}) collective-permute-start(bf16[256,512]{1,0:T(8,128)(2,1)} %get-tuple-element.98), channel_id=1, source_target_pairs={{0,15},{1,2},{2,1},{3,4},{4,3},{5,6},{6,5},{7,8},{8,7},{9,10},{10,... | collective-permute-start | bytes 786440 | tf_op jit(solution)/shard_map/ppermute | solution.py:38
  75.0 6.6 %self_remote.1 = (bf16[512,512]{1,0:T(8,128)(2,1)}, bf16[1024,512]{1,0:T(8,128)(2,1)}, f32[4,8,512]{2,1,0:T(8,128)}) custom-call(s32[1]{0:T(128)} %bitcast.info, f32[512,512]{1,0:T(8,128)} %and_select_fusion.refs_0_, bf16[512,512]{1,0:T(8,128)(2,1)} %collective-permute-done.8.refs_1_.refs_2_, bf16[512,512]{1,0:T(8,128)(2,1)} %collective-permute-done.8.refs_1_.refs_2_, ...), custom_call_target="tpu_custom_call" | custom-call | flops 12000000000 | tf_op jit(solution)/shard_map/self_remote/pallas_call | solution.py:83
  81.7 2.5 %collective-permute-start.13 = (f32[4,8,512]{2,1,0:T(8,128)}, f32[4,8,512]{2,1,0:T(8,128)}, u32[]{:S(2)}, u32[]{:S(2)}) collective-permute-start(f32[4,8,512]{2,1,0:T(8,128)} %get-tuple-element.99), channel_id=1, source_target_pairs={{0,2},{1,3},{2,4},{3,5},{4,6},{5,7},{6,8},{7,9},{8,10},{9,11},{10,... | collective-permute-start | bytes 196616 | tf_op jit(solution)/shard_map/ppermute | solution.py:38
  84.1 4.7 %collective-permute-start.14 = (bf16[512,512]{1,0:T(8,128)(2,1)}, bf16[512,512]{1,0:T(8,128)(2,1)}, u32[]{:S(2)}, u32[]{:S(2)}) collective-permute-start(bf16[512,512]{1,0:T(8,128)(2,1)} %get-tuple-element.104), channel_id=1, source_target_pairs={{0,2},{1,3},{2,4},{3,5},{4,6},{5,7},{6,8},{7,9},{8,10},{9,11},{10,... | collective-permute-start | bytes 1572872 | tf_op jit(solution)/shard_map/ppermute | solution.py:38
  89.0 6.1 %self_local.1 = (bf16[768,512]{1,0:T(8,128)(2,1)}, bf16[768,512]{1,0:T(8,128)(2,1)}) custom-call(s32[1]{0:T(128)} %bitcast.info, f32[512,512]{1,0:T(8,128)} %and_select_fusion.1.refs_0_, bf16[256,1024]{1,0:T(8,128)(2,1)} %refs_1_.3, bf16[256,1024]{1,0:T(8,128)(2,1)} %refs_2_.7, bf16[256,1024]{1,0:T(8,128)(2,1)} %refs_3_.7, bf16[256,1024]{1,0:T(8,128)(2,1)} %refs_4_.3, ...), custom_call_target="tpu_custom_call" | custom-call | flops 12000000000 | tf_op jit(solution)/shard_map/self_local/pallas_call | solution.py:83
  95.1 2.8 %cross_final.1 = (bf16[256,1024]{1,0:T(8,128)(2,1)}, bf16[2,256,1024]{2,1,0:T(8,128)(2,1)}) custom-call(s32[1]{0:T(128)} %bitcast.info, bf16[768,512]{1,0:T(8,128)(2,1)} %get-tuple-element.105.mine, bf16[768,512]{1,0:T(8,128)(2,1)} %collective-permute-done.15.theirs, bf16[256,512]{1,0:T(8,128)(2,1)} %collective-permute-done.11.dq_mine, ...), custom_call_target="tpu_custom_call" | custom-call | tf_op jit(solution)/shard_map/cross_final/pallas_call | solution.py:83
  98.9 2.9 %collective-permute-done.17.dq_theirs = bf16[512,512]{1,0:T(8,128)(2,1)} collective-permute-done((bf16[512,512]{1,0:T(8,128)(2,1)}, bf16[512,512]{1,0:T(8,128)(2,1)}, u32[]{:S(2)}, u32[]{:S(2)}) %collective-permute-start.17) | collective-permute-done | bytes 524320 | tf_op jit(solution)/shard_map/ppermute | solution.py:38
  101.7 2.7 %self_final.1 = (bf16[256,1024]{1,0:T(8,128)(2,1)}, bf16[256,1024]{1,0:T(8,128)(2,1)}, bf16[256,1024]{1,0:T(8,128)(2,1)}) custom-call(s32[1]{0:T(128)} %bitcast.info, bf16[768,512]{1,0:T(8,128)(2,1)} %get-tuple-element.102.mine, bf16[768,512]{1,0:T(8,128)(2,1)} %collective-permute-done.16.theirs, bf16[512,512]{1,0:T(8,128)(2,1)} %collective-permute-done.14.dq_mine, ...), custom_call_target="tpu_custom_call" | custom-call | tf_op jit(solution)/shard_map/self_final/pallas_call | solution.py:83
  (29 shorter events, 6.8 us)
Async XLA Ops:
  3.4 22.2 %collective-permute-start.3 = (bf16[528,512]{1,0:T(8,128)(2,1)}, bf16[528,512]{1,0:T(8,128)(2,1)}, u32[]{:S(2)}, u32[]{:S(2)}) collective-permute-start(bf16[528,512]{1,0:T(8,128)(2,1)} %get-tuple-element.70), channel_id=1, source_target_pairs={{0,15},{1,2},{2,1},{3,4},{4,3},{5,6},{6,5},{7,8},{8,7},{9,10},{10,... | collective-permute-start | bytes 1622024 | tf_op jit(solution)/shard_map/ppermute | solution.py:38
  6.0 25.1 %collective-permute-start.2 = (bf16[528,512]{1,0:T(8,128)(2,1)}, bf16[528,512]{1,0:T(8,128)(2,1)}, u32[]{:S(2)}, u32[]{:S(2)}) collective-permute-start(bf16[528,512]{1,0:T(8,128)(2,1)} %get-tuple-element.63.refs_0_), channel_id=1, source_target_pairs={{0,14},{1,3},{2,0},{3,5},{4,2},{5,7},{6,4},{7,9},{8,6},{9,11},{10,... | collective-permute-start | bytes 1622024 | tf_op jit(solution)/shard_map/ppermute | solution.py:38
  7.2 8.3 %collective-permute-start = (bf16[1040,512]{1,0:T(8,128)(2,1)}, bf16[1040,512]{1,0:T(8,128)(2,1)}, u32[]{:S(2)}, u32[]{:S(2)}) collective-permute-start(bf16[1040,512]{1,0:T(8,128)(2,1)} %get-tuple-element.61), channel_id=1, source_target_pairs={{0,1},{1,0},{2,3},{3,2},{4,5},{5,4},{6,7},{7,6},{8,9},{9,8},{10,11... | collective-permute-start | bytes 3194888 | tf_op jit(solution)/shard_map/ppermute | solution.py:38
  12.1 8.9 %collective-permute-start.1 = (bf16[1024,512]{1,0:T(8,128)(2,1)}, bf16[1024,512]{1,0:T(8,128)(2,1)}, u32[]{:S(2)}, u32[]{:S(2)}) collective-permute-start(bf16[1024,512]{1,0:T(8,128)(2,1)} %get-tuple-element.68), channel_id=1, source_target_pairs={{0,1},{1,0},{2,3},{3,2},{4,5},{5,4},{6,7},{7,6},{8,9},{9,8},{10,11... | collective-permute-start | bytes 3145736 | tf_op jit(solution)/shard_map/ppermute | solution.py:38
  19.5 11.5 %collective-permute-start.5 = (f32[4,8,256]{2,1,0:T(8,128)}, f32[4,8,256]{2,1,0:T(8,128)}, u32[]{:S(2)}, u32[]{:S(2)}) collective-permute-start(f32[4,8,256]{2,1,0:T(8,128)} %get-tuple-element.71), channel_id=1, source_target_pairs={{0,2},{1,15},{2,4},{3,1},{4,6},{5,3},{6,8},{7,5},{8,10},{9,7},{10,... | collective-permute-start | bytes 98312 | tf_op jit(solution)/shard_map/ppermute | solution.py:38
  20.7 10.7 %collective-permute-start.4 = (f32[4,8,256]{2,1,0:T(8,128)}, f32[4,8,256]{2,1,0:T(8,128)}, u32[]{:S(2)}, u32[]{:S(2)}) collective-permute-start(f32[4,8,256]{2,1,0:T(8,128)} %get-tuple-element.65), channel_id=1, source_target_pairs={{0,14},{1,3},{2,0},{3,5},{4,2},{5,7},{6,4},{7,9},{8,6},{9,11},{10,... | collective-permute-start | bytes 98312 | tf_op jit(solution)/shard_map/ppermute | solution.py:38
  31.4 17.1 %collective-permute-start.8 = (bf16[512,512]{1,0:T(8,128)(2,1)}, bf16[512,512]{1,0:T(8,128)(2,1)}, u32[]{:S(2)}, u32[]{:S(2)}) collective-permute-start(bf16[512,512]{1,0:T(8,128)(2,1)} %get-tuple-element.83), channel_id=1, source_target_pairs={{2,0},{3,1},{4,2},{5,3},{6,4},{7,5},{8,6},{9,7},{10,8},{11,9},{12,... | collective-permute-start | bytes 1572872 | tf_op jit(solution)/shard_map/ppermute | solution.py:38
  38.6 8.6 %collective-permute-start.6 = (f32[4,8,256]{2,1,0:T(8,128)}, f32[4,8,256]{2,1,0:T(8,128)}, u32[]{:S(2)}, u32[]{:S(2)}) collective-permute-start(f32[4,8,256]{2,1,0:T(8,128)} %get-tuple-element.77), channel_id=1, source_target_pairs={{0,2},{1,15},{2,4},{3,1},{4,6},{5,3},{6,8},{7,5},{8,10},{9,7},{10,... | collective-permute-start | bytes 98312 | tf_op jit(solution)/shard_map/ppermute | solution.py:38
  44.6 16.8 %collective-permute-start.7 = (f32[4,8,256]{2,1,0:T(8,128)}, f32[4,8,256]{2,1,0:T(8,128)}, u32[]{:S(2)}, u32[]{:S(2)}) collective-permute-start(f32[4,8,256]{2,1,0:T(8,128)} %get-tuple-element.79), channel_id=1, source_target_pairs={{0,14},{1,3},{2,0},{3,5},{4,2},{5,7},{6,4},{7,9},{8,6},{9,11},{10,... | collective-permute-start | bytes 98312 | tf_op jit(solution)/shard_map/ppermute | solution.py:38
  44.6 23.1 %collective-permute-start.9 = (bf16[512,512]{1,0:T(8,128)(2,1)}, bf16[512,512]{1,0:T(8,128)(2,1)}, u32[]{:S(2)}, u32[]{:S(2)}) collective-permute-start(bf16[512,512]{1,0:T(8,128)(2,1)} %get-tuple-element.89), channel_id=1, source_target_pairs={{2,1},{3,0},{4,3},{5,2},{6,5},{7,4},{8,7},{9,6},{10,9},{11,8},{12,... | collective-permute-start | bytes 1572872 | tf_op jit(solution)/shard_map/ppermute | solution.py:38
  47.2 27.8 %collective-permute-start.10 = (f32[4,8,512]{2,1,0:T(8,128)}, f32[4,8,512]{2,1,0:T(8,128)}, u32[]{:S(2)}, u32[]{:S(2)}) collective-permute-start(f32[4,8,512]{2,1,0:T(8,128)} %self_stats.1.refs_10_), channel_id=1, source_target_pairs={{2,0},{3,1},{4,2},{5,3},{6,4},{7,5},{8,6},{9,7},{10,8},{11,9},{12,... | collective-permute-start | bytes 196616 | tf_op jit(solution)/shard_map/ppermute | solution.py:38
  67.8 21.1 %collective-permute-start.11 = (bf16[256,512]{1,0:T(8,128)(2,1)}, bf16[256,512]{1,0:T(8,128)(2,1)}, u32[]{:S(2)}, u32[]{:S(2)}) collective-permute-start(bf16[256,512]{1,0:T(8,128)(2,1)} %get-tuple-element.97), channel_id=1, source_target_pairs={{0,2},{1,15},{2,4},{3,1},{4,6},{5,3},{6,8},{7,5},{8,10},{9,7},{10,... | collective-permute-start | bytes 786440 | tf_op jit(solution)/shard_map/ppermute | solution.py:38
  67.8 21.1 %collective-permute-start.12 = (bf16[256,512]{1,0:T(8,128)(2,1)}, bf16[256,512]{1,0:T(8,128)(2,1)}, u32[]{:S(2)}, u32[]{:S(2)}) collective-permute-start(bf16[256,512]{1,0:T(8,128)(2,1)} %get-tuple-element.98), channel_id=1, source_target_pairs={{0,15},{1,2},{2,1},{3,4},{4,3},{5,6},{6,5},{7,8},{8,7},{9,10},{10,... | collective-permute-start | bytes 786440 | tf_op jit(solution)/shard_map/ppermute | solution.py:38
  81.7 7.2 %collective-permute-start.13 = (f32[4,8,512]{2,1,0:T(8,128)}, f32[4,8,512]{2,1,0:T(8,128)}, u32[]{:S(2)}, u32[]{:S(2)}) collective-permute-start(f32[4,8,512]{2,1,0:T(8,128)} %get-tuple-element.99), channel_id=1, source_target_pairs={{0,2},{1,3},{2,4},{3,5},{4,6},{5,7},{6,8},{7,9},{8,10},{9,11},{10,... | collective-permute-start | bytes 196616 | tf_op jit(solution)/shard_map/ppermute | solution.py:38
  84.1 14.2 %collective-permute-start.14 = (bf16[512,512]{1,0:T(8,128)(2,1)}, bf16[512,512]{1,0:T(8,128)(2,1)}, u32[]{:S(2)}, u32[]{:S(2)}) collective-permute-start(bf16[512,512]{1,0:T(8,128)(2,1)} %get-tuple-element.104), channel_id=1, source_target_pairs={{0,2},{1,3},{2,4},{3,5},{4,6},{5,7},{6,8},{7,9},{8,10},{9,11},{10,... | collective-permute-start | bytes 1572872 | tf_op jit(solution)/shard_map/ppermute | solution.py:38
  88.9 6.2 %collective-permute-start.15 = (bf16[768,512]{1,0:T(8,128)(2,1)}, bf16[768,512]{1,0:T(8,128)(2,1)}, u32[]{:S(2)}, u32[]{:S(2)}) collective-permute-start(bf16[768,512]{1,0:T(8,128)(2,1)} %get-tuple-element.106), channel_id=1, source_target_pairs={{0,1},{1,0},{2,3},{3,2},{4,5},{5,4},{6,7},{7,6},{8,9},{9,8},{10,11... | collective-permute-start | bytes 2359304 | tf_op jit(solution)/shard_map/ppermute | solution.py:38
  98.4 3.4 %collective-permute-start.16 = (bf16[768,512]{1,0:T(8,128)(2,1)}, bf16[768,512]{1,0:T(8,128)(2,1)}, u32[]{:S(2)}, u32[]{:S(2)}) collective-permute-start(bf16[768,512]{1,0:T(8,128)(2,1)} %get-tuple-element.110), channel_id=1, source_target_pairs={{0,1},{1,0},{2,3},{3,2},{4,5},{5,4},{6,7},{7,6},{8,9},{9,8},{10,11... | collective-permute-start | bytes 2359304 | tf_op jit(solution)/shard_map/ppermute | solution.py:38
  98.4 3.4 %collective-permute-start.17 = (bf16[512,512]{1,0:T(8,128)(2,1)}, bf16[512,512]{1,0:T(8,128)(2,1)}, u32[]{:S(2)}, u32[]{:S(2)}) collective-permute-start(bf16[512,512]{1,0:T(8,128)(2,1)} %collective-permute-done.14.dq_mine), channel_id=1, source_target_pairs={{0,1},{1,0},{2,3},{3,2},{4,5},{5,4},{6,7},{7,6},{8,9},{9,8},{10,11... | collective-permute-start | bytes 1572872 | tf_op jit(solution)/shard_map/ppermute | solution.py:38

commit v11 on v8

--- a/solution.py
+++ b/solution.py
@@ -90,9 +90,9 @@
             out_specs=out_specs,
         ),
         out_shape=[jax.ShapeDtypeStruct(shape, dtype) for shape, dtype in outs],
-        compiler_params=pltpu.CompilerParams(vmem_limit_bytes=63 << 20),
+        compiler_params=pltpu.CompilerParams(vmem_limit_bytes=64 << 20),
         cost_estimate=pl.CostEstimate(flops=flops, transcendentals=0, bytes_accessed=0),
-    )(info, *[pltpu.with_memory_space_constraint(x, pltpu.HBM) for x in inputs])
+    )(info, *inputs)
 
 
 def head_of(ref, j):

time: 99.9 us -> 98.1 us (0.982); the launches traced: 99.2 us -> 96.4 us
  local copies, waits for them, and re-layouts: 5.72 us -> 0.92 us
  starting transfers between devices: 29.1 us -> 30.1 us
  waiting for transfers between devices: 17.1 us -> 18.1 us
    unnamed x28 -> x0, local copies, waits for them, and re-layouts: 4.8 us -> none
    ppermute x18, waiting for transfers between devices: 17.1 us -> 18.1 us  [send(): return lax.ppermute(value, 'ctx', pairs)]
  transfers between devices with their start and end apart: 18 -> 18, of which waited for: 6 -> 6; matrix products, arithmetic and copies ran while one was open for 3% -> 3% of each run, Pallas kernels for 39% -> 40%
where the time goes in v11:
time: 98.1 us; the launch traced here: 96.4 us
  Pallas kernels  44.1 us (45%)
  starting transfers between devices  30.1 us (31%)
  waiting for transfers between devices  18.1 us (18%)
  other arithmetic  2.4 us (2%)
    pallas_call x10, Pallas kernels, call(): pl.pallas_call(kernel, name=name, grid_spec=pltpu.PrefetchScalarGridSpec(...  44.1 us
    ppermute x18, starting transfers between devices, send(): return lax.ppermute(value, 'ctx', pairs)  30.1 us
    ppermute x18, waiting for transfers between devices, send(): return lax.ppermute(value, 'ctx', pairs)  18.1 us
  transfers between devices with their start and end apart: 18, of which 6 were waited for; matrix products, arithmetic and copies ran while one was open for 3% of the time, Pallas kernels for 40%

profile of v11, /device:TPU:1, one launch (start us, length us, event | category | flops | bytes accessed | tf_op | source)
XLA Modules:
  0.0 96.4 jit_solution(9122576228419131411)
XLA Ops:
  0.6 2.7 %pack_cross.1 = (bf16[1040,512]{1,0:T(8,128)(2,1)}, bf16[528,512]{1,0:T(8,128)(2,1)}, bf16[528,512]{1,0:T(8,128)(2,1)}) custom-call(s32[1]{0:T(128)} %bitcast.info, s32[2,4]{1,0:T(2,128)} %bitcast.8, bf16[256,1024]{1,0:T(8,128)(2,1)} %refs_2_.6, bf16[256,1024]{1,0:T(8,128)(2,1)} %refs_3_.6, bf16[256,1024]{1,0:T(8,128)(2,1)} %refs_2_.6, ...), custom_call_target="tpu_custom_call" | custom-call | tf_op jit(solution)/shard_map/pack_cross/pallas_call | solution.py:83
  3.4 2.6 %collective-permute-start.3 = (bf16[528,512]{1,0:T(8,128)(2,1)}, bf16[528,512]{1,0:T(8,128)(2,1)}, u32[]{:S(2)}, u32[]{:S(2)}) collective-permute-start(bf16[528,512]{1,0:T(8,128)(2,1)} %get-tuple-element.69), channel_id=1, source_target_pairs={{0,15},{1,2},{2,1},{3,4},{4,3},{5,6},{6,5},{7,8},{8,7},{9,10},{10,... | collective-permute-start | bytes 1622024 | tf_op jit(solution)/shard_map/ppermute | solution.py:38
  6.0 1.2 %collective-permute-start.2 = (bf16[528,512]{1,0:T(8,128)(2,1)}, bf16[528,512]{1,0:T(8,128)(2,1)}, u32[]{:S(2)}, u32[]{:S(2)}) collective-permute-start(bf16[528,512]{1,0:T(8,128)(2,1)} %get-tuple-element.62.refs_0_), channel_id=1, source_target_pairs={{0,14},{1,3},{2,0},{3,5},{4,2},{5,7},{6,4},{7,9},{8,6},{9,11},{10,... | collective-permute-start | bytes 1622024 | tf_op jit(solution)/shard_map/ppermute | solution.py:38
  7.2 2.3 %collective-permute-start = (bf16[1040,512]{1,0:T(8,128)(2,1)}, bf16[1040,512]{1,0:T(8,128)(2,1)}, u32[]{:S(2)}, u32[]{:S(2)}) collective-permute-start(bf16[1040,512]{1,0:T(8,128)(2,1)} %get-tuple-element.60), channel_id=1, source_target_pairs={{0,1},{1,0},{2,3},{3,2},{4,5},{5,4},{6,7},{7,6},{8,9},{9,8},{10,11... | collective-permute-start | bytes 3194888 | tf_op jit(solution)/shard_map/ppermute | solution.py:38
  9.5 2.6 %pack_self.1 = (bf16[1024,512]{1,0:T(8,128)(2,1)}, bf16[512,512]{1,0:T(8,128)(2,1)}, bf16[512,512]{1,0:T(8,128)(2,1)}) custom-call(s32[1]{0:T(128)} %bitcast.info, bf16[256,1024]{1,0:T(8,128)(2,1)} %refs_1_.3, bf16[256,1024]{1,0:T(8,128)(2,1)} %refs_2_.7, bf16[256,1024]{1,0:T(8,128)(2,1)} %refs_1_.3, bf16[256,1024]{1,0:T(8,128)(2,1)} %refs_2_.7, ...), custom_call_target="tpu_custom_call" | custom-call | tf_op jit(solution)/shard_map/pack_self/pallas_call | solution.py:83
  15.5 4.0 %cross_stats.1 = (f32[4,8,256]{2,1,0:T(8,128)}, f32[4,8,256]{2,1,0:T(8,128)}) custom-call(s32[1]{0:T(128)} %bitcast.info, bf16[528,512]{1,0:T(8,128)(2,1)} %get-tuple-element.62.refs_0_, bf16[1040,512]{1,0:T(8,128)(2,1)} %collective-permute-done.refs_1_.refs_5_.refs_6_.refs_7_.refs_8_, bf16[256,1024]{1,0:T(8,128)(2,1)} %refs_2_.6, ...), custom_call_target="tpu_custom_call" | custom-call | tf_op jit(solution)/shard_map/cross_stats/pallas_call | solution.py:83
  21.0 4.2 %self_stats.1.refs_10_ = f32[4,8,512]{2,1,0:T(8,128)} custom-call(s32[1]{0:T(128)} %bitcast.info, f32[512,512]{1,0:T(8,128)} %and_select_fusion.1.refs_0_, bf16[256,1024]{1,0:T(8,128)(2,1)} %refs_1_.3, bf16[256,1024]{1,0:T(8,128)(2,1)} %refs_2_.7, bf16[256,1024]{1,0:T(8,128)(2,1)} %refs_3_.7, bf16[256,1024]{1,0:T(8,128)(2,1)} %refs_4_.3, ...), custom_call_target="tpu_custom_call" | custom-call | tf_op jit(solution)/shard_map/self_stats/pallas_call | solution.py:83
  25.6 5.5 %collective-permute-done.2.refs_0_.refs_2_.refs_3_ = bf16[528,512]{1,0:T(8,128)(2,1)} collective-permute-done((bf16[528,512]{1,0:T(8,128)(2,1)}, bf16[528,512]{1,0:T(8,128)(2,1)}, u32[]{:S(2)}, u32[]{:S(2)}) %collective-permute-start.2) | collective-permute-done | bytes 540704 | tf_op jit(solution)/shard_map/ppermute | solution.py:38
  31.4 1.3 %collective-permute-start.8 = (bf16[512,512]{1,0:T(8,128)(2,1)}, bf16[512,512]{1,0:T(8,128)(2,1)}, u32[]{:S(2)}, u32[]{:S(2)}) collective-permute-start(bf16[512,512]{1,0:T(8,128)(2,1)} %get-tuple-element.80), channel_id=1, source_target_pairs={{2,0},{3,1},{4,2},{5,3},{6,4},{7,5},{8,6},{9,7},{10,8},{11,9},{12,... | collective-permute-start | bytes 1572872 | tf_op jit(solution)/shard_map/ppermute | solution.py:38
  32.7 1.3 %collective-permute-start.9 = (f32[4,8,512]{2,1,0:T(8,128)}, f32[4,8,512]{2,1,0:T(8,128)}, u32[]{:S(2)}, u32[]{:S(2)}) collective-permute-start(f32[4,8,512]{2,1,0:T(8,128)} %self_stats.1.refs_10_), channel_id=1, source_target_pairs={{2,0},{3,1},{4,2},{5,3},{6,4},{7,5},{8,6},{9,7},{10,8},{11,9},{12,... | collective-permute-start | bytes 196616 | tf_op jit(solution)/shard_map/ppermute | solution.py:38
  34.0 5.9 %cross_remote.1 = (bf16[256,512]{1,0:T(8,128)(2,1)}, bf16[256,512]{1,0:T(8,128)(2,1)}, bf16[1024,512]{1,0:T(8,128)(2,1)}, f32[4,8,256]{2,1,0:T(8,128)}, f32[4,8,256]{2,1,0:T(8,128)}) custom-call(s32[1]{0:T(128)} %bitcast.info, bf16[528,512]{1,0:T(8,128)(2,1)} %collective-permute-done.2.refs_0_.refs_2_.refs_3_, ...), custom_call_target="tpu_custom_call" | custom-call | tf_op jit(solution)/shard_map/cross_remote/pallas_call | solution.py:83
  39.9 8.2 %collective-permute-start.6 = (f32[4,8,256]{2,1,0:T(8,128)}, f32[4,8,256]{2,1,0:T(8,128)}, u32[]{:S(2)}, u32[]{:S(2)}) collective-permute-start(f32[4,8,256]{2,1,0:T(8,128)} %get-tuple-element.75), channel_id=1, source_target_pairs={{0,2},{1,15},{2,4},{3,1},{4,6},{5,3},{6,8},{7,5},{8,10},{9,7},{10,... | collective-permute-start | bytes 98312 | tf_op jit(solution)/shard_map/ppermute | solution.py:38
  48.1 1.3 %collective-permute-start.10 = (bf16[512,512]{1,0:T(8,128)(2,1)}, bf16[512,512]{1,0:T(8,128)(2,1)}, u32[]{:S(2)}, u32[]{:S(2)}) collective-permute-start(bf16[512,512]{1,0:T(8,128)(2,1)} %get-tuple-element.86), channel_id=1, source_target_pairs={{2,1},{3,0},{4,3},{5,2},{6,5},{7,4},{8,7},{9,6},{10,9},{11,8},{12,... | collective-permute-start | bytes 1572872 | tf_op jit(solution)/shard_map/ppermute | solution.py:38
  49.4 4.5 %collective-permute-done.7.refs_10_ = f32[4,8,256]{2,1,0:T(8,128)} collective-permute-done((f32[4,8,256]{2,1,0:T(8,128)}, f32[4,8,256]{2,1,0:T(8,128)}, u32[]{:S(2)}, u32[]{:S(2)}) %collective-permute-start.7) | collective-permute-done | bytes 32800 | tf_op jit(solution)/shard_map/ppermute | solution.py:38
  54.0 6.4 %cross_local.1 = (bf16[768,512]{1,0:T(8,128)(2,1)}, bf16[768,512]{1,0:T(8,128)(2,1)}) custom-call(s32[1]{0:T(128)} %bitcast.info, bf16[528,512]{1,0:T(8,128)(2,1)} %get-tuple-element.62.refs_0_, bf16[1040,512]{1,0:T(8,128)(2,1)} %collective-permute-done.refs_1_.refs_5_.refs_6_.refs_7_.refs_8_, bf16[256,1024]{1,0:T(8,128)(2,1)} %refs_2_.6, ...), custom_call_target="tpu_custom_call" | custom-call | flops 12000000000 | tf_op jit(solution)/shard_map/cross_local/pallas_call | solution.py:83
  60.4 4.3 %collective-permute-done.10.refs_3_.refs_4_ = bf16[512,512]{1,0:T(8,128)(2,1)} collective-permute-done((bf16[512,512]{1,0:T(8,128)(2,1)}, bf16[512,512]{1,0:T(8,128)(2,1)}, u32[]{:S(2)}, u32[]{:S(2)}) %collective-permute-start.10) | collective-permute-done | bytes 524320 | tf_op jit(solution)/shard_map/ppermute | solution.py:38
  65.2 6.7 %self_remote.1 = (bf16[512,512]{1,0:T(8,128)(2,1)}, bf16[1024,512]{1,0:T(8,128)(2,1)}, f32[4,8,512]{2,1,0:T(8,128)}) custom-call(s32[1]{0:T(128)} %bitcast.info, f32[512,512]{1,0:T(8,128)} %and_select_fusion.refs_0_, bf16[512,512]{1,0:T(8,128)(2,1)} %collective-permute-done.8.refs_1_.refs_2_, bf16[512,512]{1,0:T(8,128)(2,1)} %collective-permute-done.8.refs_1_.refs_2_, ...), custom_call_target="tpu_custom_call" | custom-call | flops 12000000000 | tf_op jit(solution)/shard_map/self_remote/pallas_call | solution.py:83
  71.9 4.0 %collective-permute-start.13 = (f32[4,8,512]{2,1,0:T(8,128)}, f32[4,8,512]{2,1,0:T(8,128)}, u32[]{:S(2)}, u32[]{:S(2)}) collective-permute-start(f32[4,8,512]{2,1,0:T(8,128)} %get-tuple-element.96), channel_id=1, source_target_pairs={{0,2},{1,3},{2,4},{3,5},{4,6},{5,7},{6,8},{7,9},{8,10},{9,11},{10,... | collective-permute-start | bytes 196616 | tf_op jit(solution)/shard_map/ppermute | solution.py:38
  75.9 3.1 %collective-permute-start.14 = (bf16[512,512]{1,0:T(8,128)(2,1)}, bf16[512,512]{1,0:T(8,128)(2,1)}, u32[]{:S(2)}, u32[]{:S(2)}) collective-permute-start(bf16[512,512]{1,0:T(8,128)(2,1)} %get-tuple-element.102), channel_id=1, source_target_pairs={{0,2},{1,3},{2,4},{3,5},{4,6},{5,7},{6,8},{7,9},{8,10},{9,11},{10,... | collective-permute-start | bytes 1572872 | tf_op jit(solution)/shard_map/ppermute | solution.py:38
  79.0 1.9 %collective-permute-start.15 = (bf16[768,512]{1,0:T(8,128)(2,1)}, bf16[768,512]{1,0:T(8,128)(2,1)}, u32[]{:S(2)}, u32[]{:S(2)}) collective-permute-start(bf16[768,512]{1,0:T(8,128)(2,1)} %get-tuple-element.104), channel_id=1, source_target_pairs={{0,1},{1,0},{2,3},{3,2},{4,5},{5,4},{6,7},{7,6},{8,9},{9,8},{10,11... | collective-permute-start | bytes 2359304 | tf_op jit(solution)/shard_map/ppermute | solution.py:38
  80.8 6.1 %self_local.1 = (bf16[768,512]{1,0:T(8,128)(2,1)}, bf16[768,512]{1,0:T(8,128)(2,1)}) custom-call(s32[1]{0:T(128)} %bitcast.info, f32[512,512]{1,0:T(8,128)} %and_select_fusion.1.refs_0_, bf16[256,1024]{1,0:T(8,128)(2,1)} %refs_1_.3, bf16[256,1024]{1,0:T(8,128)(2,1)} %refs_2_.7, bf16[256,1024]{1,0:T(8,128)(2,1)} %refs_3_.7, bf16[256,1024]{1,0:T(8,128)(2,1)} %refs_4_.3, ...), custom_call_target="tpu_custom_call" | custom-call | flops 12000000000 | tf_op jit(solution)/shard_map/self_local/pallas_call | solution.py:83
  86.9 2.8 %cross_final.1 = (bf16[256,1024]{1,0:T(8,128)(2,1)}, bf16[2,256,1024]{2,1,0:T(8,128)(2,1)}) custom-call(s32[1]{0:T(128)} %bitcast.info, bf16[768,512]{1,0:T(8,128)(2,1)} %get-tuple-element.103.mine, bf16[768,512]{1,0:T(8,128)(2,1)} %collective-permute-done.15.theirs, bf16[256,512]{1,0:T(8,128)(2,1)} %collective-permute-done.11.dq_mine, ...), custom_call_target="tpu_custom_call" | custom-call | tf_op jit(solution)/shard_map/cross_final/pallas_call | solution.py:83
  90.6 3.0 %collective-permute-done.17.dq_theirs = bf16[512,512]{1,0:T(8,128)(2,1)} collective-permute-done((bf16[512,512]{1,0:T(8,128)(2,1)}, bf16[512,512]{1,0:T(8,128)(2,1)}, u32[]{:S(2)}, u32[]{:S(2)}) %collective-permute-start.17) | collective-permute-done | bytes 524320 | tf_op jit(solution)/shard_map/ppermute | solution.py:38
  93.6 2.7 %self_final.1 = (bf16[256,1024]{1,0:T(8,128)(2,1)}, bf16[256,1024]{1,0:T(8,128)(2,1)}, bf16[256,1024]{1,0:T(8,128)(2,1)}) custom-call(s32[1]{0:T(128)} %bitcast.info, bf16[768,512]{1,0:T(8,128)(2,1)} %get-tuple-element.100.mine, bf16[768,512]{1,0:T(8,128)(2,1)} %collective-permute-done.16.theirs, bf16[512,512]{1,0:T(8,128)(2,1)} %collective-permute-done.14.dq_mine, ...), custom_call_target="tpu_custom_call" | custom-call | tf_op jit(solution)/shard_map/self_final/pallas_call | solution.py:83
  (29 shorter events, 7.1 us)
Async XLA Ops:
  3.4 22.2 %collective-permute-start.3 = (bf16[528,512]{1,0:T(8,128)(2,1)}, bf16[528,512]{1,0:T(8,128)(2,1)}, u32[]{:S(2)}, u32[]{:S(2)}) collective-permute-start(bf16[528,512]{1,0:T(8,128)(2,1)} %get-tuple-element.69), channel_id=1, source_target_pairs={{0,15},{1,2},{2,1},{3,4},{4,3},{5,6},{6,5},{7,8},{8,7},{9,10},{10,... | collective-permute-start | bytes 1622024 | tf_op jit(solution)/shard_map/ppermute | solution.py:38
  6.0 25.1 %collective-permute-start.2 = (bf16[528,512]{1,0:T(8,128)(2,1)}, bf16[528,512]{1,0:T(8,128)(2,1)}, u32[]{:S(2)}, u32[]{:S(2)}) collective-permute-start(bf16[528,512]{1,0:T(8,128)(2,1)} %get-tuple-element.62.refs_0_), channel_id=1, source_target_pairs={{0,14},{1,3},{2,0},{3,5},{4,2},{5,7},{6,4},{7,9},{8,6},{9,11},{10,... | collective-permute-start | bytes 1622024 | tf_op jit(solution)/shard_map/ppermute | solution.py:38
  7.2 8.3 %collective-permute-start = (bf16[1040,512]{1,0:T(8,128)(2,1)}, bf16[1040,512]{1,0:T(8,128)(2,1)}, u32[]{:S(2)}, u32[]{:S(2)}) collective-permute-start(bf16[1040,512]{1,0:T(8,128)(2,1)} %get-tuple-element.60), channel_id=1, source_target_pairs={{0,1},{1,0},{2,3},{3,2},{4,5},{5,4},{6,7},{7,6},{8,9},{9,8},{10,11... | collective-permute-start | bytes 3194888 | tf_op jit(solution)/shard_map/ppermute | solution.py:38
  12.1 8.9 %collective-permute-start.1 = (bf16[1024,512]{1,0:T(8,128)(2,1)}, bf16[1024,512]{1,0:T(8,128)(2,1)}, u32[]{:S(2)}, u32[]{:S(2)}) collective-permute-start(bf16[1024,512]{1,0:T(8,128)(2,1)} %get-tuple-element.67), channel_id=1, source_target_pairs={{0,1},{1,0},{2,3},{3,2},{4,5},{5,4},{6,7},{7,6},{8,9},{9,8},{10,11... | collective-permute-start | bytes 3145736 | tf_op jit(solution)/shard_map/ppermute | solution.py:38
  19.5 11.5 %collective-permute-start.5 = (f32[4,8,256]{2,1,0:T(8,128)}, f32[4,8,256]{2,1,0:T(8,128)}, u32[]{:S(2)}, u32[]{:S(2)}) collective-permute-start(f32[4,8,256]{2,1,0:T(8,128)} %get-tuple-element.70), channel_id=1, source_target_pairs={{0,2},{1,15},{2,4},{3,1},{4,6},{5,3},{6,8},{7,5},{8,10},{9,7},{10,... | collective-permute-start | bytes 98312 | tf_op jit(solution)/shard_map/ppermute | solution.py:38
  20.7 10.7 %collective-permute-start.4 = (f32[4,8,256]{2,1,0:T(8,128)}, f32[4,8,256]{2,1,0:T(8,128)}, u32[]{:S(2)}, u32[]{:S(2)}) collective-permute-start(f32[4,8,256]{2,1,0:T(8,128)} %get-tuple-element.64), channel_id=1, source_target_pairs={{0,14},{1,3},{2,0},{3,5},{4,2},{5,7},{6,4},{7,9},{8,6},{9,11},{10,... | collective-permute-start | bytes 98312 | tf_op jit(solution)/shard_map/ppermute | solution.py:38
  31.4 18.0 %collective-permute-start.8 = (bf16[512,512]{1,0:T(8,128)(2,1)}, bf16[512,512]{1,0:T(8,128)(2,1)}, u32[]{:S(2)}, u32[]{:S(2)}) collective-permute-start(bf16[512,512]{1,0:T(8,128)(2,1)} %get-tuple-element.80), channel_id=1, source_target_pairs={{2,0},{3,1},{4,2},{5,3},{6,4},{7,5},{8,6},{9,7},{10,8},{11,9},{12,... | collective-permute-start | bytes 1572872 | tf_op jit(solution)/shard_map/ppermute | solution.py:38
  32.7 16.7 %collective-permute-start.9 = (f32[4,8,512]{2,1,0:T(8,128)}, f32[4,8,512]{2,1,0:T(8,128)}, u32[]{:S(2)}, u32[]{:S(2)}) collective-permute-start(f32[4,8,512]{2,1,0:T(8,128)} %self_stats.1.refs_10_), channel_id=1, source_target_pairs={{2,0},{3,1},{4,2},{5,3},{6,4},{7,5},{8,6},{9,7},{10,8},{11,9},{12,... | collective-permute-start | bytes 196616 | tf_op jit(solution)/shard_map/ppermute | solution.py:38
  39.9 9.5 %collective-permute-start.6 = (f32[4,8,256]{2,1,0:T(8,128)}, f32[4,8,256]{2,1,0:T(8,128)}, u32[]{:S(2)}, u32[]{:S(2)}) collective-permute-start(f32[4,8,256]{2,1,0:T(8,128)} %get-tuple-element.75), channel_id=1, source_target_pairs={{0,2},{1,15},{2,4},{3,1},{4,6},{5,3},{6,8},{7,5},{8,10},{9,7},{10,... | collective-permute-start | bytes 98312 | tf_op jit(solution)/shard_map/ppermute | solution.py:38
  48.1 5.9 %collective-permute-start.7 = (f32[4,8,256]{2,1,0:T(8,128)}, f32[4,8,256]{2,1,0:T(8,128)}, u32[]{:S(2)}, u32[]{:S(2)}) collective-permute-start(f32[4,8,256]{2,1,0:T(8,128)} %get-tuple-element.76), channel_id=1, source_target_pairs={{0,14},{1,3},{2,0},{3,5},{4,2},{5,7},{6,4},{7,9},{8,6},{9,11},{10,... | collective-permute-start | bytes 98312 | tf_op jit(solution)/shard_map/ppermute | solution.py:38
  48.1 16.6 %collective-permute-start.10 = (bf16[512,512]{1,0:T(8,128)(2,1)}, bf16[512,512]{1,0:T(8,128)(2,1)}, u32[]{:S(2)}, u32[]{:S(2)}) collective-permute-start(bf16[512,512]{1,0:T(8,128)(2,1)} %get-tuple-element.86), channel_id=1, source_target_pairs={{2,1},{3,0},{4,3},{5,2},{6,5},{7,4},{8,7},{9,6},{10,9},{11,8},{12,... | collective-permute-start | bytes 1572872 | tf_op jit(solution)/shard_map/ppermute | solution.py:38
  64.7 14.3 %collective-permute-start.11 = (bf16[256,512]{1,0:T(8,128)(2,1)}, bf16[256,512]{1,0:T(8,128)(2,1)}, u32[]{:S(2)}, u32[]{:S(2)}) collective-permute-start(bf16[256,512]{1,0:T(8,128)(2,1)} %get-tuple-element.94), channel_id=1, source_target_pairs={{0,2},{1,15},{2,4},{3,1},{4,6},{5,3},{6,8},{7,5},{8,10},{9,7},{10,... | collective-permute-start | bytes 786440 | tf_op jit(solution)/shard_map/ppermute | solution.py:38
  64.7 14.3 %collective-permute-start.12 = (bf16[256,512]{1,0:T(8,128)(2,1)}, bf16[256,512]{1,0:T(8,128)(2,1)}, u32[]{:S(2)}, u32[]{:S(2)}) collective-permute-start(bf16[256,512]{1,0:T(8,128)(2,1)} %get-tuple-element.95), channel_id=1, source_target_pairs={{0,15},{1,2},{2,1},{3,4},{4,3},{5,6},{6,5},{7,8},{8,7},{9,10},{10,... | collective-permute-start | bytes 786440 | tf_op jit(solution)/shard_map/ppermute | solution.py:38
  71.9 7.1 %collective-permute-start.13 = (f32[4,8,512]{2,1,0:T(8,128)}, f32[4,8,512]{2,1,0:T(8,128)}, u32[]{:S(2)}, u32[]{:S(2)}) collective-permute-start(f32[4,8,512]{2,1,0:T(8,128)} %get-tuple-element.96), channel_id=1, source_target_pairs={{0,2},{1,3},{2,4},{3,5},{4,6},{5,7},{6,8},{7,9},{8,10},{9,11},{10,... | collective-permute-start | bytes 196616 | tf_op jit(solution)/shard_map/ppermute | solution.py:38
  75.9 13.8 %collective-permute-start.14 = (bf16[512,512]{1,0:T(8,128)(2,1)}, bf16[512,512]{1,0:T(8,128)(2,1)}, u32[]{:S(2)}, u32[]{:S(2)}) collective-permute-start(bf16[512,512]{1,0:T(8,128)(2,1)} %get-tuple-element.102), channel_id=1, source_target_pairs={{0,2},{1,3},{2,4},{3,5},{4,6},{5,7},{6,8},{7,9},{8,10},{9,11},{10,... | collective-permute-start | bytes 1572872 | tf_op jit(solution)/shard_map/ppermute | solution.py:38
  79.0 7.9 %collective-permute-start.15 = (bf16[768,512]{1,0:T(8,128)(2,1)}, bf16[768,512]{1,0:T(8,128)(2,1)}, u32[]{:S(2)}, u32[]{:S(2)}) collective-permute-start(bf16[768,512]{1,0:T(8,128)(2,1)} %get-tuple-element.104), channel_id=1, source_target_pairs={{0,1},{1,0},{2,3},{3,2},{4,5},{5,4},{6,7},{7,6},{8,9},{9,8},{10,11... | collective-permute-start | bytes 2359304 | tf_op jit(solution)/shard_map/ppermute | solution.py:38
  89.8 3.9 %collective-permute-start.16 = (bf16[768,512]{1,0:T(8,128)(2,1)}, bf16[768,512]{1,0:T(8,128)(2,1)}, u32[]{:S(2)}, u32[]{:S(2)}) collective-permute-start(bf16[768,512]{1,0:T(8,128)(2,1)} %get-tuple-element.108), channel_id=1, source_target_pairs={{0,1},{1,0},{2,3},{3,2},{4,5},{5,4},{6,7},{7,6},{8,9},{9,8},{10,11... | collective-permute-start | bytes 2359304 | tf_op jit(solution)/shard_map/ppermute | solution.py:38
  90.6 3.0 %collective-permute-start.17 = (bf16[512,512]{1,0:T(8,128)(2,1)}, bf16[512,512]{1,0:T(8,128)(2,1)}, u32[]{:S(2)}, u32[]{:S(2)}) collective-permute-start(bf16[512,512]{1,0:T(8,128)(2,1)} %collective-permute-done.14.dq_mine), channel_id=1, source_target_pairs={{0,1},{1,0},{2,3},{3,2},{4,5},{5,4},{6,7},{7,6},{8,9},{9,8},{10,11... | collective-permute-start | bytes 1572872 | tf_op jit(solution)/shard_map/ppermute | solution.py:38

commit v12 on v10

--- a/solution.py
+++ b/solution.py
@@ -19,6 +19,7 @@
 NBR_TOK = 128
 ROWS = 256
 EXTRA = 16
+STATS = 64
 LONG = 12 * 10**9
 FACTOR = HEAD_DIM ** (-0.5)
 MASKED = -1e30
@@ -160,7 +161,7 @@
 
 
 def merge(stats, mine):
-    t_peak, t_total, t_moment = stats[0, 0:1], stats[0, 1:2], stats[0, 2:3]
+    t_peak, t_total, t_moment = stats
     peak, total, moment = mine
     top = jnp.maximum(t_peak, peak)
     t_scale = jnp.exp(t_peak - top)
@@ -204,16 +205,42 @@
         out[2 * ROWS :] = times
 
 
-def pack_self_kernel(info, qm, gm, q, g, k, v, swap_ref, mine, other):
+def pack_self_kernel(info, q, g, k, v, swap_ref, other):
     for index, ref in enumerate((q, g, k, v)):
         swap_ref[index * ROWS : (index + 1) * ROWS] = ref[...]
-    for out, first, second in ((mine, qm, gm), (other, q, g)):
-        out[0:ROWS] = first[...]
-        out[ROWS : 2 * ROWS] = second[...]
+    other[0:ROWS] = q[...]
+    other[ROWS:] = g[...]
 
 
 def ordered(core, a, b):
     return jnp.where(core == 0, a, b), jnp.where(core == 0, b, a)
+
+
+def split3(x):
+    high = x.astype(BF16)
+    rest = x - high.astype(F32)
+    middle = rest.astype(BF16)
+    return [high, middle, (rest - middle.astype(F32)).astype(BF16)]
+
+
+def packed_stats(stats):
+    rows = []
+    for low in range(0, stats[0].shape[1], HEAD_DIM):
+        for x in stats:
+            rows += split3(x[:, low : low + HEAD_DIM])
+    rows.append(jnp.zeros((STATS - len(rows), HEAD_DIM), BF16))
+    return jnp.concatenate(rows, axis=0)
+
+
+def unpacked_stats(ref):
+    x = ref[...].astype(F32)
+    stats = []
+    for index in range(3):
+        parts = []
+        for low in range(3 * index, 9 * (2 * ROWS // HEAD_DIM), 9):
+            parts.append(x[low : low + 1] + x[low + 1 : low + 2] + x[low + 2 : low + 3])
+        stats.append(jnp.concatenate(parts, axis=1))
+    return stats
 
 
 def wide_scores(keys_x, keys_y, values_x, values_y, qs, gs, bias):
@@ -262,7 +289,10 @@
 
 def self_stats_kernel(info, *refs):
     scores = local_self(info[0] % 2, *refs[:-1])[0]
-    refs[-1][...] = stat_rows(*wide_stats(*scores)[2:])
+    out = refs[-1]
+    out[:ROWS] = refs[1][...]
+    out[ROWS : 2 * ROWS] = refs[2][...]
+    out[2 * ROWS :] = packed_stats(wide_stats(*scores)[2:])
 
 
 def cross_stats_kernel(info, *refs):
@@ -283,8 +313,7 @@
     qs, gs = both(q1, q0), both(g1, g0)
     sx, sy, dpx, dpy = wide_scores(k1, k0, v1, v0, qs, gs, bias[...])
     ex, ey, *mine = wide_stats(sx, sy, dpx, dpy)
-    known = stats[...]
-    known = jnp.concatenate([known[:, :, ROWS:], known[:, :, :ROWS]], axis=2)
+    known = [jnp.concatenate([x[:, ROWS:], x[:, :ROWS]], axis=1) for x in unpacked_stats(stats)]
     top, inverse, delta, scale = merge(known, mine)
     px, py = ex * scale, ey * scale[:, ROWS:]
     dq1, dq0, dk1, dk0, dv1, dv0 = wide_gradients(px, py, dpx, dpy, delta, qs, gs, k1, k0)
@@ -308,7 +337,8 @@
     for q, g, k, v, rows, stats, dq_ref, out_stats, place in jobs:
         s, dp = add_rows(dot_last(k, q[...]) * FACTOR, rows), dot_last(v, g[...])
         e, *mine = partial_stats(s, dp)
-        top, inverse, delta, scale = merge(stats[...], mine)
+        known = [stats[0, row : row + 1] for row in range(3)]
+        top, inverse, delta, scale = merge(known, mine)
         dq, dk, dv = gradients(e * scale, dp, delta, q[...], g[...], k)
         dq_ref[...] = dq.astype(BF16)
         out_stats[...] = stat_rows(top, inverse, delta)
@@ -318,14 +348,14 @@
 
 def self_local_kernel(info, *refs):
     stats_ref, own_ref, kv_ref, mine, theirs = refs[-5:]
-    local = own_ref[0]
+    local_peak, local_total, local_moment = unpacked_stats(own_ref)
     core = info[0] % 2
     first = info[0] < 2
     stats = stats_ref[0]
     stats = jnp.concatenate([stats[:, ROWS:], stats[:, :ROWS]], axis=1)
-    inverse = 1.0 / local[1:2]
-    top = jnp.where(first, local[0:1], stats[0:1])
-    delta = jnp.where(first, local[2:3] * inverse, stats[2:3])
+    inverse = 1.0 / local_total
+    top = jnp.where(first, local_peak, stats[0:1])
+    delta = jnp.where(first, local_moment * inverse, stats[2:3])
     inverse = jnp.where(first, inverse, stats[1:2])
     (sx, sy, dpx, dpy), qs, gs, k0, k1 = local_self(core, *refs[:-5])
     px = jnp.exp(sx - top) * inverse
@@ -375,18 +405,13 @@
     pl.when(pl.program_id(0) == 1)(lambda: write(theirs, dq_theirs))
 
 
-def assemble(kernel, name, info, inputs, pooled):
+def assemble(kernel, name, info, inputs, in_specs, pooled, count):
     half = lambda h, info: (info[0] + h) % 2
     rows_out = pl.BlockSpec((ROWS, WIDE), lambda h, info: (0, half(h, info)))
     pool_out = pl.BlockSpec((2, ROWS, WIDE), lambda h, info: (0, 0, half(h, info)))
-    full = ((ROWS, 2 * WIDE), BF16)
+    out_specs, outs = [rows_out] * count, [((ROWS, 2 * WIDE), BF16)] * count
     if pooled:
-        out_specs, outs = [rows_out, pool_out], [full, ((2, ROWS, 2 * WIDE), BF16)]
-    else:
-        out_specs, outs = [rows_out] * 3, [full] * 3
-    in_specs = [whole_spec(x.shape) for x in inputs]
-    if not pooled:
-        in_specs[2:] = [whole_spec((ROWS, WIDE)), whole_spec((ROWS, WIDE), (1, 0))]
+        out_specs, outs = out_specs + [pool_out], outs + [((2, ROWS, 2 * WIDE), BF16)]
     return call(kernel, name, info, in_specs, inputs, out_specs, outs, steps=2)
 
 
@@ -413,11 +438,11 @@
     x_cross = send(x_other, across, True)
     x_pair = send(packed, swap, False)
     queries_in, packed = lax.optimization_barrier((queries, packed))
-    sizes = (4 * ROWS, 2 * ROWS, 2 * ROWS)
-    packed, s_mine, s_other = call(
+    sizes = (4 * ROWS, 2 * ROWS)
+    packed, s_other = call(
         pack_self_kernel, "pack_self", info,
-        [mine_spec] * 2 + [their_spec] * 4,
-        (queries_in, grad_self, queries_in, grad_self, keys, values),
+        [their_spec] * 4,
+        (queries_in, grad_self, keys, values),
         [spec(rows) for rows in sizes],
         [((rows, WIDE), BF16) for rows in sizes],
     )
@@ -457,12 +482,13 @@
     t_cross = send(x_partner, inward, True)
     local_bias, x_own = lax.optimization_barrier((local_bias, x_own))
     self_args = (local_bias,) + self_args[1:]
-    (s_own,) = call(
+    (s_mine,) = call(
         per_head(self_stats_kernel), "self_stats", info, self_specs, self_args,
-        [stat_spec(2 * ROWS)], [stat(2 * ROWS)], flops=0,
-    )
-    s_mine, x_same, x_cross, t_same, t_cross, s_own = lax.optimization_barrier(
-        (s_mine, x_same, x_cross, t_same, t_cross, s_own)
+        [spec(2 * ROWS + STATS)], [((2 * ROWS + STATS, WIDE), BF16)],
+    )
+    stats_block = spec(STATS, 2 * ROWS // STATS)
+    s_mine, x_same, x_cross, t_same, t_cross = lax.optimization_barrier(
+        (s_mine, x_same, x_cross, t_same, t_cross)
     )
     s_same = send(s_mine, lambda d: d - 2, False)
 
@@ -481,8 +507,6 @@
     f_partner = send(x_fin_cross, outward, True)
     s_other, x_kv = lax.optimization_barrier((s_other, x_kv))
     s_cross = send(s_other, lambda d: (d - 2) ^ 1, False)
-    s_own, f_own = lax.optimization_barrier((s_own, f_own))
-    t_self = send(s_own, lambda d: d - 2, False)
     x_kv, s_same = lax.optimization_barrier((x_kv, s_same))
     half_out = spec(3 * ROWS)
     half_shape = ((3 * ROWS, WIDE), BF16)
@@ -502,8 +526,8 @@
     sd, s_kv, s_fin = call(
         per_head(self_remote_kernel), "self_remote", info,
         [bias_spec, spec(ROWS, 0), spec(ROWS, 1), spec(ROWS, 0), spec(ROWS, 1)]
-        + [own_spec(), own_spec(), spec(ROWS, 2), spec(ROWS, 3), stat_spec(2 * ROWS)],
-        (far_bias, s_same, s_same, s_cross, s_cross, keys, values, s_pair, s_pair, t_self),
+        + [own_spec(), own_spec(), spec(ROWS, 2), spec(ROWS, 3), stats_block],
+        (far_bias, s_same, s_same, s_cross, s_cross, keys, values, s_pair, s_pair, s_same),
         [spec(2 * ROWS), kv_out, stat_spec(2 * ROWS)],
         [((2 * ROWS, WIDE), BF16), kv_shape, stat(2 * ROWS)], flops=LONG,
     )
@@ -516,18 +540,22 @@
     x_take = send(x_give, swap, False)
     s_keep, s_give = call(
         per_head(self_local_kernel), "self_local", info,
-        self_specs + [stat_spec(2 * ROWS), stat_spec(2 * ROWS), spec(4 * ROWS)],
-        self_args + (f_self, s_own, s_kv),
+        self_specs + [stat_spec(2 * ROWS), stats_block, spec(4 * ROWS)],
+        self_args + (f_self, s_mine, s_kv),
         [half_out] * 2, [half_shape] * 2, flops=LONG,
     )
+    three, one = whole_spec((3 * ROWS, WIDE)), whole_spec((ROWS, WIDE))
+    second = whole_spec((ROWS, WIDE), (1, 0))
     grad_cq, grad_pool = assemble(
-        cross_final_kernel, "cross_final", info, (x_keep, x_take, xr_same, xr_cross), True
+        cross_final_kernel, "cross_final", info, (x_keep, x_take, xr_same, xr_cross),
+        [three, three, one, one], True, 1,
     )
     s_give, sr, grad_cq = lax.optimization_barrier((s_give, sr, grad_cq))
     s_take = send(s_give, swap, False)
     sr_take = send(sr, swap, False)
     grad_q, grad_k, grad_v = assemble(
-        self_final_kernel, "self_final", info, (s_keep, s_take, sr, sr_take), False
+        self_final_kernel, "self_final", info, (s_keep, s_take, sr, sr_take),
+        [three, three, one, second], False, 3,
     )
     return grad_q, grad_k, grad_v, grad_cq, grad_pool.reshape(pool_kv.shape)
 

time: 107 us -> 104 us (0.972); the launches traced: 104 us -> 103 us
  starting transfers between devices: 32.6 us -> 27.7 us
  waiting for transfers between devices: 23.7 us -> 26.8 us
    ppermute x18 -> x17, starting transfers between devices: 32.6 us -> 27.7 us  [send(): return lax.ppermute(value, 'ctx', pairs)]
    ppermute x18 -> x17, waiting for transfers between devices: 23.7 us -> 26.8 us  [send(): return lax.ppermute(value, 'ctx', pairs)]
  transfers between devices with their start and end apart: 18 -> 17, of which waited for: 7 -> 8; matrix products, arithmetic and copies ran while one was open for 3% -> 3% of each run, Pallas kernels for 37% -> 38%
where the time goes in v12:
time: 104 us; the launch traced here: 103 us
  Pallas kernels  44.1 us (42%)
  starting transfers between devices  27.7 us (27%)
  waiting for transfers between devices  26.8 us (26%)
  other arithmetic  2.41 us (2%)
    pallas_call x10, Pallas kernels, call(): pl.pallas_call(kernel, name=name, grid_spec=pltpu.PrefetchScalarGridSpec(...  44.1 us
    ppermute x17, starting transfers between devices, send(): return lax.ppermute(value, 'ctx', pairs)  27.7 us
    ppermute x17, waiting for transfers between devices, send(): return lax.ppermute(value, 'ctx', pairs)  26.8 us
  transfers between devices with their start and end apart: 17, of which 8 were waited for; matrix products, arithmetic and copies ran while one was open for 3% of the time, Pallas kernels for 38%

profile of v12, /device:TPU:1, one launch (start us, length us, event | category | flops | bytes accessed | tf_op | source)
XLA Modules:
  0.0 102.8 jit_solution(15437027787188907898)
XLA Ops:
  0.6 2.8 %pack_cross.1 = (bf16[1040,512]{1,0:T(8,128)(2,1)}, bf16[528,512]{1,0:T(8,128)(2,1)}, bf16[528,512]{1,0:T(8,128)(2,1)}) custom-call(s32[1]{0:T(128)} %bitcast.info, s32[2,4]{1,0:T(2,128)} %bitcast.8, bf16[256,1024]{1,0:T(8,128)(2,1)} %refs_2_.6, bf16[256,1024]{1,0:T(8,128)(2,1)} %refs_3_.6, bf16[256,1024]{1,0:T(8,128)(2,1)} %refs_2_.6, ...), custom_call_target="tpu_custom_call" | custom-call | tf_op jit(solution)/shard_map/pack_cross/pallas_call | solution.py:84
  3.4 2.6 %collective-permute-start.3 = (bf16[528,512]{1,0:T(8,128)(2,1)}, bf16[528,512]{1,0:T(8,128)(2,1)}, u32[]{:S(2)}, u32[]{:S(2)}) collective-permute-start(bf16[528,512]{1,0:T(8,128)(2,1)} %get-tuple-element.65), channel_id=1, source_target_pairs={{0,15},{1,2},{2,1},{3,4},{4,3},{5,6},{6,5},{7,8},{8,7},{9,10},{10,... | collective-permute-start | bytes 1622024 | tf_op jit(solution)/shard_map/ppermute | solution.py:39
  6.0 1.2 %collective-permute-start.2 = (bf16[528,512]{1,0:T(8,128)(2,1)}, bf16[528,512]{1,0:T(8,128)(2,1)}, u32[]{:S(2)}, u32[]{:S(2)}) collective-permute-start(bf16[528,512]{1,0:T(8,128)(2,1)} %get-tuple-element.59.refs_0_), channel_id=1, source_target_pairs={{0,14},{1,3},{2,0},{3,5},{4,2},{5,7},{6,4},{7,9},{8,6},{9,11},{10,... | collective-permute-start | bytes 1622024 | tf_op jit(solution)/shard_map/ppermute | solution.py:39
  7.3 2.3 %collective-permute-start = (bf16[1040,512]{1,0:T(8,128)(2,1)}, bf16[1040,512]{1,0:T(8,128)(2,1)}, u32[]{:S(2)}, u32[]{:S(2)}) collective-permute-start(bf16[1040,512]{1,0:T(8,128)(2,1)} %get-tuple-element.57), channel_id=1, source_target_pairs={{0,1},{1,0},{2,3},{3,2},{4,5},{5,4},{6,7},{7,6},{8,9},{9,8},{10,11... | collective-permute-start | bytes 3194888 | tf_op jit(solution)/shard_map/ppermute | solution.py:39
  9.5 2.3 %pack_self.1 = (bf16[1024,512]{1,0:T(8,128)(2,1)}, bf16[512,512]{1,0:T(8,128)(2,1)}) custom-call(s32[1]{0:T(128)} %bitcast.info, bf16[256,1024]{1,0:T(8,128)(2,1)} %refs_1_.3, bf16[256,1024]{1,0:T(8,128)(2,1)} %refs_2_.7, bf16[256,1024]{1,0:T(8,128)(2,1)} %refs_3_.7, bf16[256,1024]{1,0:T(8,128)(2,1)} %refs_4_.3), custom_call_target="tpu_custom_call" | custom-call | tf_op jit(solution)/shard_map/pack_self/pallas_call | solution.py:84
  15.3 4.0 %cross_stats.1 = (f32[4,8,256]{2,1,0:T(8,128)}, f32[4,8,256]{2,1,0:T(8,128)}) custom-call(s32[1]{0:T(128)} %bitcast.info, bf16[528,512]{1,0:T(8,128)(2,1)} %get-tuple-element.59.refs_0_, bf16[1040,512]{1,0:T(8,128)(2,1)} %collective-permute-done.refs_1_.refs_5_.refs_6_.refs_7_.refs_8_, bf16[256,1024]{1,0:T(8,128)(2,1)} %refs_2_.6, ...), custom_call_target="tpu_custom_call" | custom-call | tf_op jit(solution)/shard_map/cross_stats/pallas_call | solution.py:84
  20.8 4.4 %self_stats.1.refs_10_ = bf16[576,512]{1,0:T(8,128)(2,1)} custom-call(s32[1]{0:T(128)} %bitcast.info, f32[512,512]{1,0:T(8,128)} %and_select_fusion.1.refs_0_, bf16[256,1024]{1,0:T(8,128)(2,1)} %refs_1_.3, bf16[256,1024]{1,0:T(8,128)(2,1)} %refs_2_.7, bf16[256,1024]{1,0:T(8,128)(2,1)} %refs_3_.7, bf16[256,1024]{1,0:T(8,128)(2,1)} %refs_4_.3, ...), custom_call_target="tpu_custom_call" | custom-call | tf_op jit(solution)/shard_map/self_stats/pallas_call | solution.py:84
  25.6 5.5 %collective-permute-done.2.refs_0_.refs_2_.refs_3_ = bf16[528,512]{1,0:T(8,128)(2,1)} collective-permute-done((bf16[528,512]{1,0:T(8,128)(2,1)}, bf16[528,512]{1,0:T(8,128)(2,1)}, u32[]{:S(2)}, u32[]{:S(2)}) %collective-permute-start.2) | collective-permute-done | bytes 540704 | tf_op jit(solution)/shard_map/ppermute | solution.py:39
  31.4 1.3 %collective-permute-start.8 = (bf16[576,512]{1,0:T(8,128)(2,1)}, bf16[576,512]{1,0:T(8,128)(2,1)}, u32[]{:S(2)}, u32[]{:S(2)}) collective-permute-start(bf16[576,512]{1,0:T(8,128)(2,1)} %self_stats.1.refs_10_), channel_id=1, source_target_pairs={{2,0},{3,1},{4,2},{5,3},{6,4},{7,5},{8,6},{9,7},{10,8},{11,9},{12,... | collective-permute-start | bytes 1769480 | tf_op jit(solution)/shard_map/ppermute | solution.py:39
  32.7 6.0 %cross_remote.1 = (bf16[256,512]{1,0:T(8,128)(2,1)}, bf16[256,512]{1,0:T(8,128)(2,1)}, bf16[1024,512]{1,0:T(8,128)(2,1)}, f32[4,8,256]{2,1,0:T(8,128)}, f32[4,8,256]{2,1,0:T(8,128)}) custom-call(s32[1]{0:T(128)} %bitcast.info, bf16[528,512]{1,0:T(8,128)(2,1)} %collective-permute-done.2.refs_0_.refs_2_.refs_3_, ...), custom_call_target="tpu_custom_call" | custom-call | tf_op jit(solution)/shard_map/cross_remote/pallas_call | solution.py:84
  38.7 6.0 %collective-permute-start.6 = (f32[4,8,256]{2,1,0:T(8,128)}, f32[4,8,256]{2,1,0:T(8,128)}, u32[]{:S(2)}, u32[]{:S(2)}) collective-permute-start(f32[4,8,256]{2,1,0:T(8,128)} %get-tuple-element.71), channel_id=1, source_target_pairs={{0,2},{1,15},{2,4},{3,1},{4,6},{5,3},{6,8},{7,5},{8,10},{9,7},{10,... | collective-permute-start | bytes 98312 | tf_op jit(solution)/shard_map/ppermute | solution.py:39
  44.6 1.3 %collective-permute-start.9 = (bf16[512,512]{1,0:T(8,128)(2,1)}, bf16[512,512]{1,0:T(8,128)(2,1)}, u32[]{:S(2)}, u32[]{:S(2)}) collective-permute-start(bf16[512,512]{1,0:T(8,128)(2,1)} %get-tuple-element.82), channel_id=1, source_target_pairs={{2,1},{3,0},{4,3},{5,2},{6,5},{7,4},{8,7},{9,6},{10,9},{11,8},{12,... | collective-permute-start | bytes 1572872 | tf_op jit(solution)/shard_map/ppermute | solution.py:39
  45.9 2.0 %collective-permute-done.8.refs_1_.refs_2_.refs_9_ = bf16[576,512]{1,0:T(8,128)(2,1)} collective-permute-done((bf16[576,512]{1,0:T(8,128)(2,1)}, bf16[576,512]{1,0:T(8,128)(2,1)}, u32[]{:S(2)}, u32[]{:S(2)}) %collective-permute-start.8) | collective-permute-done | bytes 589856 | tf_op jit(solution)/shard_map/ppermute | solution.py:39
  49.0 13.1 %collective-permute-done.7.refs_10_ = f32[4,8,256]{2,1,0:T(8,128)} collective-permute-done((f32[4,8,256]{2,1,0:T(8,128)}, f32[4,8,256]{2,1,0:T(8,128)}, u32[]{:S(2)}, u32[]{:S(2)}) %collective-permute-start.7) | collective-permute-done | bytes 32800 | tf_op jit(solution)/shard_map/ppermute | solution.py:39
  62.1 6.4 %cross_local.1 = (bf16[768,512]{1,0:T(8,128)(2,1)}, bf16[768,512]{1,0:T(8,128)(2,1)}) custom-call(s32[1]{0:T(128)} %bitcast.info, bf16[528,512]{1,0:T(8,128)(2,1)} %get-tuple-element.59.refs_0_, bf16[1040,512]{1,0:T(8,128)(2,1)} %collective-permute-done.refs_1_.refs_5_.refs_6_.refs_7_.refs_8_, bf16[256,1024]{1,0:T(8,128)(2,1)} %refs_2_.6, ...), custom_call_target="tpu_custom_call" | custom-call | flops 12000000000 | tf_op jit(solution)/shard_map/cross_local/pallas_call | solution.py:84
  68.5 3.0 %collective-permute-start.11 = (bf16[256,512]{1,0:T(8,128)(2,1)}, bf16[256,512]{1,0:T(8,128)(2,1)}, u32[]{:S(2)}, u32[]{:S(2)}) collective-permute-start(bf16[256,512]{1,0:T(8,128)(2,1)} %get-tuple-element.90), channel_id=1, source_target_pairs={{0,15},{1,2},{2,1},{3,4},{4,3},{5,6},{6,5},{7,8},{8,7},{9,10},{10,... | collective-permute-start | bytes 786440 | tf_op jit(solution)/shard_map/ppermute | solution.py:39
  71.6 6.7 %self_remote.1 = (bf16[512,512]{1,0:T(8,128)(2,1)}, bf16[1024,512]{1,0:T(8,128)(2,1)}, f32[4,8,512]{2,1,0:T(8,128)}) custom-call(s32[1]{0:T(128)} %bitcast.info, f32[512,512]{1,0:T(8,128)} %and_select_fusion.refs_0_, bf16[576,512]{1,0:T(8,128)(2,1)} %collective-permute-done.8.refs_1_.refs_2_.refs_9_, ...), custom_call_target="tpu_custom_call" | custom-call | flops 12000000000 | tf_op jit(solution)/shard_map/self_remote/pallas_call | solution.py:84
  78.3 4.7 %collective-permute-start.12 = (f32[4,8,512]{2,1,0:T(8,128)}, f32[4,8,512]{2,1,0:T(8,128)}, u32[]{:S(2)}, u32[]{:S(2)}) collective-permute-start(f32[4,8,512]{2,1,0:T(8,128)} %get-tuple-element.91), channel_id=1, source_target_pairs={{0,2},{1,3},{2,4},{3,5},{4,6},{5,7},{6,8},{7,9},{8,10},{9,11},{10,... | collective-permute-start | bytes 196616 | tf_op jit(solution)/shard_map/ppermute | solution.py:39
  83.0 2.4 %collective-permute-start.13 = (bf16[512,512]{1,0:T(8,128)(2,1)}, bf16[512,512]{1,0:T(8,128)(2,1)}, u32[]{:S(2)}, u32[]{:S(2)}) collective-permute-start(bf16[512,512]{1,0:T(8,128)(2,1)} %get-tuple-element.96), channel_id=1, source_target_pairs={{0,2},{1,3},{2,4},{3,5},{4,6},{5,7},{6,8},{7,9},{8,10},{9,11},{10,... | collective-permute-start | bytes 1572872 | tf_op jit(solution)/shard_map/ppermute | solution.py:39
  85.8 6.1 %self_local.1 = (bf16[768,512]{1,0:T(8,128)(2,1)}, bf16[768,512]{1,0:T(8,128)(2,1)}) custom-call(s32[1]{0:T(128)} %bitcast.info, f32[512,512]{1,0:T(8,128)} %and_select_fusion.1.refs_0_, bf16[256,1024]{1,0:T(8,128)(2,1)} %refs_1_.3, bf16[256,1024]{1,0:T(8,128)(2,1)} %refs_2_.7, bf16[256,1024]{1,0:T(8,128)(2,1)} %refs_3_.7, bf16[256,1024]{1,0:T(8,128)(2,1)} %refs_4_.3, ...), custom_call_target="tpu_custom_call" | custom-call | flops 12000000000 | tf_op jit(solution)/shard_map/self_local/pallas_call | solution.py:84
  91.9 2.8 %cross_final.1 = (bf16[256,1024]{1,0:T(8,128)(2,1)}, bf16[2,256,1024]{2,1,0:T(8,128)(2,1)}) custom-call(s32[1]{0:T(128)} %bitcast.info, bf16[768,512]{1,0:T(8,128)(2,1)} %get-tuple-element.97.mine, bf16[768,512]{1,0:T(8,128)(2,1)} %collective-permute-done.14.theirs, bf16[256,512]{1,0:T(8,128)(2,1)} %collective-permute-done.10.dq_mine, ...), custom_call_target="tpu_custom_call" | custom-call | tf_op jit(solution)/shard_map/cross_final/pallas_call | solution.py:84
  94.8 1.4 %collective-permute-done.13.dq_mine = bf16[512,512]{1,0:T(8,128)(2,1)} collective-permute-done((bf16[512,512]{1,0:T(8,128)(2,1)}, bf16[512,512]{1,0:T(8,128)(2,1)}, u32[]{:S(2)}, u32[]{:S(2)}) %collective-permute-start.13) | collective-permute-done | bytes 524320 | tf_op jit(solution)/shard_map/ppermute | solution.py:39
  97.0 3.0 %collective-permute-done.16.dq_theirs = bf16[512,512]{1,0:T(8,128)(2,1)} collective-permute-done((bf16[512,512]{1,0:T(8,128)(2,1)}, bf16[512,512]{1,0:T(8,128)(2,1)}, u32[]{:S(2)}, u32[]{:S(2)}) %collective-permute-start.16) | collective-permute-done | bytes 524320 | tf_op jit(solution)/shard_map/ppermute | solution.py:39
  100.0 2.7 %self_final.1 = (bf16[256,1024]{1,0:T(8,128)(2,1)}, bf16[256,1024]{1,0:T(8,128)(2,1)}, bf16[256,1024]{1,0:T(8,128)(2,1)}) custom-call(s32[1]{0:T(128)} %bitcast.info, bf16[768,512]{1,0:T(8,128)(2,1)} %get-tuple-element.94.mine, bf16[768,512]{1,0:T(8,128)(2,1)} %collective-permute-done.15.theirs, bf16[512,512]{1,0:T(8,128)(2,1)} %collective-permute-done.13.dq_mine, ...), custom_call_target="tpu_custom_call" | custom-call | tf_op jit(solution)/shard_map/self_final/pallas_call | solution.py:84
  (27 shorter events, 8.1 us)
Async XLA Ops:
  3.4 22.2 %collective-permute-start.3 = (bf16[528,512]{1,0:T(8,128)(2,1)}, bf16[528,512]{1,0:T(8,128)(2,1)}, u32[]{:S(2)}, u32[]{:S(2)}) collective-permute-start(bf16[528,512]{1,0:T(8,128)(2,1)} %get-tuple-element.65), channel_id=1, source_target_pairs={{0,15},{1,2},{2,1},{3,4},{4,3},{5,6},{6,5},{7,8},{8,7},{9,10},{10,... | collective-permute-start | bytes 1622024 | tf_op jit(solution)/shard_map/ppermute | solution.py:39
  6.0 25.1 %collective-permute-start.2 = (bf16[528,512]{1,0:T(8,128)(2,1)}, bf16[528,512]{1,0:T(8,128)(2,1)}, u32[]{:S(2)}, u32[]{:S(2)}) collective-permute-start(bf16[528,512]{1,0:T(8,128)(2,1)} %get-tuple-element.59.refs_0_), channel_id=1, source_target_pairs={{0,14},{1,3},{2,0},{3,5},{4,2},{5,7},{6,4},{7,9},{8,6},{9,11},{10,... | collective-permute-start | bytes 1622024 | tf_op jit(solution)/shard_map/ppermute | solution.py:39
  7.3 8.0 %collective-permute-start = (bf16[1040,512]{1,0:T(8,128)(2,1)}, bf16[1040,512]{1,0:T(8,128)(2,1)}, u32[]{:S(2)}, u32[]{:S(2)}) collective-permute-start(bf16[1040,512]{1,0:T(8,128)(2,1)} %get-tuple-element.57), channel_id=1, source_target_pairs={{0,1},{1,0},{2,3},{3,2},{4,5},{5,4},{6,7},{7,6},{8,9},{9,8},{10,11... | collective-permute-start | bytes 3194888 | tf_op jit(solution)/shard_map/ppermute | solution.py:39
  11.9 8.9 %collective-permute-start.1 = (bf16[1024,512]{1,0:T(8,128)(2,1)}, bf16[1024,512]{1,0:T(8,128)(2,1)}, u32[]{:S(2)}, u32[]{:S(2)}) collective-permute-start(bf16[1024,512]{1,0:T(8,128)(2,1)} %get-tuple-element.64), channel_id=1, source_target_pairs={{0,1},{1,0},{2,3},{3,2},{4,5},{5,4},{6,7},{7,6},{8,9},{9,8},{10,11... | collective-permute-start | bytes 3145736 | tf_op jit(solution)/shard_map/ppermute | solution.py:39
  19.3 11.8 %collective-permute-start.5 = (f32[4,8,256]{2,1,0:T(8,128)}, f32[4,8,256]{2,1,0:T(8,128)}, u32[]{:S(2)}, u32[]{:S(2)}) collective-permute-start(f32[4,8,256]{2,1,0:T(8,128)} %get-tuple-element.66), channel_id=1, source_target_pairs={{0,2},{1,15},{2,4},{3,1},{4,6},{5,3},{6,8},{7,5},{8,10},{9,7},{10,... | collective-permute-start | bytes 98312 | tf_op jit(solution)/shard_map/ppermute | solution.py:39
  20.4 11.0 %collective-permute-start.4 = (f32[4,8,256]{2,1,0:T(8,128)}, f32[4,8,256]{2,1,0:T(8,128)}, u32[]{:S(2)}, u32[]{:S(2)}) collective-permute-start(f32[4,8,256]{2,1,0:T(8,128)} %get-tuple-element.61), channel_id=1, source_target_pairs={{0,14},{1,3},{2,0},{3,5},{4,2},{5,7},{6,4},{7,9},{8,6},{9,11},{10,... | collective-permute-start | bytes 98312 | tf_op jit(solution)/shard_map/ppermute | solution.py:39
  31.4 16.5 %collective-permute-start.8 = (bf16[576,512]{1,0:T(8,128)(2,1)}, bf16[576,512]{1,0:T(8,128)(2,1)}, u32[]{:S(2)}, u32[]{:S(2)}) collective-permute-start(bf16[576,512]{1,0:T(8,128)(2,1)} %self_stats.1.refs_10_), channel_id=1, source_target_pairs={{2,0},{3,1},{4,2},{5,3},{6,4},{7,5},{8,6},{9,7},{10,8},{11,9},{12,... | collective-permute-start | bytes 1769480 | tf_op jit(solution)/shard_map/ppermute | solution.py:39
  38.7 10.3 %collective-permute-start.6 = (f32[4,8,256]{2,1,0:T(8,128)}, f32[4,8,256]{2,1,0:T(8,128)}, u32[]{:S(2)}, u32[]{:S(2)}) collective-permute-start(f32[4,8,256]{2,1,0:T(8,128)} %get-tuple-element.71), channel_id=1, source_target_pairs={{0,2},{1,15},{2,4},{3,1},{4,6},{5,3},{6,8},{7,5},{8,10},{9,7},{10,... | collective-permute-start | bytes 98312 | tf_op jit(solution)/shard_map/ppermute | solution.py:39
  44.6 17.4 %collective-permute-start.7 = (f32[4,8,256]{2,1,0:T(8,128)}, f32[4,8,256]{2,1,0:T(8,128)}, u32[]{:S(2)}, u32[]{:S(2)}) collective-permute-start(f32[4,8,256]{2,1,0:T(8,128)} %get-tuple-element.72), channel_id=1, source_target_pairs={{0,14},{1,3},{2,0},{3,5},{4,2},{5,7},{6,4},{7,9},{8,6},{9,11},{10,... | collective-permute-start | bytes 98312 | tf_op jit(solution)/shard_map/ppermute | solution.py:39
  44.6 23.8 %collective-permute-start.9 = (bf16[512,512]{1,0:T(8,128)(2,1)}, bf16[512,512]{1,0:T(8,128)(2,1)}, u32[]{:S(2)}, u32[]{:S(2)}) collective-permute-start(bf16[512,512]{1,0:T(8,128)(2,1)} %get-tuple-element.82), channel_id=1, source_target_pairs={{2,1},{3,0},{4,3},{5,2},{6,5},{7,4},{8,7},{9,6},{10,9},{11,8},{12,... | collective-permute-start | bytes 1572872 | tf_op jit(solution)/shard_map/ppermute | solution.py:39
  68.5 16.9 %collective-permute-start.10 = (bf16[256,512]{1,0:T(8,128)(2,1)}, bf16[256,512]{1,0:T(8,128)(2,1)}, u32[]{:S(2)}, u32[]{:S(2)}) collective-permute-start(bf16[256,512]{1,0:T(8,128)(2,1)} %get-tuple-element.89), channel_id=1, source_target_pairs={{0,2},{1,15},{2,4},{3,1},{4,6},{5,3},{6,8},{7,5},{8,10},{9,7},{10,... | collective-permute-start | bytes 786440 | tf_op jit(solution)/shard_map/ppermute | solution.py:39
  68.5 16.9 %collective-permute-start.11 = (bf16[256,512]{1,0:T(8,128)(2,1)}, bf16[256,512]{1,0:T(8,128)(2,1)}, u32[]{:S(2)}, u32[]{:S(2)}) collective-permute-start(bf16[256,512]{1,0:T(8,128)(2,1)} %get-tuple-element.90), channel_id=1, source_target_pairs={{0,15},{1,2},{2,1},{3,4},{4,3},{5,6},{6,5},{7,8},{8,7},{9,10},{10,... | collective-permute-start | bytes 786440 | tf_op jit(solution)/shard_map/ppermute | solution.py:39
  78.3 7.1 %collective-permute-start.12 = (f32[4,8,512]{2,1,0:T(8,128)}, f32[4,8,512]{2,1,0:T(8,128)}, u32[]{:S(2)}, u32[]{:S(2)}) collective-permute-start(f32[4,8,512]{2,1,0:T(8,128)} %get-tuple-element.91), channel_id=1, source_target_pairs={{0,2},{1,3},{2,4},{3,5},{4,6},{5,7},{6,8},{7,9},{8,10},{9,11},{10,... | collective-permute-start | bytes 196616 | tf_op jit(solution)/shard_map/ppermute | solution.py:39
  83.0 13.2 %collective-permute-start.13 = (bf16[512,512]{1,0:T(8,128)(2,1)}, bf16[512,512]{1,0:T(8,128)(2,1)}, u32[]{:S(2)}, u32[]{:S(2)}) collective-permute-start(bf16[512,512]{1,0:T(8,128)(2,1)} %get-tuple-element.96), channel_id=1, source_target_pairs={{0,2},{1,3},{2,4},{3,5},{4,6},{5,7},{6,8},{7,9},{8,10},{9,11},{10,... | collective-permute-start | bytes 1572872 | tf_op jit(solution)/shard_map/ppermute | solution.py:39
  85.4 6.5 %collective-permute-start.14 = (bf16[768,512]{1,0:T(8,128)(2,1)}, bf16[768,512]{1,0:T(8,128)(2,1)}, u32[]{:S(2)}, u32[]{:S(2)}) collective-permute-start(bf16[768,512]{1,0:T(8,128)(2,1)} %get-tuple-element.98), channel_id=1, source_target_pairs={{0,1},{1,0},{2,3},{3,2},{4,5},{5,4},{6,7},{7,6},{8,9},{9,8},{10,11... | collective-permute-start | bytes 2359304 | tf_op jit(solution)/shard_map/ppermute | solution.py:39
  96.2 3.9 %collective-permute-start.15 = (bf16[768,512]{1,0:T(8,128)(2,1)}, bf16[768,512]{1,0:T(8,128)(2,1)}, u32[]{:S(2)}, u32[]{:S(2)}) collective-permute-start(bf16[768,512]{1,0:T(8,128)(2,1)} %get-tuple-element.102), channel_id=1, source_target_pairs={{0,1},{1,0},{2,3},{3,2},{4,5},{5,4},{6,7},{7,6},{8,9},{9,8},{10,11... | collective-permute-start | bytes 2359304 | tf_op jit(solution)/shard_map/ppermute | solution.py:39
  97.0 3.0 %collective-permute-start.16 = (bf16[512,512]{1,0:T(8,128)(2,1)}, bf16[512,512]{1,0:T(8,128)(2,1)}, u32[]{:S(2)}, u32[]{:S(2)}) collective-permute-start(bf16[512,512]{1,0:T(8,128)(2,1)} %collective-permute-done.13.dq_mine), channel_id=1, source_target_pairs={{0,1},{1,0},{2,3},{3,2},{4,5},{5,4},{6,7},{7,6},{8,9},{9,8},{10,11... | collective-permute-start | bytes 1572872 | tf_op jit(solution)/shard_map/ppermute | solution.py:39

commit v13 on v11

--- a/solution.py
+++ b/solution.py
@@ -353,12 +353,18 @@
         theirs[index * ROWS : (index + 1) * ROWS] = grad[ROWS:].astype(BF16)
 
 
-def self_final_kernel(info, mine, theirs, dq_mine, dq_theirs, *outs):
+def kv_final_kernel(info, mine, theirs, *outs):
+    def write(source):
+        outs[0][...] = source[ROWS : 2 * ROWS]
+        outs[1][...] = source[2 * ROWS :]
+
+    pl.when(pl.program_id(0) == 0)(lambda: write(mine))
+    pl.when(pl.program_id(0) == 1)(lambda: write(theirs))
+
+
+def query_final_kernel(info, mine, theirs, dq_mine, dq_theirs, out):
     def write(source, extra):
-        dq = source[:ROWS].astype(F32) + extra[...].astype(F32)
-        outs[0][...] = dq.astype(BF16)
-        outs[1][...] = source[ROWS : 2 * ROWS]
-        outs[2][...] = source[2 * ROWS :]
+        out[...] = (source[...].astype(F32) + extra[...].astype(F32)).astype(BF16)
 
     pl.when(pl.program_id(0) == 0)(lambda: write(mine, dq_mine))
     pl.when(pl.program_id(0) == 1)(lambda: write(theirs, dq_theirs))
@@ -375,18 +381,13 @@
     pl.when(pl.program_id(0) == 1)(lambda: write(theirs, dq_theirs))
 
 
-def assemble(kernel, name, info, inputs, pooled):
+def assemble(kernel, name, info, inputs, in_specs, pooled, count):
     half = lambda h, info: (info[0] + h) % 2
     rows_out = pl.BlockSpec((ROWS, WIDE), lambda h, info: (0, half(h, info)))
     pool_out = pl.BlockSpec((2, ROWS, WIDE), lambda h, info: (0, 0, half(h, info)))
-    full = ((ROWS, 2 * WIDE), BF16)
+    out_specs, outs = [rows_out] * count, [((ROWS, 2 * WIDE), BF16)] * count
     if pooled:
-        out_specs, outs = [rows_out, pool_out], [full, ((2, ROWS, 2 * WIDE), BF16)]
-    else:
-        out_specs, outs = [rows_out] * 3, [full] * 3
-    in_specs = [whole_spec(x.shape) for x in inputs]
-    if not pooled:
-        in_specs[2:] = [whole_spec((ROWS, WIDE)), whole_spec((ROWS, WIDE), (1, 0))]
+        out_specs, outs = out_specs + [pool_out], outs + [((2, ROWS, 2 * WIDE), BF16)]
     return call(kernel, name, info, in_specs, inputs, out_specs, outs, steps=2)
 
 
@@ -519,14 +520,21 @@
         self_args + (f_self, s_own, s_kv),
         [half_out] * 2, [half_shape] * 2, flops=LONG,
     )
+    three, one = whole_spec((3 * ROWS, WIDE)), whole_spec((ROWS, WIDE))
+    second = whole_spec((ROWS, WIDE), (1, 0))
+    s_take = send(s_give, swap, False)
     grad_cq, grad_pool = assemble(
-        cross_final_kernel, "cross_final", info, (x_keep, x_take, xr_same, xr_cross), True
-    )
-    s_give, sr, grad_cq = lax.optimization_barrier((s_give, sr, grad_cq))
-    s_take = send(s_give, swap, False)
+        cross_final_kernel, "cross_final", info, (x_keep, x_take, xr_same, xr_cross),
+        [three, three, one, one], True, 1,
+    )
+    grad_k, grad_v = assemble(
+        kv_final_kernel, "kv_final", info, (s_keep, s_take), [three, three], False, 2
+    )
+    sr, grad_cq = lax.optimization_barrier((sr, grad_cq))
     sr_take = send(sr, swap, False)
-    grad_q, grad_k, grad_v = assemble(
-        self_final_kernel, "self_final", info, (s_keep, s_take, sr, sr_take), False
+    (grad_q,) = assemble(
+        query_final_kernel, "query_final", info, (s_keep, s_take, sr, sr_take),
+        [one, one, one, second], False, 1,
     )
     return grad_q, grad_k, grad_v, grad_cq, grad_pool.reshape(pool_kv.shape)
 

time: 98.1 us -> 96.9 us (0.988)
  waiting for transfers between devices: 18.1 us -> 15.1 us
  Pallas kernels: 44.1 us -> 45.8 us
    ppermute x18, waiting for transfers between devices: 18.1 us -> 15.1 us  [send(): return lax.ppermute(value, 'ctx', pairs)]
    pallas_call x10 -> x11, Pallas kernels: 44.1 us -> 45.8 us  [call(): pl.pallas_call(kernel, name=name, grid_spec=pltpu.PrefetchScalarGridSpec(...]
  transfers between devices with their start and end apart: 18 -> 18, of which waited for: 6 -> 5; matrix products, arithmetic and copies ran while one was open for 3% -> 3% of each run, Pallas kernels for 40% -> 43%
where the time goes in v13:
time: 96.9 us; the launch traced here: 95.1 us
  Pallas kernels  45.8 us (47%)
  starting transfers between devices  30.1 us (31%)
  waiting for transfers between devices  15.1 us (16%)
  other arithmetic  2.4 us (2%)
    pallas_call x11, Pallas kernels, call(): pl.pallas_call(kernel, name=name, grid_spec=pltpu.PrefetchScalarGridSpec(...  45.8 us
    ppermute x18, starting transfers between devices, send(): return lax.ppermute(value, 'ctx', pairs)  30.1 us
    ppermute x18, waiting for transfers between devices, send(): return lax.ppermute(value, 'ctx', pairs)  15.1 us
  transfers between devices with their start and end apart: 18, of which 5 were waited for; matrix products, arithmetic and copies ran while one was open for 3% of the time, Pallas kernels for 43%

profile of v13, /device:TPU:1, one launch (start us, length us, event | category | flops | bytes accessed | tf_op | source)
XLA Modules:
  0.0 95.1 jit_solution(2583480194233469183)
XLA Ops:
  0.6 2.7 %pack_cross.1 = (bf16[1040,512]{1,0:T(8,128)(2,1)}, bf16[528,512]{1,0:T(8,128)(2,1)}, bf16[528,512]{1,0:T(8,128)(2,1)}) custom-call(s32[1]{0:T(128)} %bitcast.info, s32[2,4]{1,0:T(2,128)} %bitcast.8, bf16[256,1024]{1,0:T(8,128)(2,1)} %refs_2_.6, bf16[256,1024]{1,0:T(8,128)(2,1)} %refs_3_.6, bf16[256,1024]{1,0:T(8,128)(2,1)} %refs_2_.6, ...), custom_call_target="tpu_custom_call" | custom-call | tf_op jit(solution)/shard_map/pack_cross/pallas_call | solution.py:83
  3.4 2.6 %collective-permute-start.3 = (bf16[528,512]{1,0:T(8,128)(2,1)}, bf16[528,512]{1,0:T(8,128)(2,1)}, u32[]{:S(2)}, u32[]{:S(2)}) collective-permute-start(bf16[528,512]{1,0:T(8,128)(2,1)} %get-tuple-element.67), channel_id=1, source_target_pairs={{0,15},{1,2},{2,1},{3,4},{4,3},{5,6},{6,5},{7,8},{8,7},{9,10},{10,... | collective-permute-start | bytes 1622024 | tf_op jit(solution)/shard_map/ppermute | solution.py:38
  6.0 1.2 %collective-permute-start.2 = (bf16[528,512]{1,0:T(8,128)(2,1)}, bf16[528,512]{1,0:T(8,128)(2,1)}, u32[]{:S(2)}, u32[]{:S(2)}) collective-permute-start(bf16[528,512]{1,0:T(8,128)(2,1)} %get-tuple-element.60.refs_0_), channel_id=1, source_target_pairs={{0,14},{1,3},{2,0},{3,5},{4,2},{5,7},{6,4},{7,9},{8,6},{9,11},{10,... | collective-permute-start | bytes 1622024 | tf_op jit(solution)/shard_map/ppermute | solution.py:38
  7.2 2.3 %collective-permute-start = (bf16[1040,512]{1,0:T(8,128)(2,1)}, bf16[1040,512]{1,0:T(8,128)(2,1)}, u32[]{:S(2)}, u32[]{:S(2)}) collective-permute-start(bf16[1040,512]{1,0:T(8,128)(2,1)} %get-tuple-element.58), channel_id=1, source_target_pairs={{0,1},{1,0},{2,3},{3,2},{4,5},{5,4},{6,7},{7,6},{8,9},{9,8},{10,11... | collective-permute-start | bytes 3194888 | tf_op jit(solution)/shard_map/ppermute | solution.py:38
  9.5 2.6 %pack_self.1 = (bf16[1024,512]{1,0:T(8,128)(2,1)}, bf16[512,512]{1,0:T(8,128)(2,1)}, bf16[512,512]{1,0:T(8,128)(2,1)}) custom-call(s32[1]{0:T(128)} %bitcast.info, bf16[256,1024]{1,0:T(8,128)(2,1)} %refs_1_.3, bf16[256,1024]{1,0:T(8,128)(2,1)} %refs_2_.7, bf16[256,1024]{1,0:T(8,128)(2,1)} %refs_1_.3, bf16[256,1024]{1,0:T(8,128)(2,1)} %refs_2_.7, ...), custom_call_target="tpu_custom_call" | custom-call | tf_op jit(solution)/shard_map/pack_self/pallas_call | solution.py:83
  15.5 4.0 %cross_stats.1 = (f32[4,8,256]{2,1,0:T(8,128)}, f32[4,8,256]{2,1,0:T(8,128)}) custom-call(s32[1]{0:T(128)} %bitcast.info, bf16[528,512]{1,0:T(8,128)(2,1)} %get-tuple-element.60.refs_0_, bf16[1040,512]{1,0:T(8,128)(2,1)} %collective-permute-done.refs_1_.refs_5_.refs_6_.refs_7_.refs_8_, bf16[256,1024]{1,0:T(8,128)(2,1)} %refs_2_.6, ...), custom_call_target="tpu_custom_call" | custom-call | tf_op jit(solution)/shard_map/cross_stats/pallas_call | solution.py:83
  21.0 4.2 %self_stats.1.refs_10_ = f32[4,8,512]{2,1,0:T(8,128)} custom-call(s32[1]{0:T(128)} %bitcast.info, f32[512,512]{1,0:T(8,128)} %and_select_fusion.1.refs_0_, bf16[256,1024]{1,0:T(8,128)(2,1)} %refs_1_.3, bf16[256,1024]{1,0:T(8,128)(2,1)} %refs_2_.7, bf16[256,1024]{1,0:T(8,128)(2,1)} %refs_3_.7, bf16[256,1024]{1,0:T(8,128)(2,1)} %refs_4_.3, ...), custom_call_target="tpu_custom_call" | custom-call | tf_op jit(solution)/shard_map/self_stats/pallas_call | solution.py:83
  25.6 5.5 %collective-permute-done.2.refs_0_.refs_2_.refs_3_ = bf16[528,512]{1,0:T(8,128)(2,1)} collective-permute-done((bf16[528,512]{1,0:T(8,128)(2,1)}, bf16[528,512]{1,0:T(8,128)(2,1)}, u32[]{:S(2)}, u32[]{:S(2)}) %collective-permute-start.2) | collective-permute-done | bytes 540704 | tf_op jit(solution)/shard_map/ppermute | solution.py:38
  31.4 1.3 %collective-permute-start.8 = (bf16[512,512]{1,0:T(8,128)(2,1)}, bf16[512,512]{1,0:T(8,128)(2,1)}, u32[]{:S(2)}, u32[]{:S(2)}) collective-permute-start(bf16[512,512]{1,0:T(8,128)(2,1)} %get-tuple-element.78), channel_id=1, source_target_pairs={{2,0},{3,1},{4,2},{5,3},{6,4},{7,5},{8,6},{9,7},{10,8},{11,9},{12,... | collective-permute-start | bytes 1572872 | tf_op jit(solution)/shard_map/ppermute | solution.py:38
  32.7 1.3 %collective-permute-start.9 = (f32[4,8,512]{2,1,0:T(8,128)}, f32[4,8,512]{2,1,0:T(8,128)}, u32[]{:S(2)}, u32[]{:S(2)}) collective-permute-start(f32[4,8,512]{2,1,0:T(8,128)} %self_stats.1.refs_10_), channel_id=1, source_target_pairs={{2,0},{3,1},{4,2},{5,3},{6,4},{7,5},{8,6},{9,7},{10,8},{11,9},{12,... | collective-permute-start | bytes 196616 | tf_op jit(solution)/shard_map/ppermute | solution.py:38
  34.0 5.9 %cross_remote.1 = (bf16[256,512]{1,0:T(8,128)(2,1)}, bf16[256,512]{1,0:T(8,128)(2,1)}, bf16[1024,512]{1,0:T(8,128)(2,1)}, f32[4,8,256]{2,1,0:T(8,128)}, f32[4,8,256]{2,1,0:T(8,128)}) custom-call(s32[1]{0:T(128)} %bitcast.info, bf16[528,512]{1,0:T(8,128)(2,1)} %collective-permute-done.2.refs_0_.refs_2_.refs_3_, ...), custom_call_target="tpu_custom_call" | custom-call | tf_op jit(solution)/shard_map/cross_remote/pallas_call | solution.py:83
  39.9 8.2 %collective-permute-start.6 = (f32[4,8,256]{2,1,0:T(8,128)}, f32[4,8,256]{2,1,0:T(8,128)}, u32[]{:S(2)}, u32[]{:S(2)}) collective-permute-start(f32[4,8,256]{2,1,0:T(8,128)} %get-tuple-element.73), channel_id=1, source_target_pairs={{0,2},{1,15},{2,4},{3,1},{4,6},{5,3},{6,8},{7,5},{8,10},{9,7},{10,... | collective-permute-start | bytes 98312 | tf_op jit(solution)/shard_map/ppermute | solution.py:38
  48.1 1.3 %collective-permute-start.10 = (bf16[512,512]{1,0:T(8,128)(2,1)}, bf16[512,512]{1,0:T(8,128)(2,1)}, u32[]{:S(2)}, u32[]{:S(2)}) collective-permute-start(bf16[512,512]{1,0:T(8,128)(2,1)} %get-tuple-element.84), channel_id=1, source_target_pairs={{2,1},{3,0},{4,3},{5,2},{6,5},{7,4},{8,7},{9,6},{10,9},{11,8},{12,... | collective-permute-start | bytes 1572872 | tf_op jit(solution)/shard_map/ppermute | solution.py:38
  49.4 4.5 %collective-permute-done.7.refs_10_ = f32[4,8,256]{2,1,0:T(8,128)} collective-permute-done((f32[4,8,256]{2,1,0:T(8,128)}, f32[4,8,256]{2,1,0:T(8,128)}, u32[]{:S(2)}, u32[]{:S(2)}) %collective-permute-start.7) | collective-permute-done | bytes 32800 | tf_op jit(solution)/shard_map/ppermute | solution.py:38
  54.0 6.4 %cross_local.1 = (bf16[768,512]{1,0:T(8,128)(2,1)}, bf16[768,512]{1,0:T(8,128)(2,1)}) custom-call(s32[1]{0:T(128)} %bitcast.info, bf16[528,512]{1,0:T(8,128)(2,1)} %get-tuple-element.60.refs_0_, bf16[1040,512]{1,0:T(8,128)(2,1)} %collective-permute-done.refs_1_.refs_5_.refs_6_.refs_7_.refs_8_, bf16[256,1024]{1,0:T(8,128)(2,1)} %refs_2_.6, ...), custom_call_target="tpu_custom_call" | custom-call | flops 12000000000 | tf_op jit(solution)/shard_map/cross_local/pallas_call | solution.py:83
  60.4 4.3 %collective-permute-done.10.refs_3_.refs_4_ = bf16[512,512]{1,0:T(8,128)(2,1)} collective-permute-done((bf16[512,512]{1,0:T(8,128)(2,1)}, bf16[512,512]{1,0:T(8,128)(2,1)}, u32[]{:S(2)}, u32[]{:S(2)}) %collective-permute-start.10) | collective-permute-done | bytes 524320 | tf_op jit(solution)/shard_map/ppermute | solution.py:38
  65.2 6.7 %self_remote.1 = (bf16[512,512]{1,0:T(8,128)(2,1)}, bf16[1024,512]{1,0:T(8,128)(2,1)}, f32[4,8,512]{2,1,0:T(8,128)}) custom-call(s32[1]{0:T(128)} %bitcast.info, f32[512,512]{1,0:T(8,128)} %and_select_fusion.refs_0_, bf16[512,512]{1,0:T(8,128)(2,1)} %collective-permute-done.8.refs_1_.refs_2_, bf16[512,512]{1,0:T(8,128)(2,1)} %collective-permute-done.8.refs_1_.refs_2_, ...), custom_call_target="tpu_custom_call" | custom-call | flops 12000000000 | tf_op jit(solution)/shard_map/self_remote/pallas_call | solution.py:83
  71.9 4.0 %collective-permute-start.13 = (f32[4,8,512]{2,1,0:T(8,128)}, f32[4,8,512]{2,1,0:T(8,128)}, u32[]{:S(2)}, u32[]{:S(2)}) collective-permute-start(f32[4,8,512]{2,1,0:T(8,128)} %get-tuple-element.94), channel_id=1, source_target_pairs={{0,2},{1,3},{2,4},{3,5},{4,6},{5,7},{6,8},{7,9},{8,10},{9,11},{10,... | collective-permute-start | bytes 196616 | tf_op jit(solution)/shard_map/ppermute | solution.py:38
  75.9 3.1 %collective-permute-start.15 = (bf16[512,512]{1,0:T(8,128)(2,1)}, bf16[512,512]{1,0:T(8,128)(2,1)}, u32[]{:S(2)}, u32[]{:S(2)}) collective-permute-start(bf16[512,512]{1,0:T(8,128)(2,1)} %get-tuple-element.100), channel_id=1, source_target_pairs={{0,2},{1,3},{2,4},{3,5},{4,6},{5,7},{6,8},{7,9},{8,10},{9,11},{10,... | collective-permute-start | bytes 1572872 | tf_op jit(solution)/shard_map/ppermute | solution.py:38
  79.0 1.9 %collective-permute-start.16 = (bf16[768,512]{1,0:T(8,128)(2,1)}, bf16[768,512]{1,0:T(8,128)(2,1)}, u32[]{:S(2)}, u32[]{:S(2)}) collective-permute-start(bf16[768,512]{1,0:T(8,128)(2,1)} %get-tuple-element.102), channel_id=1, source_target_pairs={{0,1},{1,0},{2,3},{3,2},{4,5},{5,4},{6,7},{7,6},{8,9},{9,8},{10,11... | collective-permute-start | bytes 2359304 | tf_op jit(solution)/shard_map/ppermute | solution.py:38
  80.8 6.1 %self_local.1 = (bf16[768,512]{1,0:T(8,128)(2,1)}, bf16[768,512]{1,0:T(8,128)(2,1)}) custom-call(s32[1]{0:T(128)} %bitcast.info, f32[512,512]{1,0:T(8,128)} %and_select_fusion.1.refs_0_, bf16[256,1024]{1,0:T(8,128)(2,1)} %refs_1_.3, bf16[256,1024]{1,0:T(8,128)(2,1)} %refs_2_.7, bf16[256,1024]{1,0:T(8,128)(2,1)} %refs_3_.7, bf16[256,1024]{1,0:T(8,128)(2,1)} %refs_4_.3, ...), custom_call_target="tpu_custom_call" | custom-call | flops 12000000000 | tf_op jit(solution)/shard_map/self_local/pallas_call | solution.py:83
  87.0 2.8 %cross_final.1 = (bf16[256,1024]{1,0:T(8,128)(2,1)}, bf16[2,256,1024]{2,1,0:T(8,128)(2,1)}) custom-call(s32[1]{0:T(128)} %bitcast.info, bf16[768,512]{1,0:T(8,128)(2,1)} %get-tuple-element.101.mine, bf16[768,512]{1,0:T(8,128)(2,1)} %collective-permute-done.16.theirs, bf16[256,512]{1,0:T(8,128)(2,1)} %collective-permute-done.11.dq_mine, ...), custom_call_target="tpu_custom_call" | custom-call | tf_op jit(solution)/shard_map/cross_final/pallas_call | solution.py:83
  90.6 2.4 %kv_final.1 = (bf16[256,1024]{1,0:T(8,128)(2,1)}, bf16[256,1024]{1,0:T(8,128)(2,1)}) custom-call(s32[1]{0:T(128)} %bitcast.info, bf16[768,512]{1,0:T(8,128)(2,1)} %get-tuple-element.98.mine, bf16[768,512]{1,0:T(8,128)(2,1)} %collective-permute-done.14.theirs), custom_call_target="tpu_custom_call" | custom-call | tf_op jit(solution)/shard_map/kv_final/pallas_call | solution.py:83
  93.0 2.1 %query_final.1 = bf16[256,1024]{1,0:T(8,128)(2,1)} custom-call(s32[1]{0:T(128)} %bitcast.info, bf16[768,512]{1,0:T(8,128)(2,1)} %get-tuple-element.98.mine, bf16[768,512]{1,0:T(8,128)(2,1)} %collective-permute-done.14.theirs, bf16[512,512]{1,0:T(8,128)(2,1)} %collective-permute-done.15.dq_mine, bf16[512,512]{1,0:T(8,128)(2,1)} %collective-permute-done.17.dq_theirs), custom_call_target="tpu_custom_call" | custom-call | tf_op jit(solution)/shard_map/query_final/pallas_call | solution.py:83
  (30 shorter events, 7.1 us)
Async XLA Ops:
  3.4 22.2 %collective-permute-start.3 = (bf16[528,512]{1,0:T(8,128)(2,1)}, bf16[528,512]{1,0:T(8,128)(2,1)}, u32[]{:S(2)}, u32[]{:S(2)}) collective-permute-start(bf16[528,512]{1,0:T(8,128)(2,1)} %get-tuple-element.67), channel_id=1, source_target_pairs={{0,15},{1,2},{2,1},{3,4},{4,3},{5,6},{6,5},{7,8},{8,7},{9,10},{10,... | collective-permute-start | bytes 1622024 | tf_op jit(solution)/shard_map/ppermute | solution.py:38
  6.0 25.1 %collective-permute-start.2 = (bf16[528,512]{1,0:T(8,128)(2,1)}, bf16[528,512]{1,0:T(8,128)(2,1)}, u32[]{:S(2)}, u32[]{:S(2)}) collective-permute-start(bf16[528,512]{1,0:T(8,128)(2,1)} %get-tuple-element.60.refs_0_), channel_id=1, source_target_pairs={{0,14},{1,3},{2,0},{3,5},{4,2},{5,7},{6,4},{7,9},{8,6},{9,11},{10,... | collective-permute-start | bytes 1622024 | tf_op jit(solution)/shard_map/ppermute | solution.py:38
  7.2 8.3 %collective-permute-start = (bf16[1040,512]{1,0:T(8,128)(2,1)}, bf16[1040,512]{1,0:T(8,128)(2,1)}, u32[]{:S(2)}, u32[]{:S(2)}) collective-permute-start(bf16[1040,512]{1,0:T(8,128)(2,1)} %get-tuple-element.58), channel_id=1, source_target_pairs={{0,1},{1,0},{2,3},{3,2},{4,5},{5,4},{6,7},{7,6},{8,9},{9,8},{10,11... | collective-permute-start | bytes 3194888 | tf_op jit(solution)/shard_map/ppermute | solution.py:38
  12.1 9.0 %collective-permute-start.1 = (bf16[1024,512]{1,0:T(8,128)(2,1)}, bf16[1024,512]{1,0:T(8,128)(2,1)}, u32[]{:S(2)}, u32[]{:S(2)}) collective-permute-start(bf16[1024,512]{1,0:T(8,128)(2,1)} %get-tuple-element.65), channel_id=1, source_target_pairs={{0,1},{1,0},{2,3},{3,2},{4,5},{5,4},{6,7},{7,6},{8,9},{9,8},{10,11... | collective-permute-start | bytes 3145736 | tf_op jit(solution)/shard_map/ppermute | solution.py:38
  19.5 11.5 %collective-permute-start.5 = (f32[4,8,256]{2,1,0:T(8,128)}, f32[4,8,256]{2,1,0:T(8,128)}, u32[]{:S(2)}, u32[]{:S(2)}) collective-permute-start(f32[4,8,256]{2,1,0:T(8,128)} %get-tuple-element.68), channel_id=1, source_target_pairs={{0,2},{1,15},{2,4},{3,1},{4,6},{5,3},{6,8},{7,5},{8,10},{9,7},{10,... | collective-permute-start | bytes 98312 | tf_op jit(solution)/shard_map/ppermute | solution.py:38
  20.7 10.7 %collective-permute-start.4 = (f32[4,8,256]{2,1,0:T(8,128)}, f32[4,8,256]{2,1,0:T(8,128)}, u32[]{:S(2)}, u32[]{:S(2)}) collective-permute-start(f32[4,8,256]{2,1,0:T(8,128)} %get-tuple-element.62), channel_id=1, source_target_pairs={{0,14},{1,3},{2,0},{3,5},{4,2},{5,7},{6,4},{7,9},{8,6},{9,11},{10,... | collective-permute-start | bytes 98312 | tf_op jit(solution)/shard_map/ppermute | solution.py:38
  31.4 18.0 %collective-permute-start.8 = (bf16[512,512]{1,0:T(8,128)(2,1)}, bf16[512,512]{1,0:T(8,128)(2,1)}, u32[]{:S(2)}, u32[]{:S(2)}) collective-permute-start(bf16[512,512]{1,0:T(8,128)(2,1)} %get-tuple-element.78), channel_id=1, source_target_pairs={{2,0},{3,1},{4,2},{5,3},{6,4},{7,5},{8,6},{9,7},{10,8},{11,9},{12,... | collective-permute-start | bytes 1572872 | tf_op jit(solution)/shard_map/ppermute | solution.py:38
  32.7 16.7 %collective-permute-start.9 = (f32[4,8,512]{2,1,0:T(8,128)}, f32[4,8,512]{2,1,0:T(8,128)}, u32[]{:S(2)}, u32[]{:S(2)}) collective-permute-start(f32[4,8,512]{2,1,0:T(8,128)} %self_stats.1.refs_10_), channel_id=1, source_target_pairs={{2,0},{3,1},{4,2},{5,3},{6,4},{7,5},{8,6},{9,7},{10,8},{11,9},{12,... | collective-permute-start | bytes 196616 | tf_op jit(solution)/shard_map/ppermute | solution.py:38
  39.9 9.5 %collective-permute-start.6 = (f32[4,8,256]{2,1,0:T(8,128)}, f32[4,8,256]{2,1,0:T(8,128)}, u32[]{:S(2)}, u32[]{:S(2)}) collective-permute-start(f32[4,8,256]{2,1,0:T(8,128)} %get-tuple-element.73), channel_id=1, source_target_pairs={{0,2},{1,15},{2,4},{3,1},{4,6},{5,3},{6,8},{7,5},{8,10},{9,7},{10,... | collective-permute-start | bytes 98312 | tf_op jit(solution)/shard_map/ppermute | solution.py:38
  48.1 5.9 %collective-permute-start.7 = (f32[4,8,256]{2,1,0:T(8,128)}, f32[4,8,256]{2,1,0:T(8,128)}, u32[]{:S(2)}, u32[]{:S(2)}) collective-permute-start(f32[4,8,256]{2,1,0:T(8,128)} %get-tuple-element.74), channel_id=1, source_target_pairs={{0,14},{1,3},{2,0},{3,5},{4,2},{5,7},{6,4},{7,9},{8,6},{9,11},{10,... | collective-permute-start | bytes 98312 | tf_op jit(solution)/shard_map/ppermute | solution.py:38
  48.1 16.6 %collective-permute-start.10 = (bf16[512,512]{1,0:T(8,128)(2,1)}, bf16[512,512]{1,0:T(8,128)(2,1)}, u32[]{:S(2)}, u32[]{:S(2)}) collective-permute-start(bf16[512,512]{1,0:T(8,128)(2,1)} %get-tuple-element.84), channel_id=1, source_target_pairs={{2,1},{3,0},{4,3},{5,2},{6,5},{7,4},{8,7},{9,6},{10,9},{11,8},{12,... | collective-permute-start | bytes 1572872 | tf_op jit(solution)/shard_map/ppermute | solution.py:38
  64.7 14.3 %collective-permute-start.11 = (bf16[256,512]{1,0:T(8,128)(2,1)}, bf16[256,512]{1,0:T(8,128)(2,1)}, u32[]{:S(2)}, u32[]{:S(2)}) collective-permute-start(bf16[256,512]{1,0:T(8,128)(2,1)} %get-tuple-element.92), channel_id=1, source_target_pairs={{0,2},{1,15},{2,4},{3,1},{4,6},{5,3},{6,8},{7,5},{8,10},{9,7},{10,... | collective-permute-start | bytes 786440 | tf_op jit(solution)/shard_map/ppermute | solution.py:38
  64.7 14.3 %collective-permute-start.12 = (bf16[256,512]{1,0:T(8,128)(2,1)}, bf16[256,512]{1,0:T(8,128)(2,1)}, u32[]{:S(2)}, u32[]{:S(2)}) collective-permute-start(bf16[256,512]{1,0:T(8,128)(2,1)} %get-tuple-element.93), channel_id=1, source_target_pairs={{0,15},{1,2},{2,1},{3,4},{4,3},{5,6},{6,5},{7,8},{8,7},{9,10},{10,... | collective-permute-start | bytes 786440 | tf_op jit(solution)/shard_map/ppermute | solution.py:38
  71.9 7.1 %collective-permute-start.13 = (f32[4,8,512]{2,1,0:T(8,128)}, f32[4,8,512]{2,1,0:T(8,128)}, u32[]{:S(2)}, u32[]{:S(2)}) collective-permute-start(f32[4,8,512]{2,1,0:T(8,128)} %get-tuple-element.94), channel_id=1, source_target_pairs={{0,2},{1,3},{2,4},{3,5},{4,6},{5,7},{6,8},{7,9},{8,10},{9,11},{10,... | collective-permute-start | bytes 196616 | tf_op jit(solution)/shard_map/ppermute | solution.py:38
  75.9 13.9 %collective-permute-start.15 = (bf16[512,512]{1,0:T(8,128)(2,1)}, bf16[512,512]{1,0:T(8,128)(2,1)}, u32[]{:S(2)}, u32[]{:S(2)}) collective-permute-start(bf16[512,512]{1,0:T(8,128)(2,1)} %get-tuple-element.100), channel_id=1, source_target_pairs={{0,2},{1,3},{2,4},{3,5},{4,6},{5,7},{6,8},{7,9},{8,10},{9,11},{10,... | collective-permute-start | bytes 1572872 | tf_op jit(solution)/shard_map/ppermute | solution.py:38
  79.0 8.0 %collective-permute-start.16 = (bf16[768,512]{1,0:T(8,128)(2,1)}, bf16[768,512]{1,0:T(8,128)(2,1)}, u32[]{:S(2)}, u32[]{:S(2)}) collective-permute-start(bf16[768,512]{1,0:T(8,128)(2,1)} %get-tuple-element.102), channel_id=1, source_target_pairs={{0,1},{1,0},{2,3},{3,2},{4,5},{5,4},{6,7},{7,6},{8,9},{9,8},{10,11... | collective-permute-start | bytes 2359304 | tf_op jit(solution)/shard_map/ppermute | solution.py:38
  86.9 3.7 %collective-permute-start.14 = (bf16[768,512]{1,0:T(8,128)(2,1)}, bf16[768,512]{1,0:T(8,128)(2,1)}, u32[]{:S(2)}, u32[]{:S(2)}) collective-permute-start(bf16[768,512]{1,0:T(8,128)(2,1)} %get-tuple-element.99), channel_id=1, source_target_pairs={{0,1},{1,0},{2,3},{3,2},{4,5},{5,4},{6,7},{7,6},{8,9},{9,8},{10,11... | collective-permute-start | bytes 2359304 | tf_op jit(solution)/shard_map/ppermute | solution.py:38
  89.8 3.2 %collective-permute-start.17 = (bf16[512,512]{1,0:T(8,128)(2,1)}, bf16[512,512]{1,0:T(8,128)(2,1)}, u32[]{:S(2)}, u32[]{:S(2)}) collective-permute-start(bf16[512,512]{1,0:T(8,128)(2,1)} %collective-permute-done.15.dq_mine), channel_id=1, source_target_pairs={{0,1},{1,0},{2,3},{3,2},{4,5},{5,4},{6,7},{7,6},{8,9},{9,8},{10,11... | collective-permute-start | bytes 1572872 | tf_op jit(solution)/shard_map/ppermute | solution.py:38

commit v14 on v13

--- a/solution.py
+++ b/solution.py
@@ -177,13 +177,12 @@
     return dot_first(ds, k) * FACTOR, dot(ds, q) * FACTOR, dot(pb, g)
 
 
-def pack_cross_kernel(enc_dev, loop, info, ids_ref, qm, gm, q, g, pool, swap_ref, mine, other):
-    shape = (EXTRA, mine.shape[1])
+def naming(enc_dev, loop, me, ids, cols):
+    shape = (EXTRA, cols)
     row = lax.broadcasted_iota(jnp.int32, shape, 0)
     lane = lax.broadcasted_iota(jnp.int32, shape, 1) + pl.program_id(0) * shape[1]
-    ids = ids_ref[...]
     owner = ids // enc_dev
-    relative = owner - info[0] + 1
+    relative = owner - me + 1
     relative = jnp.where(relative < 0, relative + loop, relative)
     relative = jnp.where(relative >= loop, relative - loop, relative)
     slots = relative * enc_dev + ids - owner * enc_dev
@@ -192,16 +191,23 @@
         for s in range(ids.shape[1]):
             hit = (row == slots[n : n + 1, s : s + 1]) & (lane // STRETCH == s)
             times = times + jnp.where(hit, 1.0, 0.0)
-    times = times.astype(BF16)
+    return times.astype(BF16)
+
+
+def pack_cross_kernel(enc_dev, loop, info, ids_ref, qm, gm, q, g, mine, other):
+    times = naming(enc_dev, loop, info[0], ids_ref[...], mine.shape[1])
+    for out, first, second in ((mine, qm, gm), (other, q, g)):
+        out[0:ROWS] = first[...]
+        out[ROWS : 2 * ROWS] = second[...]
+        out[2 * ROWS :] = times
+
+
+def pack_swap_kernel(enc_dev, loop, info, ids_ref, q, g, pool, swap_ref):
     swap_ref[0:ROWS] = q[...]
     swap_ref[ROWS : 2 * ROWS] = g[...]
     swap_ref[2 * ROWS : 3 * ROWS] = pool[0]
     swap_ref[3 * ROWS : 4 * ROWS] = pool[1]
-    swap_ref[4 * ROWS :] = times
-    for out, first, second in ((mine, qm, gm), (other, q, g)):
-        out[0:ROWS] = first[...]
-        out[ROWS : 2 * ROWS] = second[...]
-        out[2 * ROWS :] = times
+    swap_ref[4 * ROWS :] = naming(enc_dev, loop, info[0], ids_ref[...], swap_ref.shape[1])
 
 
 def pack_self_kernel(info, qm, gm, q, g, k, v, swap_ref, mine, other):
@@ -353,21 +359,18 @@
         theirs[index * ROWS : (index + 1) * ROWS] = grad[ROWS:].astype(BF16)
 
 
-def kv_final_kernel(info, mine, theirs, *outs):
+def kv_final_kernel(info, mine, theirs, dq_mine, k_out, v_out, q_out):
     def write(source):
-        outs[0][...] = source[ROWS : 2 * ROWS]
-        outs[1][...] = source[2 * ROWS :]
+        k_out[...] = source[ROWS : 2 * ROWS]
+        v_out[...] = source[2 * ROWS :]
+        q_out[...] = (mine[:ROWS].astype(F32) + dq_mine[...].astype(F32)).astype(BF16)
 
     pl.when(pl.program_id(0) == 0)(lambda: write(mine))
     pl.when(pl.program_id(0) == 1)(lambda: write(theirs))
 
 
-def query_final_kernel(info, mine, theirs, dq_mine, dq_theirs, out):
-    def write(source, extra):
-        out[...] = (source[...].astype(F32) + extra[...].astype(F32)).astype(BF16)
-
-    pl.when(pl.program_id(0) == 0)(lambda: write(mine, dq_mine))
-    pl.when(pl.program_id(0) == 1)(lambda: write(theirs, dq_theirs))
+def query_final_kernel(info, theirs, dq_theirs, grad, out):
+    out[...] = (theirs[...].astype(F32) + dq_theirs[...].astype(F32)).astype(BF16)
 
 
 def cross_final_kernel(info, mine, theirs, dq_mine, dq_theirs, dq_out, pool_out):
@@ -402,16 +405,24 @@
     pool = pool_kv.reshape(2, ROWS, width)
 
     mine_spec, their_spec, their_pool = own_spec(), other_spec(), other_spec((2,))
-    sizes = (4 * ROWS + EXTRA, 2 * ROWS + EXTRA, 2 * ROWS + EXTRA)
-    packed, x_mine, x_other = call(
+    names, names_spec = neighbour_ids.T, whole_spec(neighbour_ids.shape[::-1])
+    x_mine, x_other = call(
         functools.partial(pack_cross_kernel, enc_dev, loop), "pack_cross", info,
-        [whole_spec(neighbour_ids.shape[::-1])] + [mine_spec] * 2 + [their_spec] * 2 + [their_pool],
-        (neighbour_ids.T, cross_queries, grad_cross, cross_queries, grad_cross, pool),
-        [spec(rows) for rows in sizes],
-        [((rows, WIDE), BF16) for rows in sizes],
+        [names_spec] + [mine_spec] * 2 + [their_spec] * 2,
+        (names, cross_queries, grad_cross, cross_queries, grad_cross),
+        [spec(2 * ROWS + EXTRA)] * 2,
+        [((2 * ROWS + EXTRA, WIDE), BF16)] * 2,
     )
     x_same = send(x_mine, outward, True)
     x_cross = send(x_other, across, True)
+    names, x_mine = lax.optimization_barrier((names, x_mine))
+    (packed,) = call(
+        functools.partial(pack_swap_kernel, enc_dev, loop), "pack_swap", info,
+        [names_spec] + [their_spec] * 2 + [their_pool],
+        (names, cross_queries, grad_cross, pool),
+        [spec(4 * ROWS + EXTRA)],
+        [((4 * ROWS + EXTRA, WIDE), BF16)],
+    )
     x_pair = send(packed, swap, False)
     queries_in, packed = lax.optimization_barrier((queries, packed))
     sizes = (4 * ROWS, 2 * ROWS, 2 * ROWS)
@@ -521,21 +532,34 @@
         [half_out] * 2, [half_shape] * 2, flops=LONG,
     )
     three, one = whole_spec((3 * ROWS, WIDE)), whole_spec((ROWS, WIDE))
-    second = whole_spec((ROWS, WIDE), (1, 0))
     s_take = send(s_give, swap, False)
     grad_cq, grad_pool = assemble(
         cross_final_kernel, "cross_final", info, (x_keep, x_take, xr_same, xr_cross),
         [three, three, one, one], True, 1,
     )
-    grad_k, grad_v = assemble(
-        kv_final_kernel, "kv_final", info, (s_keep, s_take), [three, three], False, 2
-    )
     sr, grad_cq = lax.optimization_barrier((sr, grad_cq))
     sr_take = send(sr, swap, False)
-    (grad_q,) = assemble(
-        query_final_kernel, "query_final", info, (s_keep, s_take, sr, sr_take),
-        [one, one, one, second], False, 1,
-    )
+    grad_k, grad_v, grad_q = assemble(
+        kv_final_kernel, "kv_final", info, (s_keep, s_take, sr), [three, three, one], False, 3
+    )
+    grad_q = pl.pallas_call(
+        query_final_kernel,
+        name="query_final",
+        grid_spec=pltpu.PrefetchScalarGridSpec(
+            num_scalar_prefetch=1,
+            grid=(2,),
+            in_specs=[
+                pl.BlockSpec((ROWS // 2, WIDE), lambda h, info: (h, 0)),
+                pl.BlockSpec((ROWS // 2, WIDE), lambda h, info: (2 + h, 0)),
+                pl.BlockSpec(memory_space=pl.ANY),
+            ],
+            out_specs=pl.BlockSpec((ROWS // 2, WIDE), lambda h, info: (h, 1 - info[0] % 2)),
+        ),
+        out_shape=jax.ShapeDtypeStruct(grad_q.shape, BF16),
+        input_output_aliases={3: 0},
+        compiler_params=pltpu.CompilerParams(vmem_limit_bytes=64 << 20),
+        cost_estimate=pl.CostEstimate(flops=0, transcendentals=0, bytes_accessed=0),
+    )(info, s_take, sr_take, grad_q)
     return grad_q, grad_k, grad_v, grad_cq, grad_pool.reshape(pool_kv.shape)
 
 

time: 96.9 us -> 96.5 us (level)
  waiting for transfers between devices: 15.1 us -> 12.9 us
  Pallas kernels: 45.8 us -> 47.6 us
    ppermute x18, waiting for transfers between devices: 15.1 us -> 12.9 us  [send(): return lax.ppermute(value, 'ctx', pairs)]
    pallas_call x0 -> x1, Pallas kernels: none -> 1.8 us  [body(): pl.pallas_call(query_final_kernel, name='query_final', grid_spec=pltpu.Pr...]
  transfers between devices with their start and end apart: 18 -> 18, of which waited for: 5 -> 4; matrix products, arithmetic and copies ran while one was open for 3% -> 4% of each run, Pallas kernels for 43% -> 46%
where the time goes in v14:
time: 96.5 us; the launch traced here: 94.7 us
  Pallas kernels  47.6 us (49%)
  starting transfers between devices  30.1 us (31%)
  waiting for transfers between devices  12.9 us (13%)
  other arithmetic  2.4 us (2%)
    pallas_call x11, Pallas kernels, call(): pl.pallas_call(kernel, name=name, grid_spec=pltpu.PrefetchScalarGridSpec(...  45.8 us
    ppermute x18, starting transfers between devices, send(): return lax.ppermute(value, 'ctx', pairs)  30.1 us
    ppermute x18, waiting for transfers between devices, send(): return lax.ppermute(value, 'ctx', pairs)  12.9 us
  transfers between devices with their start and end apart: 18, of which 4 were waited for; matrix products, arithmetic and copies ran while one was open for 4% of the time, Pallas kernels for 46%

profile of v14, /device:TPU:1, one launch (start us, length us, event | category | flops | bytes accessed | tf_op | source)
XLA Modules:
  0.0 94.7 jit_solution(14483041829677819070)
XLA Ops:
  0.6 2.3 %pack_cross.1 = (bf16[528,512]{1,0:T(8,128)(2,1)}, bf16[528,512]{1,0:T(8,128)(2,1)}) custom-call(s32[1]{0:T(128)} %bitcast.info, s32[2,4]{1,0:T(2,128)} %bitcast.8, bf16[256,1024]{1,0:T(8,128)(2,1)} %refs_2_.6, bf16[256,1024]{1,0:T(8,128)(2,1)} %refs_3_.6, bf16[256,1024]{1,0:T(8,128)(2,1)} %refs_2_.6, bf16[256,1024]{1,0:T(8,128)(2,1)} %refs_3_.6), custom_call_target="tpu_custom_call" | custom-call | tf_op jit(solution)/shard_map/pack_cross/pallas_call | solution.py:83
  3.0 2.6 %collective-permute-start.3 = (bf16[528,512]{1,0:T(8,128)(2,1)}, bf16[528,512]{1,0:T(8,128)(2,1)}, u32[]{:S(2)}, u32[]{:S(2)}) collective-permute-start(bf16[528,512]{1,0:T(8,128)(2,1)} %get-tuple-element.70), channel_id=1, source_target_pairs={{0,15},{1,2},{2,1},{3,4},{4,3},{5,6},{6,5},{7,8},{8,7},{9,10},{10,... | collective-permute-start | bytes 1622024 | tf_op jit(solution)/shard_map/ppermute | solution.py:38
  6.8 2.2 %pack_swap.1 = bf16[1040,512]{1,0:T(8,128)(2,1)} custom-call(s32[1]{0:T(128)} %bitcast.info, s32[2,4]{1,0:T(2,128)} %bitcast.9, bf16[256,1024]{1,0:T(8,128)(2,1)} %refs_2_.6, bf16[256,1024]{1,0:T(8,128)(2,1)} %refs_3_.6, bf16[2,256,1024]{2,1,0:T(8,128)(2,1)} %bitcast.4), custom_call_target="tpu_custom_call" | custom-call | tf_op jit(solution)/shard_map/pack_swap/pallas_call | solution.py:83
  9.1 2.3 %collective-permute-start = (bf16[1040,512]{1,0:T(8,128)(2,1)}, bf16[1040,512]{1,0:T(8,128)(2,1)}, u32[]{:S(2)}, u32[]{:S(2)}) collective-permute-start(bf16[1040,512]{1,0:T(8,128)(2,1)} %pack_swap.1), channel_id=1, source_target_pairs={{0,1},{1,0},{2,3},{3,2},{4,5},{5,4},{6,7},{7,6},{8,9},{9,8},{10,11... | collective-permute-start | bytes 3194888 | tf_op jit(solution)/shard_map/ppermute | solution.py:38
  11.3 2.6 %pack_self.1 = (bf16[1024,512]{1,0:T(8,128)(2,1)}, bf16[512,512]{1,0:T(8,128)(2,1)}, bf16[512,512]{1,0:T(8,128)(2,1)}) custom-call(s32[1]{0:T(128)} %bitcast.info, bf16[256,1024]{1,0:T(8,128)(2,1)} %refs_1_.3, bf16[256,1024]{1,0:T(8,128)(2,1)} %refs_2_.7, bf16[256,1024]{1,0:T(8,128)(2,1)} %refs_1_.3, bf16[256,1024]{1,0:T(8,128)(2,1)} %refs_2_.7, ...), custom_call_target="tpu_custom_call" | custom-call | tf_op jit(solution)/shard_map/pack_self/pallas_call | solution.py:83
  17.4 4.0 %cross_stats.1 = (f32[4,8,256]{2,1,0:T(8,128)}, f32[4,8,256]{2,1,0:T(8,128)}) custom-call(s32[1]{0:T(128)} %bitcast.info, bf16[528,512]{1,0:T(8,128)(2,1)} %get-tuple-element.63.refs_0_, bf16[1040,512]{1,0:T(8,128)(2,1)} %collective-permute-done.refs_1_.refs_5_.refs_6_.refs_7_.refs_8_, bf16[256,1024]{1,0:T(8,128)(2,1)} %refs_2_.6, ...), custom_call_target="tpu_custom_call" | custom-call | tf_op jit(solution)/shard_map/cross_stats/pallas_call | solution.py:83
  22.9 4.2 %self_stats.1.refs_10_ = f32[4,8,512]{2,1,0:T(8,128)} custom-call(s32[1]{0:T(128)} %bitcast.info, f32[512,512]{1,0:T(8,128)} %and_select_fusion.1.refs_0_, bf16[256,1024]{1,0:T(8,128)(2,1)} %refs_1_.3, bf16[256,1024]{1,0:T(8,128)(2,1)} %refs_2_.7, bf16[256,1024]{1,0:T(8,128)(2,1)} %refs_3_.7, bf16[256,1024]{1,0:T(8,128)(2,1)} %refs_4_.3, ...), custom_call_target="tpu_custom_call" | custom-call | tf_op jit(solution)/shard_map/self_stats/pallas_call | solution.py:83
  27.0 3.6 %collective-permute-done.2.refs_0_.refs_2_.refs_3_ = bf16[528,512]{1,0:T(8,128)(2,1)} collective-permute-done((bf16[528,512]{1,0:T(8,128)(2,1)}, bf16[528,512]{1,0:T(8,128)(2,1)}, u32[]{:S(2)}, u32[]{:S(2)}) %collective-permute-start.2) | collective-permute-done | bytes 540704 | tf_op jit(solution)/shard_map/ppermute | solution.py:38
  31.0 1.3 %collective-permute-start.8 = (bf16[512,512]{1,0:T(8,128)(2,1)}, bf16[512,512]{1,0:T(8,128)(2,1)}, u32[]{:S(2)}, u32[]{:S(2)}) collective-permute-start(bf16[512,512]{1,0:T(8,128)(2,1)} %get-tuple-element.81), channel_id=1, source_target_pairs={{2,0},{3,1},{4,2},{5,3},{6,4},{7,5},{8,6},{9,7},{10,8},{11,9},{12,... | collective-permute-start | bytes 1572872 | tf_op jit(solution)/shard_map/ppermute | solution.py:38
  32.3 1.3 %collective-permute-start.9 = (f32[4,8,512]{2,1,0:T(8,128)}, f32[4,8,512]{2,1,0:T(8,128)}, u32[]{:S(2)}, u32[]{:S(2)}) collective-permute-start(f32[4,8,512]{2,1,0:T(8,128)} %self_stats.1.refs_10_), channel_id=1, source_target_pairs={{2,0},{3,1},{4,2},{5,3},{6,4},{7,5},{8,6},{9,7},{10,8},{11,9},{12,... | collective-permute-start | bytes 196616 | tf_op jit(solution)/shard_map/ppermute | solution.py:38
  33.6 5.9 %cross_remote.1 = (bf16[256,512]{1,0:T(8,128)(2,1)}, bf16[256,512]{1,0:T(8,128)(2,1)}, bf16[1024,512]{1,0:T(8,128)(2,1)}, f32[4,8,256]{2,1,0:T(8,128)}, f32[4,8,256]{2,1,0:T(8,128)}) custom-call(s32[1]{0:T(128)} %bitcast.info, bf16[528,512]{1,0:T(8,128)(2,1)} %collective-permute-done.2.refs_0_.refs_2_.refs_3_, ...), custom_call_target="tpu_custom_call" | custom-call | tf_op jit(solution)/shard_map/cross_remote/pallas_call | solution.py:83
  39.5 8.2 %collective-permute-start.6 = (f32[4,8,256]{2,1,0:T(8,128)}, f32[4,8,256]{2,1,0:T(8,128)}, u32[]{:S(2)}, u32[]{:S(2)}) collective-permute-start(f32[4,8,256]{2,1,0:T(8,128)} %get-tuple-element.76), channel_id=1, source_target_pairs={{0,2},{1,15},{2,4},{3,1},{4,6},{5,3},{6,8},{7,5},{8,10},{9,7},{10,... | collective-permute-start | bytes 98312 | tf_op jit(solution)/shard_map/ppermute | solution.py:38
  47.7 1.3 %collective-permute-start.10 = (bf16[512,512]{1,0:T(8,128)(2,1)}, bf16[512,512]{1,0:T(8,128)(2,1)}, u32[]{:S(2)}, u32[]{:S(2)}) collective-permute-start(bf16[512,512]{1,0:T(8,128)(2,1)} %get-tuple-element.87), channel_id=1, source_target_pairs={{2,1},{3,0},{4,3},{5,2},{6,5},{7,4},{8,7},{9,6},{10,9},{11,8},{12,... | collective-permute-start | bytes 1572872 | tf_op jit(solution)/shard_map/ppermute | solution.py:38
  49.0 4.5 %collective-permute-done.7.refs_10_ = f32[4,8,256]{2,1,0:T(8,128)} collective-permute-done((f32[4,8,256]{2,1,0:T(8,128)}, f32[4,8,256]{2,1,0:T(8,128)}, u32[]{:S(2)}, u32[]{:S(2)}) %collective-permute-start.7) | collective-permute-done | bytes 32800 | tf_op jit(solution)/shard_map/ppermute | solution.py:38
  53.6 6.4 %cross_local.1 = (bf16[768,512]{1,0:T(8,128)(2,1)}, bf16[768,512]{1,0:T(8,128)(2,1)}) custom-call(s32[1]{0:T(128)} %bitcast.info, bf16[528,512]{1,0:T(8,128)(2,1)} %get-tuple-element.63.refs_0_, bf16[1040,512]{1,0:T(8,128)(2,1)} %collective-permute-done.refs_1_.refs_5_.refs_6_.refs_7_.refs_8_, bf16[256,1024]{1,0:T(8,128)(2,1)} %refs_2_.6, ...), custom_call_target="tpu_custom_call" | custom-call | flops 12000000000 | tf_op jit(solution)/shard_map/cross_local/pallas_call | solution.py:83
  60.0 4.3 %collective-permute-done.10.refs_3_.refs_4_ = bf16[512,512]{1,0:T(8,128)(2,1)} collective-permute-done((bf16[512,512]{1,0:T(8,128)(2,1)}, bf16[512,512]{1,0:T(8,128)(2,1)}, u32[]{:S(2)}, u32[]{:S(2)}) %collective-permute-start.10) | collective-permute-done | bytes 524320 | tf_op jit(solution)/shard_map/ppermute | solution.py:38
  64.8 6.6 %self_remote.1 = (bf16[512,512]{1,0:T(8,128)(2,1)}, bf16[1024,512]{1,0:T(8,128)(2,1)}, f32[4,8,512]{2,1,0:T(8,128)}) custom-call(s32[1]{0:T(128)} %bitcast.info, f32[512,512]{1,0:T(8,128)} %and_select_fusion.refs_0_, bf16[512,512]{1,0:T(8,128)(2,1)} %collective-permute-done.8.refs_1_.refs_2_, bf16[512,512]{1,0:T(8,128)(2,1)} %collective-permute-done.8.refs_1_.refs_2_, ...), custom_call_target="tpu_custom_call" | custom-call | flops 12000000000 | tf_op jit(solution)/shard_map/self_remote/pallas_call | solution.py:83
  71.4 4.1 %collective-permute-start.13 = (f32[4,8,512]{2,1,0:T(8,128)}, f32[4,8,512]{2,1,0:T(8,128)}, u32[]{:S(2)}, u32[]{:S(2)}) collective-permute-start(f32[4,8,512]{2,1,0:T(8,128)} %get-tuple-element.97), channel_id=1, source_target_pairs={{0,2},{1,3},{2,4},{3,5},{4,6},{5,7},{6,8},{7,9},{8,10},{9,11},{10,... | collective-permute-start | bytes 196616 | tf_op jit(solution)/shard_map/ppermute | solution.py:38
  75.5 3.1 %collective-permute-start.15 = (bf16[512,512]{1,0:T(8,128)(2,1)}, bf16[512,512]{1,0:T(8,128)(2,1)}, u32[]{:S(2)}, u32[]{:S(2)}) collective-permute-start(bf16[512,512]{1,0:T(8,128)(2,1)} %get-tuple-element.102), channel_id=1, source_target_pairs={{0,2},{1,3},{2,4},{3,5},{4,6},{5,7},{6,8},{7,9},{8,10},{9,11},{10,... | collective-permute-start | bytes 1572872 | tf_op jit(solution)/shard_map/ppermute | solution.py:38
  78.6 1.9 %collective-permute-start.16 = (bf16[768,512]{1,0:T(8,128)(2,1)}, bf16[768,512]{1,0:T(8,128)(2,1)}, u32[]{:S(2)}, u32[]{:S(2)}) collective-permute-start(bf16[768,512]{1,0:T(8,128)(2,1)} %get-tuple-element.104), channel_id=1, source_target_pairs={{0,1},{1,0},{2,3},{3,2},{4,5},{5,4},{6,7},{7,6},{8,9},{9,8},{10,11... | collective-permute-start | bytes 2359304 | tf_op jit(solution)/shard_map/ppermute | solution.py:38
  80.4 6.1 %self_local.1 = (bf16[768,512]{1,0:T(8,128)(2,1)}, bf16[768,512]{1,0:T(8,128)(2,1)}) custom-call(s32[1]{0:T(128)} %bitcast.info, f32[512,512]{1,0:T(8,128)} %and_select_fusion.1.refs_0_, bf16[256,1024]{1,0:T(8,128)(2,1)} %refs_1_.3, bf16[256,1024]{1,0:T(8,128)(2,1)} %refs_2_.7, bf16[256,1024]{1,0:T(8,128)(2,1)} %refs_3_.7, bf16[256,1024]{1,0:T(8,128)(2,1)} %refs_4_.3, ...), custom_call_target="tpu_custom_call" | custom-call | flops 12000000000 | tf_op jit(solution)/shard_map/self_local/pallas_call | solution.py:83
  86.6 2.8 %cross_final.1 = (bf16[256,1024]{1,0:T(8,128)(2,1)}, bf16[2,256,1024]{2,1,0:T(8,128)(2,1)}) custom-call(s32[1]{0:T(128)} %bitcast.info, bf16[768,512]{1,0:T(8,128)(2,1)} %get-tuple-element.103.mine, bf16[768,512]{1,0:T(8,128)(2,1)} %collective-permute-done.16.theirs, bf16[256,512]{1,0:T(8,128)(2,1)} %collective-permute-done.11.dq_mine, ...), custom_call_target="tpu_custom_call" | custom-call | tf_op jit(solution)/shard_map/cross_final/pallas_call | solution.py:83
  90.2 2.7 %kv_final.1 = (bf16[256,1024]{1,0:T(8,128)(2,1)}, bf16[256,1024]{1,0:T(8,128)(2,1)}, bf16[256,1024]{1,0:T(8,128)(2,1)}) custom-call(s32[1]{0:T(128)} %bitcast.info, bf16[768,512]{1,0:T(8,128)(2,1)} %get-tuple-element.109.mine, bf16[768,512]{1,0:T(8,128)(2,1)} %collective-permute-done.14.theirs, bf16[512,512]{1,0:T(8,128)(2,1)} %collective-permute-done.15.dq_mine), custom_call_target="tpu_custom_call" | custom-call | tf_op jit(solution)/shard_map/kv_final/pallas_call | solution.py:83
  92.9 1.8 %query_final.1 = bf16[256,1024]{1,0:T(8,128)(2,1)} custom-call(s32[1]{0:T(128)} %bitcast.info, bf16[768,512]{1,0:T(8,128)(2,1)} %collective-permute-done.14.theirs, bf16[512,512]{1,0:T(8,128)(2,1)} %collective-permute-done.17.dq_theirs, bf16[256,1024]{1,0:T(8,128)(2,1)} %get-tuple-element.110.grad), custom_call_target="tpu_custom_call", output_to_operand_aliasing={{}: (3, {})} | custom-call | tf_op jit(solution)/shard_map/query_final/pallas_call | solution.py:545
  (31 shorter events, 8.0 us)
Async XLA Ops:
  3.0 24.1 %collective-permute-start.3 = (bf16[528,512]{1,0:T(8,128)(2,1)}, bf16[528,512]{1,0:T(8,128)(2,1)}, u32[]{:S(2)}, u32[]{:S(2)}) collective-permute-start(bf16[528,512]{1,0:T(8,128)(2,1)} %get-tuple-element.70), channel_id=1, source_target_pairs={{0,15},{1,2},{2,1},{3,4},{4,3},{5,6},{6,5},{7,8},{8,7},{9,10},{10,... | collective-permute-start | bytes 1622024 | tf_op jit(solution)/shard_map/ppermute | solution.py:38
  5.6 25.1 %collective-permute-start.2 = (bf16[528,512]{1,0:T(8,128)(2,1)}, bf16[528,512]{1,0:T(8,128)(2,1)}, u32[]{:S(2)}, u32[]{:S(2)}) collective-permute-start(bf16[528,512]{1,0:T(8,128)(2,1)} %get-tuple-element.63.refs_0_), channel_id=1, source_target_pairs={{0,14},{1,3},{2,0},{3,5},{4,2},{5,7},{6,4},{7,9},{8,6},{9,11},{10,... | collective-permute-start | bytes 1622024 | tf_op jit(solution)/shard_map/ppermute | solution.py:38
  9.1 8.3 %collective-permute-start = (bf16[1040,512]{1,0:T(8,128)(2,1)}, bf16[1040,512]{1,0:T(8,128)(2,1)}, u32[]{:S(2)}, u32[]{:S(2)}) collective-permute-start(bf16[1040,512]{1,0:T(8,128)(2,1)} %pack_swap.1), channel_id=1, source_target_pairs={{0,1},{1,0},{2,3},{3,2},{4,5},{5,4},{6,7},{7,6},{8,9},{9,8},{10,11... | collective-permute-start | bytes 3194888 | tf_op jit(solution)/shard_map/ppermute | solution.py:38
  13.9 9.0 %collective-permute-start.1 = (bf16[1024,512]{1,0:T(8,128)(2,1)}, bf16[1024,512]{1,0:T(8,128)(2,1)}, u32[]{:S(2)}, u32[]{:S(2)}) collective-permute-start(bf16[1024,512]{1,0:T(8,128)(2,1)} %get-tuple-element.68), channel_id=1, source_target_pairs={{0,1},{1,0},{2,3},{3,2},{4,5},{5,4},{6,7},{7,6},{8,9},{9,8},{10,11... | collective-permute-start | bytes 3145736 | tf_op jit(solution)/shard_map/ppermute | solution.py:38
  21.4 9.3 %collective-permute-start.5 = (f32[4,8,256]{2,1,0:T(8,128)}, f32[4,8,256]{2,1,0:T(8,128)}, u32[]{:S(2)}, u32[]{:S(2)}) collective-permute-start(f32[4,8,256]{2,1,0:T(8,128)} %get-tuple-element.71), channel_id=1, source_target_pairs={{0,2},{1,15},{2,4},{3,1},{4,6},{5,3},{6,8},{7,5},{8,10},{9,7},{10,... | collective-permute-start | bytes 98312 | tf_op jit(solution)/shard_map/ppermute | solution.py:38
  22.5 8.5 %collective-permute-start.4 = (f32[4,8,256]{2,1,0:T(8,128)}, f32[4,8,256]{2,1,0:T(8,128)}, u32[]{:S(2)}, u32[]{:S(2)}) collective-permute-start(f32[4,8,256]{2,1,0:T(8,128)} %get-tuple-element.65), channel_id=1, source_target_pairs={{0,14},{1,3},{2,0},{3,5},{4,2},{5,7},{6,4},{7,9},{8,6},{9,11},{10,... | collective-permute-start | bytes 98312 | tf_op jit(solution)/shard_map/ppermute | solution.py:38
  31.0 18.0 %collective-permute-start.8 = (bf16[512,512]{1,0:T(8,128)(2,1)}, bf16[512,512]{1,0:T(8,128)(2,1)}, u32[]{:S(2)}, u32[]{:S(2)}) collective-permute-start(bf16[512,512]{1,0:T(8,128)(2,1)} %get-tuple-element.81), channel_id=1, source_target_pairs={{2,0},{3,1},{4,2},{5,3},{6,4},{7,5},{8,6},{9,7},{10,8},{11,9},{12,... | collective-permute-start | bytes 1572872 | tf_op jit(solution)/shard_map/ppermute | solution.py:38
  32.3 16.7 %collective-permute-start.9 = (f32[4,8,512]{2,1,0:T(8,128)}, f32[4,8,512]{2,1,0:T(8,128)}, u32[]{:S(2)}, u32[]{:S(2)}) collective-permute-start(f32[4,8,512]{2,1,0:T(8,128)} %self_stats.1.refs_10_), channel_id=1, source_target_pairs={{2,0},{3,1},{4,2},{5,3},{6,4},{7,5},{8,6},{9,7},{10,8},{11,9},{12,... | collective-permute-start | bytes 196616 | tf_op jit(solution)/shard_map/ppermute | solution.py:38
  39.5 9.5 %collective-permute-start.6 = (f32[4,8,256]{2,1,0:T(8,128)}, f32[4,8,256]{2,1,0:T(8,128)}, u32[]{:S(2)}, u32[]{:S(2)}) collective-permute-start(f32[4,8,256]{2,1,0:T(8,128)} %get-tuple-element.76), channel_id=1, source_target_pairs={{0,2},{1,15},{2,4},{3,1},{4,6},{5,3},{6,8},{7,5},{8,10},{9,7},{10,... | collective-permute-start | bytes 98312 | tf_op jit(solution)/shard_map/ppermute | solution.py:38
  47.7 5.9 %collective-permute-start.7 = (f32[4,8,256]{2,1,0:T(8,128)}, f32[4,8,256]{2,1,0:T(8,128)}, u32[]{:S(2)}, u32[]{:S(2)}) collective-permute-start(f32[4,8,256]{2,1,0:T(8,128)} %get-tuple-element.77), channel_id=1, source_target_pairs={{0,14},{1,3},{2,0},{3,5},{4,2},{5,7},{6,4},{7,9},{8,6},{9,11},{10,... | collective-permute-start | bytes 98312 | tf_op jit(solution)/shard_map/ppermute | solution.py:38
  47.7 16.6 %collective-permute-start.10 = (bf16[512,512]{1,0:T(8,128)(2,1)}, bf16[512,512]{1,0:T(8,128)(2,1)}, u32[]{:S(2)}, u32[]{:S(2)}) collective-permute-start(bf16[512,512]{1,0:T(8,128)(2,1)} %get-tuple-element.87), channel_id=1, source_target_pairs={{2,1},{3,0},{4,3},{5,2},{6,5},{7,4},{8,7},{9,6},{10,9},{11,8},{12,... | collective-permute-start | bytes 1572872 | tf_op jit(solution)/shard_map/ppermute | solution.py:38
  64.3 14.3 %collective-permute-start.11 = (bf16[256,512]{1,0:T(8,128)(2,1)}, bf16[256,512]{1,0:T(8,128)(2,1)}, u32[]{:S(2)}, u32[]{:S(2)}) collective-permute-start(bf16[256,512]{1,0:T(8,128)(2,1)} %get-tuple-element.95), channel_id=1, source_target_pairs={{0,2},{1,15},{2,4},{3,1},{4,6},{5,3},{6,8},{7,5},{8,10},{9,7},{10,... | collective-permute-start | bytes 786440 | tf_op jit(solution)/shard_map/ppermute | solution.py:38
  64.3 14.3 %collective-permute-start.12 = (bf16[256,512]{1,0:T(8,128)(2,1)}, bf16[256,512]{1,0:T(8,128)(2,1)}, u32[]{:S(2)}, u32[]{:S(2)}) collective-permute-start(bf16[256,512]{1,0:T(8,128)(2,1)} %get-tuple-element.96), channel_id=1, source_target_pairs={{0,15},{1,2},{2,1},{3,4},{4,3},{5,6},{6,5},{7,8},{8,7},{9,10},{10,... | collective-permute-start | bytes 786440 | tf_op jit(solution)/shard_map/ppermute | solution.py:38
  71.4 7.1 %collective-permute-start.13 = (f32[4,8,512]{2,1,0:T(8,128)}, f32[4,8,512]{2,1,0:T(8,128)}, u32[]{:S(2)}, u32[]{:S(2)}) collective-permute-start(f32[4,8,512]{2,1,0:T(8,128)} %get-tuple-element.97), channel_id=1, source_target_pairs={{0,2},{1,3},{2,4},{3,5},{4,6},{5,7},{6,8},{7,9},{8,10},{9,11},{10,... | collective-permute-start | bytes 196616 | tf_op jit(solution)/shard_map/ppermute | solution.py:38
  75.5 13.9 %collective-permute-start.15 = (bf16[512,512]{1,0:T(8,128)(2,1)}, bf16[512,512]{1,0:T(8,128)(2,1)}, u32[]{:S(2)}, u32[]{:S(2)}) collective-permute-start(bf16[512,512]{1,0:T(8,128)(2,1)} %get-tuple-element.102), channel_id=1, source_target_pairs={{0,2},{1,3},{2,4},{3,5},{4,6},{5,7},{6,8},{7,9},{8,10},{9,11},{10,... | collective-permute-start | bytes 1572872 | tf_op jit(solution)/shard_map/ppermute | solution.py:38
  78.6 8.0 %collective-permute-start.16 = (bf16[768,512]{1,0:T(8,128)(2,1)}, bf16[768,512]{1,0:T(8,128)(2,1)}, u32[]{:S(2)}, u32[]{:S(2)}) collective-permute-start(bf16[768,512]{1,0:T(8,128)(2,1)} %get-tuple-element.104), channel_id=1, source_target_pairs={{0,1},{1,0},{2,3},{3,2},{4,5},{5,4},{6,7},{7,6},{8,9},{9,8},{10,11... | collective-permute-start | bytes 2359304 | tf_op jit(solution)/shard_map/ppermute | solution.py:38
  86.5 3.7 %collective-permute-start.14 = (bf16[768,512]{1,0:T(8,128)(2,1)}, bf16[768,512]{1,0:T(8,128)(2,1)}, u32[]{:S(2)}, u32[]{:S(2)}) collective-permute-start(bf16[768,512]{1,0:T(8,128)(2,1)} %get-tuple-element.101), channel_id=1, source_target_pairs={{0,1},{1,0},{2,3},{3,2},{4,5},{5,4},{6,7},{7,6},{8,9},{9,8},{10,11... | collective-permute-start | bytes 2359304 | tf_op jit(solution)/shard_map/ppermute | solution.py:38
  89.4 3.5 %collective-permute-start.17 = (bf16[512,512]{1,0:T(8,128)(2,1)}, bf16[512,512]{1,0:T(8,128)(2,1)}, u32[]{:S(2)}, u32[]{:S(2)}) collective-permute-start(bf16[512,512]{1,0:T(8,128)(2,1)} %collective-permute-done.15.dq_mine), channel_id=1, source_target_pairs={{0,1},{1,0},{2,3},{3,2},{4,5},{5,4},{6,7},{7,6},{8,9},{9,8},{10,11... | collective-permute-start | bytes 1572872 | tf_op jit(solution)/shard_map/ppermute | solution.py:38

commit v15 on v14

--- a/solution.py
+++ b/solution.py
@@ -18,7 +18,7 @@
 STRETCH = 64
 NBR_TOK = 128
 ROWS = 256
-EXTRA = 16
+EXTRA = 8
 LONG = 12 * 10**9
 FACTOR = HEAD_DIM ** (-0.5)
 MASKED = -1e30

time: 96.5 us -> 96.2 us (level)
  no operation moved by 1% of the time
where the time goes in v15:
time: 96.2 us; the launch traced here: 94.3 us
  Pallas kernels  47.7 us (50%)
  starting transfers between devices  30.1 us (31%)
  waiting for transfers between devices  12.6 us (13%)
  other arithmetic  2.4 us (2%)
    pallas_call x11, Pallas kernels, call(): pl.pallas_call(kernel, name=name, grid_spec=pltpu.PrefetchScalarGridSpec(...  45.9 us
    ppermute x18, starting transfers between devices, send(): return lax.ppermute(value, 'ctx', pairs)  30.1 us
    ppermute x18, waiting for transfers between devices, send(): return lax.ppermute(value, 'ctx', pairs)  12.6 us
  transfers between devices with their start and end apart: 18, of which 4 were waited for; matrix products, arithmetic and copies ran while one was open for 4% of the time, Pallas kernels for 46%

profile of v15, /device:TPU:1, one launch (start us, length us, event | category | flops | bytes accessed | tf_op | source)
XLA Modules:
  0.0 94.3 jit_solution(2347556050173348418)
XLA Ops:
  0.6 2.3 %pack_cross.1 = (bf16[520,512]{1,0:T(8,128)(2,1)}, bf16[520,512]{1,0:T(8,128)(2,1)}) custom-call(s32[1]{0:T(128)} %bitcast.info, s32[2,4]{1,0:T(2,128)} %bitcast.8, bf16[256,1024]{1,0:T(8,128)(2,1)} %refs_2_.6, bf16[256,1024]{1,0:T(8,128)(2,1)} %refs_3_.6, bf16[256,1024]{1,0:T(8,128)(2,1)} %refs_2_.6, bf16[256,1024]{1,0:T(8,128)(2,1)} %refs_3_.6), custom_call_target="tpu_custom_call" | custom-call | tf_op jit(solution)/shard_map/pack_cross/pallas_call | solution.py:83
  3.0 2.6 %collective-permute-start.3 = (bf16[520,512]{1,0:T(8,128)(2,1)}, bf16[520,512]{1,0:T(8,128)(2,1)}, u32[]{:S(2)}, u32[]{:S(2)}) collective-permute-start(bf16[520,512]{1,0:T(8,128)(2,1)} %get-tuple-element.70), channel_id=1, source_target_pairs={{0,15},{1,2},{2,1},{3,4},{4,3},{5,6},{6,5},{7,8},{8,7},{9,10},{10,... | collective-permute-start | bytes 1597448 | tf_op jit(solution)/shard_map/ppermute | solution.py:38
  6.8 2.2 %pack_swap.1 = bf16[1032,512]{1,0:T(8,128)(2,1)} custom-call(s32[1]{0:T(128)} %bitcast.info, s32[2,4]{1,0:T(2,128)} %bitcast.9, bf16[256,1024]{1,0:T(8,128)(2,1)} %refs_2_.6, bf16[256,1024]{1,0:T(8,128)(2,1)} %refs_3_.6, bf16[2,256,1024]{2,1,0:T(8,128)(2,1)} %bitcast.4), custom_call_target="tpu_custom_call" | custom-call | tf_op jit(solution)/shard_map/pack_swap/pallas_call | solution.py:83
  9.1 2.3 %collective-permute-start = (bf16[1032,512]{1,0:T(8,128)(2,1)}, bf16[1032,512]{1,0:T(8,128)(2,1)}, u32[]{:S(2)}, u32[]{:S(2)}) collective-permute-start(bf16[1032,512]{1,0:T(8,128)(2,1)} %pack_swap.1), channel_id=1, source_target_pairs={{0,1},{1,0},{2,3},{3,2},{4,5},{5,4},{6,7},{7,6},{8,9},{9,8},{10,11... | collective-permute-start | bytes 3170312 | tf_op jit(solution)/shard_map/ppermute | solution.py:38
  11.3 2.6 %pack_self.1 = (bf16[1024,512]{1,0:T(8,128)(2,1)}, bf16[512,512]{1,0:T(8,128)(2,1)}, bf16[512,512]{1,0:T(8,128)(2,1)}) custom-call(s32[1]{0:T(128)} %bitcast.info, bf16[256,1024]{1,0:T(8,128)(2,1)} %refs_1_.3, bf16[256,1024]{1,0:T(8,128)(2,1)} %refs_2_.7, bf16[256,1024]{1,0:T(8,128)(2,1)} %refs_1_.3, bf16[256,1024]{1,0:T(8,128)(2,1)} %refs_2_.7, ...), custom_call_target="tpu_custom_call" | custom-call | tf_op jit(solution)/shard_map/pack_self/pallas_call | solution.py:83
  17.3 4.0 %cross_stats.1 = (f32[4,8,256]{2,1,0:T(8,128)}, f32[4,8,256]{2,1,0:T(8,128)}) custom-call(s32[1]{0:T(128)} %bitcast.info, bf16[520,512]{1,0:T(8,128)(2,1)} %get-tuple-element.63.refs_0_, bf16[1032,512]{1,0:T(8,128)(2,1)} %collective-permute-done.refs_1_.refs_5_.refs_6_.refs_7_.refs_8_, bf16[256,1024]{1,0:T(8,128)(2,1)} %refs_2_.6, ...), custom_call_target="tpu_custom_call" | custom-call | tf_op jit(solution)/shard_map/cross_stats/pallas_call | solution.py:83
  22.9 4.2 %self_stats.1.refs_10_ = f32[4,8,512]{2,1,0:T(8,128)} custom-call(s32[1]{0:T(128)} %bitcast.info, f32[512,512]{1,0:T(8,128)} %and_select_fusion.1.refs_0_, bf16[256,1024]{1,0:T(8,128)(2,1)} %refs_1_.3, bf16[256,1024]{1,0:T(8,128)(2,1)} %refs_2_.7, bf16[256,1024]{1,0:T(8,128)(2,1)} %refs_3_.7, bf16[256,1024]{1,0:T(8,128)(2,1)} %refs_4_.3, ...), custom_call_target="tpu_custom_call" | custom-call | tf_op jit(solution)/shard_map/self_stats/pallas_call | solution.py:83
  27.0 3.3 %collective-permute-done.2.refs_0_.refs_2_.refs_3_ = bf16[520,512]{1,0:T(8,128)(2,1)} collective-permute-done((bf16[520,512]{1,0:T(8,128)(2,1)}, bf16[520,512]{1,0:T(8,128)(2,1)}, u32[]{:S(2)}, u32[]{:S(2)}) %collective-permute-start.2) | collective-permute-done | bytes 532512 | tf_op jit(solution)/shard_map/ppermute | solution.py:38
  30.6 1.3 %collective-permute-start.8 = (bf16[512,512]{1,0:T(8,128)(2,1)}, bf16[512,512]{1,0:T(8,128)(2,1)}, u32[]{:S(2)}, u32[]{:S(2)}) collective-permute-start(bf16[512,512]{1,0:T(8,128)(2,1)} %get-tuple-element.81), channel_id=1, source_target_pairs={{2,0},{3,1},{4,2},{5,3},{6,4},{7,5},{8,6},{9,7},{10,8},{11,9},{12,... | collective-permute-start | bytes 1572872 | tf_op jit(solution)/shard_map/ppermute | solution.py:38
  31.9 1.3 %collective-permute-start.9 = (f32[4,8,512]{2,1,0:T(8,128)}, f32[4,8,512]{2,1,0:T(8,128)}, u32[]{:S(2)}, u32[]{:S(2)}) collective-permute-start(f32[4,8,512]{2,1,0:T(8,128)} %self_stats.1.refs_10_), channel_id=1, source_target_pairs={{2,0},{3,1},{4,2},{5,3},{6,4},{7,5},{8,6},{9,7},{10,8},{11,9},{12,... | collective-permute-start | bytes 196616 | tf_op jit(solution)/shard_map/ppermute | solution.py:38
  33.2 5.9 %cross_remote.1 = (bf16[256,512]{1,0:T(8,128)(2,1)}, bf16[256,512]{1,0:T(8,128)(2,1)}, bf16[1024,512]{1,0:T(8,128)(2,1)}, f32[4,8,256]{2,1,0:T(8,128)}, f32[4,8,256]{2,1,0:T(8,128)}) custom-call(s32[1]{0:T(128)} %bitcast.info, bf16[520,512]{1,0:T(8,128)(2,1)} %collective-permute-done.2.refs_0_.refs_2_.refs_3_, ...), custom_call_target="tpu_custom_call" | custom-call | tf_op jit(solution)/shard_map/cross_remote/pallas_call | solution.py:83
  39.2 8.2 %collective-permute-start.6 = (f32[4,8,256]{2,1,0:T(8,128)}, f32[4,8,256]{2,1,0:T(8,128)}, u32[]{:S(2)}, u32[]{:S(2)}) collective-permute-start(f32[4,8,256]{2,1,0:T(8,128)} %get-tuple-element.76), channel_id=1, source_target_pairs={{0,2},{1,15},{2,4},{3,1},{4,6},{5,3},{6,8},{7,5},{8,10},{9,7},{10,... | collective-permute-start | bytes 98312 | tf_op jit(solution)/shard_map/ppermute | solution.py:38
  47.3 1.3 %collective-permute-start.10 = (bf16[512,512]{1,0:T(8,128)(2,1)}, bf16[512,512]{1,0:T(8,128)(2,1)}, u32[]{:S(2)}, u32[]{:S(2)}) collective-permute-start(bf16[512,512]{1,0:T(8,128)(2,1)} %get-tuple-element.87), channel_id=1, source_target_pairs={{2,1},{3,0},{4,3},{5,2},{6,5},{7,4},{8,7},{9,6},{10,9},{11,8},{12,... | collective-permute-start | bytes 1572872 | tf_op jit(solution)/shard_map/ppermute | solution.py:38
  48.7 4.5 %collective-permute-done.7.refs_10_ = f32[4,8,256]{2,1,0:T(8,128)} collective-permute-done((f32[4,8,256]{2,1,0:T(8,128)}, f32[4,8,256]{2,1,0:T(8,128)}, u32[]{:S(2)}, u32[]{:S(2)}) %collective-permute-start.7) | collective-permute-done | bytes 32800 | tf_op jit(solution)/shard_map/ppermute | solution.py:38
  53.2 6.4 %cross_local.1 = (bf16[768,512]{1,0:T(8,128)(2,1)}, bf16[768,512]{1,0:T(8,128)(2,1)}) custom-call(s32[1]{0:T(128)} %bitcast.info, bf16[520,512]{1,0:T(8,128)(2,1)} %get-tuple-element.63.refs_0_, bf16[1032,512]{1,0:T(8,128)(2,1)} %collective-permute-done.refs_1_.refs_5_.refs_6_.refs_7_.refs_8_, bf16[256,1024]{1,0:T(8,128)(2,1)} %refs_2_.6, ...), custom_call_target="tpu_custom_call" | custom-call | flops 12000000000 | tf_op jit(solution)/shard_map/cross_local/pallas_call | solution.py:83
  59.6 4.4 %collective-permute-done.10.refs_3_.refs_4_ = bf16[512,512]{1,0:T(8,128)(2,1)} collective-permute-done((bf16[512,512]{1,0:T(8,128)(2,1)}, bf16[512,512]{1,0:T(8,128)(2,1)}, u32[]{:S(2)}, u32[]{:S(2)}) %collective-permute-start.10) | collective-permute-done | bytes 524320 | tf_op jit(solution)/shard_map/ppermute | solution.py:38
  64.5 6.6 %self_remote.1 = (bf16[512,512]{1,0:T(8,128)(2,1)}, bf16[1024,512]{1,0:T(8,128)(2,1)}, f32[4,8,512]{2,1,0:T(8,128)}) custom-call(s32[1]{0:T(128)} %bitcast.info, f32[512,512]{1,0:T(8,128)} %and_select_fusion.refs_0_, bf16[512,512]{1,0:T(8,128)(2,1)} %collective-permute-done.8.refs_1_.refs_2_, bf16[512,512]{1,0:T(8,128)(2,1)} %collective-permute-done.8.refs_1_.refs_2_, ...), custom_call_target="tpu_custom_call" | custom-call | flops 12000000000 | tf_op jit(solution)/shard_map/self_remote/pallas_call | solution.py:83
  71.1 4.1 %collective-permute-start.13 = (f32[4,8,512]{2,1,0:T(8,128)}, f32[4,8,512]{2,1,0:T(8,128)}, u32[]{:S(2)}, u32[]{:S(2)}) collective-permute-start(f32[4,8,512]{2,1,0:T(8,128)} %get-tuple-element.97), channel_id=1, source_target_pairs={{0,2},{1,3},{2,4},{3,5},{4,6},{5,7},{6,8},{7,9},{8,10},{9,11},{10,... | collective-permute-start | bytes 196616 | tf_op jit(solution)/shard_map/ppermute | solution.py:38
  75.2 3.0 %collective-permute-start.15 = (bf16[512,512]{1,0:T(8,128)(2,1)}, bf16[512,512]{1,0:T(8,128)(2,1)}, u32[]{:S(2)}, u32[]{:S(2)}) collective-permute-start(bf16[512,512]{1,0:T(8,128)(2,1)} %get-tuple-element.102), channel_id=1, source_target_pairs={{0,2},{1,3},{2,4},{3,5},{4,6},{5,7},{6,8},{7,9},{8,10},{9,11},{10,... | collective-permute-start | bytes 1572872 | tf_op jit(solution)/shard_map/ppermute | solution.py:38
  78.2 1.9 %collective-permute-start.16 = (bf16[768,512]{1,0:T(8,128)(2,1)}, bf16[768,512]{1,0:T(8,128)(2,1)}, u32[]{:S(2)}, u32[]{:S(2)}) collective-permute-start(bf16[768,512]{1,0:T(8,128)(2,1)} %get-tuple-element.104), channel_id=1, source_target_pairs={{0,1},{1,0},{2,3},{3,2},{4,5},{5,4},{6,7},{7,6},{8,9},{9,8},{10,11... | collective-permute-start | bytes 2359304 | tf_op jit(solution)/shard_map/ppermute | solution.py:38
  80.1 6.1 %self_local.1 = (bf16[768,512]{1,0:T(8,128)(2,1)}, bf16[768,512]{1,0:T(8,128)(2,1)}) custom-call(s32[1]{0:T(128)} %bitcast.info, f32[512,512]{1,0:T(8,128)} %and_select_fusion.1.refs_0_, bf16[256,1024]{1,0:T(8,128)(2,1)} %refs_1_.3, bf16[256,1024]{1,0:T(8,128)(2,1)} %refs_2_.7, bf16[256,1024]{1,0:T(8,128)(2,1)} %refs_3_.7, bf16[256,1024]{1,0:T(8,128)(2,1)} %refs_4_.3, ...), custom_call_target="tpu_custom_call" | custom-call | flops 12000000000 | tf_op jit(solution)/shard_map/self_local/pallas_call | solution.py:83
  86.3 2.8 %cross_final.1 = (bf16[256,1024]{1,0:T(8,128)(2,1)}, bf16[2,256,1024]{2,1,0:T(8,128)(2,1)}) custom-call(s32[1]{0:T(128)} %bitcast.info, bf16[768,512]{1,0:T(8,128)(2,1)} %get-tuple-element.103.mine, bf16[768,512]{1,0:T(8,128)(2,1)} %collective-permute-done.16.theirs, bf16[256,512]{1,0:T(8,128)(2,1)} %collective-permute-done.11.dq_mine, ...), custom_call_target="tpu_custom_call" | custom-call | tf_op jit(solution)/shard_map/cross_final/pallas_call | solution.py:83
  89.9 2.7 %kv_final.1 = (bf16[256,1024]{1,0:T(8,128)(2,1)}, bf16[256,1024]{1,0:T(8,128)(2,1)}, bf16[256,1024]{1,0:T(8,128)(2,1)}) custom-call(s32[1]{0:T(128)} %bitcast.info, bf16[768,512]{1,0:T(8,128)(2,1)} %get-tuple-element.109.mine, bf16[768,512]{1,0:T(8,128)(2,1)} %collective-permute-done.14.theirs, bf16[512,512]{1,0:T(8,128)(2,1)} %collective-permute-done.15.dq_mine), custom_call_target="tpu_custom_call" | custom-call | tf_op jit(solution)/shard_map/kv_final/pallas_call | solution.py:83
  92.5 1.8 %query_final.1 = bf16[256,1024]{1,0:T(8,128)(2,1)} custom-call(s32[1]{0:T(128)} %bitcast.info, bf16[768,512]{1,0:T(8,128)(2,1)} %collective-permute-done.14.theirs, bf16[512,512]{1,0:T(8,128)(2,1)} %collective-permute-done.17.dq_theirs, bf16[256,1024]{1,0:T(8,128)(2,1)} %get-tuple-element.110.grad), custom_call_target="tpu_custom_call", output_to_operand_aliasing={{}: (3, {})} | custom-call | tf_op jit(solution)/shard_map/query_final/pallas_call | solution.py:545
  (31 shorter events, 7.9 us)
Async XLA Ops:
  3.0 24.1 %collective-permute-start.3 = (bf16[520,512]{1,0:T(8,128)(2,1)}, bf16[520,512]{1,0:T(8,128)(2,1)}, u32[]{:S(2)}, u32[]{:S(2)}) collective-permute-start(bf16[520,512]{1,0:T(8,128)(2,1)} %get-tuple-element.70), channel_id=1, source_target_pairs={{0,15},{1,2},{2,1},{3,4},{4,3},{5,6},{6,5},{7,8},{8,7},{9,10},{10,... | collective-permute-start | bytes 1597448 | tf_op jit(solution)/shard_map/ppermute | solution.py:38
  5.6 24.7 %collective-permute-start.2 = (bf16[520,512]{1,0:T(8,128)(2,1)}, bf16[520,512]{1,0:T(8,128)(2,1)}, u32[]{:S(2)}, u32[]{:S(2)}) collective-permute-start(bf16[520,512]{1,0:T(8,128)(2,1)} %get-tuple-element.63.refs_0_), channel_id=1, source_target_pairs={{0,14},{1,3},{2,0},{3,5},{4,2},{5,7},{6,4},{7,9},{8,6},{9,11},{10,... | collective-permute-start | bytes 1597448 | tf_op jit(solution)/shard_map/ppermute | solution.py:38
  9.1 8.3 %collective-permute-start = (bf16[1032,512]{1,0:T(8,128)(2,1)}, bf16[1032,512]{1,0:T(8,128)(2,1)}, u32[]{:S(2)}, u32[]{:S(2)}) collective-permute-start(bf16[1032,512]{1,0:T(8,128)(2,1)} %pack_swap.1), channel_id=1, source_target_pairs={{0,1},{1,0},{2,3},{3,2},{4,5},{5,4},{6,7},{7,6},{8,9},{9,8},{10,11... | collective-permute-start | bytes 3170312 | tf_op jit(solution)/shard_map/ppermute | solution.py:38
  13.9 8.9 %collective-permute-start.1 = (bf16[1024,512]{1,0:T(8,128)(2,1)}, bf16[1024,512]{1,0:T(8,128)(2,1)}, u32[]{:S(2)}, u32[]{:S(2)}) collective-permute-start(bf16[1024,512]{1,0:T(8,128)(2,1)} %get-tuple-element.68), channel_id=1, source_target_pairs={{0,1},{1,0},{2,3},{3,2},{4,5},{5,4},{6,7},{7,6},{8,9},{9,8},{10,11... | collective-permute-start | bytes 3145736 | tf_op jit(solution)/shard_map/ppermute | solution.py:38
  21.4 8.9 %collective-permute-start.5 = (f32[4,8,256]{2,1,0:T(8,128)}, f32[4,8,256]{2,1,0:T(8,128)}, u32[]{:S(2)}, u32[]{:S(2)}) collective-permute-start(f32[4,8,256]{2,1,0:T(8,128)} %get-tuple-element.71), channel_id=1, source_target_pairs={{0,2},{1,15},{2,4},{3,1},{4,6},{5,3},{6,8},{7,5},{8,10},{9,7},{10,... | collective-permute-start | bytes 98312 | tf_op jit(solution)/shard_map/ppermute | solution.py:38
  22.5 8.1 %collective-permute-start.4 = (f32[4,8,256]{2,1,0:T(8,128)}, f32[4,8,256]{2,1,0:T(8,128)}, u32[]{:S(2)}, u32[]{:S(2)}) collective-permute-start(f32[4,8,256]{2,1,0:T(8,128)} %get-tuple-element.65), channel_id=1, source_target_pairs={{0,14},{1,3},{2,0},{3,5},{4,2},{5,7},{6,4},{7,9},{8,6},{9,11},{10,... | collective-permute-start | bytes 98312 | tf_op jit(solution)/shard_map/ppermute | solution.py:38
  30.6 18.0 %collective-permute-start.8 = (bf16[512,512]{1,0:T(8,128)(2,1)}, bf16[512,512]{1,0:T(8,128)(2,1)}, u32[]{:S(2)}, u32[]{:S(2)}) collective-permute-start(bf16[512,512]{1,0:T(8,128)(2,1)} %get-tuple-element.81), channel_id=1, source_target_pairs={{2,0},{3,1},{4,2},{5,3},{6,4},{7,5},{8,6},{9,7},{10,8},{11,9},{12,... | collective-permute-start | bytes 1572872 | tf_op jit(solution)/shard_map/ppermute | solution.py:38
  31.9 16.7 %collective-permute-start.9 = (f32[4,8,512]{2,1,0:T(8,128)}, f32[4,8,512]{2,1,0:T(8,128)}, u32[]{:S(2)}, u32[]{:S(2)}) collective-permute-start(f32[4,8,512]{2,1,0:T(8,128)} %self_stats.1.refs_10_), channel_id=1, source_target_pairs={{2,0},{3,1},{4,2},{5,3},{6,4},{7,5},{8,6},{9,7},{10,8},{11,9},{12,... | collective-permute-start | bytes 196616 | tf_op jit(solution)/shard_map/ppermute | solution.py:38
  39.2 9.5 %collective-permute-start.6 = (f32[4,8,256]{2,1,0:T(8,128)}, f32[4,8,256]{2,1,0:T(8,128)}, u32[]{:S(2)}, u32[]{:S(2)}) collective-permute-start(f32[4,8,256]{2,1,0:T(8,128)} %get-tuple-element.76), channel_id=1, source_target_pairs={{0,2},{1,15},{2,4},{3,1},{4,6},{5,3},{6,8},{7,5},{8,10},{9,7},{10,... | collective-permute-start | bytes 98312 | tf_op jit(solution)/shard_map/ppermute | solution.py:38
  47.3 5.9 %collective-permute-start.7 = (f32[4,8,256]{2,1,0:T(8,128)}, f32[4,8,256]{2,1,0:T(8,128)}, u32[]{:S(2)}, u32[]{:S(2)}) collective-permute-start(f32[4,8,256]{2,1,0:T(8,128)} %get-tuple-element.77), channel_id=1, source_target_pairs={{0,14},{1,3},{2,0},{3,5},{4,2},{5,7},{6,4},{7,9},{8,6},{9,11},{10,... | collective-permute-start | bytes 98312 | tf_op jit(solution)/shard_map/ppermute | solution.py:38
  47.3 16.6 %collective-permute-start.10 = (bf16[512,512]{1,0:T(8,128)(2,1)}, bf16[512,512]{1,0:T(8,128)(2,1)}, u32[]{:S(2)}, u32[]{:S(2)}) collective-permute-start(bf16[512,512]{1,0:T(8,128)(2,1)} %get-tuple-element.87), channel_id=1, source_target_pairs={{2,1},{3,0},{4,3},{5,2},{6,5},{7,4},{8,7},{9,6},{10,9},{11,8},{12,... | collective-permute-start | bytes 1572872 | tf_op jit(solution)/shard_map/ppermute | solution.py:38
  64.0 14.3 %collective-permute-start.11 = (bf16[256,512]{1,0:T(8,128)(2,1)}, bf16[256,512]{1,0:T(8,128)(2,1)}, u32[]{:S(2)}, u32[]{:S(2)}) collective-permute-start(bf16[256,512]{1,0:T(8,128)(2,1)} %get-tuple-element.95), channel_id=1, source_target_pairs={{0,2},{1,15},{2,4},{3,1},{4,6},{5,3},{6,8},{7,5},{8,10},{9,7},{10,... | collective-permute-start | bytes 786440 | tf_op jit(solution)/shard_map/ppermute | solution.py:38
  64.0 14.3 %collective-permute-start.12 = (bf16[256,512]{1,0:T(8,128)(2,1)}, bf16[256,512]{1,0:T(8,128)(2,1)}, u32[]{:S(2)}, u32[]{:S(2)}) collective-permute-start(bf16[256,512]{1,0:T(8,128)(2,1)} %get-tuple-element.96), channel_id=1, source_target_pairs={{0,15},{1,2},{2,1},{3,4},{4,3},{5,6},{6,5},{7,8},{8,7},{9,10},{10,... | collective-permute-start | bytes 786440 | tf_op jit(solution)/shard_map/ppermute | solution.py:38
  71.1 7.1 %collective-permute-start.13 = (f32[4,8,512]{2,1,0:T(8,128)}, f32[4,8,512]{2,1,0:T(8,128)}, u32[]{:S(2)}, u32[]{:S(2)}) collective-permute-start(f32[4,8,512]{2,1,0:T(8,128)} %get-tuple-element.97), channel_id=1, source_target_pairs={{0,2},{1,3},{2,4},{3,5},{4,6},{5,7},{6,8},{7,9},{8,10},{9,11},{10,... | collective-permute-start | bytes 196616 | tf_op jit(solution)/shard_map/ppermute | solution.py:38
  75.2 13.9 %collective-permute-start.15 = (bf16[512,512]{1,0:T(8,128)(2,1)}, bf16[512,512]{1,0:T(8,128)(2,1)}, u32[]{:S(2)}, u32[]{:S(2)}) collective-permute-start(bf16[512,512]{1,0:T(8,128)(2,1)} %get-tuple-element.102), channel_id=1, source_target_pairs={{0,2},{1,3},{2,4},{3,5},{4,6},{5,7},{6,8},{7,9},{8,10},{9,11},{10,... | collective-permute-start | bytes 1572872 | tf_op jit(solution)/shard_map/ppermute | solution.py:38
  78.2 8.1 %collective-permute-start.16 = (bf16[768,512]{1,0:T(8,128)(2,1)}, bf16[768,512]{1,0:T(8,128)(2,1)}, u32[]{:S(2)}, u32[]{:S(2)}) collective-permute-start(bf16[768,512]{1,0:T(8,128)(2,1)} %get-tuple-element.104), channel_id=1, source_target_pairs={{0,1},{1,0},{2,3},{3,2},{4,5},{5,4},{6,7},{7,6},{8,9},{9,8},{10,11... | collective-permute-start | bytes 2359304 | tf_op jit(solution)/shard_map/ppermute | solution.py:38
  86.2 3.7 %collective-permute-start.14 = (bf16[768,512]{1,0:T(8,128)(2,1)}, bf16[768,512]{1,0:T(8,128)(2,1)}, u32[]{:S(2)}, u32[]{:S(2)}) collective-permute-start(bf16[768,512]{1,0:T(8,128)(2,1)} %get-tuple-element.101), channel_id=1, source_target_pairs={{0,1},{1,0},{2,3},{3,2},{4,5},{5,4},{6,7},{7,6},{8,9},{9,8},{10,11... | collective-permute-start | bytes 2359304 | tf_op jit(solution)/shard_map/ppermute | solution.py:38
  89.1 3.4 %collective-permute-start.17 = (bf16[512,512]{1,0:T(8,128)(2,1)}, bf16[512,512]{1,0:T(8,128)(2,1)}, u32[]{:S(2)}, u32[]{:S(2)}) collective-permute-start(bf16[512,512]{1,0:T(8,128)(2,1)} %collective-permute-done.15.dq_mine), channel_id=1, source_target_pairs={{0,1},{1,0},{2,3},{3,2},{4,5},{5,4},{6,7},{7,6},{8,9},{9,8},{10,11... | collective-permute-start | bytes 1572872 | tf_op jit(solution)/shard_map/ppermute | solution.py:38

commit v16 on v15

--- a/solution.py
+++ b/solution.py
@@ -504,11 +504,8 @@
         [half_out] * 2, [half_shape] * 2, flops=LONG,
     )
 
-    xd_same, xd_cross, s_cross, x_keep = lax.optimization_barrier(
-        (xd_same, xd_cross, s_cross, x_keep)
-    )
+    xd_same, s_cross, x_keep = lax.optimization_barrier((xd_same, s_cross, x_keep))
     xr_same = send(xd_same, inward, True)
-    xr_cross = send(xd_cross, across, True)
     far_bias, x_keep = lax.optimization_barrier((far_bias, x_keep))
     sd, s_kv, s_fin = call(
         per_head(self_remote_kernel), "self_remote", info,
@@ -521,9 +518,10 @@
     f_self = send(s_fin, lambda d: d + 2, False)
     sr = send(sd, lambda d: d + 2, False)
 
-    x_give, s_kv, xr_same, xr_cross, f_self = lax.optimization_barrier(
-        (x_give, s_kv, xr_same, xr_cross, f_self)
-    )
+    x_give, s_kv, xr_same, xd_cross, f_self = lax.optimization_barrier(
+        (x_give, s_kv, xr_same, xd_cross, f_self)
+    )
+    xr_cross = send(xd_cross, across, True)
     x_take = send(x_give, swap, False)
     s_keep, s_give = call(
         per_head(self_local_kernel), "self_local", info,

time: 96.2 us -> 102 us (1.060)
  waiting for transfers between devices: 12.6 us -> 21.4 us
  starting transfers between devices: 30.1 us -> 27.9 us
    ppermute x18, waiting for transfers between devices: 12.6 us -> 21.4 us  [send(): return lax.ppermute(value, 'ctx', pairs)]
    ppermute x18, starting transfers between devices: 30.1 us -> 27.9 us  [send(): return lax.ppermute(value, 'ctx', pairs)]
  transfers between devices with their start and end apart: 18 -> 18, of which waited for: 4 -> 5; matrix products, arithmetic and copies ran while one was open for 4% -> 3% of each run, Pallas kernels for 46% -> 43%
where the time goes in v16:
time: 102 us; the launch traced here: 101 us
  Pallas kernels  47.7 us (47%)
  starting transfers between devices  27.9 us (27%)
  waiting for transfers between devices  21.4 us (21%)
  other arithmetic  2.4 us (2%)
    pallas_call x11, Pallas kernels, call(): pl.pallas_call(kernel, name=name, grid_spec=pltpu.PrefetchScalarGridSpec(...  45.9 us
    ppermute x18, starting transfers between devices, send(): return lax.ppermute(value, 'ctx', pairs)  27.9 us
    ppermute x18, waiting for transfers between devices, send(): return lax.ppermute(value, 'ctx', pairs)  21.4 us
  transfers between devices with their start and end apart: 18, of which 5 were waited for; matrix products, arithmetic and copies ran while one was open for 3% of the time, Pallas kernels for 43%

profile of v16, /device:TPU:1, one launch (start us, length us, event | category | flops | bytes accessed | tf_op | source)
XLA Modules:
  0.0 101.1 jit_solution(1807090881807917127)
XLA Ops:
  0.6 2.3 %pack_cross.1 = (bf16[520,512]{1,0:T(8,128)(2,1)}, bf16[520,512]{1,0:T(8,128)(2,1)}) custom-call(s32[1]{0:T(128)} %bitcast.info, s32[2,4]{1,0:T(2,128)} %bitcast.8, bf16[256,1024]{1,0:T(8,128)(2,1)} %refs_2_.6, bf16[256,1024]{1,0:T(8,128)(2,1)} %refs_3_.6, bf16[256,1024]{1,0:T(8,128)(2,1)} %refs_2_.6, bf16[256,1024]{1,0:T(8,128)(2,1)} %refs_3_.6), custom_call_target="tpu_custom_call" | custom-call | tf_op jit(solution)/shard_map/pack_cross/pallas_call | solution.py:83
  3.0 2.6 %collective-permute-start.3 = (bf16[520,512]{1,0:T(8,128)(2,1)}, bf16[520,512]{1,0:T(8,128)(2,1)}, u32[]{:S(2)}, u32[]{:S(2)}) collective-permute-start(bf16[520,512]{1,0:T(8,128)(2,1)} %get-tuple-element.69), channel_id=1, source_target_pairs={{0,15},{1,2},{2,1},{3,4},{4,3},{5,6},{6,5},{7,8},{8,7},{9,10},{10,... | collective-permute-start | bytes 1597448 | tf_op jit(solution)/shard_map/ppermute | solution.py:38
  6.8 2.2 %pack_swap.1 = bf16[1032,512]{1,0:T(8,128)(2,1)} custom-call(s32[1]{0:T(128)} %bitcast.info, s32[2,4]{1,0:T(2,128)} %bitcast.9, bf16[256,1024]{1,0:T(8,128)(2,1)} %refs_2_.6, bf16[256,1024]{1,0:T(8,128)(2,1)} %refs_3_.6, bf16[2,256,1024]{2,1,0:T(8,128)(2,1)} %bitcast.4), custom_call_target="tpu_custom_call" | custom-call | tf_op jit(solution)/shard_map/pack_swap/pallas_call | solution.py:83
  9.1 2.3 %collective-permute-start = (bf16[1032,512]{1,0:T(8,128)(2,1)}, bf16[1032,512]{1,0:T(8,128)(2,1)}, u32[]{:S(2)}, u32[]{:S(2)}) collective-permute-start(bf16[1032,512]{1,0:T(8,128)(2,1)} %pack_swap.1), channel_id=1, source_target_pairs={{0,1},{1,0},{2,3},{3,2},{4,5},{5,4},{6,7},{7,6},{8,9},{9,8},{10,11... | collective-permute-start | bytes 3170312 | tf_op jit(solution)/shard_map/ppermute | solution.py:38
  11.3 2.6 %pack_self.1 = (bf16[1024,512]{1,0:T(8,128)(2,1)}, bf16[512,512]{1,0:T(8,128)(2,1)}, bf16[512,512]{1,0:T(8,128)(2,1)}) custom-call(s32[1]{0:T(128)} %bitcast.info, bf16[256,1024]{1,0:T(8,128)(2,1)} %refs_1_.3, bf16[256,1024]{1,0:T(8,128)(2,1)} %refs_2_.7, bf16[256,1024]{1,0:T(8,128)(2,1)} %refs_1_.3, bf16[256,1024]{1,0:T(8,128)(2,1)} %refs_2_.7, ...), custom_call_target="tpu_custom_call" | custom-call | tf_op jit(solution)/shard_map/pack_self/pallas_call | solution.py:83
  17.3 4.0 %cross_stats.1 = (f32[4,8,256]{2,1,0:T(8,128)}, f32[4,8,256]{2,1,0:T(8,128)}) custom-call(s32[1]{0:T(128)} %bitcast.info, bf16[520,512]{1,0:T(8,128)(2,1)} %get-tuple-element.62.refs_0_, bf16[1032,512]{1,0:T(8,128)(2,1)} %collective-permute-done.refs_1_.refs_5_.refs_6_.refs_7_.refs_8_, bf16[256,1024]{1,0:T(8,128)(2,1)} %refs_2_.6, ...), custom_call_target="tpu_custom_call" | custom-call | tf_op jit(solution)/shard_map/cross_stats/pallas_call | solution.py:83
  22.9 4.2 %self_stats.1.refs_10_ = f32[4,8,512]{2,1,0:T(8,128)} custom-call(s32[1]{0:T(128)} %bitcast.info, f32[512,512]{1,0:T(8,128)} %and_select_fusion.1.refs_0_, bf16[256,1024]{1,0:T(8,128)(2,1)} %refs_1_.3, bf16[256,1024]{1,0:T(8,128)(2,1)} %refs_2_.7, bf16[256,1024]{1,0:T(8,128)(2,1)} %refs_3_.7, bf16[256,1024]{1,0:T(8,128)(2,1)} %refs_4_.3, ...), custom_call_target="tpu_custom_call" | custom-call | tf_op jit(solution)/shard_map/self_stats/pallas_call | solution.py:83
  27.0 3.3 %collective-permute-done.2.refs_0_.refs_2_.refs_3_ = bf16[520,512]{1,0:T(8,128)(2,1)} collective-permute-done((bf16[520,512]{1,0:T(8,128)(2,1)}, bf16[520,512]{1,0:T(8,128)(2,1)}, u32[]{:S(2)}, u32[]{:S(2)}) %collective-permute-start.2) | collective-permute-done | bytes 532512 | tf_op jit(solution)/shard_map/ppermute | solution.py:38
  31.9 1.3 %collective-permute-start.9 = (f32[4,8,512]{2,1,0:T(8,128)}, f32[4,8,512]{2,1,0:T(8,128)}, u32[]{:S(2)}, u32[]{:S(2)}) collective-permute-start(f32[4,8,512]{2,1,0:T(8,128)} %self_stats.1.refs_10_), channel_id=1, source_target_pairs={{2,0},{3,1},{4,2},{5,3},{6,4},{7,5},{8,6},{9,7},{10,8},{11,9},{12,... | collective-permute-start | bytes 196616 | tf_op jit(solution)/shard_map/ppermute | solution.py:38
  33.2 5.9 %cross_remote.1 = (bf16[256,512]{1,0:T(8,128)(2,1)}, bf16[256,512]{1,0:T(8,128)(2,1)}, bf16[1024,512]{1,0:T(8,128)(2,1)}, f32[4,8,256]{2,1,0:T(8,128)}, f32[4,8,256]{2,1,0:T(8,128)}) custom-call(s32[1]{0:T(128)} %bitcast.info, bf16[520,512]{1,0:T(8,128)(2,1)} %collective-permute-done.2.refs_0_.refs_2_.refs_3_, ...), custom_call_target="tpu_custom_call" | custom-call | tf_op jit(solution)/shard_map/cross_remote/pallas_call | solution.py:83
  39.2 8.2 %collective-permute-start.6 = (f32[4,8,256]{2,1,0:T(8,128)}, f32[4,8,256]{2,1,0:T(8,128)}, u32[]{:S(2)}, u32[]{:S(2)}) collective-permute-start(f32[4,8,256]{2,1,0:T(8,128)} %get-tuple-element.75), channel_id=1, source_target_pairs={{0,2},{1,15},{2,4},{3,1},{4,6},{5,3},{6,8},{7,5},{8,10},{9,7},{10,... | collective-permute-start | bytes 98312 | tf_op jit(solution)/shard_map/ppermute | solution.py:38
  47.3 1.3 %collective-permute-start.10 = (bf16[512,512]{1,0:T(8,128)(2,1)}, bf16[512,512]{1,0:T(8,128)(2,1)}, u32[]{:S(2)}, u32[]{:S(2)}) collective-permute-start(bf16[512,512]{1,0:T(8,128)(2,1)} %get-tuple-element.85), channel_id=1, source_target_pairs={{2,1},{3,0},{4,3},{5,2},{6,5},{7,4},{8,7},{9,6},{10,9},{11,8},{12,... | collective-permute-start | bytes 1572872 | tf_op jit(solution)/shard_map/ppermute | solution.py:38
  48.7 4.5 %collective-permute-done.7.refs_10_ = f32[4,8,256]{2,1,0:T(8,128)} collective-permute-done((f32[4,8,256]{2,1,0:T(8,128)}, f32[4,8,256]{2,1,0:T(8,128)}, u32[]{:S(2)}, u32[]{:S(2)}) %collective-permute-start.7) | collective-permute-done | bytes 32800 | tf_op jit(solution)/shard_map/ppermute | solution.py:38
  53.2 6.4 %cross_local.1 = (bf16[768,512]{1,0:T(8,128)(2,1)}, bf16[768,512]{1,0:T(8,128)(2,1)}) custom-call(s32[1]{0:T(128)} %bitcast.info, bf16[520,512]{1,0:T(8,128)(2,1)} %get-tuple-element.62.refs_0_, bf16[1032,512]{1,0:T(8,128)(2,1)} %collective-permute-done.refs_1_.refs_5_.refs_6_.refs_7_.refs_8_, bf16[256,1024]{1,0:T(8,128)(2,1)} %refs_2_.6, ...), custom_call_target="tpu_custom_call" | custom-call | flops 12000000000 | tf_op jit(solution)/shard_map/cross_local/pallas_call | solution.py:83
  59.6 4.4 %collective-permute-done.10.refs_3_.refs_4_ = bf16[512,512]{1,0:T(8,128)(2,1)} collective-permute-done((bf16[512,512]{1,0:T(8,128)(2,1)}, bf16[512,512]{1,0:T(8,128)(2,1)}, u32[]{:S(2)}, u32[]{:S(2)}) %collective-permute-start.10) | collective-permute-done | bytes 524320 | tf_op jit(solution)/shard_map/ppermute | solution.py:38
  64.0 6.7 %self_remote.1 = (bf16[512,512]{1,0:T(8,128)(2,1)}, bf16[1024,512]{1,0:T(8,128)(2,1)}, f32[4,8,512]{2,1,0:T(8,128)}) custom-call(s32[1]{0:T(128)} %bitcast.info, f32[512,512]{1,0:T(8,128)} %and_select_fusion.refs_0_, bf16[512,512]{1,0:T(8,128)(2,1)} %collective-permute-done.8.refs_1_.refs_2_, bf16[512,512]{1,0:T(8,128)(2,1)} %collective-permute-done.8.refs_1_.refs_2_, ...), custom_call_target="tpu_custom_call" | custom-call | flops 12000000000 | tf_op jit(solution)/shard_map/self_remote/pallas_call | solution.py:83
  70.6 4.0 %collective-permute-start.12 = (f32[4,8,512]{2,1,0:T(8,128)}, f32[4,8,512]{2,1,0:T(8,128)}, u32[]{:S(2)}, u32[]{:S(2)}) collective-permute-start(f32[4,8,512]{2,1,0:T(8,128)} %get-tuple-element.95), channel_id=1, source_target_pairs={{0,2},{1,3},{2,4},{3,5},{4,6},{5,7},{6,8},{7,9},{8,10},{9,11},{10,... | collective-permute-start | bytes 196616 | tf_op jit(solution)/shard_map/ppermute | solution.py:38
  74.6 2.3 %collective-permute-start.14 = (bf16[512,512]{1,0:T(8,128)(2,1)}, bf16[512,512]{1,0:T(8,128)(2,1)}, u32[]{:S(2)}, u32[]{:S(2)}) collective-permute-start(bf16[512,512]{1,0:T(8,128)(2,1)} %get-tuple-element.100), channel_id=1, source_target_pairs={{0,2},{1,3},{2,4},{3,5},{4,6},{5,7},{6,8},{7,9},{8,10},{9,11},{10,... | collective-permute-start | bytes 1572872 | tf_op jit(solution)/shard_map/ppermute | solution.py:38
  76.9 1.4 %collective-permute-start.16 = (bf16[256,512]{1,0:T(8,128)(2,1)}, bf16[256,512]{1,0:T(8,128)(2,1)}, u32[]{:S(2)}, u32[]{:S(2)}) collective-permute-start(bf16[256,512]{1,0:T(8,128)(2,1)} %get-tuple-element.104), channel_id=1, source_target_pairs={{0,15},{1,2},{2,1},{3,4},{4,3},{5,6},{6,5},{7,8},{8,7},{9,10},{10,... | collective-permute-start | bytes 786440 | tf_op jit(solution)/shard_map/ppermute | solution.py:38
  78.5 6.1 %self_local.1 = (bf16[768,512]{1,0:T(8,128)(2,1)}, bf16[768,512]{1,0:T(8,128)(2,1)}) custom-call(s32[1]{0:T(128)} %bitcast.info, f32[512,512]{1,0:T(8,128)} %and_select_fusion.1.refs_0_, bf16[256,1024]{1,0:T(8,128)(2,1)} %refs_1_.3, bf16[256,1024]{1,0:T(8,128)(2,1)} %refs_2_.7, bf16[256,1024]{1,0:T(8,128)(2,1)} %refs_3_.7, bf16[256,1024]{1,0:T(8,128)(2,1)} %refs_4_.3, ...), custom_call_target="tpu_custom_call" | custom-call | flops 12000000000 | tf_op jit(solution)/shard_map/self_local/pallas_call | solution.py:83
  84.9 8.8 %collective-permute-done.16.dq_theirs = bf16[256,512]{1,0:T(8,128)(2,1)} collective-permute-done((bf16[256,512]{1,0:T(8,128)(2,1)}, bf16[256,512]{1,0:T(8,128)(2,1)}, u32[]{:S(2)}, u32[]{:S(2)}) %collective-permute-start.16) | collective-permute-done | bytes 262176 | tf_op jit(solution)/shard_map/ppermute | solution.py:38
  93.7 2.8 %cross_final.1 = (bf16[256,1024]{1,0:T(8,128)(2,1)}, bf16[2,256,1024]{2,1,0:T(8,128)(2,1)}) custom-call(s32[1]{0:T(128)} %bitcast.info, bf16[768,512]{1,0:T(8,128)(2,1)} %get-tuple-element.101.mine, bf16[768,512]{1,0:T(8,128)(2,1)} %collective-permute-done.15.theirs, bf16[256,512]{1,0:T(8,128)(2,1)} %collective-permute-done.11.dq_mine, ...), custom_call_target="tpu_custom_call" | custom-call | tf_op jit(solution)/shard_map/cross_final/pallas_call | solution.py:83
  96.5 2.7 %kv_final.1 = (bf16[256,1024]{1,0:T(8,128)(2,1)}, bf16[256,1024]{1,0:T(8,128)(2,1)}, bf16[256,1024]{1,0:T(8,128)(2,1)}) custom-call(s32[1]{0:T(128)} %bitcast.info, bf16[768,512]{1,0:T(8,128)(2,1)} %get-tuple-element.107.mine, bf16[768,512]{1,0:T(8,128)(2,1)} %collective-permute-done.13.theirs, bf16[512,512]{1,0:T(8,128)(2,1)} %collective-permute-done.14.dq_mine), custom_call_target="tpu_custom_call" | custom-call | tf_op jit(solution)/shard_map/kv_final/pallas_call | solution.py:83
  99.3 1.8 %query_final.1 = bf16[256,1024]{1,0:T(8,128)(2,1)} custom-call(s32[1]{0:T(128)} %bitcast.info, bf16[768,512]{1,0:T(8,128)(2,1)} %collective-permute-done.13.theirs, bf16[512,512]{1,0:T(8,128)(2,1)} %collective-permute-done.17.dq_theirs, bf16[256,1024]{1,0:T(8,128)(2,1)} %get-tuple-element.108.grad), custom_call_target="tpu_custom_call", output_to_operand_aliasing={{}: (3, {})} | custom-call | tf_op jit(solution)/shard_map/query_final/pallas_call | solution.py:543
  (31 shorter events, 8.4 us)
Async XLA Ops:
  3.0 24.1 %collective-permute-start.3 = (bf16[520,512]{1,0:T(8,128)(2,1)}, bf16[520,512]{1,0:T(8,128)(2,1)}, u32[]{:S(2)}, u32[]{:S(2)}) collective-permute-start(bf16[520,512]{1,0:T(8,128)(2,1)} %get-tuple-element.69), channel_id=1, source_target_pairs={{0,15},{1,2},{2,1},{3,4},{4,3},{5,6},{6,5},{7,8},{8,7},{9,10},{10,... | collective-permute-start | bytes 1597448 | tf_op jit(solution)/shard_map/ppermute | solution.py:38
  5.6 24.7 %collective-permute-start.2 = (bf16[520,512]{1,0:T(8,128)(2,1)}, bf16[520,512]{1,0:T(8,128)(2,1)}, u32[]{:S(2)}, u32[]{:S(2)}) collective-permute-start(bf16[520,512]{1,0:T(8,128)(2,1)} %get-tuple-element.62.refs_0_), channel_id=1, source_target_pairs={{0,14},{1,3},{2,0},{3,5},{4,2},{5,7},{6,4},{7,9},{8,6},{9,11},{10,... | collective-permute-start | bytes 1597448 | tf_op jit(solution)/shard_map/ppermute | solution.py:38
  9.1 8.3 %collective-permute-start = (bf16[1032,512]{1,0:T(8,128)(2,1)}, bf16[1032,512]{1,0:T(8,128)(2,1)}, u32[]{:S(2)}, u32[]{:S(2)}) collective-permute-start(bf16[1032,512]{1,0:T(8,128)(2,1)} %pack_swap.1), channel_id=1, source_target_pairs={{0,1},{1,0},{2,3},{3,2},{4,5},{5,4},{6,7},{7,6},{8,9},{9,8},{10,11... | collective-permute-start | bytes 3170312 | tf_op jit(solution)/shard_map/ppermute | solution.py:38
  13.9 8.9 %collective-permute-start.1 = (bf16[1024,512]{1,0:T(8,128)(2,1)}, bf16[1024,512]{1,0:T(8,128)(2,1)}, u32[]{:S(2)}, u32[]{:S(2)}) collective-permute-start(bf16[1024,512]{1,0:T(8,128)(2,1)} %get-tuple-element.67), channel_id=1, source_target_pairs={{0,1},{1,0},{2,3},{3,2},{4,5},{5,4},{6,7},{7,6},{8,9},{9,8},{10,11... | collective-permute-start | bytes 3145736 | tf_op jit(solution)/shard_map/ppermute | solution.py:38
  21.4 8.9 %collective-permute-start.5 = (f32[4,8,256]{2,1,0:T(8,128)}, f32[4,8,256]{2,1,0:T(8,128)}, u32[]{:S(2)}, u32[]{:S(2)}) collective-permute-start(f32[4,8,256]{2,1,0:T(8,128)} %get-tuple-element.70), channel_id=1, source_target_pairs={{0,2},{1,15},{2,4},{3,1},{4,6},{5,3},{6,8},{7,5},{8,10},{9,7},{10,... | collective-permute-start | bytes 98312 | tf_op jit(solution)/shard_map/ppermute | solution.py:38
  22.5 8.1 %collective-permute-start.4 = (f32[4,8,256]{2,1,0:T(8,128)}, f32[4,8,256]{2,1,0:T(8,128)}, u32[]{:S(2)}, u32[]{:S(2)}) collective-permute-start(f32[4,8,256]{2,1,0:T(8,128)} %get-tuple-element.64), channel_id=1, source_target_pairs={{0,14},{1,3},{2,0},{3,5},{4,2},{5,7},{6,4},{7,9},{8,6},{9,11},{10,... | collective-permute-start | bytes 98312 | tf_op jit(solution)/shard_map/ppermute | solution.py:38
  30.6 18.0 %collective-permute-start.8 = (bf16[512,512]{1,0:T(8,128)(2,1)}, bf16[512,512]{1,0:T(8,128)(2,1)}, u32[]{:S(2)}, u32[]{:S(2)}) collective-permute-start(bf16[512,512]{1,0:T(8,128)(2,1)} %get-tuple-element.80), channel_id=1, source_target_pairs={{2,0},{3,1},{4,2},{5,3},{6,4},{7,5},{8,6},{9,7},{10,8},{11,9},{12,... | collective-permute-start | bytes 1572872 | tf_op jit(solution)/shard_map/ppermute | solution.py:38
  31.9 16.7 %collective-permute-start.9 = (f32[4,8,512]{2,1,0:T(8,128)}, f32[4,8,512]{2,1,0:T(8,128)}, u32[]{:S(2)}, u32[]{:S(2)}) collective-permute-start(f32[4,8,512]{2,1,0:T(8,128)} %self_stats.1.refs_10_), channel_id=1, source_target_pairs={{2,0},{3,1},{4,2},{5,3},{6,4},{7,5},{8,6},{9,7},{10,8},{11,9},{12,... | collective-permute-start | bytes 196616 | tf_op jit(solution)/shard_map/ppermute | solution.py:38
  39.2 9.5 %collective-permute-start.6 = (f32[4,8,256]{2,1,0:T(8,128)}, f32[4,8,256]{2,1,0:T(8,128)}, u32[]{:S(2)}, u32[]{:S(2)}) collective-permute-start(f32[4,8,256]{2,1,0:T(8,128)} %get-tuple-element.75), channel_id=1, source_target_pairs={{0,2},{1,15},{2,4},{3,1},{4,6},{5,3},{6,8},{7,5},{8,10},{9,7},{10,... | collective-permute-start | bytes 98312 | tf_op jit(solution)/shard_map/ppermute | solution.py:38
  47.3 5.9 %collective-permute-start.7 = (f32[4,8,256]{2,1,0:T(8,128)}, f32[4,8,256]{2,1,0:T(8,128)}, u32[]{:S(2)}, u32[]{:S(2)}) collective-permute-start(f32[4,8,256]{2,1,0:T(8,128)} %get-tuple-element.76), channel_id=1, source_target_pairs={{0,14},{1,3},{2,0},{3,5},{4,2},{5,7},{6,4},{7,9},{8,6},{9,11},{10,... | collective-permute-start | bytes 98312 | tf_op jit(solution)/shard_map/ppermute | solution.py:38
  47.3 16.6 %collective-permute-start.10 = (bf16[512,512]{1,0:T(8,128)(2,1)}, bf16[512,512]{1,0:T(8,128)(2,1)}, u32[]{:S(2)}, u32[]{:S(2)}) collective-permute-start(bf16[512,512]{1,0:T(8,128)(2,1)} %get-tuple-element.85), channel_id=1, source_target_pairs={{2,1},{3,0},{4,3},{5,2},{6,5},{7,4},{8,7},{9,6},{10,9},{11,8},{12,... | collective-permute-start | bytes 1572872 | tf_op jit(solution)/shard_map/ppermute | solution.py:38
  64.0 12.9 %collective-permute-start.11 = (bf16[256,512]{1,0:T(8,128)(2,1)}, bf16[256,512]{1,0:T(8,128)(2,1)}, u32[]{:S(2)}, u32[]{:S(2)}) collective-permute-start(bf16[256,512]{1,0:T(8,128)(2,1)} %get-tuple-element.93), channel_id=1, source_target_pairs={{0,2},{1,15},{2,4},{3,1},{4,6},{5,3},{6,8},{7,5},{8,10},{9,7},{10,... | collective-permute-start | bytes 786440 | tf_op jit(solution)/shard_map/ppermute | solution.py:38
  70.6 6.3 %collective-permute-start.12 = (f32[4,8,512]{2,1,0:T(8,128)}, f32[4,8,512]{2,1,0:T(8,128)}, u32[]{:S(2)}, u32[]{:S(2)}) collective-permute-start(f32[4,8,512]{2,1,0:T(8,128)} %get-tuple-element.95), channel_id=1, source_target_pairs={{0,2},{1,3},{2,4},{3,5},{4,6},{5,7},{6,8},{7,9},{8,10},{9,11},{10,... | collective-permute-start | bytes 196616 | tf_op jit(solution)/shard_map/ppermute | solution.py:38
  74.6 21.9 %collective-permute-start.14 = (bf16[512,512]{1,0:T(8,128)(2,1)}, bf16[512,512]{1,0:T(8,128)(2,1)}, u32[]{:S(2)}, u32[]{:S(2)}) collective-permute-start(bf16[512,512]{1,0:T(8,128)(2,1)} %get-tuple-element.100), channel_id=1, source_target_pairs={{0,2},{1,3},{2,4},{3,5},{4,6},{5,7},{6,8},{7,9},{8,10},{9,11},{10,... | collective-permute-start | bytes 1572872 | tf_op jit(solution)/shard_map/ppermute | solution.py:38
  76.9 16.9 %collective-permute-start.16 = (bf16[256,512]{1,0:T(8,128)(2,1)}, bf16[256,512]{1,0:T(8,128)(2,1)}, u32[]{:S(2)}, u32[]{:S(2)}) collective-permute-start(bf16[256,512]{1,0:T(8,128)(2,1)} %get-tuple-element.104), channel_id=1, source_target_pairs={{0,15},{1,2},{2,1},{3,4},{4,3},{5,6},{6,5},{7,8},{8,7},{9,10},{10,... | collective-permute-start | bytes 786440 | tf_op jit(solution)/shard_map/ppermute | solution.py:38
  78.3 15.5 %collective-permute-start.15 = (bf16[768,512]{1,0:T(8,128)(2,1)}, bf16[768,512]{1,0:T(8,128)(2,1)}, u32[]{:S(2)}, u32[]{:S(2)}) collective-permute-start(bf16[768,512]{1,0:T(8,128)(2,1)} %get-tuple-element.102), channel_id=1, source_target_pairs={{0,1},{1,0},{2,3},{3,2},{4,5},{5,4},{6,7},{7,6},{8,9},{9,8},{10,11... | collective-permute-start | bytes 2359304 | tf_op jit(solution)/shard_map/ppermute | solution.py:38
  84.6 11.9 %collective-permute-start.13 = (bf16[768,512]{1,0:T(8,128)(2,1)}, bf16[768,512]{1,0:T(8,128)(2,1)}, u32[]{:S(2)}, u32[]{:S(2)}) collective-permute-start(bf16[768,512]{1,0:T(8,128)(2,1)} %get-tuple-element.99), channel_id=1, source_target_pairs={{0,1},{1,0},{2,3},{3,2},{4,5},{5,4},{6,7},{7,6},{8,9},{9,8},{10,11... | collective-permute-start | bytes 2359304 | tf_op jit(solution)/shard_map/ppermute | solution.py:38
  96.5 2.8 %collective-permute-start.17 = (bf16[512,512]{1,0:T(8,128)(2,1)}, bf16[512,512]{1,0:T(8,128)(2,1)}, u32[]{:S(2)}, u32[]{:S(2)}) collective-permute-start(bf16[512,512]{1,0:T(8,128)(2,1)} %collective-permute-done.14.dq_mine), channel_id=1, source_target_pairs={{0,1},{1,0},{2,3},{3,2},{4,5},{5,4},{6,7},{7,6},{8,9},{9,8},{10,11... | collective-permute-start | bytes 1572872 | tf_op jit(solution)/shard_map/ppermute | solution.py:38

commit v17 on v15

--- a/solution.py
+++ b/solution.py
@@ -547,13 +547,13 @@
         name="query_final",
         grid_spec=pltpu.PrefetchScalarGridSpec(
             num_scalar_prefetch=1,
-            grid=(2,),
+            grid=(1,),
             in_specs=[
-                pl.BlockSpec((ROWS // 2, WIDE), lambda h, info: (h, 0)),
-                pl.BlockSpec((ROWS // 2, WIDE), lambda h, info: (2 + h, 0)),
+                pl.BlockSpec((ROWS, WIDE), lambda h, info: (0, 0)),
+                pl.BlockSpec((ROWS, WIDE), lambda h, info: (1, 0)),
                 pl.BlockSpec(memory_space=pl.ANY),
             ],
-            out_specs=pl.BlockSpec((ROWS // 2, WIDE), lambda h, info: (h, 1 - info[0] % 2)),
+            out_specs=pl.BlockSpec((ROWS, WIDE), lambda h, info: (0, 1 - info[0] % 2)),
         ),
         out_shape=jax.ShapeDtypeStruct(grad_q.shape, BF16),
         input_output_aliases={3: 0},

time: 96.2 us -> 96.2 us (level)
  no operation moved by 1% of the time
where the time goes in v17:
time: 96.2 us; the launch traced here: 94.3 us
  Pallas kernels  47.6 us (49%)
  starting transfers between devices  30.1 us (31%)
  waiting for transfers between devices  12.6 us (13%)
  other arithmetic  2.4 us (2%)
    pallas_call x11, Pallas kernels, call(): pl.pallas_call(kernel, name=name, grid_spec=pltpu.PrefetchScalarGridSpec(...  45.9 us
    ppermute x18, starting transfers between devices, send(): return lax.ppermute(value, 'ctx', pairs)  30.1 us
    ppermute x18, waiting for transfers between devices, send(): return lax.ppermute(value, 'ctx', pairs)  12.6 us
  transfers between devices with their start and end apart: 18, of which 4 were waited for; matrix products, arithmetic and copies ran while one was open for 4% of the time, Pallas kernels for 46%

profile of v17, /device:TPU:1, one launch (start us, length us, event | category | flops | bytes accessed | tf_op | source)
XLA Modules:
  0.0 94.3 jit_solution(15330124269102613914)
XLA Ops:
  0.6 2.3 %pack_cross.1 = (bf16[520,512]{1,0:T(8,128)(2,1)}, bf16[520,512]{1,0:T(8,128)(2,1)}) custom-call(s32[1]{0:T(128)} %bitcast.info, s32[2,4]{1,0:T(2,128)} %bitcast.8, bf16[256,1024]{1,0:T(8,128)(2,1)} %refs_2_.6, bf16[256,1024]{1,0:T(8,128)(2,1)} %refs_3_.6, bf16[256,1024]{1,0:T(8,128)(2,1)} %refs_2_.6, bf16[256,1024]{1,0:T(8,128)(2,1)} %refs_3_.6), custom_call_target="tpu_custom_call" | custom-call | tf_op jit(solution)/shard_map/pack_cross/pallas_call | solution.py:83
  3.0 2.6 %collective-permute-start.3 = (bf16[520,512]{1,0:T(8,128)(2,1)}, bf16[520,512]{1,0:T(8,128)(2,1)}, u32[]{:S(2)}, u32[]{:S(2)}) collective-permute-start(bf16[520,512]{1,0:T(8,128)(2,1)} %get-tuple-element.70), channel_id=1, source_target_pairs={{0,15},{1,2},{2,1},{3,4},{4,3},{5,6},{6,5},{7,8},{8,7},{9,10},{10,... | collective-permute-start | bytes 1597448 | tf_op jit(solution)/shard_map/ppermute | solution.py:38
  6.8 2.2 %pack_swap.1 = bf16[1032,512]{1,0:T(8,128)(2,1)} custom-call(s32[1]{0:T(128)} %bitcast.info, s32[2,4]{1,0:T(2,128)} %bitcast.9, bf16[256,1024]{1,0:T(8,128)(2,1)} %refs_2_.6, bf16[256,1024]{1,0:T(8,128)(2,1)} %refs_3_.6, bf16[2,256,1024]{2,1,0:T(8,128)(2,1)} %bitcast.4), custom_call_target="tpu_custom_call" | custom-call | tf_op jit(solution)/shard_map/pack_swap/pallas_call | solution.py:83
  9.1 2.3 %collective-permute-start = (bf16[1032,512]{1,0:T(8,128)(2,1)}, bf16[1032,512]{1,0:T(8,128)(2,1)}, u32[]{:S(2)}, u32[]{:S(2)}) collective-permute-start(bf16[1032,512]{1,0:T(8,128)(2,1)} %pack_swap.1), channel_id=1, source_target_pairs={{0,1},{1,0},{2,3},{3,2},{4,5},{5,4},{6,7},{7,6},{8,9},{9,8},{10,11... | collective-permute-start | bytes 3170312 | tf_op jit(solution)/shard_map/ppermute | solution.py:38
  11.3 2.6 %pack_self.1 = (bf16[1024,512]{1,0:T(8,128)(2,1)}, bf16[512,512]{1,0:T(8,128)(2,1)}, bf16[512,512]{1,0:T(8,128)(2,1)}) custom-call(s32[1]{0:T(128)} %bitcast.info, bf16[256,1024]{1,0:T(8,128)(2,1)} %refs_1_.3, bf16[256,1024]{1,0:T(8,128)(2,1)} %refs_2_.7, bf16[256,1024]{1,0:T(8,128)(2,1)} %refs_1_.3, bf16[256,1024]{1,0:T(8,128)(2,1)} %refs_2_.7, ...), custom_call_target="tpu_custom_call" | custom-call | tf_op jit(solution)/shard_map/pack_self/pallas_call | solution.py:83
  17.3 4.0 %cross_stats.1 = (f32[4,8,256]{2,1,0:T(8,128)}, f32[4,8,256]{2,1,0:T(8,128)}) custom-call(s32[1]{0:T(128)} %bitcast.info, bf16[520,512]{1,0:T(8,128)(2,1)} %get-tuple-element.63.refs_0_, bf16[1032,512]{1,0:T(8,128)(2,1)} %collective-permute-done.refs_1_.refs_5_.refs_6_.refs_7_.refs_8_, bf16[256,1024]{1,0:T(8,128)(2,1)} %refs_2_.6, ...), custom_call_target="tpu_custom_call" | custom-call | tf_op jit(solution)/shard_map/cross_stats/pallas_call | solution.py:83
  22.9 4.2 %self_stats.1.refs_10_ = f32[4,8,512]{2,1,0:T(8,128)} custom-call(s32[1]{0:T(128)} %bitcast.info, f32[512,512]{1,0:T(8,128)} %and_select_fusion.1.refs_0_, bf16[256,1024]{1,0:T(8,128)(2,1)} %refs_1_.3, bf16[256,1024]{1,0:T(8,128)(2,1)} %refs_2_.7, bf16[256,1024]{1,0:T(8,128)(2,1)} %refs_3_.7, bf16[256,1024]{1,0:T(8,128)(2,1)} %refs_4_.3, ...), custom_call_target="tpu_custom_call" | custom-call | tf_op jit(solution)/shard_map/self_stats/pallas_call | solution.py:83
  27.0 3.3 %collective-permute-done.2.refs_0_.refs_2_.refs_3_ = bf16[520,512]{1,0:T(8,128)(2,1)} collective-permute-done((bf16[520,512]{1,0:T(8,128)(2,1)}, bf16[520,512]{1,0:T(8,128)(2,1)}, u32[]{:S(2)}, u32[]{:S(2)}) %collective-permute-start.2) | collective-permute-done | bytes 532512 | tf_op jit(solution)/shard_map/ppermute | solution.py:38
  30.6 1.3 %collective-permute-start.8 = (bf16[512,512]{1,0:T(8,128)(2,1)}, bf16[512,512]{1,0:T(8,128)(2,1)}, u32[]{:S(2)}, u32[]{:S(2)}) collective-permute-start(bf16[512,512]{1,0:T(8,128)(2,1)} %get-tuple-element.81), channel_id=1, source_target_pairs={{2,0},{3,1},{4,2},{5,3},{6,4},{7,5},{8,6},{9,7},{10,8},{11,9},{12,... | collective-permute-start | bytes 1572872 | tf_op jit(solution)/shard_map/ppermute | solution.py:38
  31.9 1.3 %collective-permute-start.9 = (f32[4,8,512]{2,1,0:T(8,128)}, f32[4,8,512]{2,1,0:T(8,128)}, u32[]{:S(2)}, u32[]{:S(2)}) collective-permute-start(f32[4,8,512]{2,1,0:T(8,128)} %self_stats.1.refs_10_), channel_id=1, source_target_pairs={{2,0},{3,1},{4,2},{5,3},{6,4},{7,5},{8,6},{9,7},{10,8},{11,9},{12,... | collective-permute-start | bytes 196616 | tf_op jit(solution)/shard_map/ppermute | solution.py:38
  33.2 5.9 %cross_remote.1 = (bf16[256,512]{1,0:T(8,128)(2,1)}, bf16[256,512]{1,0:T(8,128)(2,1)}, bf16[1024,512]{1,0:T(8,128)(2,1)}, f32[4,8,256]{2,1,0:T(8,128)}, f32[4,8,256]{2,1,0:T(8,128)}) custom-call(s32[1]{0:T(128)} %bitcast.info, bf16[520,512]{1,0:T(8,128)(2,1)} %collective-permute-done.2.refs_0_.refs_2_.refs_3_, ...), custom_call_target="tpu_custom_call" | custom-call | tf_op jit(solution)/shard_map/cross_remote/pallas_call | solution.py:83
  39.2 8.2 %collective-permute-start.6 = (f32[4,8,256]{2,1,0:T(8,128)}, f32[4,8,256]{2,1,0:T(8,128)}, u32[]{:S(2)}, u32[]{:S(2)}) collective-permute-start(f32[4,8,256]{2,1,0:T(8,128)} %get-tuple-element.76), channel_id=1, source_target_pairs={{0,2},{1,15},{2,4},{3,1},{4,6},{5,3},{6,8},{7,5},{8,10},{9,7},{10,... | collective-permute-start | bytes 98312 | tf_op jit(solution)/shard_map/ppermute | solution.py:38
  47.3 1.3 %collective-permute-start.10 = (bf16[512,512]{1,0:T(8,128)(2,1)}, bf16[512,512]{1,0:T(8,128)(2,1)}, u32[]{:S(2)}, u32[]{:S(2)}) collective-permute-start(bf16[512,512]{1,0:T(8,128)(2,1)} %get-tuple-element.87), channel_id=1, source_target_pairs={{2,1},{3,0},{4,3},{5,2},{6,5},{7,4},{8,7},{9,6},{10,9},{11,8},{12,... | collective-permute-start | bytes 1572872 | tf_op jit(solution)/shard_map/ppermute | solution.py:38
  48.7 4.5 %collective-permute-done.7.refs_10_ = f32[4,8,256]{2,1,0:T(8,128)} collective-permute-done((f32[4,8,256]{2,1,0:T(8,128)}, f32[4,8,256]{2,1,0:T(8,128)}, u32[]{:S(2)}, u32[]{:S(2)}) %collective-permute-start.7) | collective-permute-done | bytes 32800 | tf_op jit(solution)/shard_map/ppermute | solution.py:38
  53.2 6.4 %cross_local.1 = (bf16[768,512]{1,0:T(8,128)(2,1)}, bf16[768,512]{1,0:T(8,128)(2,1)}) custom-call(s32[1]{0:T(128)} %bitcast.info, bf16[520,512]{1,0:T(8,128)(2,1)} %get-tuple-element.63.refs_0_, bf16[1032,512]{1,0:T(8,128)(2,1)} %collective-permute-done.refs_1_.refs_5_.refs_6_.refs_7_.refs_8_, bf16[256,1024]{1,0:T(8,128)(2,1)} %refs_2_.6, ...), custom_call_target="tpu_custom_call" | custom-call | flops 12000000000 | tf_op jit(solution)/shard_map/cross_local/pallas_call | solution.py:83
  59.6 4.4 %collective-permute-done.10.refs_3_.refs_4_ = bf16[512,512]{1,0:T(8,128)(2,1)} collective-permute-done((bf16[512,512]{1,0:T(8,128)(2,1)}, bf16[512,512]{1,0:T(8,128)(2,1)}, u32[]{:S(2)}, u32[]{:S(2)}) %collective-permute-start.10) | collective-permute-done | bytes 524320 | tf_op jit(solution)/shard_map/ppermute | solution.py:38
  64.5 6.6 %self_remote.1 = (bf16[512,512]{1,0:T(8,128)(2,1)}, bf16[1024,512]{1,0:T(8,128)(2,1)}, f32[4,8,512]{2,1,0:T(8,128)}) custom-call(s32[1]{0:T(128)} %bitcast.info, f32[512,512]{1,0:T(8,128)} %and_select_fusion.refs_0_, bf16[512,512]{1,0:T(8,128)(2,1)} %collective-permute-done.8.refs_1_.refs_2_, bf16[512,512]{1,0:T(8,128)(2,1)} %collective-permute-done.8.refs_1_.refs_2_, ...), custom_call_target="tpu_custom_call" | custom-call | flops 12000000000 | tf_op jit(solution)/shard_map/self_remote/pallas_call | solution.py:83
  71.1 4.1 %collective-permute-start.13 = (f32[4,8,512]{2,1,0:T(8,128)}, f32[4,8,512]{2,1,0:T(8,128)}, u32[]{:S(2)}, u32[]{:S(2)}) collective-permute-start(f32[4,8,512]{2,1,0:T(8,128)} %get-tuple-element.97), channel_id=1, source_target_pairs={{0,2},{1,3},{2,4},{3,5},{4,6},{5,7},{6,8},{7,9},{8,10},{9,11},{10,... | collective-permute-start | bytes 196616 | tf_op jit(solution)/shard_map/ppermute | solution.py:38
  75.2 3.0 %collective-permute-start.15 = (bf16[512,512]{1,0:T(8,128)(2,1)}, bf16[512,512]{1,0:T(8,128)(2,1)}, u32[]{:S(2)}, u32[]{:S(2)}) collective-permute-start(bf16[512,512]{1,0:T(8,128)(2,1)} %get-tuple-element.102), channel_id=1, source_target_pairs={{0,2},{1,3},{2,4},{3,5},{4,6},{5,7},{6,8},{7,9},{8,10},{9,11},{10,... | collective-permute-start | bytes 1572872 | tf_op jit(solution)/shard_map/ppermute | solution.py:38
  78.2 1.9 %collective-permute-start.16 = (bf16[768,512]{1,0:T(8,128)(2,1)}, bf16[768,512]{1,0:T(8,128)(2,1)}, u32[]{:S(2)}, u32[]{:S(2)}) collective-permute-start(bf16[768,512]{1,0:T(8,128)(2,1)} %get-tuple-element.104), channel_id=1, source_target_pairs={{0,1},{1,0},{2,3},{3,2},{4,5},{5,4},{6,7},{7,6},{8,9},{9,8},{10,11... | collective-permute-start | bytes 2359304 | tf_op jit(solution)/shard_map/ppermute | solution.py:38
  80.1 6.1 %self_local.1 = (bf16[768,512]{1,0:T(8,128)(2,1)}, bf16[768,512]{1,0:T(8,128)(2,1)}) custom-call(s32[1]{0:T(128)} %bitcast.info, f32[512,512]{1,0:T(8,128)} %and_select_fusion.1.refs_0_, bf16[256,1024]{1,0:T(8,128)(2,1)} %refs_1_.3, bf16[256,1024]{1,0:T(8,128)(2,1)} %refs_2_.7, bf16[256,1024]{1,0:T(8,128)(2,1)} %refs_3_.7, bf16[256,1024]{1,0:T(8,128)(2,1)} %refs_4_.3, ...), custom_call_target="tpu_custom_call" | custom-call | flops 12000000000 | tf_op jit(solution)/shard_map/self_local/pallas_call | solution.py:83
  86.3 2.8 %cross_final.1 = (bf16[256,1024]{1,0:T(8,128)(2,1)}, bf16[2,256,1024]{2,1,0:T(8,128)(2,1)}) custom-call(s32[1]{0:T(128)} %bitcast.info, bf16[768,512]{1,0:T(8,128)(2,1)} %get-tuple-element.103.mine, bf16[768,512]{1,0:T(8,128)(2,1)} %collective-permute-done.16.theirs, bf16[256,512]{1,0:T(8,128)(2,1)} %collective-permute-done.11.dq_mine, ...), custom_call_target="tpu_custom_call" | custom-call | tf_op jit(solution)/shard_map/cross_final/pallas_call | solution.py:83
  89.9 2.7 %kv_final.1 = (bf16[256,1024]{1,0:T(8,128)(2,1)}, bf16[256,1024]{1,0:T(8,128)(2,1)}, bf16[256,1024]{1,0:T(8,128)(2,1)}) custom-call(s32[1]{0:T(128)} %bitcast.info, bf16[768,512]{1,0:T(8,128)(2,1)} %get-tuple-element.109.mine, bf16[768,512]{1,0:T(8,128)(2,1)} %collective-permute-done.14.theirs, bf16[512,512]{1,0:T(8,128)(2,1)} %collective-permute-done.15.dq_mine), custom_call_target="tpu_custom_call" | custom-call | tf_op jit(solution)/shard_map/kv_final/pallas_call | solution.py:83
  92.5 1.8 %query_final.1 = bf16[256,1024]{1,0:T(8,128)(2,1)} custom-call(s32[1]{0:T(128)} %bitcast.info, bf16[768,512]{1,0:T(8,128)(2,1)} %collective-permute-done.14.theirs, bf16[512,512]{1,0:T(8,128)(2,1)} %collective-permute-done.17.dq_theirs, bf16[256,1024]{1,0:T(8,128)(2,1)} %get-tuple-element.110.grad), custom_call_target="tpu_custom_call", output_to_operand_aliasing={{}: (3, {})} | custom-call | tf_op jit(solution)/shard_map/query_final/pallas_call | solution.py:545
  (31 shorter events, 7.9 us)
Async XLA Ops:
  3.0 24.1 %collective-permute-start.3 = (bf16[520,512]{1,0:T(8,128)(2,1)}, bf16[520,512]{1,0:T(8,128)(2,1)}, u32[]{:S(2)}, u32[]{:S(2)}) collective-permute-start(bf16[520,512]{1,0:T(8,128)(2,1)} %get-tuple-element.70), channel_id=1, source_target_pairs={{0,15},{1,2},{2,1},{3,4},{4,3},{5,6},{6,5},{7,8},{8,7},{9,10},{10,... | collective-permute-start | bytes 1597448 | tf_op jit(solution)/shard_map/ppermute | solution.py:38
  5.6 24.7 %collective-permute-start.2 = (bf16[520,512]{1,0:T(8,128)(2,1)}, bf16[520,512]{1,0:T(8,128)(2,1)}, u32[]{:S(2)}, u32[]{:S(2)}) collective-permute-start(bf16[520,512]{1,0:T(8,128)(2,1)} %get-tuple-element.63.refs_0_), channel_id=1, source_target_pairs={{0,14},{1,3},{2,0},{3,5},{4,2},{5,7},{6,4},{7,9},{8,6},{9,11},{10,... | collective-permute-start | bytes 1597448 | tf_op jit(solution)/shard_map/ppermute | solution.py:38
  9.1 8.3 %collective-permute-start = (bf16[1032,512]{1,0:T(8,128)(2,1)}, bf16[1032,512]{1,0:T(8,128)(2,1)}, u32[]{:S(2)}, u32[]{:S(2)}) collective-permute-start(bf16[1032,512]{1,0:T(8,128)(2,1)} %pack_swap.1), channel_id=1, source_target_pairs={{0,1},{1,0},{2,3},{3,2},{4,5},{5,4},{6,7},{7,6},{8,9},{9,8},{10,11... | collective-permute-start | bytes 3170312 | tf_op jit(solution)/shard_map/ppermute | solution.py:38
  13.9 8.9 %collective-permute-start.1 = (bf16[1024,512]{1,0:T(8,128)(2,1)}, bf16[1024,512]{1,0:T(8,128)(2,1)}, u32[]{:S(2)}, u32[]{:S(2)}) collective-permute-start(bf16[1024,512]{1,0:T(8,128)(2,1)} %get-tuple-element.68), channel_id=1, source_target_pairs={{0,1},{1,0},{2,3},{3,2},{4,5},{5,4},{6,7},{7,6},{8,9},{9,8},{10,11... | collective-permute-start | bytes 3145736 | tf_op jit(solution)/shard_map/ppermute | solution.py:38
  21.4 8.9 %collective-permute-start.5 = (f32[4,8,256]{2,1,0:T(8,128)}, f32[4,8,256]{2,1,0:T(8,128)}, u32[]{:S(2)}, u32[]{:S(2)}) collective-permute-start(f32[4,8,256]{2,1,0:T(8,128)} %get-tuple-element.71), channel_id=1, source_target_pairs={{0,2},{1,15},{2,4},{3,1},{4,6},{5,3},{6,8},{7,5},{8,10},{9,7},{10,... | collective-permute-start | bytes 98312 | tf_op jit(solution)/shard_map/ppermute | solution.py:38
  22.5 8.1 %collective-permute-start.4 = (f32[4,8,256]{2,1,0:T(8,128)}, f32[4,8,256]{2,1,0:T(8,128)}, u32[]{:S(2)}, u32[]{:S(2)}) collective-permute-start(f32[4,8,256]{2,1,0:T(8,128)} %get-tuple-element.65), channel_id=1, source_target_pairs={{0,14},{1,3},{2,0},{3,5},{4,2},{5,7},{6,4},{7,9},{8,6},{9,11},{10,... | collective-permute-start | bytes 98312 | tf_op jit(solution)/shard_map/ppermute | solution.py:38
  30.6 18.0 %collective-permute-start.8 = (bf16[512,512]{1,0:T(8,128)(2,1)}, bf16[512,512]{1,0:T(8,128)(2,1)}, u32[]{:S(2)}, u32[]{:S(2)}) collective-permute-start(bf16[512,512]{1,0:T(8,128)(2,1)} %get-tuple-element.81), channel_id=1, source_target_pairs={{2,0},{3,1},{4,2},{5,3},{6,4},{7,5},{8,6},{9,7},{10,8},{11,9},{12,... | collective-permute-start | bytes 1572872 | tf_op jit(solution)/shard_map/ppermute | solution.py:38
  31.9 16.7 %collective-permute-start.9 = (f32[4,8,512]{2,1,0:T(8,128)}, f32[4,8,512]{2,1,0:T(8,128)}, u32[]{:S(2)}, u32[]{:S(2)}) collective-permute-start(f32[4,8,512]{2,1,0:T(8,128)} %self_stats.1.refs_10_), channel_id=1, source_target_pairs={{2,0},{3,1},{4,2},{5,3},{6,4},{7,5},{8,6},{9,7},{10,8},{11,9},{12,... | collective-permute-start | bytes 196616 | tf_op jit(solution)/shard_map/ppermute | solution.py:38
  39.2 9.5 %collective-permute-start.6 = (f32[4,8,256]{2,1,0:T(8,128)}, f32[4,8,256]{2,1,0:T(8,128)}, u32[]{:S(2)}, u32[]{:S(2)}) collective-permute-start(f32[4,8,256]{2,1,0:T(8,128)} %get-tuple-element.76), channel_id=1, source_target_pairs={{0,2},{1,15},{2,4},{3,1},{4,6},{5,3},{6,8},{7,5},{8,10},{9,7},{10,... | collective-permute-start | bytes 98312 | tf_op jit(solution)/shard_map/ppermute | solution.py:38
  47.3 5.9 %collective-permute-start.7 = (f32[4,8,256]{2,1,0:T(8,128)}, f32[4,8,256]{2,1,0:T(8,128)}, u32[]{:S(2)}, u32[]{:S(2)}) collective-permute-start(f32[4,8,256]{2,1,0:T(8,128)} %get-tuple-element.77), channel_id=1, source_target_pairs={{0,14},{1,3},{2,0},{3,5},{4,2},{5,7},{6,4},{7,9},{8,6},{9,11},{10,... | collective-permute-start | bytes 98312 | tf_op jit(solution)/shard_map/ppermute | solution.py:38
  47.3 16.6 %collective-permute-start.10 = (bf16[512,512]{1,0:T(8,128)(2,1)}, bf16[512,512]{1,0:T(8,128)(2,1)}, u32[]{:S(2)}, u32[]{:S(2)}) collective-permute-start(bf16[512,512]{1,0:T(8,128)(2,1)} %get-tuple-element.87), channel_id=1, source_target_pairs={{2,1},{3,0},{4,3},{5,2},{6,5},{7,4},{8,7},{9,6},{10,9},{11,8},{12,... | collective-permute-start | bytes 1572872 | tf_op jit(solution)/shard_map/ppermute | solution.py:38
  64.0 14.3 %collective-permute-start.11 = (bf16[256,512]{1,0:T(8,128)(2,1)}, bf16[256,512]{1,0:T(8,128)(2,1)}, u32[]{:S(2)}, u32[]{:S(2)}) collective-permute-start(bf16[256,512]{1,0:T(8,128)(2,1)} %get-tuple-element.95), channel_id=1, source_target_pairs={{0,2},{1,15},{2,4},{3,1},{4,6},{5,3},{6,8},{7,5},{8,10},{9,7},{10,... | collective-permute-start | bytes 786440 | tf_op jit(solution)/shard_map/ppermute | solution.py:38
  64.0 14.3 %collective-permute-start.12 = (bf16[256,512]{1,0:T(8,128)(2,1)}, bf16[256,512]{1,0:T(8,128)(2,1)}, u32[]{:S(2)}, u32[]{:S(2)}) collective-permute-start(bf16[256,512]{1,0:T(8,128)(2,1)} %get-tuple-element.96), channel_id=1, source_target_pairs={{0,15},{1,2},{2,1},{3,4},{4,3},{5,6},{6,5},{7,8},{8,7},{9,10},{10,... | collective-permute-start | bytes 786440 | tf_op jit(solution)/shard_map/ppermute | solution.py:38
  71.1 7.1 %collective-permute-start.13 = (f32[4,8,512]{2,1,0:T(8,128)}, f32[4,8,512]{2,1,0:T(8,128)}, u32[]{:S(2)}, u32[]{:S(2)}) collective-permute-start(f32[4,8,512]{2,1,0:T(8,128)} %get-tuple-element.97), channel_id=1, source_target_pairs={{0,2},{1,3},{2,4},{3,5},{4,6},{5,7},{6,8},{7,9},{8,10},{9,11},{10,... | collective-permute-start | bytes 196616 | tf_op jit(solution)/shard_map/ppermute | solution.py:38
  75.2 13.9 %collective-permute-start.15 = (bf16[512,512]{1,0:T(8,128)(2,1)}, bf16[512,512]{1,0:T(8,128)(2,1)}, u32[]{:S(2)}, u32[]{:S(2)}) collective-permute-start(bf16[512,512]{1,0:T(8,128)(2,1)} %get-tuple-element.102), channel_id=1, source_target_pairs={{0,2},{1,3},{2,4},{3,5},{4,6},{5,7},{6,8},{7,9},{8,10},{9,11},{10,... | collective-permute-start | bytes 1572872 | tf_op jit(solution)/shard_map/ppermute | solution.py:38
  78.2 8.1 %collective-permute-start.16 = (bf16[768,512]{1,0:T(8,128)(2,1)}, bf16[768,512]{1,0:T(8,128)(2,1)}, u32[]{:S(2)}, u32[]{:S(2)}) collective-permute-start(bf16[768,512]{1,0:T(8,128)(2,1)} %get-tuple-element.104), channel_id=1, source_target_pairs={{0,1},{1,0},{2,3},{3,2},{4,5},{5,4},{6,7},{7,6},{8,9},{9,8},{10,11... | collective-permute-start | bytes 2359304 | tf_op jit(solution)/shard_map/ppermute | solution.py:38
  86.2 3.7 %collective-permute-start.14 = (bf16[768,512]{1,0:T(8,128)(2,1)}, bf16[768,512]{1,0:T(8,128)(2,1)}, u32[]{:S(2)}, u32[]{:S(2)}) collective-permute-start(bf16[768,512]{1,0:T(8,128)(2,1)} %get-tuple-element.101), channel_id=1, source_target_pairs={{0,1},{1,0},{2,3},{3,2},{4,5},{5,4},{6,7},{7,6},{8,9},{9,8},{10,11... | collective-permute-start | bytes 2359304 | tf_op jit(solution)/shard_map/ppermute | solution.py:38
  89.1 3.4 %collective-permute-start.17 = (bf16[512,512]{1,0:T(8,128)(2,1)}, bf16[512,512]{1,0:T(8,128)(2,1)}, u32[]{:S(2)}, u32[]{:S(2)}) collective-permute-start(bf16[512,512]{1,0:T(8,128)(2,1)} %collective-permute-done.15.dq_mine), channel_id=1, source_target_pairs={{0,1},{1,0},{2,3},{3,2},{4,5},{5,4},{6,7},{7,6},{8,9},{9,8},{10,11... | collective-permute-start | bytes 1572872 | tf_op jit(solution)/shard_map/ppermute | solution.py:38
